TPU v7x, 512 devices: a whole 4x8x8 slice. The times are simulated.
512 devices in a mesh: dp: 32 (over x, y), segment: 2 (over core), mp: 8 (over z).
Axes of the slice: x: 4, y: 8, z: 8, core: 2. Of those that a mesh axis runs over, the one named last changes fastest.
Arguments:
- frames: bfloat16 [2, 8192, 1280], P(None, ('dp', 'mp')), may hold values from -8 to 8
- dec_states: bfloat16 [2, 2048, 1280], P(None, 'dp'), may hold values from -8 to 8
- out_grad: bfloat16 [2, 2048, 1280], P(None, 'dp'), may hold values from -3 to 3
- frame_lengths: int32 [2, 32, 4], P(None, 'dp'), may hold values from 1 to 128, 256 in all within a row
- token_lengths: int32 [2, 32, 4], P(None, 'dp'), may hold values from 1 to 32, 64 in all within a row
- weights: bfloat16 [2, 4, 1024, 1280], P('segment', None, 'mp'), may hold values from -1 to 1
- norm_gains: float32 [3, 1280], replicated, may hold values from 0.25 to 1.75
- norm_biases: float32 [3, 1280], replicated, may hold values from -2 to 2
Outputs:
- gradient: float32 [2, 3, 1024, 1280], P('segment', None, 'mp')
Inputs may be any that keep to these rules, and one draw needn't show every extreme that they name: `frame_lengths`: the 4 utterance lengths of each micro-batch and group sum to 256. `token_lengths`: the 4 token counts of each micro-batch and group sum to 64.
All inputs are finite; a program needn't handle non-finite values.
Results may differ from a plain program's by a relative error of at most 0.04.
Values may be sent and summed in bfloat16 or wider, within the bound.
No kernel may reach another device: no remote copies, remote signals or barrier semaphores. Data moves between devices by JAX's collectives and lax.ppermute only.
A program may use at most 64 MiB of HBM per device.

v0:
```python
import math

import jax
import jax.numpy as jnp
from jax import lax
from jax.sharding import PartitionSpec as P

HS = 64


EPSILON = 1e-05
ROWS_DIMS = (((0,), (0,)), ((), ()))
FEAT_DIMS = (((1,), (1,)), ((), ()))


def partner(shard, axis, apart):
    return lax.ppermute(shard, axis, [(i, i ^ 1 << apart) for i in range(lax.axis_size(axis))])


def layer_norm(values, norm_gain, offset):
    center = values - jnp.mean(values, axis=-1, keepdims=True)
    variance = jnp.mean(center * center, axis=-1, keepdims=True)
    return center * lax.rsqrt(variance + EPSILON) * norm_gain + offset


def norm_backward(grad_out, values, norm_gain):
    center = values - jnp.mean(values, axis=-1, keepdims=True)
    variance = jnp.mean(center * center, axis=-1, keepdims=True)
    inverse = lax.rsqrt(variance + EPSILON)
    normed = center * inverse
    scaled = grad_out * norm_gain
    return inverse * (
        scaled
        - jnp.mean(scaled, axis=-1, keepdims=True)
        - normed * jnp.mean(scaled * normed, axis=-1, keepdims=True)
    )


def utterance_ids(lengths, row_count):
    bounds = jnp.cumsum(lengths, axis=1, dtype=jnp.int32)
    places = jnp.arange(row_count, dtype=jnp.int32)
    local_ids = jnp.sum((places[None, :, None] >= bounds[:, None, :]).astype(jnp.int32), axis=2)
    offsets = jnp.arange(lengths.shape[0], dtype=jnp.int32)[:, None] * lengths.shape[1]
    return (local_ids + offsets).reshape(-1)


def project(row_block, matrix):
    return lax.dot_general(row_block, matrix, FEAT_DIMS, preferred_element_type=jnp.float32).astype(
        jnp.bfloat16
    )


def outer_rows(left_rows, right_rows):
    return lax.dot_general(left_rows, right_rows, ROWS_DIMS, preferred_element_type=jnp.float32)


def split_heads(row_block):
    return row_block.reshape(row_block.shape[0], -1, HS)


def attend(queries, key_rows, value_rows, allowed):
    scaling = 1.0 / math.sqrt(HS)
    scores = (
        jnp.einsum(
            "qhd,khd->hqk",
            split_heads(queries),
            split_heads(key_rows),
            preferred_element_type=jnp.float32,
        )
        * scaling
    )
    scores = jnp.where(allowed[None], scores, -1e30)
    highest = jnp.max(scores, axis=-1, keepdims=True)
    raised = jnp.exp(scores - highest)
    attn_probs = raised / jnp.sum(raised, axis=-1, keepdims=True)
    context = jnp.einsum(
        "hqk,khd->qhd",
        attn_probs.astype(jnp.bfloat16),
        split_heads(value_rows),
        preferred_element_type=jnp.float32,
    )
    return (context.reshape(queries.shape[0], -1).astype(jnp.bfloat16), attn_probs)


def attend_backward(queries, key_rows, value_rows, attn_probs, grad_context):
    scaling = 1.0 / math.sqrt(HS)
    grad_heads = split_heads(grad_context)
    grad_probs = jnp.einsum(
        "qhd,khd->hqk", grad_heads, split_heads(value_rows), preferred_element_type=jnp.float32
    )
    grad_scores = (
        attn_probs * (grad_probs - jnp.sum(grad_probs * attn_probs, axis=-1, keepdims=True))
    ).astype(jnp.bfloat16)
    key_grad = (
        jnp.einsum(
            "hqk,qhd->khd", grad_scores, split_heads(queries), preferred_element_type=jnp.float32
        )
        * scaling
    )
    key_grad = key_grad.reshape(key_rows.shape[0], -1).astype(jnp.bfloat16)
    value_grad = jnp.einsum(
        "hqk,qhd->khd",
        attn_probs.astype(jnp.bfloat16),
        grad_heads,
        preferred_element_type=jnp.float32,
    )
    value_grad = value_grad.reshape(key_rows.shape[0], -1).astype(jnp.bfloat16)
    return (key_grad, value_grad)


def shards(
    frames, dec_states, out_grad, frame_lengths, token_lengths, weights, norm_gains, norm_biases
):
    is_encoder = lax.axis_index("segment") == 0
    matrices = weights[0]
    micro_count = frames.shape[0]
    shard_rows = frames.shape[1]
    features = frames.shape[2]
    head_cols = matrices.shape[1]
    head_count = head_cols // HS
    frame_count = shard_rows * lax.axis_size("mp")
    token_count = dec_states.shape[1]
    unit_count = micro_count // micro_count
    unit_rows = micro_count * frame_count
    received = jnp.zeros((micro_count, shard_rows, features), jnp.bfloat16)

    def empty_state():
        return (
            jnp.zeros((unit_rows, features), jnp.bfloat16),
            jnp.zeros((unit_rows, head_cols), jnp.bfloat16),
            jnp.zeros((unit_rows, head_cols), jnp.bfloat16),
            jnp.zeros((unit_rows, head_cols), jnp.bfloat16),
            jnp.zeros((unit_rows, head_cols), jnp.bfloat16),
            jnp.zeros((head_count, unit_rows, unit_rows), jnp.float32),
        )

    stored = {}
    totals = jnp.zeros((3, head_cols, features), jnp.float32)
    for moment in range(unit_count + 2):
        run_enc = moment < unit_count
        run_dec = 1 <= moment <= unit_count
        run_back = moment >= 2
        if run_enc:
            inputs = frames
        else:
            inputs = jnp.zeros((micro_count, shard_rows, features), jnp.bfloat16)
        enc_full, dec_full = (
            lax.all_gather(inputs, "mp", axis=1, tiled=True),
            lax.all_gather(received, "mp", axis=1, tiled=True),
        )

        def encoder_part():
            partial_value = jnp.zeros((unit_rows, features), jnp.float32)
            grad_step = jnp.zeros((3, head_cols, features), jnp.float32)
            saved_state = empty_state()
            if run_enc:
                lengths = frame_lengths[moment * micro_count : (moment + 1) * micro_count, 0]
                frame_ids = utterance_ids(lengths, frame_count)
                row_input = enc_full.reshape(unit_rows, features)
                normed = layer_norm(
                    row_input.astype(jnp.float32), norm_gains[0], norm_biases[0]
                ).astype(jnp.bfloat16)
                queries = project(normed, matrices[0])
                key_rows = project(normed, matrices[1])
                value_rows = project(normed, matrices[2])
                context, attn_probs = attend(
                    queries, key_rows, value_rows, frame_ids[:, None] == frame_ids[None, :]
                )
                partial_value = jnp.dot(context, matrices[3], preferred_element_type=jnp.float32)
                saved_state = (normed, queries, key_rows, value_rows, context, attn_probs)
            if run_back:
                normed_old, queries_old, keys_old, values_old, context_old, probs_old = stored[
                    moment - 2
                ]
                grad_rows = dec_full.reshape(unit_rows, features)
                out_weight_grad = outer_rows(context_old, grad_rows)
                grad_context = project(grad_rows, matrices[3])
                key_grad, value_grad = attend_backward(
                    queries_old, keys_old, values_old, probs_old, grad_context
                )
                grad_step = jnp.stack(
                    [
                        outer_rows(key_grad, normed_old),
                        outer_rows(value_grad, normed_old),
                        out_weight_grad,
                    ]
                )
            return (partial_value, grad_step, saved_state)

        def decoder_part():
            partial_value = jnp.zeros((unit_rows, features), jnp.float32)
            grad_step = jnp.zeros((3, head_cols, features), jnp.float32)
            if run_dec:
                batch_index = moment - 1
                first_micro = batch_index * micro_count
                frame_ids = utterance_ids(
                    frame_lengths[first_micro : first_micro + micro_count, 0], frame_count
                )
                token_ids = utterance_ids(
                    token_lengths[first_micro : first_micro + micro_count, 0], token_count
                )
                tokens = dec_states.reshape(micro_count * token_count, features)
                upstream = out_grad.reshape(micro_count * token_count, features)
                states_in = dec_full.reshape(unit_rows, features)
                normed = layer_norm(
                    states_in.astype(jnp.float32), norm_gains[2], norm_biases[2]
                ).astype(jnp.bfloat16)
                token_normed = layer_norm(
                    tokens.astype(jnp.float32), norm_gains[1], norm_biases[1]
                ).astype(jnp.bfloat16)
                queries = project(token_normed, matrices[0])
                key_rows = project(normed, matrices[1])
                value_rows = project(normed, matrices[2])
                context, attn_probs = attend(
                    queries, key_rows, value_rows, token_ids[:, None] == frame_ids[None, :]
                )
                grad_context = project(upstream, matrices[3])
                out_weight_grad = outer_rows(context, upstream)
                key_grad, value_grad = attend_backward(
                    queries, key_rows, value_rows, attn_probs, grad_context
                )
                grad_step = jnp.stack(
                    [outer_rows(key_grad, normed), outer_rows(value_grad, normed), out_weight_grad]
                )
                partial_value = jnp.dot(
                    key_grad, matrices[1], preferred_element_type=jnp.float32
                ) + jnp.dot(value_grad, matrices[2], preferred_element_type=jnp.float32)
            return (partial_value, grad_step, empty_state())

        partial_value, grad_step, saved_state = lax.cond(is_encoder, encoder_part, decoder_part)
        totals = totals + grad_step
        if run_enc:
            stored[moment] = saved_state
        if run_enc or run_dec:
            partial_value = partial_value.reshape(micro_count, frame_count, features)
            summed = lax.psum_scatter(
                partial_value.astype(jnp.bfloat16), "mp", scatter_dimension=1, tiled=True
            ).astype(jnp.float32)
            states_out = (inputs.astype(jnp.float32) + summed).astype(jnp.bfloat16)
            grads_out = norm_backward(summed, received.astype(jnp.float32), norm_gains[2]).astype(
                jnp.bfloat16
            )
            received = partner(jnp.where(is_encoder, states_out, grads_out), "segment", 0)
    gradient = lax.psum(totals.astype(jnp.bfloat16), "dp").astype(jnp.float32)
    return gradient[None]


def solution(mesh):
    placed = (
        P(None, ("dp", "mp"), None),
        P(None, "dp", None),
        P(None, "dp", None),
        P(None, "dp", None),
        P(None, "dp", None),
        P("segment", None, "mp", None),
        P(),
        P(),
    )
    return jax.shard_map(
        shards,
        mesh=mesh,
        in_specs=placed,
        out_specs=P("segment", None, "mp", None),
        check_vma=False,
    )
```

profile of v0, /device:TPU:1, one launch (start us, length us, event | category | flops | bytes accessed | tf_op | source)
XLA Modules:
  0.0 462.3 jit_solution(17567042108536954914)
XLA Ops:
  6.5 0.7 all-gather.4.cloned.1.call-update
  7.3 45.8 %all-gather.4.cloned.1.call-done = bf16[2,256,1280]{2,1,0:T(8,128)(2,1)} async-done(((bf16[2,32,1280]{2,1,0:T(8,128)(2,1)}), bf16[2,256,1280]{2,1,0:T(8,128)(2,1)}) %all-gather.4.cloned.1.call-update) | async-done | bytes 1310736 | tf_op jit(solution)/shard_map/all_gather | solution.py:148
  53.1 3.9 conditional.3
  53.1 1.1 broadcast.378
  54.3 0.2 broadcast.381
  54.5 1.2 broadcast.379
  55.7 0.7 broadcast.380
  56.4 0.7 broadcast.380.clone.1
  57.1 0.8 slice_reduce_fusion.6
  57.9 58.5 %reduce-scatter.3.cloned.1.call-done = bf16[2,32,1280]{2,1,0:T(8,128)(2,1)} async-done(((bf16[2,256,1280]{2,1,0:T(8,128)(2,1)}), bf16[2,32,1280]{2,1,0:T(8,128)(2,1)}) %reduce-scatter.3.cloned.1.call-update) | async-done | bytes 163856 | tf_op jit(solution)/shard_map/reduce_scatter | solution.py:236
  116.4 1.0 fusion.69
  117.5 1.1 fusion.86
  118.6 6.9 %collective-permute-start = (bf16[2,32,1280]{2,1,0:T(8,128)(2,1)S(1)}, bf16[2,32,1280]{2,1,0:T(8,128)(2,1)S(1)}, u32[]{:S(2)}, u32[]{:S(2)}) collective-permute-start(bf16[2,32,1280]{2,1,0:T(8,128)(2,1)S(1)} %fusion.86), channel_id=1, source_target_pairs={{0,8},{8,0},{1,9},{9,1},{2,10},{10,2},{3,11},{11,3},{4,12},{12,4},... | collective-permute-start | bytes 491528 | tf_op jit(solution)/shard_map/ppermute | solution.py:17
  125.5 1.0 collective-permute-done
  126.5 0.7 copy-done.4
  127.2 36.1 %all-gather.6.cloned.1.call-done = bf16[2,256,1280]{2,1,0:T(8,128)(2,1)} async-done(((bf16[2,32,1280]{2,1,0:T(8,128)(2,1)}), bf16[2,256,1280]{2,1,0:T(8,128)(2,1)}) %all-gather.6.cloned.1.call-update) | async-done | bytes 1310736 | tf_op jit(solution)/shard_map/all_gather | solution.py:149
  163.3 35.1 %conditional.4 = (bf16[512,1280]{1,0:T(8,128)(2,1)}, f32[3,128,1280]{2,1,0:T(8,128)}) conditional(s32[]{:T(128)} %convert_element_type.217, (bf16[2,64,1280]{2,1,0:T(8,128)(2,1)S(1)}, f32[3,1280]{1,0:T(4,128)S(1)}, f32[3,1280]{1,0:T(4,128)S(1)}, bf16[4,128,1280]{2,1,0:T(8,128)(2,1)}, s32[2,1,4]{2,1,0:T(1,128)}, ...), branch_computations={%region_11.23_spmd, %region_23.24_spmd} | conditional | flops 1282403072 | bytes 40412088 | solution.py:230
  163.3 0.1 slice_reduce_fusion.2
  163.4 0.1 convert_reduce_fusion.3
  163.5 0.2 fusion.43
  163.8 0.3 fusion.46
  164.0 1.8 convolution_convert_fusion.10
  165.9 0.2 convert_reduce_fusion.2
  166.1 0.5 fusion.33
  166.6 0.6 fusion.36
  167.2 2.2 convolution_convert_fusion.8
  169.4 0.2 reduce_window_sum.21
  169.6 0.1 convert_reduce_fusion.4
  169.7 0.1 add_bitcast_fusion.1
  169.7 0.4 copy-done.18
  170.2 0.8 reduce_window_sum.19
  171.0 0.1 convert_reduce_fusion.5
  171.1 0.7 broadcast_add_fusion
  171.8 0.6 add.144
  172.4 1.4 broadcast_compare_fusion.1
  173.8 2.1 fusion.88
  175.9 1.4 convolution_convert_fusion.9
  177.3 1.5 convolution_convert_fusion.7
  178.8 0.6 copy-done.19
  179.5 1.1 multiply_reduce_fusion.2
  180.5 2.5 fusion.40
  183.0 3.1 fusion.50
  186.1 2.2 convolution_convert_fusion.6
  188.3 3.5 convolution_add_fusion
  191.9 2.3 convolution_convert_fusion.11
  194.1 1.3 convolution_bitcast_fusion.3
  195.4 1.2 convolution_bitcast_fusion.4
  196.7 0.3 convolution_bitcast_fusion.5
  197.0 1.4 pad_maximum_fusion.1
  198.5 0.2 all-gather.8.cloned.1.call-start
  198.7 1.0 convert_reduce_fusion.6
  199.7 1.1 fusion.78
  200.8 34.5 %reduce-scatter.5.cloned.1.call-done = bf16[2,32,1280]{2,1,0:T(8,128)(2,1)} async-done(((bf16[2,256,1280]{2,1,0:T(8,128)(2,1)}), bf16[2,32,1280]{2,1,0:T(8,128)(2,1)}) %reduce-scatter.5.cloned.1.call-update) | async-done | bytes 163856 | tf_op jit(solution)/shard_map/reduce_scatter | solution.py:236
  235.4 1.2 fusion.84
  236.6 1.2 fusion.85
  237.8 6.9 %collective-permute-start.1 = (bf16[2,32,1280]{2,1,0:T(8,128)(2,1)S(1)}, bf16[2,32,1280]{2,1,0:T(8,128)(2,1)S(1)}, u32[]{:S(2)}, u32[]{:S(2)}) collective-permute-start(bf16[2,32,1280]{2,1,0:T(8,128)(2,1)S(1)} %fusion.85), channel_id=1, source_target_pairs={{0,8},{8,0},{1,9},{9,1},{2,10},{10,2},{3,11},{11,3},{4,12},{12,4},... | collective-permute-start | bytes 491528 | tf_op jit(solution)/shard_map/ppermute | solution.py:17
  244.7 1.0 collective-permute-done.1
  245.7 0.7 copy-done.11
  246.4 36.0 %all-gather.8.cloned.1.call-done = bf16[2,256,1280]{2,1,0:T(8,128)(2,1)} async-done(((bf16[2,32,1280]{2,1,0:T(8,128)(2,1)}), bf16[2,256,1280]{2,1,0:T(8,128)(2,1)}) %all-gather.8.cloned.1.call-update) | async-done | bytes 1310736 | tf_op jit(solution)/shard_map/all_gather | solution.py:149
  282.4 0.2 conditional.5
  282.4 0.1 broadcast.395
  282.6 2.7 fusion.66
  285.3 167.5 %all-reduce.2.cloned.1.call-done = bf16[1,3,128,1280]{3,2,1,0:T(8,128)(2,1)} async-done(((bf16[1,3,128,1280]{3,2,1,0:T(8,128)(2,1)}), bf16[1,3,128,1280]{3,2,1,0:T(8,128)(2,1)}) %all-reduce.2.cloned.1.call-update) | async-done | bytes 983056 | tf_op jit(solution)/shard_map/psum | solution.py:244
  452.9 2.6 broadcast_in_dim.37
  (44 shorter events, 0.4 us)
Async XLA Ops:
  6.5 46.6 %all-gather.4.cloned.1.call-start = ((), (), s32[]{:S(2)}) async-start(), calls=%async_computation.2 | async-start | bytes 1474560 | tf_op jit(solution)/shard_map/all_gather | solution.py:148
  7.3 109.2 %reduce-scatter.3.cloned.1.call-start = ((), (), s32[]{:S(2)}) async-start(), calls=%async_computation.3 | async-start | bytes 1474560 | tf_op jit(solution)/shard_map/reduce_scatter | solution.py:236
  57.0 106.2 %copy-start.6 = (bf16[2,64,1280]{2,1,0:T(8,128)(2,1)S(1)}, bf16[2,64,1280]{2,1,0:T(8,128)(2,1)}, u32[]{:S(2)}) copy-start(bf16[2,64,1280]{2,1,0:T(8,128)(2,1)} %param.15) | copy-start | bytes 983044
  57.0 106.2 %copy-start.12 = (f32[3,1280]{1,0:T(4,128)S(1)}, f32[3,1280]{1,0:T(4,128)}, u32[]{:S(2)}) copy-start(f32[3,1280]{1,0:T(4,128)} %param.20) | copy-start | bytes 46084
  57.0 106.2 %copy-start.13 = (f32[3,1280]{1,0:T(4,128)S(1)}, f32[3,1280]{1,0:T(4,128)}, u32[]{:S(2)}) copy-start(f32[3,1280]{1,0:T(4,128)} %param.21) | copy-start | bytes 46084
  57.0 106.2 %copy-start.16 = (s32[2,1,4]{2,1,0:T(1,128)S(1)}, s32[2,1,4]{2,1,0:T(1,128)}, u32[]{:S(2)}) copy-start(s32[2,1,4]{2,1,0:T(1,128)} %param.17) | copy-start | bytes 100
  57.1 106.2 %all-gather.6.cloned.1.call-start = ((), (), s32[]{:S(2)}) async-start(), calls=%async_computation.4 | async-start | bytes 1474560 | tf_op jit(solution)/shard_map/all_gather | solution.py:149
  118.6 7.9 %collective-permute-start = (bf16[2,32,1280]{2,1,0:T(8,128)(2,1)S(1)}, bf16[2,32,1280]{2,1,0:T(8,128)(2,1)S(1)}, u32[]{:S(2)}, u32[]{:S(2)}) collective-permute-start(bf16[2,32,1280]{2,1,0:T(8,128)(2,1)S(1)} %fusion.86), channel_id=1, source_target_pairs={{0,8},{8,0},{1,9},{9,1},{2,10},{10,2},{3,11},{11,3},{4,12},{12,4},... | collective-permute-start | bytes 491528 | tf_op jit(solution)/shard_map/ppermute | solution.py:17
  126.5 0.7 copy-start.4
  127.2 108.2 %reduce-scatter.5.cloned.1.call-start = ((), (), s32[]{:S(2)}) async-start(), calls=%async_computation.5 | async-start | bytes 1474560 | tf_op jit(solution)/shard_map/reduce_scatter | solution.py:236
  163.3 2.6 copy-start.3
  169.7 0.5 copy-start.18
  175.9 3.6 copy-start.21
  177.3 3.3 copy-start.20
  178.8 0.7 copy-start.19
  194.1 2.5 copy-start.10
  198.4 38.1 %copy-start.5 = (bf16[2,32,1280]{2,1,0:T(8,128)(2,1)S(1)}, bf16[2,32,1280]{2,1,0:T(8,128)(2,1)}, u32[]{:S(2)}) copy-start(bf16[2,32,1280]{2,1,0:T(8,128)(2,1)} %copy-done.4) | copy-start | bytes 491524
  198.5 83.9 %all-gather.8.cloned.1.call-start = ((), (), s32[]{:S(2)}) async-start(), calls=%async_computation.6 | async-start | bytes 1474560 | tf_op jit(solution)/shard_map/all_gather | solution.py:149
  237.8 7.9 %collective-permute-start.1 = (bf16[2,32,1280]{2,1,0:T(8,128)(2,1)S(1)}, bf16[2,32,1280]{2,1,0:T(8,128)(2,1)S(1)}, u32[]{:S(2)}, u32[]{:S(2)}) collective-permute-start(bf16[2,32,1280]{2,1,0:T(8,128)(2,1)S(1)} %fusion.85), channel_id=1, source_target_pairs={{0,8},{8,0},{1,9},{9,1},{2,10},{10,2},{3,11},{11,3},{4,12},{12,4},... | collective-permute-start | bytes 491528 | tf_op jit(solution)/shard_map/ppermute | solution.py:17
  245.7 0.7 copy-start.11
  246.4 206.5 %all-reduce.2.cloned.1.call-start = ((), (), s32[]{:S(2)}) async-start(), calls=%async_computation.7 | async-start | bytes 1966080 | tf_op jit(solution)/shard_map/psum | solution.py:244
Sparse Core Ops, SparseCore 0:
  9.4 43.6 all-gather.3
  57.2 59.1 reduce-scatter.2
  127.3 35.9 all-gather.5
  198.6 36.7 reduce-scatter.4
  246.5 35.8 all-gather.7
  285.7 167.1 all-reduce.1
where the time goes:
time: 466 us; the launch traced here: 462 us
  waiting for transfers between devices  381 us (82%)
  matrix products  26.5 us (6%)
  other arithmetic  18.8 us (4%)
  starting transfers between devices  14.1 us (3%)
  between operations  13.5 us (3%)
  local copies, waits for them, and re-layouts  7.95 us (2%)
    psum x1, waiting for transfers between devices, shards(): gradient = lax.psum(totals.astype(jnp.bfloat16), 'dp').astype(jnp.float32)  168 us
    reduce_scatter x2, waiting for transfers between devices, shards(): lax.psum_scatter(partial_value.astype(jnp.bfloat16), 'mp', scatter_dimens...  93 us
    all_gather x2, waiting for transfers between devices, shards(): lax.all_gather(received, 'mp', axis=1, tiled=True)  72.1 us
    all_gather x1, waiting for transfers between devices, shards(): lax.all_gather(inputs, 'mp', axis=1, tiled=True)  45.8 us
    ppermute x2, starting transfers between devices, partner(): lax.ppermute(shard, axis, [(i, i ^ 1 << apart) for i in range(lax.axis_si...  13.7 us
  transfers between devices with their start and end apart: 8, of which 8 were waited for; matrix products, arithmetic and copies ran while one was open for 1% of the time, Pallas kernels for 0%

commit v1 on v0

v1 whole, which is shorter than its diff:
```python
import math

import jax
import jax.numpy as jnp
from jax import lax
from jax.sharding import PartitionSpec as P

HS = 64
EPSILON = 1e-05
ROWS_DIMS = (((0,), (0,)), ((), ()))
FEAT_DIMS = (((1,), (1,)), ((), ()))


def layer_norm(values, norm_gain, offset):
    center = values - jnp.mean(values, axis=-1, keepdims=True)
    variance = jnp.mean(center * center, axis=-1, keepdims=True)
    return center * lax.rsqrt(variance + EPSILON) * norm_gain + offset


def norm_backward(grad_out, values, norm_gain):
    center = values - jnp.mean(values, axis=-1, keepdims=True)
    variance = jnp.mean(center * center, axis=-1, keepdims=True)
    inverse = lax.rsqrt(variance + EPSILON)
    normed = center * inverse
    scaled = grad_out * norm_gain
    return inverse * (
        scaled
        - jnp.mean(scaled, axis=-1, keepdims=True)
        - normed * jnp.mean(scaled * normed, axis=-1, keepdims=True)
    )


def utterance_ids(lengths, row_count):
    bounds = jnp.cumsum(lengths, dtype=jnp.int32)
    places = jnp.arange(row_count, dtype=jnp.int32)
    return jnp.sum((places[:, None] >= bounds[None, :]).astype(jnp.int32), axis=1)


def project(row_block, matrix):
    return lax.dot_general(row_block, matrix, FEAT_DIMS, preferred_element_type=jnp.float32).astype(
        jnp.bfloat16
    )


def outer_rows(left_rows, right_rows):
    return lax.dot_general(left_rows, right_rows, ROWS_DIMS, preferred_element_type=jnp.float32)


def split_heads(row_block):
    return row_block.reshape(row_block.shape[0], -1, HS)


def attend(queries, key_rows, value_rows, allowed):
    scaling = 1.0 / math.sqrt(HS)
    scores = (
        jnp.einsum(
            "qhd,khd->hqk",
            split_heads(queries),
            split_heads(key_rows),
            preferred_element_type=jnp.float32,
        )
        * scaling
    )
    scores = jnp.where(allowed[None], scores, -1e30)
    highest = jnp.max(scores, axis=-1, keepdims=True)
    raised = jnp.exp(scores - highest)
    attn_probs = raised / jnp.sum(raised, axis=-1, keepdims=True)
    context = jnp.einsum(
        "hqk,khd->qhd",
        attn_probs.astype(jnp.bfloat16),
        split_heads(value_rows),
        preferred_element_type=jnp.float32,
    )
    return (context.reshape(queries.shape[0], -1).astype(jnp.bfloat16), attn_probs)


def attend_backward(queries, key_rows, value_rows, attn_probs, grad_context):
    scaling = 1.0 / math.sqrt(HS)
    grad_heads = split_heads(grad_context)
    grad_probs = jnp.einsum(
        "qhd,khd->hqk", grad_heads, split_heads(value_rows), preferred_element_type=jnp.float32
    )
    grad_scores = (
        attn_probs * (grad_probs - jnp.sum(grad_probs * attn_probs, axis=-1, keepdims=True))
    ).astype(jnp.bfloat16)
    key_grad = (
        jnp.einsum(
            "hqk,qhd->khd", grad_scores, split_heads(queries), preferred_element_type=jnp.float32
        )
        * scaling
    )
    key_grad = key_grad.reshape(key_rows.shape[0], -1).astype(jnp.bfloat16)
    value_grad = jnp.einsum(
        "hqk,qhd->khd",
        attn_probs.astype(jnp.bfloat16),
        grad_heads,
        preferred_element_type=jnp.float32,
    )
    value_grad = value_grad.reshape(key_rows.shape[0], -1).astype(jnp.bfloat16)
    return (key_grad, value_grad)


def spread(block, axis):
    size = lax.axis_size(axis)
    return lax.all_to_all(jnp.broadcast_to(block[None], (size,) + block.shape), axis, 0, 0)


def share_sum(blocks, axis):
    return jnp.sum(lax.all_to_all(blocks, axis, 0, 0).astype(jnp.float32), axis=0)


def shards(
    frames, dec_states, out_grad, frame_lengths, token_lengths, weights, norm_gains, norm_biases
):
    core = lax.axis_index("segment")
    first = core == 0
    own = weights[0]
    other = lax.ppermute(own, "segment", [(0, 1), (1, 0)])
    shard_rows, features = frames.shape[1:]
    mp = lax.axis_size("mp")
    head_cols = own.shape[1]
    rows = shard_rows * mp

    def mine(array):
        return lax.dynamic_index_in_dim(array, core, 0, keepdims=False)

    inputs = mine(frames)
    tokens = mine(dec_states)
    upstream = mine(out_grad)
    frame_ids = utterance_ids(mine(frame_lengths)[0], rows)
    token_ids = utterance_ids(mine(token_lengths)[0], tokens.shape[0])

    enc_full = spread(inputs, "mp").reshape(rows, features)
    enc = jnp.where(first, own, other)
    dec = jnp.where(first, other, own)

    normed = layer_norm(enc_full.astype(jnp.float32), norm_gains[0], norm_biases[0]).astype(
        jnp.bfloat16
    )
    queries = project(normed, enc[0])
    key_rows = project(normed, enc[1])
    value_rows = project(normed, enc[2])
    context, probs = attend(queries, key_rows, value_rows, frame_ids[:, None] == frame_ids[None, :])
    partial = jnp.dot(context, enc[3], preferred_element_type=jnp.float32).astype(jnp.bfloat16)
    summed = share_sum(partial.reshape(mp, shard_rows, features), "mp")
    states = (inputs.astype(jnp.float32) + summed).astype(jnp.bfloat16)
    states_full = spread(states, "mp").reshape(rows, features)

    state_normed = layer_norm(
        states_full.astype(jnp.float32), norm_gains[2], norm_biases[2]
    ).astype(jnp.bfloat16)
    token_normed = layer_norm(tokens.astype(jnp.float32), norm_gains[1], norm_biases[1]).astype(
        jnp.bfloat16
    )
    dec_queries = project(token_normed, dec[0])
    dec_keys = project(state_normed, dec[1])
    dec_values = project(state_normed, dec[2])
    dec_context, dec_probs = attend(
        dec_queries, dec_keys, dec_values, token_ids[:, None] == frame_ids[None, :]
    )
    grad_context = project(upstream, dec[3])
    dec_key_grad, dec_value_grad = attend_backward(
        dec_queries, dec_keys, dec_values, dec_probs, grad_context
    )
    partial = (
        jnp.dot(dec_key_grad, dec[1], preferred_element_type=jnp.float32)
        + jnp.dot(dec_value_grad, dec[2], preferred_element_type=jnp.float32)
    ).astype(jnp.bfloat16)
    summed = share_sum(partial.reshape(mp, shard_rows, features), "mp")
    grads = norm_backward(summed, states.astype(jnp.float32), norm_gains[2]).astype(jnp.bfloat16)
    dec_term = jnp.concatenate(
        [
            outer_rows(dec_key_grad, state_normed),
            outer_rows(dec_value_grad, state_normed),
            outer_rows(dec_context, upstream),
        ]
    )
    dec_sent = lax.ppermute(dec_term.astype(jnp.bfloat16), "segment", [(0, 1)])
    grads_full = spread(grads, "mp").reshape(rows, features)

    att_grad = project(grads_full, enc[3])
    enc_key_grad, enc_value_grad = attend_backward(queries, key_rows, value_rows, probs, att_grad)
    enc_term = jnp.concatenate(
        [
            outer_rows(enc_key_grad, normed),
            outer_rows(enc_value_grad, normed),
            outer_rows(context, grads_full),
        ]
    )
    enc_sent = lax.ppermute(enc_term.astype(jnp.bfloat16), "segment", [(1, 0)])
    term = jnp.where(
        first,
        enc_term + enc_sent.astype(jnp.float32),
        dec_term + dec_sent.astype(jnp.float32),
    ).astype(jnp.bfloat16)

    dp = lax.axis_size("dp")
    high, wide = 3 * head_cols // 8, features // 128
    tiles = term.reshape(high, 8, wide, 128).transpose(0, 2, 1, 3)
    tiles = tiles.reshape(dp, high * wide // dp, 8, 128)
    total = share_sum(tiles, "dp").astype(jnp.bfloat16)
    gradient = spread(total, "dp").astype(jnp.float32)
    gradient = gradient.reshape(high, wide, 8, 128).transpose(0, 2, 1, 3)
    return gradient.reshape(1, 3, head_cols, features)


def solution(mesh):
    placed = (
        P(None, ("dp", "mp"), None),
        P(None, "dp", None),
        P(None, "dp", None),
        P(None, "dp", None),
        P(None, "dp", None),
        P("segment", None, "mp", None),
        P(),
        P(),
    )
    return jax.shard_map(
        shards,
        mesh=mesh,
        in_specs=placed,
        out_specs=P("segment", None, "mp", None),
        check_vma=False,
    )
```

time: 466 us -> 239 us (0.51)
  the two profiles are of different devices: /device:TPU:1 before, /device:TPU:8 now
where the time goes in v1:
time: 239 us; the launch traced here: 238 us
  waiting for transfers between devices  93.8 us (39%)
  blocking collectives  69.1 us (29%)
  starting transfers between devices  31.8 us (13%)
  matrix products  26.1 us (11%)
  other arithmetic  10.6 us (4%)
  local copies, waits for them, and re-layouts  5.87 us (2%)
    all_to_all x3, waiting for transfers between devices, spread(): lax.all_to_all(jnp.broadcast_to(block[None], (size,) + block.shape), axis...  49.9 us
    all_to_all x2, waiting for transfers between devices, share_sum(): lax.all_to_all(blocks, axis, 0, 0).astype(jnp.float32)  40.7 us
    all_to_all x1, blocking collectives, share_sum(): lax.all_to_all(blocks, axis, 0, 0).astype(jnp.float32)  37.5 us
    all_to_all x1, blocking collectives, spread(): lax.all_to_all(jnp.broadcast_to(block[None], (size,) + block.shape), axis...  31.6 us
    all_to_all x3, starting transfers between devices, spread(): lax.all_to_all(jnp.broadcast_to(block[None], (size,) + block.shape), axis...  18 us
    all_to_all x2, starting transfers between devices, share_sum(): lax.all_to_all(blocks, axis, 0, 0).astype(jnp.float32)  7.34 us
    dot_general x8, matrix products, project(): lax.dot_general(row_block, matrix, FEAT_DIMS, preferred_element_type=jnp....  6.34 us
  transfers between devices with their start and end apart: 8, of which 6 were waited for; matrix products, arithmetic and copies ran while one was open for 7% of the time, Pallas kernels for 0%

profile of v1, /device:TPU:8, one launch (start us, length us, event | category | flops | bytes accessed | tf_op | source)
XLA Modules:
  0.0 237.9 jit_solution(14403867604316053281)
XLA Ops:
  0.0 1.0 dynamic-slice_bitcast_fusion
  1.1 0.9 broadcast_in_dim.35
  1.9 10.3 %all-to-all-start = ((bf16[8,32,1280]{2,1,0:T(8,128)(2,1)}), bf16[8,32,1280]{2,1,0:T(8,128)(2,1)S(1)}, u32[]{:S(2)}, u32[]{:S(2)}) async-start(bf16[8,32,1280]{2,1,0:T(8,128)(2,1)} %broadcast_in_dim.35), calls=%async_computation | async-start | bytes 1310720 | tf_op jit(solution)/shard_map/all_to_all | solution.py:105
  12.3 1.9 collective-permute-start
  14.2 0.2 reduce-window.16
  14.7 17.8 %all-to-all-done = bf16[8,32,1280]{2,1,0:T(8,128)(2,1)S(1)} async-done(((bf16[8,32,1280]{2,1,0:T(8,128)(2,1)}), bf16[8,32,1280]{2,1,0:T(8,128)(2,1)S(1)}, u32[]{:S(2)}, u32[]{:S(2)}) %all-to-all-start) | async-done | bytes 655392 | tf_op jit(solution)/shard_map/all_to_all | solution.py:105
  32.6 0.2 convert_reduce_fusion.1
  32.7 0.3 fusion.13
  33.1 0.3 fusion.16
  33.4 0.5 copy-done.6
  33.9 2.5 %broadcast_select_fusion = (bf16[4,128,1280]{2,1,0:T(8,128)(2,1)}, bf16[4,128,1280]{2,1,0:T(8,128)(2,1)S(1)}) fusion(bf16[4,128,1280]{2,1,0:T(8,128)(2,1)} %collective-permute-done, pred[]{:T(512)S(6)} %eq.37, bf16[1,4,128,1280]{3,2,1,0:T(8,128)(2,1)S(1)} %copy-done.6), kind=kLoop, calls=%fused_computation.28 | loop fusion | flops 1310720 | bytes 5242881 | tf_op jit(solution)/shard_map/jit(_where)/select_n | solution.py:135
  36.4 0.4 convolution_convert_fusion.7
  36.8 0.4 convolution_convert_fusion.6
  37.2 0.4 convolution_convert_fusion.5
  37.5 1.2 fusion.73
  38.7 0.5 convolution_convert_fusion.9
  39.3 1.2 convolution_convert_fusion
  40.5 3.7 %all-to-all-start.1 = ((bf16[8,32,1280]{2,1,0:T(8,128)(2,1)}), bf16[8,32,1280]{2,1,0:T(8,128)(2,1)S(1)}, u32[]{:S(2)}, u32[]{:S(2)}) async-start(bf16[8,32,1280]{2,1,0:T(8,128)(2,1)} %bitcast.14), calls=%async_computation.1 | async-start | bytes 1310720 | tf_op jit(solution)/shard_map/all_to_all | solution.py:109
  44.2 0.2 reduce-window.17
  44.5 20.4 %all-to-all-done.1 = bf16[8,32,1280]{2,1,0:T(8,128)(2,1)S(1)} async-done(((bf16[8,32,1280]{2,1,0:T(8,128)(2,1)}), bf16[8,32,1280]{2,1,0:T(8,128)(2,1)S(1)}, u32[]{:S(2)}, u32[]{:S(2)}) %all-to-all-start.1) | async-done | bytes 655392 | tf_op jit(solution)/shard_map/all_to_all | solution.py:109
  65.0 0.9 broadcast_in_dim.44
  65.9 3.5 %all-to-all-start.2 = ((bf16[8,32,1280]{2,1,0:T(8,128)(2,1)}), bf16[8,32,1280]{2,1,0:T(8,128)(2,1)S(1)}, u32[]{:S(2)}, u32[]{:S(2)}) async-start(bf16[8,32,1280]{2,1,0:T(8,128)(2,1)} %broadcast_in_dim.44), calls=%async_computation.2 | async-start | bytes 1310720 | tf_op jit(solution)/shard_map/all_to_all | solution.py:105
  69.6 0.2 fusion.31
  69.9 1.2 convolution_convert_fusion.12
  71.3 1.2 convolution_convert_fusion.11
  72.6 17.5 %all-to-all-done.2 = bf16[8,32,1280]{2,1,0:T(8,128)(2,1)S(1)} async-done(((bf16[8,32,1280]{2,1,0:T(8,128)(2,1)}), bf16[8,32,1280]{2,1,0:T(8,128)(2,1)S(1)}, u32[]{:S(2)}, u32[]{:S(2)}) %all-to-all-start.2) | async-done | bytes 655392 | tf_op jit(solution)/shard_map/all_to_all | solution.py:105
  90.3 0.3 fusion.9
  90.7 0.3 fusion.12
  91.0 0.5 copy-done.3
  91.5 0.4 convolution_convert_fusion.4
  91.8 1.0 convolution_convert_fusion.3
  92.8 1.0 fusion.74
  93.8 0.6 copy-done.32
  94.4 0.4 convolution_convert_fusion.2
  94.9 1.4 fusion.32
  96.3 1.5 multiply_reduce_fusion.2
  97.7 1.4 fusion.24
  99.2 2.2 fusion.2
  101.4 3.7 %all-to-all-start.3 = ((bf16[8,32,1280]{2,1,0:T(8,128)(2,1)}), bf16[8,32,1280]{2,1,0:T(8,128)(2,1)S(1)}, u32[]{:S(2)}, u32[]{:S(2)}) async-start(bf16[8,32,1280]{2,1,0:T(8,128)(2,1)} %bitcast.173), calls=%async_computation.3 | async-start | bytes 1310720 | tf_op jit(solution)/shard_map/all_to_all | solution.py:109
  105.2 0.2 fusion.36
  105.4 20.3 %all-to-all-done.3 = bf16[8,32,1280]{2,1,0:T(8,128)(2,1)S(1)} async-done(((bf16[8,32,1280]{2,1,0:T(8,128)(2,1)}), bf16[8,32,1280]{2,1,0:T(8,128)(2,1)S(1)}, u32[]{:S(2)}, u32[]{:S(2)}) %all-to-all-start.3) | async-done | bytes 655392 | tf_op jit(solution)/shard_map/all_to_all | solution.py:109
  125.9 0.2 multiply_reduce_fusion.1
  126.2 0.9 broadcast_in_dim.47
  127.1 4.2 %all-to-all-start.4 = ((bf16[8,32,1280]{2,1,0:T(8,128)(2,1)}), bf16[8,32,1280]{2,1,0:T(8,128)(2,1)}, u32[]{:S(2)}, u32[]{:S(2)}) async-start(bf16[8,32,1280]{2,1,0:T(8,128)(2,1)} %broadcast_in_dim.47), calls=%async_computation.4 | async-start | bytes 1310720 | tf_op jit(solution)/shard_map/all_to_all | solution.py:105
  131.3 1.2 convolution_convert_fusion.10
  132.5 0.2 fusion.45
  132.7 0.3 fusion.78
  133.0 0.3 fusion.79
  133.3 1.1 fusion.7
  134.4 3.0 %collective-permute-start.2 = (bf16[384,1280]{1,0:T(8,128)(2,1)}, bf16[384,1280]{1,0:T(8,128)(2,1)}, u32[]{:S(2)}, u32[]{:S(2)}) collective-permute-start(bf16[384,1280]{1,0:T(8,128)(2,1)} %fusion.7), channel_id=1, source_target_pairs={{0,8},{1,9},{2,10},{3,11},{4,12},{5,13},{6,14},{7,15},{16,24},{17,... | collective-permute-start | bytes 2949128 | tf_op jit(solution)/shard_map/ppermute | solution.py:178
  137.5 14.6 %all-to-all-done.4 = bf16[8,32,1280]{2,1,0:T(8,128)(2,1)} async-done(((bf16[8,32,1280]{2,1,0:T(8,128)(2,1)}), bf16[8,32,1280]{2,1,0:T(8,128)(2,1)}, u32[]{:S(2)}, u32[]{:S(2)}) %all-to-all-start.4) | async-done | bytes 655392 | tf_op jit(solution)/shard_map/all_to_all | solution.py:105
  152.1 1.5 convolution_convert_fusion.1
  153.6 1.3 fusion.77
  155.0 1.4 convolution_convert_fusion.8
  156.4 2.1 multiply_reduce_fusion
  158.5 1.7 fusion.23
  160.2 0.3 fusion.75
  160.4 0.3 fusion.76
  160.8 1.4 collective-permute-start.1
  162.3 3.1 %collective-permute-done.1 = bf16[384,1280]{1,0:T(8,128)(2,1)S(1)} collective-permute-done((bf16[384,1280]{1,0:T(8,128)(2,1)S(1)}, bf16[384,1280]{1,0:T(8,128)(2,1)S(1)}, u32[]{:S(2)}, u32[]{:S(2)}) %collective-permute-start.1) | collective-permute-done | bytes 983072 | tf_op jit(solution)/shard_map/ppermute | solution.py:190
  165.4 1.7 select_convert_fusion
  167.1 37.5 %all_to_all.35 = bf16[32,15,8,128]{3,2,1,0:T(8,128)(2,1)S(1)} all-to-all(bf16[32,15,8,128]{3,2,1,0:T(8,128)(2,1)S(1)} %bitcast.171), channel_id=1, replica_groups=mesh['dp'=32,'segment'=2,'mp'=8] {'dp'}, dimensions={0} | all-to-all | bytes 1966080 | tf_op jit(solution)/shard_map/all_to_all | solution.py:109
  204.9 31.6 %all_to_all.36 = bf16[32,15,8,128]{3,2,1,0:T(8,128)(2,1)S(1)} all-to-all(bf16[32,15,8,128]{3,2,1,0:T(8,128)(2,1)S(1)} %broadcast_in_dim.48), channel_id=1, replica_groups=mesh['dp'=32,'segment'=2,'mp'=8] {'dp'}, dimensions={0} | all-to-all | bytes 1966080 | tf_op jit(solution)/shard_map/all_to_all | solution.py:105
  236.5 1.4 convert.4
  (101 shorter events, 2.1 us)
Async XLA Ops:
  0.0 71.3 %copy-start = (bf16[2,64,1280]{2,1,0:T(8,128)(2,1)S(1)}, bf16[2,64,1280]{2,1,0:T(8,128)(2,1)}, u32[]{:S(2)}) copy-start(bf16[2,64,1280]{2,1,0:T(8,128)(2,1)} %param.10) | copy-start | bytes 983044
  0.0 12.3 %copy-start.5 = (bf16[1,4,128,1280]{3,2,1,0:T(8,128)(2,1)S(1)}, bf16[1,4,128,1280]{3,2,1,0:T(8,128)(2,1)}, u32[]{:S(2)}) copy-start(bf16[1,4,128,1280]{3,2,1,0:T(8,128)(2,1)} %param.13) | copy-start | bytes 3932164
  0.0 14.2 %copy-start.19 = (s32[2,1,4]{2,1,0:T(1,128)S(1)}, s32[2,1,4]{2,1,0:T(1,128)}, u32[]{:S(2)}) copy-start(s32[2,1,4]{2,1,0:T(1,128)} %param.11) | copy-start | bytes 100
  0.0 14.2 %copy-start.20 = (s32[2,1,4]{2,1,0:T(1,128)S(1)}, s32[2,1,4]{2,1,0:T(1,128)}, u32[]{:S(2)}) copy-start(s32[2,1,4]{2,1,0:T(1,128)} %param.12) | copy-start | bytes 100
  0.0 14.6 %copy-start.18 = (f32[3,1280]{1,0:T(4,128)S(1)}, f32[3,1280]{1,0:T(4,128)}, u32[]{:S(2)}) copy-start(f32[3,1280]{1,0:T(4,128)} %param.14) | copy-start | bytes 46084
  0.0 14.6 %copy-start.17 = (f32[3,1280]{1,0:T(4,128)S(1)}, f32[3,1280]{1,0:T(4,128)}, u32[]{:S(2)}) copy-start(f32[3,1280]{1,0:T(4,128)} %param.15) | copy-start | bytes 46084
  1.9 30.6 %all-to-all-start = ((bf16[8,32,1280]{2,1,0:T(8,128)(2,1)}), bf16[8,32,1280]{2,1,0:T(8,128)(2,1)S(1)}, u32[]{:S(2)}, u32[]{:S(2)}) async-start(bf16[8,32,1280]{2,1,0:T(8,128)(2,1)} %broadcast_in_dim.35), calls=%async_computation | async-start | bytes 1310720 | tf_op jit(solution)/shard_map/all_to_all | solution.py:105
  12.3 21.1 %collective-permute-start = (bf16[4,128,1280]{2,1,0:T(8,128)(2,1)S(1)}, bf16[4,128,1280]{2,1,0:T(8,128)(2,1)}, u32[]{:S(2)}, u32[]{:S(2)}) collective-permute-start(bf16[4,128,1280]{2,1,0:T(8,128)(2,1)S(1)} %bitcast.174), channel_id=1, source_target_pairs={{0,8},{8,0},{1,9},{9,1},{2,10},{10,2},{3,11},{11,3},{4,12},{12,4},... | collective-permute-start | bytes 3932168 | tf_op jit(solution)/shard_map/ppermute | solution.py:118
  14.6 24.1 %copy-start.11 = (pred[256,256]{0,1:T(8,128)(4,1)}, pred[256,256]{0,1:T(8,128)(4,1)S(1)}, u32[]{:S(2)}) copy-start(pred[256,256]{0,1:T(8,128)(4,1)S(1)} %broadcast_compare_fusion) | copy-start | bytes 196612
  14.7 75.9 %copy-start.9 = (f32[1280]{0:T(1024)}, f32[1280]{0:T(1024)S(1)}, u32[]{:S(2)}) copy-start(f32[1280]{0:T(1024)S(1)} %get-tuple-element.27) | copy-start | bytes 15364
  32.6 1.3 copy-start.6
  36.4 2.9 %copy-start.4 = (bf16[4,128,1280]{2,1,0:T(8,128)(2,1)}, bf16[4,128,1280]{2,1,0:T(8,128)(2,1)S(1)}, u32[]{:S(2)}) copy-start(bf16[4,128,1280]{2,1,0:T(8,128)(2,1)S(1)} %get-tuple-element.16) | copy-start | bytes 3932164
  36.8 1.9 copy-start.21
  37.2 2.1 copy-start.23
  37.5 1.7 copy-start.25
  38.7 1.8 copy-start.35
  39.3 5.1 %copy-start.8 = (bf16[2,64,1280]{2,1,0:T(8,128)(2,1)S(1)}, bf16[2,64,1280]{2,1,0:T(8,128)(2,1)}, u32[]{:S(2)}) copy-start(bf16[2,64,1280]{2,1,0:T(8,128)(2,1)} %param.9) | copy-start | bytes 983044
  40.5 24.5 %copy-start.7 = (bf16[2,32,1280]{2,1,0:T(8,128)(2,1)S(1)}, bf16[2,32,1280]{2,1,0:T(8,128)(2,1)}, u32[]{:S(2)}) copy-start(bf16[2,32,1280]{2,1,0:T(8,128)(2,1)} %param.8) | copy-start | bytes 491524
  40.5 24.4 %all-to-all-start.1 = ((bf16[8,32,1280]{2,1,0:T(8,128)(2,1)}), bf16[8,32,1280]{2,1,0:T(8,128)(2,1)S(1)}, u32[]{:S(2)}, u32[]{:S(2)}) async-start(bf16[8,32,1280]{2,1,0:T(8,128)(2,1)} %bitcast.14), calls=%async_computation.1 | async-start | bytes 1310720 | tf_op jit(solution)/shard_map/all_to_all | solution.py:109
  65.9 24.2 %all-to-all-start.2 = ((bf16[8,32,1280]{2,1,0:T(8,128)(2,1)}), bf16[8,32,1280]{2,1,0:T(8,128)(2,1)S(1)}, u32[]{:S(2)}, u32[]{:S(2)}) async-start(bf16[8,32,1280]{2,1,0:T(8,128)(2,1)} %broadcast_in_dim.44), calls=%async_computation.2 | async-start | bytes 1310720 | tf_op jit(solution)/shard_map/all_to_all | solution.py:105
  69.9 23.9 %copy-start.16 = (pred[64,256]{1,0:T(8,128)(4,1)}, pred[64,256]{1,0:T(8,128)(4,1)S(1)}, u32[]{:S(2)}) copy-start(pred[64,256]{1,0:T(8,128)(4,1)S(1)} %broadcast_compare_fusion.1) | copy-start | bytes 49156
  71.3 22.5 %copy-start.12 = (bf16[64,128]{0,1:T(8,128)(2,1)}, bf16[64,128]{0,1:T(8,128)(2,1)S(1)}, u32[]{:S(2)}) copy-start(bf16[64,128]{0,1:T(8,128)(2,1)S(1)} %copy.26) | copy-start | bytes 49156
  72.6 21.2 %copy-start.14 = (bf16[64,128]{0,1:T(8,128)(2,1)}, bf16[64,128]{0,1:T(8,128)(2,1)S(1)}, u32[]{:S(2)}) copy-start(bf16[64,128]{0,1:T(8,128)(2,1)S(1)} %copy.27) | copy-start | bytes 49156
  90.2 1.3 copy-start.3
  91.8 3.0 %copy-start.27 = (bf16[256,128]{0,1:T(8,128)(2,1)}, bf16[256,128]{0,1:T(8,128)(2,1)S(1)}, u32[]{:S(2)}) copy-start(bf16[256,128]{0,1:T(8,128)(2,1)S(1)} %convolution_convert_fusion.4) | copy-start | bytes 196612
  93.8 0.6 copy-start.32
  94.8 1.4 copy-start.15
  94.8 1.4 copy-start.29
  94.8 1.4 copy-start.31
  94.8 1.4 copy-start.33
  101.4 24.5 %copy-start.10 = (f32[1280]{0:T(1024)S(1)}, f32[1280]{0:T(1024)}, u32[]{:S(2)}) copy-start(f32[1280]{0:T(1024)} %copy-done.9) | copy-start | bytes 15364
  101.4 24.4 %all-to-all-start.3 = ((bf16[8,32,1280]{2,1,0:T(8,128)(2,1)}), bf16[8,32,1280]{2,1,0:T(8,128)(2,1)S(1)}, u32[]{:S(2)}, u32[]{:S(2)}) async-start(bf16[8,32,1280]{2,1,0:T(8,128)(2,1)} %bitcast.173), calls=%async_computation.3 | async-start | bytes 1310720 | tf_op jit(solution)/shard_map/all_to_all | solution.py:109
  125.8 5.5 %copy-start.13 = (bf16[64,128]{0,1:T(8,128)(2,1)S(1)}, bf16[64,128]{0,1:T(8,128)(2,1)}, u32[]{:S(2)}) copy-start(bf16[64,128]{0,1:T(8,128)(2,1)} %copy-done.12) | copy-start | bytes 49156
  125.8 5.5 %copy-start.28 = (bf16[256,128]{0,1:T(8,128)(2,1)S(1)}, bf16[256,128]{0,1:T(8,128)(2,1)}, u32[]{:S(2)}) copy-start(bf16[256,128]{0,1:T(8,128)(2,1)} %copy-done.27) | copy-start | bytes 196612
  125.9 5.5 %copy-start.30 = (bf16[256,128]{0,1:T(8,128)(2,1)S(1)}, bf16[256,128]{0,1:T(8,128)(2,1)}, u32[]{:S(2)}) copy-start(bf16[256,128]{0,1:T(8,128)(2,1)} %convolution_convert_fusion.3) | copy-start | bytes 196612
  125.9 5.5 %copy-start.34 = (f32[2,64]{1,0:T(2,128)S(1)}, f32[2,64]{1,0:T(2,128)}, u32[]{:S(2)}) copy-start(f32[2,64]{1,0:T(2,128)} %copy-done.32) | copy-start | bytes 1540
  127.1 25.0 %all-to-all-start.4 = ((bf16[8,32,1280]{2,1,0:T(8,128)(2,1)}), bf16[8,32,1280]{2,1,0:T(8,128)(2,1)}, u32[]{:S(2)}, u32[]{:S(2)}) async-start(bf16[8,32,1280]{2,1,0:T(8,128)(2,1)} %broadcast_in_dim.47), calls=%async_computation.4 | async-start | bytes 1310720 | tf_op jit(solution)/shard_map/all_to_all | solution.py:105
  133.3 1.2 copy-start.1
  134.4 20.5 %copy-start.22 = (bf16[256,128]{0,1:T(8,128)(2,1)S(1)}, bf16[256,128]{0,1:T(8,128)(2,1)}, u32[]{:S(2)}) copy-start(bf16[256,128]{0,1:T(8,128)(2,1)} %copy-done.21) | copy-start | bytes 196612
  134.4 20.5 %copy-start.24 = (bf16[256,128]{0,1:T(8,128)(2,1)S(1)}, bf16[256,128]{0,1:T(8,128)(2,1)}, u32[]{:S(2)}) copy-start(bf16[256,128]{0,1:T(8,128)(2,1)} %copy-done.23) | copy-start | bytes 196612
  134.4 20.6 %copy-start.36 = (f32[2,256]{1,0:T(2,128)S(1)}, f32[2,256]{1,0:T(2,128)}, u32[]{:S(2)}) copy-start(f32[2,256]{1,0:T(2,128)} %copy-done.35) | copy-start | bytes 6148
  134.4 27.8 %collective-permute-start.2 = (bf16[384,1280]{1,0:T(8,128)(2,1)}, bf16[384,1280]{1,0:T(8,128)(2,1)}, u32[]{:S(2)}, u32[]{:S(2)}) collective-permute-start(bf16[384,1280]{1,0:T(8,128)(2,1)} %fusion.7), channel_id=1, source_target_pairs={{0,8},{1,9},{2,10},{3,11},{4,12},{5,13},{6,14},{7,15},{16,24},{17,... | collective-permute-start | bytes 2949128 | tf_op jit(solution)/shard_map/ppermute | solution.py:178
  154.9 1.4 copy-start.26
  160.7 4.7 %copy-start.2 = (f32[128,1280]{1,0:T(8,128)S(1)}, f32[128,1280]{1,0:T(8,128)}, u32[]{:S(2)}) copy-start(f32[128,1280]{1,0:T(8,128)} %copy-done.1) | copy-start | bytes 1966084
  160.8 4.6 %collective-permute-start.1 = (bf16[384,1280]{1,0:T(8,128)(2,1)S(1)}, bf16[384,1280]{1,0:T(8,128)(2,1)S(1)}, u32[]{:S(2)}, u32[]{:S(2)}) collective-permute-start(bf16[384,1280]{1,0:T(8,128)(2,1)S(1)} %fusion.8), channel_id=1, source_target_pairs={{8,0},{9,1},{10,2},{11,3},{12,4},{13,5},{14,6},{15,7},{24,16},{25,... | collective-permute-start | bytes 2949128 | tf_op jit(solution)/shard_map/ppermute | solution.py:190

commit v2 on v1

--- a/solution.py
+++ b/solution.py
@@ -109,17 +109,36 @@
     return jnp.sum(lax.all_to_all(blocks, axis, 0, 0).astype(jnp.float32), axis=0)
 
 
+def swap(block):
+    return lax.ppermute(block, "segment", [(0, 1), (1, 0)])
+
+
+def to_chunks(block, parts):
+    high, wide = block.shape[0] // 8, block.shape[1] // 128
+    tiles = block.reshape(high, 8, wide, 128).transpose(0, 2, 1, 3).reshape(-1, 8, 128)
+    each = -(-tiles.shape[0] // parts)
+    tiles = jnp.pad(tiles, ((0, each * parts - tiles.shape[0]), (0, 0), (0, 0)))
+    return tiles.reshape(parts, each, 8, 128)
+
+
+def from_chunks(chunks, rows, cols):
+    high, wide = rows // 8, cols // 128
+    tiles = chunks.reshape(-1, 8, 128)[: high * wide]
+    return tiles.reshape(high, wide, 8, 128).transpose(0, 2, 1, 3).reshape(rows, cols)
+
+
 def shards(
     frames, dec_states, out_grad, frame_lengths, token_lengths, weights, norm_gains, norm_biases
 ):
     core = lax.axis_index("segment")
     first = core == 0
     own = weights[0]
-    other = lax.ppermute(own, "segment", [(0, 1), (1, 0)])
     shard_rows, features = frames.shape[1:]
     mp = lax.axis_size("mp")
+    dp = lax.axis_size("dp")
     head_cols = own.shape[1]
     rows = shard_rows * mp
+    half = features // 2
 
     def mine(array):
         return lax.dynamic_index_in_dim(array, core, 0, keepdims=False)
@@ -130,7 +149,13 @@
     frame_ids = utterance_ids(mine(frame_lengths)[0], rows)
     token_ids = utterance_ids(mine(token_lengths)[0], tokens.shape[0])
 
+    out_sent = lax.ppermute(own[3, :, half:], "segment", [(0, 1)])
+    out_part = jnp.where(first, own[3, :, :half], out_sent)
+    out_part = lax.all_gather(out_part, "mp", axis=0, tiled=True)
+    out_rest = swap(out_part)
+
     enc_full = spread(inputs, "mp").reshape(rows, features)
+    other = swap(own)
     enc = jnp.where(first, own, other)
     dec = jnp.where(first, other, own)
 
@@ -141,10 +166,16 @@
     key_rows = project(normed, enc[1])
     value_rows = project(normed, enc[2])
     context, probs = attend(queries, key_rows, value_rows, frame_ids[:, None] == frame_ids[None, :])
-    partial = jnp.dot(context, enc[3], preferred_element_type=jnp.float32).astype(jnp.bfloat16)
-    summed = share_sum(partial.reshape(mp, shard_rows, features), "mp")
-    states = (inputs.astype(jnp.float32) + summed).astype(jnp.bfloat16)
-    states_full = spread(states, "mp").reshape(rows, features)
+    context_full = spread(context, "mp").transpose(1, 0, 2).reshape(rows, mp * head_cols)
+    out_mine = jnp.dot(context_full, out_part, preferred_element_type=jnp.float32)
+    out_other = jnp.dot(context_full, out_rest, preferred_element_type=jnp.float32)
+    summed = jnp.concatenate(
+        [jnp.where(first, out_mine, out_other), jnp.where(first, out_other, out_mine)], axis=1
+    )
+    states_full = (enc_full.astype(jnp.float32) + summed).astype(jnp.bfloat16)
+    states = lax.dynamic_slice_in_dim(
+        states_full, lax.axis_index("mp") * shard_rows, shard_rows, 0
+    )
 
     state_normed = layer_norm(
         states_full.astype(jnp.float32), norm_gains[2], norm_biases[2]
@@ -166,8 +197,16 @@
         jnp.dot(dec_key_grad, dec[1], preferred_element_type=jnp.float32)
         + jnp.dot(dec_value_grad, dec[2], preferred_element_type=jnp.float32)
     ).astype(jnp.bfloat16)
-    summed = share_sum(partial.reshape(mp, shard_rows, features), "mp")
-    grads = norm_backward(summed, states.astype(jnp.float32), norm_gains[2]).astype(jnp.bfloat16)
+
+    def combine(term):
+        left, right = term[:, :half], term[:, half:]
+        sent = swap(jnp.where(first, right, left).astype(jnp.bfloat16))
+        return (jnp.where(first, left, right) + sent.astype(jnp.float32)).astype(jnp.bfloat16)
+
+    def reduce_groups(term):
+        total = share_sum(to_chunks(term, dp), "dp").astype(jnp.bfloat16)
+        return from_chunks(spread(total, "dp"), 3 * head_cols, half)
+
     dec_term = jnp.concatenate(
         [
             outer_rows(dec_key_grad, state_normed),
@@ -175,7 +214,11 @@
             outer_rows(dec_context, upstream),
         ]
     )
-    dec_sent = lax.ppermute(dec_term.astype(jnp.bfloat16), "segment", [(0, 1)])
+    pieces = lax.all_to_all(partial.reshape(mp, shard_rows, features), "mp", 0, 0)
+    pieces, dec_part = lax.optimization_barrier((pieces, combine(dec_term)))
+    dec_total = lax.psum(dec_part, "dp")
+    summed = jnp.sum(pieces.astype(jnp.float32), axis=0)
+    grads = norm_backward(summed, states.astype(jnp.float32), norm_gains[2]).astype(jnp.bfloat16)
     grads_full = spread(grads, "mp").reshape(rows, features)
 
     att_grad = project(grads_full, enc[3])
@@ -187,20 +230,12 @@
             outer_rows(context, grads_full),
         ]
     )
-    enc_sent = lax.ppermute(enc_term.astype(jnp.bfloat16), "segment", [(1, 0)])
-    term = jnp.where(
-        first,
-        enc_term + enc_sent.astype(jnp.float32),
-        dec_term + dec_sent.astype(jnp.float32),
-    ).astype(jnp.bfloat16)
-
-    dp = lax.axis_size("dp")
-    high, wide = 3 * head_cols // 8, features // 128
-    tiles = term.reshape(high, 8, wide, 128).transpose(0, 2, 1, 3)
-    tiles = tiles.reshape(dp, high * wide // dp, 8, 128)
-    total = share_sum(tiles, "dp").astype(jnp.bfloat16)
-    gradient = spread(total, "dp").astype(jnp.float32)
-    gradient = gradient.reshape(high, wide, 8, 128).transpose(0, 2, 1, 3)
+    enc_total = reduce_groups(combine(enc_term))
+    kept = jnp.where(first, enc_total, dec_total)
+    got = swap(jnp.where(first, dec_total, enc_total))
+    gradient = jnp.concatenate(
+        [jnp.where(first, kept, got), jnp.where(first, got, kept)], axis=1
+    ).astype(jnp.float32)
     return gradient.reshape(1, 3, head_cols, features)
 
 

time: 239 us -> 380 us (1.59)
  the two profiles are of different devices: /device:TPU:8 before, /device:TPU:1 now
where the time goes in v2:
time: 380 us; the launch traced here: 379 us
  waiting for transfers between devices  220 us (58%)
  starting transfers between devices  51.7 us (14%)
  blocking collectives  45.5 us (12%)
  matrix products  25.7 us (7%)
  between operations  14 us (4%)
  other arithmetic  13.8 us (4%)
  local copies, waits for them, and re-layouts  8.81 us (2%)
    psum x1, waiting for transfers between devices, shards(): dec_total = lax.psum(dec_part, 'dp')  140 us
    all_to_all x3, waiting for transfers between devices, spread(): lax.all_to_all(jnp.broadcast_to(block[None], (size,) + block.shape), axis...  38.3 us
    ppermute x5, starting transfers between devices, swap(): return lax.ppermute(block, 'segment', [(0, 1), (1, 0)])  23.9 us
    all_to_all x1, blocking collectives, share_sum(): lax.all_to_all(blocks, axis, 0, 0).astype(jnp.float32)  23.2 us
    all_gather x1, waiting for transfers between devices, shards(): out_part = lax.all_gather(out_part, 'mp', axis=0, tiled=True)  23.2 us
    all_to_all x3, starting transfers between devices, spread(): lax.all_to_all(jnp.broadcast_to(block[None], (size,) + block.shape), axis...  22.8 us
    all_to_all x1, blocking collectives, spread(): lax.all_to_all(jnp.broadcast_to(block[None], (size,) + block.shape), axis...  22.3 us
    all_to_all x1, waiting for transfers between devices, shards(): lax.all_to_all(partial.reshape(mp, shard_rows, features), 'mp', 0, 0)  14.1 us
  transfers between devices with their start and end apart: 12, of which 9 were waited for; matrix products, arithmetic and copies ran while one was open for 5% of the time, Pallas kernels for 0%

profile of v2, /device:TPU:1, one launch (start us, length us, event | category | flops | bytes accessed | tf_op | source)
XLA Modules:
  0.0 379.2 jit_solution(9192799755561751875)
XLA Ops:
  6.6 1.0 dynamic-slice_bitcast_fusion
  7.6 0.9 broadcast_in_dim.31
  8.5 10.9 %all-to-all-start = ((bf16[8,32,1280]{2,1,0:T(8,128)(2,1)}), bf16[8,32,1280]{2,1,0:T(8,128)(2,1)S(1)}, u32[]{:S(2)}, u32[]{:S(2)}) async-start(bf16[8,32,1280]{2,1,0:T(8,128)(2,1)} %broadcast_in_dim.31), calls=%async_computation | async-start | bytes 1310720 | tf_op jit(solution)/shard_map/all_to_all | solution.py:105
  19.4 2.9 collective-permute-start
  22.3 1.3 collective-permute-start.1
  24.5 0.7 broadcast_compare_fusion.1
  25.3 0.6 add_rsqrt_fusion.2
  25.9 0.7 slice_reduce_fusion
  26.6 0.7 fusion.41
  27.3 12.8 %all-to-all-done = bf16[8,32,1280]{2,1,0:T(8,128)(2,1)S(1)} async-done(((bf16[8,32,1280]{2,1,0:T(8,128)(2,1)}), bf16[8,32,1280]{2,1,0:T(8,128)(2,1)S(1)}, u32[]{:S(2)}, u32[]{:S(2)}) %all-to-all-start) | async-done | bytes 655392 | tf_op jit(solution)/shard_map/all_to_all | solution.py:105
  40.6 0.3 add_convert_fusion
  41.0 0.5 copy-done.5
  41.4 1.5 broadcast_select_fusion.1
  42.9 0.4 convolution_convert_fusion.5
  43.3 0.4 convolution_convert_fusion.6
  44.0 0.4 convolution_convert_fusion.4
  44.4 23.2 %all-gather.2.cloned.1.call-done = bf16[1024,640]{1,0:T(8,128)(2,1)} async-done(((bf16[128,640]{1,0:T(8,128)(2,1)}), bf16[1024,640]{1,0:T(8,128)(2,1)}) %all-gather.2.cloned.1.call-update) | async-done | bytes 1310736 | tf_op jit(solution)/shard_map/all_gather | solution.py:154
  67.6 7.2 %collective-permute-start.2 = (bf16[1024,640]{1,0:T(8,128)(2,1)}, bf16[1024,640]{1,0:T(8,128)(2,1)}, u32[]{:S(2)}, u32[]{:S(2)}) collective-permute-start(bf16[1024,640]{1,0:T(8,128)(2,1)} %all-gather.2.cloned.1.call-done), channel_id=1, source_target_pairs={{0,8},{8,0},{1,9},{9,1},{2,10},{10,2},{3,11},{11,3},{4,12},{12,4},... | collective-permute-start | bytes 3932168 | tf_op jit(solution)/shard_map/ppermute | solution.py:113
  74.8 1.2 fusion.70
  76.0 0.5 convolution_convert_fusion.8
  76.5 0.8 broadcast_in_dim.34
  77.4 3.9 %all-to-all-start.1 = ((bf16[8,256,128]{1,2,0:T(8,128)(2,1)}), bf16[8,256,128]{1,2,0:T(8,128)(2,1)S(1)}, u32[]{:S(2)}, u32[]{:S(2)}) async-start(bf16[8,256,128]{1,2,0:T(8,128)(2,1)} %broadcast_in_dim.34), calls=%async_computation.1 | async-start | bytes 1048576 | tf_op jit(solution)/shard_map/all_to_all | solution.py:105
  81.3 1.2 bitcast_convert_fusion
  82.5 0.9 convolution_convert_fusion.11
  83.4 1.4 copy.34
  84.8 0.8 convolution_convert_fusion.10
  85.7 1.4 copy.35
  87.1 12.2 %all-to-all-done.1 = bf16[8,256,128]{1,2,0:T(8,128)(2,1)S(1)} async-done(((bf16[8,256,128]{1,2,0:T(8,128)(2,1)}), bf16[8,256,128]{1,2,0:T(8,128)(2,1)S(1)}, u32[]{:S(2)}, u32[]{:S(2)}) %all-to-all-start.1) | async-done | bytes 524320 | tf_op jit(solution)/shard_map/all_to_all | solution.py:105
  99.3 1.9 fusion.72
  101.2 1.9 broadcast_select_fusion.7
  104.0 0.6 copy-done.3
  104.6 0.3 convolution_convert_fusion.2
  105.0 0.4 convolution_convert_fusion.3
  105.4 0.4 fusion.71
  105.8 0.4 convolution_convert_fusion.1
  106.2 1.1 fusion.74
  107.3 2.4 fusion.25
  109.7 0.4 convolution_convert_fusion.9
  110.2 0.9 multiply_reduce_fusion.3
  111.0 1.3 fusion.17
  112.4 1.1 fusion.73
  113.5 1.1 fusion.42
  114.6 2.2 fusion.2
  116.8 3.5 all-to-all-start.2
  120.3 1.6 pad_maximum_fusion
  122.0 2.4 collective-permute-start.3
  124.4 1.0 convert_reduce_fusion.4
  125.9 1.0 add_convert_fusion.2
  126.9 14.1 %all-to-all-done.2 = bf16[8,32,1280]{2,1,0:T(8,128)(2,1)S(1)} async-done(((bf16[8,32,1280]{2,1,0:T(8,128)(2,1)}), bf16[8,32,1280]{2,1,0:T(8,128)(2,1)S(1)}, u32[]{:S(2)}, u32[]{:S(2)}) %all-to-all-start.2) | async-done | bytes 655392 | tf_op jit(solution)/shard_map/all_to_all | solution.py:217
  141.5 22.3 %all_to_all.30 = bf16[8,32,1280]{2,1,0:T(8,128)(2,1)S(1)} all-to-all(bf16[8,32,1280]{2,1,0:T(8,128)(2,1)S(1)} %broadcast_in_dim.37), channel_id=1, replica_groups=mesh['dp'=32,'segment'=2,'mp'=8] {'mp'}, dimensions={0} | all-to-all | bytes 1310720 | tf_op jit(solution)/shard_map/all_to_all | solution.py:105
  163.8 1.4 convolution_convert_fusion
  165.5 1.5 convolution_convert_fusion.7
  167.3 1.4 fusion.16
  169.5 3.2 collective-permute-start.4
  172.7 1.5 collective-permute-done.4
  174.4 23.2 %all_to_all.31 = bf16[32,8,8,128]{3,2,1,0:T(8,128)(2,1)S(1)} all-to-all(bf16[32,8,8,128]{3,2,1,0:T(8,128)(2,1)S(1)} %bitcast.176), channel_id=1, replica_groups=mesh['dp'=32,'segment'=2,'mp'=8] {'dp'}, dimensions={0} | all-to-all | bytes 1048576 | tf_op jit(solution)/shard_map/all_to_all | solution.py:109
  197.7 0.9 broadcast_in_dim.42
  198.6 8.1 %all-to-all-start.5 = ((bf16[32,8,8,128]{3,2,1,0:T(8,128)(2,1)}), bf16[32,8,8,128]{3,2,1,0:T(8,128)(2,1)S(1)}, u32[]{:S(2)}, u32[]{:S(2)}) async-start(bf16[32,8,8,128]{3,2,1,0:T(8,128)(2,1)} %broadcast_in_dim.42), calls=%async_computation.5 | async-start | bytes 1048576 | tf_op jit(solution)/shard_map/all_to_all | solution.py:105
  206.8 0.7 all-reduce.3.cloned.1.call-update
  207.5 13.3 %all-to-all-done.5 = bf16[32,8,8,128]{3,2,1,0:T(8,128)(2,1)S(1)} async-done(((bf16[32,8,8,128]{3,2,1,0:T(8,128)(2,1)}), bf16[32,8,8,128]{3,2,1,0:T(8,128)(2,1)S(1)}, u32[]{:S(2)}, u32[]{:S(2)}) %all-to-all-start.5) | async-done | bytes 524320 | tf_op jit(solution)/shard_map/all_to_all | solution.py:105
  220.8 140.2 %all-reduce.3.cloned.1.call-done = bf16[384,640]{1,0:T(8,128)(2,1)} async-done(((bf16[384,640]{1,0:T(8,128)(2,1)}), bf16[384,640]{1,0:T(8,128)(2,1)}) %all-reduce.3.cloned.1.call-update) | async-done | bytes 491536 | tf_op jit(solution)/shard_map/psum | solution.py:219
  361.1 8.2 %collective-permute-start.5 = (bf16[384,640]{1,0:T(8,128)(2,1)S(1)}, bf16[384,640]{1,0:T(8,128)(2,1)S(1)}, u32[]{:S(2)}, u32[]{:S(2)}) collective-permute-start(bf16[384,640]{1,0:T(8,128)(2,1)S(1)} %broadcast_select_fusion.4), channel_id=1, source_target_pairs={{0,8},{8,0},{1,9},{9,1},{2,10},{10,2},{3,11},{11,3},{4,12},{12,4},... | collective-permute-start | bytes 1474568 | tf_op jit(solution)/shard_map/ppermute | solution.py:113
  369.3 1.5 collective-permute-done.5
  370.9 1.4 maximum_convert_fusion
  (110 shorter events, 5.7 us)
Async XLA Ops:
  6.5 78.3 %copy-start = (bf16[2,64,1280]{2,1,0:T(8,128)(2,1)S(1)}, bf16[2,64,1280]{2,1,0:T(8,128)(2,1)}, u32[]{:S(2)}) copy-start(bf16[2,64,1280]{2,1,0:T(8,128)(2,1)} %param.10) | copy-start | bytes 983044
  6.5 12.9 %copy-start.4 = (bf16[1,4,128,1280]{3,2,1,0:T(8,128)(2,1)S(1)}, bf16[1,4,128,1280]{3,2,1,0:T(8,128)(2,1)}, u32[]{:S(2)}) copy-start(bf16[1,4,128,1280]{3,2,1,0:T(8,128)(2,1)} %param.13) | copy-start | bytes 3932164
  6.5 17.1 %copy-start.20 = (s32[2,1,4]{2,1,0:T(1,128)S(1)}, s32[2,1,4]{2,1,0:T(1,128)}, u32[]{:S(2)}) copy-start(s32[2,1,4]{2,1,0:T(1,128)} %param.11) | copy-start | bytes 100
  6.5 17.1 %copy-start.21 = (s32[2,1,4]{2,1,0:T(1,128)S(1)}, s32[2,1,4]{2,1,0:T(1,128)}, u32[]{:S(2)}) copy-start(s32[2,1,4]{2,1,0:T(1,128)} %param.12) | copy-start | bytes 100
  6.5 17.4 %copy-start.8 = (bf16[2,64,1280]{2,1,0:T(8,128)(2,1)S(1)}, bf16[2,64,1280]{2,1,0:T(8,128)(2,1)}, u32[]{:S(2)}) copy-start(bf16[2,64,1280]{2,1,0:T(8,128)(2,1)} %param.9) | copy-start | bytes 983044
  7.6 18.3 %copy-start.14 = (f32[3,1280]{1,0:T(4,128)S(1)}, f32[3,1280]{1,0:T(4,128)}, u32[]{:S(2)}) copy-start(f32[3,1280]{1,0:T(4,128)} %param.15) | copy-start | bytes 46084
  7.6 18.3 %copy-start.15 = (f32[3,1280]{1,0:T(4,128)S(1)}, f32[3,1280]{1,0:T(4,128)}, u32[]{:S(2)}) copy-start(f32[3,1280]{1,0:T(4,128)} %param.14) | copy-start | bytes 46084
  8.5 31.6 %all-to-all-start = ((bf16[8,32,1280]{2,1,0:T(8,128)(2,1)}), bf16[8,32,1280]{2,1,0:T(8,128)(2,1)S(1)}, u32[]{:S(2)}, u32[]{:S(2)}) async-start(bf16[8,32,1280]{2,1,0:T(8,128)(2,1)} %broadcast_in_dim.31), calls=%async_computation | async-start | bytes 1310720 | tf_op jit(solution)/shard_map/all_to_all | solution.py:105
  19.3 48.2 %all-gather.2.cloned.1.call-start = ((), (), s32[]{:S(2)}) async-start(), calls=%async_computation.6 | async-start | bytes 1474560 | tf_op jit(solution)/shard_map/all_gather | solution.py:154
  19.4 21.6 %collective-permute-start = (bf16[4,128,1280]{2,1,0:T(8,128)(2,1)S(1)}, bf16[4,128,1280]{2,1,0:T(8,128)(2,1)}, u32[]{:S(2)}, u32[]{:S(2)}) collective-permute-start(bf16[4,128,1280]{2,1,0:T(8,128)(2,1)S(1)} %bitcast.177), channel_id=1, source_target_pairs={{0,8},{8,0},{1,9},{9,1},{2,10},{10,2},{3,11},{11,3},{4,12},{12,4},... | collective-permute-start | bytes 3932168 | tf_op jit(solution)/shard_map/ppermute | solution.py:113
  22.3 4.3 %collective-permute-start.1 = (bf16[128,640]{1,0:T(8,128)(2,1)S(1)}, bf16[128,640]{1,0:T(8,128)(2,1)S(1)}, u32[]{:S(2)}, u32[]{:S(2)}) collective-permute-start(bf16[128,640]{1,0:T(8,128)(2,1)S(1)} %slice_bitcast_fusion.18), channel_id=1, source_target_pairs={{0,8},{1,9},{2,10},{3,11},{4,12},{5,13},{6,14},{7,15},{16,24},{17,... | collective-permute-start | bytes 491528 | tf_op jit(solution)/shard_map/ppermute | solution.py:152
  24.0 1.9 copy-start.18
  25.3 50.7 %copy-start.10 = (pred[256,256]{0,1:T(8,128)(4,1)}, pred[256,256]{0,1:T(8,128)(4,1)S(1)}, u32[]{:S(2)}) copy-start(pred[256,256]{0,1:T(8,128)(4,1)S(1)} %broadcast_compare_fusion) | copy-start | bytes 196612
  40.1 1.3 copy-start.5
  42.9 1.1 copy-start.7
  42.9 41.9 %copy-start.2 = (bf16[4,128,1280]{2,1,0:T(8,128)(2,1)}, bf16[4,128,1280]{2,1,0:T(8,128)(2,1)S(1)}, u32[]{:S(2)}) copy-start(bf16[4,128,1280]{2,1,0:T(8,128)(2,1)S(1)} %get-tuple-element.22) | copy-start | bytes 3932164
  43.3 32.7 %copy-start.22 = (bf16[256,128]{0,1:T(8,128)(2,1)}, bf16[256,128]{0,1:T(8,128)(2,1)S(1)}, u32[]{:S(2)}) copy-start(bf16[256,128]{0,1:T(8,128)(2,1)S(1)} %convolution_convert_fusion.5) | copy-start | bytes 196612
  44.0 32.5 %copy-start.24 = (bf16[256,128]{0,1:T(8,128)(2,1)}, bf16[256,128]{0,1:T(8,128)(2,1)S(1)}, u32[]{:S(2)}) copy-start(bf16[256,128]{0,1:T(8,128)(2,1)S(1)} %convolution_convert_fusion.6) | copy-start | bytes 196612
  44.3 32.2 %copy-start.26 = (bf16[256,128]{0,1:T(8,128)(2,1)}, bf16[256,128]{0,1:T(8,128)(2,1)S(1)}, u32[]{:S(2)}) copy-start(bf16[256,128]{0,1:T(8,128)(2,1)S(1)} %convolution_convert_fusion.4) | copy-start | bytes 196612
  67.6 31.7 %collective-permute-start.2 = (bf16[1024,640]{1,0:T(8,128)(2,1)}, bf16[1024,640]{1,0:T(8,128)(2,1)}, u32[]{:S(2)}, u32[]{:S(2)}) collective-permute-start(bf16[1024,640]{1,0:T(8,128)(2,1)} %all-gather.2.cloned.1.call-done), channel_id=1, source_target_pairs={{0,8},{8,0},{1,9},{9,1},{2,10},{10,2},{3,11},{11,3},{4,12},{12,4},... | collective-permute-start | bytes 3932168 | tf_op jit(solution)/shard_map/ppermute | solution.py:113
  76.0 1.4 copy-start.30
  77.4 21.9 %all-to-all-start.1 = ((bf16[8,256,128]{1,2,0:T(8,128)(2,1)}), bf16[8,256,128]{1,2,0:T(8,128)(2,1)S(1)}, u32[]{:S(2)}, u32[]{:S(2)}) async-start(bf16[8,256,128]{1,2,0:T(8,128)(2,1)} %broadcast_in_dim.34), calls=%async_computation.1 | async-start | bytes 1048576 | tf_op jit(solution)/shard_map/all_to_all | solution.py:105
  81.2 1.3 copy-start.9
  81.2 1.3 copy-start.16
  81.2 1.2 copy-start.17
  81.3 1.2 copy-start.19
  81.3 1.2 copy-start.28
  103.3 1.3 copy-start.3
  104.0 1.4 copy-start.11
  104.0 1.4 copy-start.13
  104.0 1.7 copy-start.12
  112.4 2.2 copy-start.1
  116.8 24.2 %all-to-all-start.2 = ((bf16[8,32,1280]{2,1,0:T(8,128)(2,1)}), bf16[8,32,1280]{2,1,0:T(8,128)(2,1)S(1)}, u32[]{:S(2)}, u32[]{:S(2)}) async-start(bf16[8,32,1280]{2,1,0:T(8,128)(2,1)} %bitcast.37), calls=%async_computation.2 | async-start | bytes 1310720 | tf_op jit(solution)/shard_map/all_to_all | solution.py:217
  122.0 3.9 %collective-permute-start.3 = (bf16[384,640]{1,0:T(8,128)(2,1)S(1)}, bf16[384,640]{1,0:T(8,128)(2,1)S(1)}, u32[]{:S(2)}, u32[]{:S(2)}) collective-permute-start(bf16[384,640]{1,0:T(8,128)(2,1)S(1)} %select_convert_fusion.1), channel_id=1, source_target_pairs={{0,8},{8,0},{1,9},{9,1},{2,10},{10,2},{3,11},{11,3},{4,12},{12,4},... | collective-permute-start | bytes 1474568 | tf_op jit(solution)/shard_map/ppermute | solution.py:113
  163.8 1.7 copy-start.23
  163.8 1.7 copy-start.25
  163.8 1.7 copy-start.31
  165.4 1.5 copy-start.27
  165.5 1.5 copy-start.29
  169.5 4.7 %collective-permute-start.4 = (bf16[384,640]{1,0:T(8,128)(2,1)S(1)}, bf16[384,640]{1,0:T(8,128)(2,1)S(1)}, u32[]{:S(2)}, u32[]{:S(2)}) collective-permute-start(bf16[384,640]{1,0:T(8,128)(2,1)S(1)} %select_convert_fusion), channel_id=1, source_target_pairs={{0,8},{8,0},{1,9},{9,1},{2,10},{10,2},{3,11},{11,3},{4,12},{12,4},... | collective-permute-start | bytes 1474568 | tf_op jit(solution)/shard_map/ppermute | solution.py:113
  198.6 22.2 %all-to-all-start.5 = ((bf16[32,8,8,128]{3,2,1,0:T(8,128)(2,1)}), bf16[32,8,8,128]{3,2,1,0:T(8,128)(2,1)S(1)}, u32[]{:S(2)}, u32[]{:S(2)}) async-start(bf16[32,8,8,128]{3,2,1,0:T(8,128)(2,1)} %broadcast_in_dim.42), calls=%async_computation.5 | async-start | bytes 1048576 | tf_op jit(solution)/shard_map/all_to_all | solution.py:105
  206.7 154.3 %all-reduce.3.cloned.1.call-start = ((), (), s32[]{:S(2)}) async-start(), calls=%async_computation.7 | async-start | bytes 983040 | tf_op jit(solution)/shard_map/psum | solution.py:219
  361.0 9.8 %copy-start.6 = (bf16[384,640]{1,0:T(8,128)(2,1)S(1)}, bf16[384,640]{1,0:T(8,128)(2,1)}, u32[]{:S(2)}) copy-start(bf16[384,640]{1,0:T(8,128)(2,1)} %all-reduce.3.cloned.1.call-done) | copy-start | bytes 1474564
  361.1 9.7 %collective-permute-start.5 = (bf16[384,640]{1,0:T(8,128)(2,1)S(1)}, bf16[384,640]{1,0:T(8,128)(2,1)S(1)}, u32[]{:S(2)}, u32[]{:S(2)}) collective-permute-start(bf16[384,640]{1,0:T(8,128)(2,1)S(1)} %broadcast_select_fusion.4), channel_id=1, source_target_pairs={{0,8},{8,0},{1,9},{9,1},{2,10},{10,2},{3,11},{11,3},{4,12},{12,4},... | collective-permute-start | bytes 1474568 | tf_op jit(solution)/shard_map/ppermute | solution.py:113
Sparse Core Ops, SparseCore 0:
  27.4 40.0 all-gather.1
  210.9 150.0 all-reduce.2

commit v3 on v1

v3 whole, which is shorter than its diff:
```python
import functools
import math

import jax
import jax.numpy as jnp
from jax import lax
from jax.experimental import pallas as pl
from jax.experimental.pallas import tpu as pltpu
from jax.sharding import PartitionSpec as P

HS = 64
SCALING = 1.0 / math.sqrt(HS)
EPSILON = 1e-05
ROWS_DIMS = (((0,), (0,)), ((), ()))
FEAT_DIMS = (((1,), (1,)), ((), ()))


def dot_nn(a, b):
    return lax.dot_general(a, b, (((1,), (0,)), ((), ())), preferred_element_type=jnp.float32)


def dot_nt(a, b):
    return lax.dot_general(a, b, FEAT_DIMS, preferred_element_type=jnp.float32)


def dot_tn(a, b):
    return lax.dot_general(a, b, ROWS_DIMS, preferred_element_type=jnp.float32)


def row_stats(values):
    center = values - jnp.mean(values, axis=-1, keepdims=True)
    variance = jnp.mean(center * center, axis=-1, keepdims=True)
    return center, lax.rsqrt(variance + EPSILON)


def layer_norm(values, norm_gain, offset):
    center, inverse = row_stats(values.astype(jnp.float32))
    return (center * inverse * norm_gain + offset).astype(jnp.bfloat16)


def ids_along(lengths_ref, shape, axis):
    places = lax.broadcasted_iota(jnp.int32, shape, axis)
    bound = 0
    ids = jnp.zeros(shape, jnp.int32)
    for piece in range(lengths_ref.shape[0]):
        bound = bound + lengths_ref[piece]
        ids = ids + (places >= bound).astype(jnp.int32)
    return ids


def softmax(queries, keys, allowed):
    scores = jnp.where(allowed, dot_nt(queries, keys) * SCALING, -1e30)
    raised = jnp.exp(scores - jnp.max(scores, axis=-1, keepdims=True))
    return raised / jnp.sum(raised, axis=-1, keepdims=True)


def scores_grad(probs, grad_context, values):
    grad_probs = dot_nt(grad_context, values)
    inner = jnp.sum(grad_probs * probs, axis=-1, keepdims=True)
    return (probs * (grad_probs - inner)).astype(jnp.bfloat16)


def side_by_side(parts):
    return jnp.concatenate(parts, axis=1).astype(jnp.bfloat16)


def enc_forward_kernel(
    core, lengths, x, own, other, gains, biases, normed, queries, keys, values, context, probs
):
    first = core[0] == 0
    rows = x.shape[0]
    normed_rows = layer_norm(x[...], gains[0:1, :], biases[0:1, :])
    normed[...] = normed_rows
    projected = []
    for kind, out in enumerate((queries, keys, values)):
        matrix = jnp.where(first, own[kind], other[kind])
        block = dot_nt(normed_rows, matrix).astype(jnp.bfloat16)
        out[...] = block
        projected.append(block)
    allowed = ids_along(lengths, (rows, 1), 0) == ids_along(lengths, (1, rows), 1)
    parts = []
    for head in range(queries.shape[1] // HS):
        at = slice(head * HS, (head + 1) * HS)
        weights = softmax(projected[0][:, at], projected[1][:, at], allowed)
        probs[head] = weights
        parts.append(dot_nn(weights.astype(jnp.bfloat16), projected[2][:, at]))
    block = side_by_side(parts)
    for copy in range(context.shape[0]):
        context[copy] = block


def dec_kernel(
    core, place, frame_lens, token_lens, x, context, out_part, out_rest, own, other, tokens,
    upstream, gains, biases, partial, states, normed, key_grad, value_grad, dec_context, scratch,
):
    first = core[0] == 0
    rows, features = x.shape
    half = features // 2
    all_context = jnp.concatenate([context[c] for c in range(context.shape[0])], axis=1)
    mine = dot_nn(all_context, out_part[...])
    rest = dot_nn(all_context, out_rest[...])
    summed = jnp.concatenate(
        [jnp.where(first, mine, rest), jnp.where(first, rest, mine)], axis=1
    )
    scratch[...] = x[...].astype(jnp.float32) + summed
    all_states = scratch[...].astype(jnp.bfloat16)
    shard = states.shape[0]
    start = pl.multiple_of(place[0] * shard, shard)
    states[...] = scratch[pl.ds(start, shard), :].astype(jnp.bfloat16)
    normed_rows = layer_norm(all_states, gains[2:3, :], biases[2:3, :])
    normed[...] = normed_rows
    normed_tokens = layer_norm(tokens[...], gains[1:2, :], biases[1:2, :])
    matrix = [jnp.where(first, other[kind], own[kind]) for kind in range(4)]
    queries = dot_nt(normed_tokens, matrix[0]).astype(jnp.bfloat16)
    keys = dot_nt(normed_rows, matrix[1]).astype(jnp.bfloat16)
    values = dot_nt(normed_rows, matrix[2]).astype(jnp.bfloat16)
    grad_context = dot_nt(upstream[...], matrix[3]).astype(jnp.bfloat16)
    count = tokens.shape[0]
    allowed = ids_along(token_lens, (count, 1), 0) == ids_along(frame_lens, (1, rows), 1)
    key_parts, value_parts, context_parts = [], [], []
    for head in range(queries.shape[1] // HS):
        at = slice(head * HS, (head + 1) * HS)
        weights = softmax(queries[:, at], keys[:, at], allowed)
        rounded = weights.astype(jnp.bfloat16)
        context_parts.append(dot_nn(rounded, values[:, at]))
        grad_scores = scores_grad(weights, grad_context[:, at], values[:, at])
        key_parts.append(dot_tn(grad_scores, queries[:, at]) * SCALING)
        value_parts.append(dot_tn(rounded, grad_context[:, at]))
    key_block, value_block = side_by_side(key_parts), side_by_side(value_parts)
    key_grad[...] = key_block
    value_grad[...] = value_block
    dec_context[...] = side_by_side(context_parts)
    partial[...] = (dot_nn(key_block, matrix[1]) + dot_nn(value_block, matrix[2])).astype(
        jnp.bfloat16
    )


def store_terms(products, term):
    high = products[0].shape[0]
    for index, product in enumerate(products):
        term[index * high : (index + 1) * high, :] = product.astype(jnp.bfloat16)


def dec_terms_kernel(key_grad, value_grad, context, normed, upstream, term):
    products = [
        dot_tn(key_grad[...], normed[...]),
        dot_tn(value_grad[...], normed[...]),
        dot_tn(context[...], upstream[...]),
    ]
    store_terms(products, term)


def norm_backward_kernel(pieces, states, gains, grads):
    summed = pieces[0].astype(jnp.float32)
    for index in range(1, pieces.shape[0]):
        summed = summed + pieces[index].astype(jnp.float32)
    center, inverse = row_stats(states[...].astype(jnp.float32))
    normed = center * inverse
    scaled = summed * gains[2:3, :]
    result = inverse * (
        scaled
        - jnp.mean(scaled, axis=-1, keepdims=True)
        - normed * jnp.mean(scaled * normed, axis=-1, keepdims=True)
    )
    block = result.astype(jnp.bfloat16)
    for copy in range(grads.shape[0]):
        grads[copy] = block


def enc_backward_kernel(
    core, grads, own, other, queries, values, probs, context, normed, term
):
    first = core[0] == 0
    grad_rows = grads[...]
    att_grad = dot_nt(grad_rows, jnp.where(first, own[0], other[0])).astype(jnp.bfloat16)
    query_rows, value_rows = queries[...], values[...]
    key_parts, value_parts = [], []
    for head in range(query_rows.shape[1] // HS):
        at = slice(head * HS, (head + 1) * HS)
        weights = probs[head]
        grad_scores = scores_grad(weights, att_grad[:, at], value_rows[:, at])
        key_parts.append(dot_tn(grad_scores, query_rows[:, at]) * SCALING)
        value_parts.append(dot_tn(weights.astype(jnp.bfloat16), att_grad[:, at]))
    products = [
        dot_tn(side_by_side(key_parts), normed[...]),
        dot_tn(side_by_side(value_parts), normed[...]),
        dot_tn(context[0], grad_rows),
    ]
    store_terms(products, term)


def chunks_kernel(core, enc_term, enc_sent, dec_term, dec_sent, tiles):
    first = core[0] == 0
    rows, cols = enc_term.shape
    high = rows // 8
    for block in range(cols // 128):
        at = slice(block * 128, (block + 1) * 128)
        kept = jnp.where(first, enc_term[:, at], dec_term[:, at])
        received = jnp.where(first, enc_sent[:, at], dec_sent[:, at])
        total = kept.astype(jnp.float32) + received.astype(jnp.float32)
        part = total.reshape(high, 8, 128)
        tiles[block * high : (block + 1) * high] = part.astype(jnp.bfloat16)


def sum_kernel(pieces, total):
    summed = pieces[0].astype(jnp.float32)
    for index in range(1, pieces.shape[0]):
        summed = summed + pieces[index].astype(jnp.float32)
    total[...] = summed.astype(jnp.bfloat16)


def sum_copies_kernel(pieces, copies):
    summed = pieces[0].astype(jnp.float32)
    for index in range(1, pieces.shape[0]):
        summed = summed + pieces[index].astype(jnp.float32)
    block = summed.astype(jnp.bfloat16)
    for copy in range(copies.shape[0]):
        copies[copy] = block


def copies_kernel(block, copies):
    for copy in range(copies.shape[0]):
        copies[copy] = block[...]


def from_chunks_kernel(tiles, gradient):
    rows, cols = gradient.shape
    high = rows // 8
    for block in range(cols // 128):
        part = tiles[block * high : (block + 1) * high].astype(jnp.float32)
        gradient[:, block * 128 : (block + 1) * 128] = part.reshape(rows, 128)


def call(kernel, outs, scalars, arrays, blocks=None, scratch=()):
    blocks = blocks or {}

    def spec(index, array):
        shape, at = blocks.get(index, (array.shape, (0,) * array.ndim))
        return pl.BlockSpec(shape, lambda i: at)

    result = pl.pallas_call(
        kernel,
        grid=(1,),
        out_shape=[jax.ShapeDtypeStruct(shape, dtype) for shape, dtype in outs],
        in_specs=[pl.BlockSpec(memory_space=pltpu.SMEM) for _ in scalars]
        + [spec(index, array) for index, array in enumerate(arrays)],
        out_specs=[
            pl.BlockSpec(shape, functools.partial(lambda n, i: (0,) * n, len(shape)))
            for shape, _ in outs
        ],
        scratch_shapes=list(scratch),
        compiler_params=pltpu.CompilerParams(vmem_limit_bytes=48 << 20),
    )(*scalars, *arrays)
    return result[0] if len(outs) == 1 else result


def swap(block):
    return lax.ppermute(block, "segment", [(0, 1), (1, 0)])


def shards(
    frames, dec_states, out_grad, frame_lengths, token_lengths, weights, norm_gains, norm_biases
):
    bf16, f32 = jnp.bfloat16, jnp.float32
    core = lax.axis_index("segment")
    first = core == 0
    own = weights[0]
    shard_rows, features = frames.shape[1:]
    mp = lax.axis_size("mp")
    dp = lax.axis_size("dp")
    head_cols = own.shape[1]
    heads = head_cols // HS
    rows = shard_rows * mp
    half = features // 2
    slow = 4 if dp % 4 == 0 else 1
    quick = dp // slow
    slow_groups = [[a * quick + b for a in range(slow)] for b in range(quick)]
    quick_groups = [[a * quick + b for b in range(quick)] for a in range(slow)]

    def mine(array):
        return lax.dynamic_index_in_dim(array, core, 0, keepdims=False)

    def exchange(blocks, axis="mp", groups=None):
        return lax.all_to_all(blocks, axis, 0, 0, axis_index_groups=groups)

    core_id = core.astype(jnp.int32).reshape(1)
    place = lax.axis_index("mp").astype(jnp.int32).reshape(1)
    inputs = mine(frames)
    tokens = mine(dec_states)
    upstream = mine(out_grad)
    frame_lens = mine(frame_lengths)[0]
    token_lens = mine(token_lengths)[0]

    out_sent = lax.ppermute(own[3, :, half:], "segment", [(0, 1)])
    out_part = jnp.where(first, own[3, :, :half], out_sent)
    out_part = lax.all_gather(out_part, "mp", axis=0, tiled=True)

    copies = jnp.broadcast_to(inputs[None], (mp, shard_rows, features))
    enc_full = exchange(copies).reshape(rows, features)
    other = swap(own)

    weight_block = ((3, head_cols, features), (0, 0, 0))
    normed, queries, keys, values, context, probs = call(
        enc_forward_kernel,
        [
            ((rows, features), bf16),
            ((rows, head_cols), bf16),
            ((rows, head_cols), bf16),
            ((rows, head_cols), bf16),
            ((mp, rows, head_cols), bf16),
            ((heads, rows, rows), f32),
        ],
        (core_id, frame_lens),
        (enc_full, own, other, norm_gains, norm_biases),
        {1: weight_block, 2: weight_block},
    )
    context_full, out_part = lax.optimization_barrier((exchange(context), out_part))
    out_rest = swap(out_part)
    partial, states, state_normed, dec_key_grad, dec_value_grad, dec_context = call(
        dec_kernel,
        [
            ((rows, features), bf16),
            ((shard_rows, features), bf16),
            ((rows, features), bf16),
            ((rows, head_cols), bf16),
            ((rows, head_cols), bf16),
            ((tokens.shape[0], head_cols), bf16),
        ],
        (core_id, place, frame_lens, token_lens),
        (
            enc_full, context_full, out_part, out_rest, own, other, tokens, upstream,
            norm_gains, norm_biases,
        ),
        scratch=[pltpu.VMEM((rows, features), f32)],
    )
    pieces = exchange(partial.reshape(mp, shard_rows, features))
    whole = [((3 * head_cols, features), bf16)]
    dec_term = call(
        dec_terms_kernel,
        whole,
        (),
        (dec_key_grad, dec_value_grad, dec_context, state_normed, upstream),
    )
    grads = call(
        norm_backward_kernel,
        [((mp, shard_rows, features), bf16)],
        (),
        (pieces, states, norm_gains),
    )
    grads_full = exchange(grads).reshape(rows, features)
    last_block = ((1, head_cols, features), (3, 0, 0))
    first_context = ((1, rows, head_cols), (0, 0, 0))
    enc_term = call(
        enc_backward_kernel,
        whole,
        (core_id,),
        (grads_full, own, other, queries, values, probs, context, normed),
        {1: last_block, 2: last_block, 6: first_context},
    )
    dec_sent = lax.ppermute(dec_term, "segment", [(0, 1)])
    enc_sent = lax.ppermute(enc_term, "segment", [(1, 0)])
    count = 3 * head_cols * features // 1024
    tiles = call(
        chunks_kernel,
        [((count, 8, 128), bf16)],
        (core_id,),
        (enc_term, enc_sent, dec_term, dec_sent),
    )
    parts = exchange(tiles.reshape(slow, count // slow, 8, 128), "dp", slow_groups)
    parts = call(sum_kernel, [((count // slow, 8, 128), bf16)], (), (parts,))
    parts = exchange(parts.reshape(quick, count // dp, 8, 128), "dp", quick_groups)
    parts = call(sum_copies_kernel, [((quick, count // dp, 8, 128), bf16)], (), (parts,))
    parts = exchange(parts, "dp", quick_groups).reshape(count // slow, 8, 128)
    parts = call(copies_kernel, [((slow, count // slow, 8, 128), bf16)], (), (parts,))
    parts = exchange(parts, "dp", slow_groups).reshape(count, 8, 128)
    gradient = call(from_chunks_kernel, [((3 * head_cols, features), f32)], (), (parts,))
    return gradient.reshape(1, 3, head_cols, features)


def solution(mesh):
    placed = (
        P(None, ("dp", "mp"), None),
        P(None, "dp", None),
        P(None, "dp", None),
        P(None, "dp", None),
        P(None, "dp", None),
        P("segment", None, "mp", None),
        P(),
        P(),
    )
    return jax.shard_map(
        shards,
        mesh=mesh,
        in_specs=placed,
        out_specs=P("segment", None, "mp", None),
        check_vma=False,
    )
```

time: 239 us -> 222 us (0.929)
  the two profiles are of different devices: /device:TPU:8 before, /device:TPU:1 now
where the time goes in v3:
time: 222 us; the launch traced here: 218 us
  blocking collectives  100 us (45%)
  waiting for transfers between devices  49.3 us (22%)
  starting transfers between devices  20.2 us (9%)
  local copies, waits for them, and re-layouts  16.7 us (8%)
  Pallas kernels  16 us (7%)
  between operations  13.6 us (6%)
    all_to_all x6, blocking collectives, exchange(): return lax.all_to_all(blocks, axis, 0, 0, axis_index_groups=groups)  100 us
    all_to_all x2, waiting for transfers between devices, exchange(): return lax.all_to_all(blocks, axis, 0, 0, axis_index_groups=groups)  37.7 us
    pallas_call x10, Pallas kernels, call(): pl.pallas_call(kernel, grid=(1,), out_shape=[jax.ShapeDtypeStruct(shape,...  16 us
    unnamed x56, local copies, waits for them, and re-layouts  13.8 us
    all_to_all x2, starting transfers between devices, exchange(): return lax.all_to_all(blocks, axis, 0, 0, axis_index_groups=groups)  8.78 us
    ppermute x1, waiting for transfers between devices, shards(): out_sent = lax.ppermute(own[3, :, half:], 'segment', [(0, 1)])  7.74 us
    ppermute x2, starting transfers between devices, swap(): return lax.ppermute(block, 'segment', [(0, 1), (1, 0)])  4.88 us
  transfers between devices with their start and end apart: 8, of which 5 were waited for; matrix products, arithmetic and copies ran while one was open for 1% of the time, Pallas kernels for 3%

profile of v3, /device:TPU:1, one launch (start us, length us, event | category | flops | bytes accessed | tf_op | source)
XLA Modules:
  0.0 217.9 jit_solution(12488469995242227596)
XLA Ops:
  6.5 0.0 copy-start
  6.5 0.0 all-gather.2.cloned.1.call-start
  6.5 1.0 slice_bitcast_fusion
  7.5 1.3 collective-permute-start.1
  8.8 7.7 %collective-permute-done.1 = bf16[128,640]{1,0:T(8,128)(2,1)S(1)} collective-permute-done((bf16[128,640]{1,0:T(8,128)(2,1)S(1)}, bf16[128,640]{1,0:T(8,128)(2,1)S(1)}, u32[]{:S(2)}, u32[]{:S(2)}) %collective-permute-start.1) | collective-permute-done | bytes 163872 | tf_op jit(solution)/shard_map/ppermute | solution.py:294
  16.6 1.6 fusion
  18.2 0.0 all-gather.2.cloned.1.call-update
  18.2 2.2 %collective-permute-start = (bf16[4,128,1280]{2,1,0:T(8,128)(2,1)}, bf16[4,128,1280]{2,1,0:T(8,128)(2,1)S(1)}, u32[]{:S(2)}, u32[]{:S(2)}) collective-permute-start(bf16[4,128,1280]{2,1,0:T(8,128)(2,1)} %bitcast.29), channel_id=1, source_target_pairs={{0,8},{8,0},{1,9},{9,1},{2,10},{10,2},{3,11},{11,3},{4,12},{12,4},... | collective-permute-start | bytes 3932168 | tf_op jit(solution)/shard_map/ppermute | solution.py:258
  20.4 0.0 copy-done
  20.4 0.9 broadcast_in_dim.9
  21.3 5.1 %all-to-all-start = ((bf16[8,32,1280]{2,1,0:T(8,128)(2,1)}), bf16[8,32,1280]{2,1,0:T(8,128)(2,1)S(1)}, u32[]{:S(2)}, u32[]{:S(2)}) async-start(bf16[8,32,1280]{2,1,0:T(8,128)(2,1)} %broadcast_in_dim.9), calls=%async_computation | async-start | bytes 1310720 | tf_op jit(solution)/shard_map/all_to_all | solution.py:284
  26.4 0.0 copy-done.26
  26.4 25.7 %all-to-all-done = bf16[8,32,1280]{2,1,0:T(8,128)(2,1)S(1)} async-done(((bf16[8,32,1280]{2,1,0:T(8,128)(2,1)}), bf16[8,32,1280]{2,1,0:T(8,128)(2,1)S(1)}, u32[]{:S(2)}, u32[]{:S(2)}) %all-to-all-start) | async-done | bytes 655392 | tf_op jit(solution)/shard_map/all_to_all | solution.py:284
  52.1 0.0 collective-permute-done.other
  52.1 0.0 copy-done.1
  52.1 0.0 copy-done.16
  52.1 0.0 copy-done.17
  52.2 0.0 copy-start.27
  52.2 2.5 %shard_map.82 = (bf16[256,1280]{1,0:T(8,128)(2,1)S(1)}, bf16[256,128]{1,0:T(8,128)(2,1)S(1)}, bf16[256,128]{1,0:T(8,128)(2,1)}, bf16[256,128]{1,0:T(8,128)(2,1)S...) custom-call(s32[1]{0:T(128)} %bitcast.core, s32[4]{0:T(128)S(1)} %fusion.1.lengths.frame_lens, ...), custom_call_target="tpu_custom_call" | custom-call | tf_op jit(solution)/shard_map/pallas_call | solution.py:241
  54.7 0.0 copy-done.3
  54.7 0.0 copy-start.10
  54.7 0.8 copy-done.10
  55.5 0.8 copy-done.14
  56.3 0.6 copy-done.18
  57.0 19.6 %all_to_all.40.context = bf16[8,256,128]{2,1,0:T(8,128)(2,1)S(1)} all-to-all(bf16[8,256,128]{2,1,0:T(8,128)(2,1)S(1)} %get-tuple-element.18.context), channel_id=1, replica_groups=mesh['dp'=32,'segment'=2,'mp'=8] {'mp'}, dimensions={0} | all-to-all | bytes 1048576 | tf_op jit(solution)/shard_map/all_to_all | solution.py:284
  76.6 0.8 copy-done.5
  77.4 2.7 %collective-permute-start.2 = (bf16[1024,640]{1,0:T(8,128)(2,1)}, bf16[1024,640]{1,0:T(8,128)(2,1)S(1)}, u32[]{:S(2)}, u32[]{:S(2)}) collective-permute-start(bf16[1024,640]{1,0:T(8,128)(2,1)} %all-gather.2.cloned.1.call-done.out_part), channel_id=1, source_target_pairs={{0,8},{8,0},{1,9},{9,1},{2,10},{10,2},{3,11},{11,3},{4,12},{12,4},... | collective-permute-start | bytes 3932168 | tf_op jit(solution)/shard_map/ppermute | solution.py:258
  80.1 0.0 copy-done.27
  80.1 1.0 dynamic-slice_bitcast_fusion
  81.2 0.0 copy-start.7
  81.2 1.8 collective-permute-done.2.out_rest
  83.0 1.3 copy-done.9
  84.3 5.4 %shard_map.83 = (bf16[256,1280]{1,0:T(8,128)(2,1)S(1)}, bf16[32,1280]{1,0:T(8,128)(2,1)S(1)}, bf16[256,1280]{1,0:T(8,128)(2,1)S(1)}, bf16[256,128]{1,0:T(8,128)(...) custom-call(s32[1]{0:T(128)} %bitcast.core, s32[1]{0:T(128)} %bitcast.1.place, ...), custom_call_target="tpu_custom_call" | custom-call | tf_op jit(solution)/shard_map/pallas_call | solution.py:241
  89.7 0.0 copy-done.7
  89.8 0.8 copy-done.12
  90.6 21.9 %all_to_all.41.pieces = bf16[8,32,1280]{2,1,0:T(8,128)(2,1)S(1)} all-to-all(bf16[8,32,1280]{2,1,0:T(8,128)(2,1)S(1)} %bitcast.40), channel_id=1, replica_groups=mesh['dp'=32,'segment'=2,'mp'=8] {'mp'}, dimensions={0} | all-to-all | bytes 1310720 | tf_op jit(solution)/shard_map/all_to_all | solution.py:284
  112.6 1.2 shard_map.84
  113.7 3.7 %all-to-all-start.3 = ((bf16[8,32,1280]{2,1,0:T(8,128)(2,1)}), bf16[8,32,1280]{2,1,0:T(8,128)(2,1)S(1)}, u32[]{:S(2)}, u32[]{:S(2)}) async-start(bf16[8,32,1280]{2,1,0:T(8,128)(2,1)} %shard_map.84), calls=%async_computation.3 | async-start | bytes 1310720 | tf_op jit(solution)/shard_map/all_to_all | solution.py:284
  117.4 0.0 copy-start.2
  117.4 1.0 copy-done.8
  118.5 1.1 copy-done.13
  119.5 0.8 copy-done.21
  120.4 0.8 copy-done.23
  121.2 0.7 copy-done.25
  121.9 1.4 shard_map.86.dec_term
  123.3 1.3 collective-permute-start.4
  124.6 12.0 %all-to-all-done.3 = bf16[8,32,1280]{2,1,0:T(8,128)(2,1)S(1)} async-done(((bf16[8,32,1280]{2,1,0:T(8,128)(2,1)}), bf16[8,32,1280]{2,1,0:T(8,128)(2,1)S(1)}, u32[]{:S(2)}, u32[]{:S(2)}) %all-to-all-start.3) | async-done | bytes 655392 | tf_op jit(solution)/shard_map/all_to_all | solution.py:284
  136.6 0.0 copy-done.2
  136.6 1.0 copy-done.6
  137.7 1.1 copy-done.11
  138.7 1.0 copy-done.15
  139.8 0.8 copy-done.19
  140.6 1.9 shard_map.85.enc_term
  142.5 3.9 %collective-permute-start.3 = (bf16[384,1280]{1,0:T(8,128)(2,1)S(1)}, bf16[384,1280]{1,0:T(8,128)(2,1)S(1)}, u32[]{:S(2)}, u32[]{:S(2)}) collective-permute-start(bf16[384,1280]{1,0:T(8,128)(2,1)S(1)} %shard_map.85.enc_term), channel_id=1, source_target_pairs={{8,0},{9,1},{10,2},{11,3},{12,4},{13,5},{14,6},{15,7},{24,16},{25,... | collective-permute-start | bytes 2949128 | tf_op jit(solution)/shard_map/ppermute | solution.py:361
  146.5 0.0 collective-permute-done.4.dec_sent
  146.5 2.1 collective-permute-done.3.enc_sent
  148.6 1.9 shard_map.87
  150.5 17.7 %all_to_all.42.pieces = bf16[4,120,8,128]{3,2,1,0:T(8,128)(2,1)S(1)} all-to-all(bf16[4,120,8,128]{3,2,1,0:T(8,128)(2,1)S(1)} %bitcast.35), channel_id=1, replica_groups={{0,128,256,384},{16,144,272,400},{32,160,288,416},{48,176,304,432},{64,..., dimensions={0} | all-to-all | bytes 1966080 | tf_op jit(solution)/shard_map/all_to_all | solution.py:284
  168.2 0.1 shard_map.88
  168.3 16.3 %all_to_all.43.pieces = bf16[8,15,8,128]{3,2,1,0:T(8,128)(2,1)S(1)} all-to-all(bf16[8,15,8,128]{3,2,1,0:T(8,128)(2,1)S(1)} %bitcast.38), channel_id=1, replica_groups={{0,16,32,48,64,80,96,112},{128,144,160,176,192,208,224,240},{256,272,28..., dimensions={0} | all-to-all | bytes 491520 | tf_op jit(solution)/shard_map/all_to_all | solution.py:284
  184.6 12.2 %all_to_all.44 = bf16[8,15,8,128]{3,2,1,0:T(8,128)(2,1)S(1)} all-to-all(bf16[8,15,8,128]{3,2,1,0:T(8,128)(2,1)S(1)} %shard_map.89), channel_id=1, replica_groups={{0,16,32,48,64,80,96,112},{128,144,160,176,192,208,224,240},{256,272,28..., dimensions={0} | all-to-all | bytes 491520 | tf_op jit(solution)/shard_map/all_to_all | solution.py:284
  196.8 0.1 shard_map.90
  196.9 12.7 %all_to_all.45 = bf16[4,120,8,128]{3,2,1,0:T(8,128)(2,1)S(1)} all-to-all(bf16[4,120,8,128]{3,2,1,0:T(8,128)(2,1)S(1)} %shard_map.90), channel_id=1, replica_groups={{0,128,256,384},{16,144,272,400},{32,160,288,416},{48,176,304,432},{64,..., dimensions={0} | all-to-all | bytes 1966080 | tf_op jit(solution)/shard_map/all_to_all | solution.py:284
  209.7 1.4 shard_map.91
  (32 shorter events, 0.1 us)
Async XLA Ops:
  6.5 13.9 %copy-start = (bf16[2,32,1280]{2,1,0:T(8,128)(2,1)S(1)}, bf16[2,32,1280]{2,1,0:T(8,128)(2,1)}, u32[]{:S(2)}) copy-start(bf16[2,32,1280]{2,1,0:T(8,128)(2,1)} %param.8) | copy-start | bytes 491524
  6.5 70.9 %all-gather.2.cloned.1.call-start = ((), (), s32[]{:S(2)}) async-start(), calls=%async_computation.8 | async-start | bytes 1474560 | tf_op jit(solution)/shard_map/all_gather | solution.py:296
  7.5 9.0 %collective-permute-start.1 = (bf16[128,640]{1,0:T(8,128)(2,1)S(1)}, bf16[128,640]{1,0:T(8,128)(2,1)S(1)}, u32[]{:S(2)}, u32[]{:S(2)}) collective-permute-start(bf16[128,640]{1,0:T(8,128)(2,1)S(1)} %slice_bitcast_fusion), channel_id=1, source_target_pairs={{0,8},{1,9},{2,10},{3,11},{4,12},{5,13},{6,14},{7,15},{16,24},{17,... | collective-permute-start | bytes 491528 | tf_op jit(solution)/shard_map/ppermute | solution.py:294
  18.2 8.3 %copy-start.26 = (s32[2,1,4]{2,1,0:T(1,128)S(1)}, s32[2,1,4]{2,1,0:T(1,128)}, u32[]{:S(2)}) copy-start(s32[2,1,4]{2,1,0:T(1,128)} %param.11) | copy-start | bytes 100
  18.2 34.0 %copy-start.1 = (bf16[1,4,128,1280]{3,2,1,0:T(8,128)(2,1)S(1)}, bf16[1,4,128,1280]{3,2,1,0:T(8,128)(2,1)}, u32[]{:S(2)}) copy-start(bf16[1,4,128,1280]{3,2,1,0:T(8,128)(2,1)} %param.13) | copy-start | bytes 3932164
  18.2 34.0 %copy-start.16 = (f32[3,1280]{1,0:T(4,128)S(1)}, f32[3,1280]{1,0:T(4,128)}, u32[]{:S(2)}) copy-start(f32[3,1280]{1,0:T(4,128)} %gains.5) | copy-start | bytes 46084
  18.2 34.0 %copy-start.17 = (f32[3,1280]{1,0:T(4,128)S(1)}, f32[3,1280]{1,0:T(4,128)}, u32[]{:S(2)}) copy-start(f32[3,1280]{1,0:T(4,128)} %biases.3) | copy-start | bytes 46084
  18.2 33.9 %collective-permute-start = (bf16[4,128,1280]{2,1,0:T(8,128)(2,1)}, bf16[4,128,1280]{2,1,0:T(8,128)(2,1)S(1)}, u32[]{:S(2)}, u32[]{:S(2)}) collective-permute-start(bf16[4,128,1280]{2,1,0:T(8,128)(2,1)} %bitcast.29), channel_id=1, source_target_pairs={{0,8},{8,0},{1,9},{9,1},{2,10},{10,2},{3,11},{11,3},{4,12},{12,4},... | collective-permute-start | bytes 3932168 | tf_op jit(solution)/shard_map/ppermute | solution.py:258
  21.3 30.8 %all-to-all-start = ((bf16[8,32,1280]{2,1,0:T(8,128)(2,1)}), bf16[8,32,1280]{2,1,0:T(8,128)(2,1)S(1)}, u32[]{:S(2)}, u32[]{:S(2)}) async-start(bf16[8,32,1280]{2,1,0:T(8,128)(2,1)} %broadcast_in_dim.9), calls=%async_computation | async-start | bytes 1310720 | tf_op jit(solution)/shard_map/all_to_all | solution.py:284
  52.1 2.6 %copy-start.3 = (bf16[4,128,1280]{2,1,0:T(8,128)(2,1)}, bf16[4,128,1280]{2,1,0:T(8,128)(2,1)S(1)}, u32[]{:S(2)}) copy-start(bf16[4,128,1280]{2,1,0:T(8,128)(2,1)S(1)} %collective-permute-done.other) | copy-start | bytes 3932164
  52.2 28.0 %copy-start.27 = (s32[2,1,4]{2,1,0:T(1,128)S(1)}, s32[2,1,4]{2,1,0:T(1,128)}, u32[]{:S(2)}) copy-start(s32[2,1,4]{2,1,0:T(1,128)} %param.12) | copy-start | bytes 100
  54.7 0.9 copy-start.10
  55.5 0.8 copy-start.14
  56.3 0.6 copy-start.18
  76.6 0.8 copy-start.5
  77.4 5.6 %collective-permute-start.2 = (bf16[1024,640]{1,0:T(8,128)(2,1)}, bf16[1024,640]{1,0:T(8,128)(2,1)S(1)}, u32[]{:S(2)}, u32[]{:S(2)}) collective-permute-start(bf16[1024,640]{1,0:T(8,128)(2,1)} %all-gather.2.cloned.1.call-done.out_part), channel_id=1, source_target_pairs={{0,8},{8,0},{1,9},{9,1},{2,10},{10,2},{3,11},{11,3},{4,12},{12,4},... | collective-permute-start | bytes 3932168 | tf_op jit(solution)/shard_map/ppermute | solution.py:258
  81.2 8.6 %copy-start.7 = (bf16[64,1280]{1,0:T(8,128)(2,1)}, bf16[64,1280]{1,0:T(8,128)(2,1)S(1)}, u32[]{:S(2)}) copy-start(bf16[64,1280]{1,0:T(8,128)(2,1)S(1)} %get-tuple-element.31.upstream) | copy-start | bytes 491524
  83.0 1.3 copy-start.9
  89.8 0.8 copy-start.12
  90.6 22.0 %copy-start.20 = (bf16[256,128]{1,0:T(8,128)(2,1)}, bf16[256,128]{1,0:T(8,128)(2,1)S(1)}, u32[]{:S(2)}) copy-start(bf16[256,128]{1,0:T(8,128)(2,1)S(1)} %get-tuple-element.27.key_grad) | copy-start | bytes 196612
  90.6 22.0 %copy-start.22 = (bf16[256,128]{1,0:T(8,128)(2,1)}, bf16[256,128]{1,0:T(8,128)(2,1)S(1)}, u32[]{:S(2)}) copy-start(bf16[256,128]{1,0:T(8,128)(2,1)S(1)} %get-tuple-element.28.value_grad) | copy-start | bytes 196612
  90.6 22.0 %copy-start.24 = (bf16[64,128]{1,0:T(8,128)(2,1)}, bf16[64,128]{1,0:T(8,128)(2,1)S(1)}, u32[]{:S(2)}) copy-start(bf16[64,128]{1,0:T(8,128)(2,1)S(1)} %get-tuple-element.29.context) | copy-start | bytes 49156
  113.7 22.9 %copy-start.4 = (bf16[4,128,1280]{2,1,0:T(8,128)(2,1)S(1)}, bf16[4,128,1280]{2,1,0:T(8,128)(2,1)}, u32[]{:S(2)}) copy-start(bf16[4,128,1280]{2,1,0:T(8,128)(2,1)} %copy-done.3) | copy-start | bytes 3932164
  113.7 22.9 %all-to-all-start.3 = ((bf16[8,32,1280]{2,1,0:T(8,128)(2,1)}), bf16[8,32,1280]{2,1,0:T(8,128)(2,1)S(1)}, u32[]{:S(2)}, u32[]{:S(2)}) async-start(bf16[8,32,1280]{2,1,0:T(8,128)(2,1)} %shard_map.84), calls=%async_computation.3 | async-start | bytes 1310720 | tf_op jit(solution)/shard_map/all_to_all | solution.py:284
  117.4 19.2 %copy-start.2 = (bf16[1,4,128,1280]{3,2,1,0:T(8,128)(2,1)S(1)}, bf16[1,4,128,1280]{3,2,1,0:T(8,128)(2,1)}, u32[]{:S(2)}) copy-start(bf16[1,4,128,1280]{3,2,1,0:T(8,128)(2,1)} %param.13) | copy-start | bytes 3932164
  117.4 1.0 copy-start.8
  118.5 1.1 copy-start.13
  119.5 0.8 copy-start.21
  120.4 0.8 copy-start.23
  121.2 0.7 copy-start.25
  123.3 23.2 %collective-permute-start.4 = (bf16[384,1280]{1,0:T(8,128)(2,1)}, bf16[384,1280]{1,0:T(8,128)(2,1)}, u32[]{:S(2)}, u32[]{:S(2)}) collective-permute-start(bf16[384,1280]{1,0:T(8,128)(2,1)} %shard_map.86.dec_term), channel_id=1, source_target_pairs={{0,8},{1,9},{2,10},{3,11},{4,12},{5,13},{6,14},{7,15},{16,24},{17,... | collective-permute-start | bytes 2949128 | tf_op jit(solution)/shard_map/ppermute | solution.py:360
  136.6 1.0 copy-start.6
  137.7 1.1 copy-start.11
  138.7 1.0 copy-start.15
  139.8 0.8 copy-start.19
  142.5 6.1 %collective-permute-start.3 = (bf16[384,1280]{1,0:T(8,128)(2,1)S(1)}, bf16[384,1280]{1,0:T(8,128)(2,1)S(1)}, u32[]{:S(2)}, u32[]{:S(2)}) collective-permute-start(bf16[384,1280]{1,0:T(8,128)(2,1)S(1)} %shard_map.85.enc_term), channel_id=1, source_target_pairs={{8,0},{9,1},{10,2},{11,3},{12,4},{13,5},{14,6},{15,7},{24,16},{25,... | collective-permute-start | bytes 2949128 | tf_op jit(solution)/shard_map/ppermute | solution.py:361
Sparse Core Ops, SparseCore 0:
  18.3 43.6 all-gather.1

commit v4 on v3

--- a/solution.py
+++ b/solution.py
@@ -38,12 +38,12 @@
     return (center * inverse * norm_gain + offset).astype(jnp.bfloat16)
 
 
-def ids_along(lengths_ref, shape, axis):
+def ids_along(lengths_ref, row, shape, axis):
     places = lax.broadcasted_iota(jnp.int32, shape, axis)
     bound = 0
     ids = jnp.zeros(shape, jnp.int32)
-    for piece in range(lengths_ref.shape[0]):
-        bound = bound + lengths_ref[piece]
+    for piece in range(lengths_ref.shape[2]):
+        bound = bound + lengths_ref[row, 0, piece]
         ids = ids + (places >= bound).astype(jnp.int32)
     return ids
 
@@ -65,19 +65,19 @@
 
 
 def enc_forward_kernel(
-    core, lengths, x, own, other, gains, biases, normed, queries, keys, values, context, probs
+    core, lengths, x, own, other, gains, biases, normed, queries, values, context, copies, probs
 ):
     first = core[0] == 0
     rows = x.shape[0]
     normed_rows = layer_norm(x[...], gains[0:1, :], biases[0:1, :])
     normed[...] = normed_rows
     projected = []
-    for kind, out in enumerate((queries, keys, values)):
+    for kind in range(3):
         matrix = jnp.where(first, own[kind], other[kind])
-        block = dot_nt(normed_rows, matrix).astype(jnp.bfloat16)
-        out[...] = block
-        projected.append(block)
-    allowed = ids_along(lengths, (rows, 1), 0) == ids_along(lengths, (1, rows), 1)
+        projected.append(dot_nt(normed_rows, matrix).astype(jnp.bfloat16))
+    queries[...] = projected[0]
+    values[...] = projected[2]
+    allowed = ids_along(lengths, core[0], (rows, 1), 0) == ids_along(lengths, core[0], (1, rows), 1)
     parts = []
     for head in range(queries.shape[1] // HS):
         at = slice(head * HS, (head + 1) * HS)
@@ -85,38 +85,57 @@
         probs[head] = weights
         parts.append(dot_nn(weights.astype(jnp.bfloat16), projected[2][:, at]))
     block = side_by_side(parts)
-    for copy in range(context.shape[0]):
-        context[copy] = block
+    context[...] = block
+    for copy in range(copies.shape[0]):
+        copies[copy] = block
+
+
+def token_kernel(core, tokens, upstream, own, other, gains, biases, queries, grad_context):
+    first = core[0] == 0
+    own_tokens = jnp.where(first, tokens[0], tokens[1])
+    normed_tokens = layer_norm(own_tokens, gains[1:2, :], biases[1:2, :])
+    matrix = jnp.where(first, other[0], own[0])
+    queries[...] = dot_nt(normed_tokens, matrix).astype(jnp.bfloat16)
+    matrix = jnp.where(first, other[3], own[3])
+    own_upstream = jnp.where(first, upstream[0], upstream[1])
+    grad_context[...] = dot_nt(own_upstream, matrix).astype(jnp.bfloat16)
+
+
+def half_context(context, second):
+    heads = []
+    for device in range(context.shape[0]):
+        block = context[device]
+        heads.append(jnp.where(second, block[:, HS:], block[:, :HS]))
+    return jnp.concatenate(heads, axis=1)
+
+
+def half_states_kernel(core, x, context, out_part, states):
+    left = half_context(context, core[0] == 1)
+    states[...] = x[...].astype(jnp.float32) + dot_nn(left, out_part[...])
 
 
 def dec_kernel(
-    core, place, frame_lens, token_lens, x, context, out_part, out_rest, own, other, tokens,
-    upstream, gains, biases, partial, states, normed, key_grad, value_grad, dec_context, scratch,
+    core, place, frame_lens, token_lens, half_states, context, out_rest, own, other, token_queries,
+    token_grads, gains, biases, partial, states, normed, key_grad, value_grad, dec_context, scratch,
 ):
     first = core[0] == 0
-    rows, features = x.shape
-    half = features // 2
-    all_context = jnp.concatenate([context[c] for c in range(context.shape[0])], axis=1)
-    mine = dot_nn(all_context, out_part[...])
-    rest = dot_nn(all_context, out_rest[...])
-    summed = jnp.concatenate(
-        [jnp.where(first, mine, rest), jnp.where(first, rest, mine)], axis=1
-    )
-    scratch[...] = x[...].astype(jnp.float32) + summed
+    rows = half_states.shape[0]
+    left = half_context(context, core[0] == 0)
+    scratch[...] = half_states[...] + dot_nn(left, out_rest[...])
     all_states = scratch[...].astype(jnp.bfloat16)
     shard = states.shape[0]
     start = pl.multiple_of(place[0] * shard, shard)
     states[...] = scratch[pl.ds(start, shard), :].astype(jnp.bfloat16)
     normed_rows = layer_norm(all_states, gains[2:3, :], biases[2:3, :])
     normed[...] = normed_rows
-    normed_tokens = layer_norm(tokens[...], gains[1:2, :], biases[1:2, :])
-    matrix = [jnp.where(first, other[kind], own[kind]) for kind in range(4)]
-    queries = dot_nt(normed_tokens, matrix[0]).astype(jnp.bfloat16)
-    keys = dot_nt(normed_rows, matrix[1]).astype(jnp.bfloat16)
-    values = dot_nt(normed_rows, matrix[2]).astype(jnp.bfloat16)
-    grad_context = dot_nt(upstream[...], matrix[3]).astype(jnp.bfloat16)
-    count = tokens.shape[0]
-    allowed = ids_along(token_lens, (count, 1), 0) == ids_along(frame_lens, (1, rows), 1)
+    matrix = [jnp.where(first, other[kind], own[kind]) for kind in (1, 2)]
+    queries = token_queries[...]
+    grad_context = token_grads[...]
+    keys = dot_nt(normed_rows, matrix[0]).astype(jnp.bfloat16)
+    values = dot_nt(normed_rows, matrix[1]).astype(jnp.bfloat16)
+    count = queries.shape[0]
+    token_ids = ids_along(token_lens, core[0], (count, 1), 0)
+    allowed = token_ids == ids_along(frame_lens, core[0], (1, rows), 1)
     key_parts, value_parts, context_parts = [], [], []
     for head in range(queries.shape[1] // HS):
         at = slice(head * HS, (head + 1) * HS)
@@ -130,7 +149,7 @@
     key_grad[...] = key_block
     value_grad[...] = value_block
     dec_context[...] = side_by_side(context_parts)
-    partial[...] = (dot_nn(key_block, matrix[1]) + dot_nn(value_block, matrix[2])).astype(
+    partial[...] = (dot_nn(key_block, matrix[0]) + dot_nn(value_block, matrix[1])).astype(
         jnp.bfloat16
     )
 
@@ -141,11 +160,11 @@
         term[index * high : (index + 1) * high, :] = product.astype(jnp.bfloat16)
 
 
-def dec_terms_kernel(key_grad, value_grad, context, normed, upstream, term):
+def dec_terms_kernel(core, key_grad, value_grad, context, normed, upstream, term):
     products = [
         dot_tn(key_grad[...], normed[...]),
         dot_tn(value_grad[...], normed[...]),
-        dot_tn(context[...], upstream[...]),
+        dot_tn(context[...], jnp.where(core[0] == 0, upstream[0], upstream[1])),
     ]
     store_terms(products, term)
 
@@ -184,7 +203,7 @@
     products = [
         dot_tn(side_by_side(key_parts), normed[...]),
         dot_tn(side_by_side(value_parts), normed[...]),
-        dot_tn(context[0], grad_rows),
+        dot_tn(context[...], grad_rows),
     ]
     store_terms(products, term)
 
@@ -202,13 +221,6 @@
         tiles[block * high : (block + 1) * high] = part.astype(jnp.bfloat16)
 
 
-def sum_kernel(pieces, total):
-    summed = pieces[0].astype(jnp.float32)
-    for index in range(1, pieces.shape[0]):
-        summed = summed + pieces[index].astype(jnp.float32)
-    total[...] = summed.astype(jnp.bfloat16)
-
-
 def sum_copies_kernel(pieces, copies):
     summed = pieces[0].astype(jnp.float32)
     for index in range(1, pieces.shape[0]):
@@ -218,9 +230,10 @@
         copies[copy] = block
 
 
-def copies_kernel(block, copies):
+def pick_copies_kernel(core, blocks, copies):
+    block = jnp.where(core[0] == 0, blocks[0], blocks[1])
     for copy in range(copies.shape[0]):
-        copies[copy] = block[...]
+        copies[copy] = block
 
 
 def from_chunks_kernel(tiles, gradient):
@@ -231,17 +244,24 @@
         gradient[:, block * 128 : (block + 1) * 128] = part.reshape(rows, 128)
 
 
-def call(kernel, outs, scalars, arrays, blocks=None, scratch=()):
+def call(kernel, outs, scalars, arrays, blocks=None, scratch=(), kept=(), read=()):
     blocks = blocks or {}
 
     def spec(index, array):
         shape, at = blocks.get(index, (array.shape, (0,) * array.ndim))
         return pl.BlockSpec(shape, lambda i: at)
 
+    def out(index, shape, dtype):
+        return pltpu.HBM(shape, dtype) if index in kept else jax.ShapeDtypeStruct(shape, dtype)
+
+    arrays = [
+        pltpu.with_memory_space_constraint(array, pltpu.HBM) if index in read else array
+        for index, array in enumerate(arrays)
+    ]
     result = pl.pallas_call(
         kernel,
         grid=(1,),
-        out_shape=[jax.ShapeDtypeStruct(shape, dtype) for shape, dtype in outs],
+        out_shape=[out(index, *what) for index, what in enumerate(outs)],
         in_specs=[pl.BlockSpec(memory_space=pltpu.SMEM) for _ in scalars]
         + [spec(index, array) for index, array in enumerate(arrays)],
         out_specs=[
@@ -271,36 +291,36 @@
     head_cols = own.shape[1]
     heads = head_cols // HS
     rows = shard_rows * mp
-    half = features // 2
-    slow = 4 if dp % 4 == 0 else 1
-    quick = dp // slow
-    slow_groups = [[a * quick + b for a in range(slow)] for b in range(quick)]
-    quick_groups = [[a * quick + b for b in range(quick)] for a in range(slow)]
-
-    def mine(array):
-        return lax.dynamic_index_in_dim(array, core, 0, keepdims=False)
+    count = dec_states.shape[1]
+    near_groups = [[x * 8 + y * 2 + b for x in range(4) for b in range(2)] for y in range(4)]
+    far_groups = [[x * 8 + y * 2 + b for y in range(4)] for x in range(4) for b in range(2)]
+    near, far = len(near_groups[0]), len(far_groups[0])
 
     def exchange(blocks, axis="mp", groups=None):
         return lax.all_to_all(blocks, axis, 0, 0, axis_index_groups=groups)
 
     core_id = core.astype(jnp.int32).reshape(1)
     place = lax.axis_index("mp").astype(jnp.int32).reshape(1)
-    inputs = mine(frames)
-    tokens = mine(dec_states)
-    upstream = mine(out_grad)
-    frame_lens = mine(frame_lengths)[0]
-    token_lens = mine(token_lengths)[0]
-
-    out_sent = lax.ppermute(own[3, :, half:], "segment", [(0, 1)])
-    out_part = jnp.where(first, own[3, :, :half], out_sent)
+
+    out_sent = lax.ppermute(own[3, HS:], "segment", [(0, 1)])
+    copies = call(
+        pick_copies_kernel, [((mp, shard_rows, features), bf16)], (core_id,), (frames,)
+    )
+    out_part = jnp.where(first, own[3, :HS], out_sent)
     out_part = lax.all_gather(out_part, "mp", axis=0, tiled=True)
-
-    copies = jnp.broadcast_to(inputs[None], (mp, shard_rows, features))
     enc_full = exchange(copies).reshape(rows, features)
     other = swap(own)
 
+    token_queries, token_grads = call(
+        token_kernel,
+        [((count, head_cols), bf16)] * 2,
+        (core_id,),
+        (dec_states, out_grad, own, other, norm_gains, norm_biases),
+        kept=(0, 1),
+        read=(0, 1, 2, 3),
+    )
     weight_block = ((3, head_cols, features), (0, 0, 0))
-    normed, queries, keys, values, context, probs = call(
+    normed, queries, values, context, context_copies, probs = call(
         enc_forward_kernel,
         [
             ((rows, features), bf16),
@@ -310,12 +330,21 @@
             ((mp, rows, head_cols), bf16),
             ((heads, rows, rows), f32),
         ],
-        (core_id, frame_lens),
+        (core_id, frame_lengths),
         (enc_full, own, other, norm_gains, norm_biases),
         {1: weight_block, 2: weight_block},
-    )
-    context_full, out_part = lax.optimization_barrier((exchange(context), out_part))
+        kept=(0, 1, 2, 3, 5),
+        read=(1,),
+    )
+    context_full, out_part = lax.optimization_barrier((exchange(context_copies), out_part))
     out_rest = swap(out_part)
+    half_states = call(
+        half_states_kernel,
+        [((rows, features), f32)],
+        (core_id,),
+        (enc_full, context_full, out_part),
+        read=(2,),
+    )
     partial, states, state_normed, dec_key_grad, dec_value_grad, dec_context = call(
         dec_kernel,
         [
@@ -324,55 +353,60 @@
             ((rows, features), bf16),
             ((rows, head_cols), bf16),
             ((rows, head_cols), bf16),
-            ((tokens.shape[0], head_cols), bf16),
+            ((count, head_cols), bf16),
         ],
-        (core_id, place, frame_lens, token_lens),
+        (core_id, place, frame_lengths, token_lengths),
         (
-            enc_full, context_full, out_part, out_rest, own, other, tokens, upstream,
+            half_states, context_full, out_rest, own, other, token_queries, token_grads,
             norm_gains, norm_biases,
         ),
         scratch=[pltpu.VMEM((rows, features), f32)],
+        kept=(1, 2, 3, 4, 5),
+        read=(3, 4, 5, 6),
     )
     pieces = exchange(partial.reshape(mp, shard_rows, features))
     whole = [((3 * head_cols, features), bf16)]
     dec_term = call(
         dec_terms_kernel,
         whole,
-        (),
-        (dec_key_grad, dec_value_grad, dec_context, state_normed, upstream),
+        (core_id,),
+        (dec_key_grad, dec_value_grad, dec_context, state_normed, out_grad),
+        kept=(0,),
+        read=(0, 1, 2, 3, 4),
     )
     grads = call(
         norm_backward_kernel,
         [((mp, shard_rows, features), bf16)],
         (),
         (pieces, states, norm_gains),
+        read=(1,),
     )
     grads_full = exchange(grads).reshape(rows, features)
     last_block = ((1, head_cols, features), (3, 0, 0))
-    first_context = ((1, rows, head_cols), (0, 0, 0))
     enc_term = call(
         enc_backward_kernel,
         whole,
         (core_id,),
         (grads_full, own, other, queries, values, probs, context, normed),
-        {1: last_block, 2: last_block, 6: first_context},
+        {1: last_block, 2: last_block},
+        read=(1, 2, 3, 4, 5, 6, 7),
     )
     dec_sent = lax.ppermute(dec_term, "segment", [(0, 1)])
     enc_sent = lax.ppermute(enc_term, "segment", [(1, 0)])
-    count = 3 * head_cols * features // 1024
+    size = 3 * head_cols * features // 1024
+    each = size // near
     tiles = call(
         chunks_kernel,
-        [((count, 8, 128), bf16)],
+        [((size, 8, 128), bf16)],
         (core_id,),
         (enc_term, enc_sent, dec_term, dec_sent),
-    )
-    parts = exchange(tiles.reshape(slow, count // slow, 8, 128), "dp", slow_groups)
-    parts = call(sum_kernel, [((count // slow, 8, 128), bf16)], (), (parts,))
-    parts = exchange(parts.reshape(quick, count // dp, 8, 128), "dp", quick_groups)
-    parts = call(sum_copies_kernel, [((quick, count // dp, 8, 128), bf16)], (), (parts,))
-    parts = exchange(parts, "dp", quick_groups).reshape(count // slow, 8, 128)
-    parts = call(copies_kernel, [((slow, count // slow, 8, 128), bf16)], (), (parts,))
-    parts = exchange(parts, "dp", slow_groups).reshape(count, 8, 128)
+        read=(2,),
+    )
+    parts = exchange(tiles.reshape(near, each, 8, 128), "dp", near_groups)
+    parts = call(sum_copies_kernel, [((far, each, 8, 128), bf16)], (), (parts,))
+    parts = exchange(parts, "dp", far_groups)
+    parts = call(sum_copies_kernel, [((near, each, 8, 128), bf16)], (), (parts,))
+    parts = exchange(parts, "dp", near_groups).reshape(size, 8, 128)
     gradient = call(from_chunks_kernel, [((3 * head_cols, features), f32)], (), (parts,))
     return gradient.reshape(1, 3, head_cols, features)
 

time: 222 us -> 212 us (0.955)
  blocking collectives: 100 us -> 127 us
  waiting for transfers between devices: 49.3 us -> 26.6 us
  local copies, waits for them, and re-layouts: 16.7 us -> 1.86 us
  Pallas kernels: 16 us -> 26 us
  starting transfers between devices: 20.2 us -> 13.9 us
    all_to_all x6, blocking collectives: 100 us -> 127 us  [exchange(): return lax.all_to_all(blocks, axis, 0, 0, axis_index_groups=groups)]
    all_to_all x2 -> x1, waiting for transfers between devices: 37.7 us -> 16.8 us  [exchange(): return lax.all_to_all(blocks, axis, 0, 0, axis_index_groups=groups)]
    unnamed x56 -> x12, local copies, waits for them, and re-layouts: 13.8 us -> 0.94 us
    pallas_call x10 -> x12, Pallas kernels: 16 us -> 26 us  [call(): pl.pallas_call(kernel, grid=(1,), out_shape=[out(index, *what) for index,...]
    all_to_all x2 -> x1, starting transfers between devices: 8.78 us -> 3.54 us  [exchange(): return lax.all_to_all(blocks, axis, 0, 0, axis_index_groups=groups)]
  transfers between devices with their start and end apart: 8 -> 7, of which waited for: 5 -> 3; matrix products, arithmetic and copies ran while one was open for 1% -> 0% of each run, Pallas kernels for 3% -> 7%
where the time goes in v4:
time: 212 us; the launch traced here: 210 us
  blocking collectives  127 us (60%)
  waiting for transfers between devices  26.6 us (13%)
  Pallas kernels  26 us (12%)
  starting transfers between devices  13.9 us (7%)
  between operations  13.6 us (6%)
    all_to_all x6, blocking collectives, exchange(): return lax.all_to_all(blocks, axis, 0, 0, axis_index_groups=groups)  127 us
    pallas_call x12, Pallas kernels, call(): pl.pallas_call(kernel, grid=(1,), out_shape=[out(index, *what) for index,...  26 us
    all_to_all x1, waiting for transfers between devices, exchange(): return lax.all_to_all(blocks, axis, 0, 0, axis_index_groups=groups)  16.8 us
    ppermute x1, waiting for transfers between devices, shards(): out_sent = lax.ppermute(own[3, HS:], 'segment', [(0, 1)])  7.7 us
    ppermute x2, starting transfers between devices, swap(): return lax.ppermute(block, 'segment', [(0, 1), (1, 0)])  5.33 us
  transfers between devices with their start and end apart: 7, of which 3 were waited for; matrix products, arithmetic and copies ran while one was open for 0% of the time, Pallas kernels for 7%

profile of v4, /device:TPU:1, one launch (start us, length us, event | category | flops | bytes accessed | tf_op | source)
XLA Modules:
  0.0 210.1 jit_solution(10772851422875522295)
XLA Ops:
  6.5 0.0 all-gather.2.cloned.1.call-start
  6.5 0.9 slice_bitcast_fusion
  7.5 1.3 collective-permute-start.1
  8.8 0.0 copy-start.1
  8.8 0.0 copy-start.2
  8.8 0.0 copy-start.4
  8.8 7.7 %collective-permute-done.1 = bf16[64,1280]{1,0:T(8,128)(2,1)S(1)} collective-permute-done((bf16[64,1280]{1,0:T(8,128)(2,1)S(1)}, bf16[64,1280]{1,0:T(8,128)(2,1)S(1)}, u32[]{:S(2)}, u32[]{:S(2)}) %collective-permute-start.1) | collective-permute-done | bytes 163872 | tf_op jit(solution)/shard_map/ppermute | solution.py:305
  16.5 1.6 fusion
  18.1 0.0 all-gather.2.cloned.1.call-update
  18.1 2.1 collective-permute-start
  20.2 0.0 copy-start.3
  20.2 0.9 copy-done.3
  21.2 28.6 %all_to_all.35 = bf16[8,32,1280]{2,1,0:T(8,128)(2,1)S(1)} all-to-all(bf16[8,32,1280]{2,1,0:T(8,128)(2,1)S(1)} %shard_map.82), channel_id=1, replica_groups=mesh['dp'=32,'segment'=2,'mp'=8] {'mp'}, dimensions={0} | all-to-all | bytes 1310720 | tf_op jit(solution)/shard_map/all_to_all | solution.py:300
  49.8 0.0 collective-permute-done.other
  49.8 0.0 copy-start
  49.8 0.0 copy-done.1
  49.8 0.0 copy-done.2
  49.8 0.0 copy-done.4
  49.8 4.4 %shard_map.83 = (bf16[256,1280]{1,0:T(8,128)(2,1)}, bf16[256,128]{1,0:T(8,128)(2,1)}, bf16[256,128]{1,0:T(8,128)(2,1)}, bf16[256,128]{1,0:T(8,128)(2,1)}, bf16[8...) custom-call(s32[1]{0:T(128)} %bitcast.core, s32[2,1,4]{2,1,0:T(1,128)S(1)} %copy-done.4, ...), custom_call_target="tpu_custom_call" | custom-call | tf_op jit(solution)/shard_map/pallas_call | solution.py:261
  54.3 0.0 copy-done
  54.3 20.1 %all_to_all.36.context = bf16[8,256,128]{2,1,0:T(8,128)(2,1)S(1)} all-to-all(bf16[8,256,128]{2,1,0:T(8,128)(2,1)S(1)} %get-tuple-element.21), channel_id=1, replica_groups=mesh['dp'=32,'segment'=2,'mp'=8] {'mp'}, dimensions={0} | all-to-all | bytes 1048576 | tf_op jit(solution)/shard_map/all_to_all | solution.py:300
  74.4 0.0 all-gather.2.cloned.1.call-done.out_part
  74.4 3.3 %collective-permute-start.2 = (bf16[512,1280]{1,0:T(8,128)(2,1)}, bf16[512,1280]{1,0:T(8,128)(2,1)S(1)}, u32[]{:S(2)}, u32[]{:S(2)}) collective-permute-start(bf16[512,1280]{1,0:T(8,128)(2,1)} %all-gather.2.cloned.1.call-done.out_part), channel_id=1, source_target_pairs={{0,8},{8,0},{1,9},{9,1},{2,10},{10,2},{3,11},{11,3},{4,12},{12,4},... | collective-permute-start | bytes 3932168 | tf_op jit(solution)/shard_map/ppermute | solution.py:278
  77.6 3.0 %shard_map.85 = (bf16[64,128]{1,0:T(8,128)(2,1)}, bf16[64,128]{1,0:T(8,128)(2,1)}) custom-call(s32[1]{0:T(128)} %bitcast.core, bf16[2,64,1280]{2,1,0:T(8,128)(2,1)} %tokens.1, bf16[2,64,1280]{2,1,0:T(8,128)(2,1)} %upstream.3, bf16[4,128,1280]{2,1,0:T(8,128)(2,1)} %bitcast.25, bf16[4,128,1280]{2,1,0:T(8,128)(2,1)} %copy-done, f32[3,1280]{1,0:T(4,128)S(1)} %copy-done.1, ...), custom_call_target="tpu_custom_call" | custom-call | tf_op jit(solution)/shard_map/pallas_call | solution.py:261
  80.7 0.0 copy-start.5
  80.7 2.2 %shard_map.84.half_states = f32[256,1280]{1,0:T(8,128)S(1)} custom-call(s32[1]{0:T(128)} %bitcast.core, bf16[256,1280]{1,0:T(8,128)(2,1)S(1)} %bitcast.16, bf16[8,256,128]{2,1,0:T(8,128)(2,1)S(1)} %all_to_all.36.context, bf16[512,1280]{1,0:T(8,128)(2,1)} %all-gather.2.cloned.1.call-done.out_part), custom_call_target="tpu_custom_call" | custom-call | tf_op jit(solution)/shard_map/pallas_call | solution.py:261
  82.8 0.0 collective-permute-done.2.out_rest
  82.8 0.0 copy-done.5
  82.9 5.0 %shard_map.86 = (bf16[256,1280]{1,0:T(8,128)(2,1)S(1)}, bf16[32,1280]{1,0:T(8,128)(2,1)}, bf16[256,1280]{1,0:T(8,128)(2,1)}, bf16[256,128]{1,0:T(8,128)(2,1)}, b...) custom-call(s32[1]{0:T(128)} %bitcast.core, s32[1]{0:T(128)} %bitcast.1.place, s32[2,1,4]{2,1,0:T(1,128)S(1)} %copy-done.4, ...), custom_call_target="tpu_custom_call" | custom-call | tf_op jit(solution)/shard_map/pallas_call | solution.py:261
  87.9 23.2 %all_to_all.37.pieces = bf16[8,32,1280]{2,1,0:T(8,128)(2,1)S(1)} all-to-all(bf16[8,32,1280]{2,1,0:T(8,128)(2,1)S(1)} %bitcast.20), channel_id=1, replica_groups=mesh['dp'=32,'segment'=2,'mp'=8] {'mp'}, dimensions={0} | all-to-all | bytes 1310720 | tf_op jit(solution)/shard_map/all_to_all | solution.py:300
  111.0 2.1 shard_map.87
  113.1 3.5 %all-to-all-start.3 = ((bf16[8,32,1280]{2,1,0:T(8,128)(2,1)}), bf16[8,32,1280]{2,1,0:T(8,128)(2,1)S(1)}, u32[]{:S(2)}, u32[]{:S(2)}) async-start(bf16[8,32,1280]{2,1,0:T(8,128)(2,1)} %shard_map.87), calls=%async_computation.3 | async-start | bytes 1310720 | tf_op jit(solution)/shard_map/all_to_all | solution.py:300
  116.7 2.6 %shard_map.89.dec_term = bf16[384,1280]{1,0:T(8,128)(2,1)} custom-call(s32[1]{0:T(128)} %bitcast.core, bf16[256,128]{1,0:T(8,128)(2,1)} %get-tuple-element.33.key_grad, bf16[256,128]{1,0:T(8,128)(2,1)} %get-tuple-element.34.value_grad, bf16[64,128]{1,0:T(8,128)(2,1)} %get-tuple-element.35.context, bf16[256,1280]{1,0:T(8,128)(2,1)} %get-tuple-element.36.normed, ...), custom_call_target="tpu_custom_call" | custom-call | tf_op jit(solution)/shard_map/pallas_call | solution.py:261
  119.3 1.3 collective-permute-start.4
  120.6 16.8 %all-to-all-done.3 = bf16[8,32,1280]{2,1,0:T(8,128)(2,1)S(1)} async-done(((bf16[8,32,1280]{2,1,0:T(8,128)(2,1)}), bf16[8,32,1280]{2,1,0:T(8,128)(2,1)S(1)}, u32[]{:S(2)}, u32[]{:S(2)}) %all-to-all-start.3) | async-done | bytes 655392 | tf_op jit(solution)/shard_map/all_to_all | solution.py:300
  137.3 3.4 %shard_map.88.enc_term = bf16[384,1280]{1,0:T(8,128)(2,1)S(1)} custom-call(s32[1]{0:T(128)} %bitcast.core, bf16[256,1280]{1,0:T(8,128)(2,1)S(1)} %bitcast.19, bf16[4,128,1280]{2,1,0:T(8,128)(2,1)} %bitcast.27, bf16[4,128,1280]{2,1,0:T(8,128)(2,1)} %copy-done, bf16[256,128]{1,0:T(8,128)(2,1)} %get-tuple-element.28.queries, ...), custom_call_target="tpu_custom_call" | custom-call | tf_op jit(solution)/shard_map/pallas_call | solution.py:261
  140.8 2.5 %collective-permute-start.3 = (bf16[384,1280]{1,0:T(8,128)(2,1)S(1)}, bf16[384,1280]{1,0:T(8,128)(2,1)S(1)}, u32[]{:S(2)}, u32[]{:S(2)}) collective-permute-start(bf16[384,1280]{1,0:T(8,128)(2,1)S(1)} %shard_map.88.enc_term), channel_id=1, source_target_pairs={{8,0},{9,1},{10,2},{11,3},{12,4},{13,5},{14,6},{15,7},{24,16},{25,... | collective-permute-start | bytes 2949128 | tf_op jit(solution)/shard_map/ppermute | solution.py:395
  143.2 0.0 collective-permute-done.4.dec_sent
  143.2 2.1 %collective-permute-done.3.enc_sent = bf16[384,1280]{1,0:T(8,128)(2,1)S(1)} collective-permute-done((bf16[384,1280]{1,0:T(8,128)(2,1)S(1)}, bf16[384,1280]{1,0:T(8,128)(2,1)S(1)}, u32[]{:S(2)}, u32[]{:S(2)}) %collective-permute-start.3) | collective-permute-done | bytes 983072 | tf_op jit(solution)/shard_map/ppermute | solution.py:395
  145.3 1.6 shard_map.90
  146.9 19.3 %all_to_all.38.pieces = bf16[8,60,8,128]{3,2,1,0:T(8,128)(2,1)S(1)} all-to-all(bf16[8,60,8,128]{3,2,1,0:T(8,128)(2,1)S(1)} %bitcast.17), channel_id=1, replica_groups={{0,16,128,144,256,272,384,400},{32,48,160,176,288,304,416,432},{64,80,1..., dimensions={0} | all-to-all | bytes 1966080 | tf_op jit(solution)/shard_map/all_to_all | solution.py:300
  166.3 0.1 shard_map.91
  166.4 18.3 %all_to_all.39.pieces = bf16[4,60,8,128]{3,2,1,0:T(8,128)(2,1)S(1)} all-to-all(bf16[4,60,8,128]{3,2,1,0:T(8,128)(2,1)S(1)} %shard_map.91), channel_id=1, replica_groups={{0,32,64,96},{16,48,80,112},{128,160,192,224},{144,176,208,240},{256,28..., dimensions={0} | all-to-all | bytes 983040 | tf_op jit(solution)/shard_map/all_to_all | solution.py:300
  184.7 0.1 shard_map.92
  184.8 17.1 %all_to_all.40 = bf16[8,60,8,128]{3,2,1,0:T(8,128)(2,1)S(1)} all-to-all(bf16[8,60,8,128]{3,2,1,0:T(8,128)(2,1)S(1)} %shard_map.92), channel_id=1, replica_groups={{0,16,128,144,256,272,384,400},{32,48,160,176,288,304,416,432},{64,80,1..., dimensions={0} | all-to-all | bytes 1966080 | tf_op jit(solution)/shard_map/all_to_all | solution.py:300
  201.9 1.4 shard_map.93
  (1 shorter events, 0.0 us)
Async XLA Ops:
  6.5 67.8 %all-gather.2.cloned.1.call-start = ((), (), s32[]{:S(2)}) async-start(), calls=%async_computation.7 | async-start | bytes 1474560 | tf_op jit(solution)/shard_map/all_gather | solution.py:310
  7.5 9.0 %collective-permute-start.1 = (bf16[64,1280]{1,0:T(8,128)(2,1)S(1)}, bf16[64,1280]{1,0:T(8,128)(2,1)S(1)}, u32[]{:S(2)}, u32[]{:S(2)}) collective-permute-start(bf16[64,1280]{1,0:T(8,128)(2,1)S(1)} %slice_bitcast_fusion), channel_id=1, source_target_pairs={{0,8},{1,9},{2,10},{3,11},{4,12},{5,13},{6,14},{7,15},{16,24},{17,... | collective-permute-start | bytes 491528 | tf_op jit(solution)/shard_map/ppermute | solution.py:305
  8.8 41.0 %copy-start.1 = (f32[3,1280]{1,0:T(4,128)S(1)}, f32[3,1280]{1,0:T(4,128)}, u32[]{:S(2)}) copy-start(f32[3,1280]{1,0:T(4,128)} %gains.7) | copy-start | bytes 46084
  8.8 41.0 %copy-start.2 = (f32[3,1280]{1,0:T(4,128)S(1)}, f32[3,1280]{1,0:T(4,128)}, u32[]{:S(2)}) copy-start(f32[3,1280]{1,0:T(4,128)} %biases.5) | copy-start | bytes 46084
  8.8 41.0 %copy-start.4 = (s32[2,1,4]{2,1,0:T(1,128)S(1)}, s32[2,1,4]{2,1,0:T(1,128)}, u32[]{:S(2)}) copy-start(s32[2,1,4]{2,1,0:T(1,128)} %frame_lens.1) | copy-start | bytes 100
  18.1 31.7 %collective-permute-start = (bf16[4,128,1280]{2,1,0:T(8,128)(2,1)}, bf16[4,128,1280]{2,1,0:T(8,128)(2,1)S(1)}, u32[]{:S(2)}, u32[]{:S(2)}) collective-permute-start(bf16[4,128,1280]{2,1,0:T(8,128)(2,1)} %bitcast.23), channel_id=1, source_target_pairs={{0,8},{8,0},{1,9},{9,1},{2,10},{10,2},{3,11},{11,3},{4,12},{12,4},... | collective-permute-start | bytes 3932168 | tf_op jit(solution)/shard_map/ppermute | solution.py:278
  20.2 0.9 copy-start.3
  49.8 4.4 %copy-start = (bf16[4,128,1280]{2,1,0:T(8,128)(2,1)}, bf16[4,128,1280]{2,1,0:T(8,128)(2,1)S(1)}, u32[]{:S(2)}) copy-start(bf16[4,128,1280]{2,1,0:T(8,128)(2,1)S(1)} %collective-permute-done.other) | copy-start | bytes 3932164
  74.4 8.5 %collective-permute-start.2 = (bf16[512,1280]{1,0:T(8,128)(2,1)}, bf16[512,1280]{1,0:T(8,128)(2,1)S(1)}, u32[]{:S(2)}, u32[]{:S(2)}) collective-permute-start(bf16[512,1280]{1,0:T(8,128)(2,1)} %all-gather.2.cloned.1.call-done.out_part), channel_id=1, source_target_pairs={{0,8},{8,0},{1,9},{9,1},{2,10},{10,2},{3,11},{11,3},{4,12},{12,4},... | collective-permute-start | bytes 3932168 | tf_op jit(solution)/shard_map/ppermute | solution.py:278
  80.7 2.2 %copy-start.5 = (s32[2,1,4]{2,1,0:T(1,128)S(1)}, s32[2,1,4]{2,1,0:T(1,128)}, u32[]{:S(2)}) copy-start(s32[2,1,4]{2,1,0:T(1,128)} %token_lens.1) | copy-start | bytes 100
  113.1 24.2 %all-to-all-start.3 = ((bf16[8,32,1280]{2,1,0:T(8,128)(2,1)}), bf16[8,32,1280]{2,1,0:T(8,128)(2,1)S(1)}, u32[]{:S(2)}, u32[]{:S(2)}) async-start(bf16[8,32,1280]{2,1,0:T(8,128)(2,1)} %shard_map.87), calls=%async_computation.3 | async-start | bytes 1310720 | tf_op jit(solution)/shard_map/all_to_all | solution.py:300
  119.3 23.9 %collective-permute-start.4 = (bf16[384,1280]{1,0:T(8,128)(2,1)}, bf16[384,1280]{1,0:T(8,128)(2,1)S(1)}, u32[]{:S(2)}, u32[]{:S(2)}) collective-permute-start(bf16[384,1280]{1,0:T(8,128)(2,1)} %shard_map.89.dec_term), channel_id=1, source_target_pairs={{0,8},{1,9},{2,10},{3,11},{4,12},{5,13},{6,14},{7,15},{16,24},{17,... | collective-permute-start | bytes 2949128 | tf_op jit(solution)/shard_map/ppermute | solution.py:394
  140.8 4.6 %collective-permute-start.3 = (bf16[384,1280]{1,0:T(8,128)(2,1)S(1)}, bf16[384,1280]{1,0:T(8,128)(2,1)S(1)}, u32[]{:S(2)}, u32[]{:S(2)}) collective-permute-start(bf16[384,1280]{1,0:T(8,128)(2,1)S(1)} %shard_map.88.enc_term), channel_id=1, source_target_pairs={{8,0},{9,1},{10,2},{11,3},{12,4},{13,5},{14,6},{15,7},{24,16},{25,... | collective-permute-start | bytes 2949128 | tf_op jit(solution)/shard_map/ppermute | solution.py:395
Sparse Core Ops, SparseCore 0:
  18.3 44.8 all-gather.1

commit v5 on v4

--- a/solution.py
+++ b/solution.py
@@ -244,7 +244,9 @@
         gradient[:, block * 128 : (block + 1) * 128] = part.reshape(rows, 128)
 
 
-def call(kernel, outs, scalars, arrays, blocks=None, scratch=(), kept=(), read=()):
+def call(
+    kernel, outs, scalars, arrays, blocks=None, scratch=(), kept=(), read=(), cost=None
+):
     blocks = blocks or {}
 
     def spec(index, array):
@@ -269,6 +271,7 @@
             for shape, _ in outs
         ],
         scratch_shapes=list(scratch),
+        cost_estimate=cost,
         compiler_params=pltpu.CompilerParams(vmem_limit_bytes=48 << 20),
     )(*scalars, *arrays)
     return result[0] if len(outs) == 1 else result
@@ -302,14 +305,13 @@
     core_id = core.astype(jnp.int32).reshape(1)
     place = lax.axis_index("mp").astype(jnp.int32).reshape(1)
 
-    out_sent = lax.ppermute(own[3, HS:], "segment", [(0, 1)])
+    other = swap(own)
     copies = call(
         pick_copies_kernel, [((mp, shard_rows, features), bf16)], (core_id,), (frames,)
     )
-    out_part = jnp.where(first, own[3, :HS], out_sent)
+    out_part = jnp.where(first, own[3, :HS], other[3, HS:])
     out_part = lax.all_gather(out_part, "mp", axis=0, tiled=True)
     enc_full = exchange(copies).reshape(rows, features)
-    other = swap(own)
 
     token_queries, token_grads = call(
         token_kernel,
@@ -335,8 +337,11 @@
         {1: weight_block, 2: weight_block},
         kept=(0, 1, 2, 3, 5),
         read=(1,),
-    )
-    context_full, out_part = lax.optimization_barrier((exchange(context_copies), out_part))
+        cost=pl.CostEstimate(flops=3_000_000_000, transcendentals=0, bytes_accessed=0),
+    )
+    context_full, out_part, token_queries, token_grads = lax.optimization_barrier(
+        (exchange(context_copies), out_part, token_queries, token_grads)
+    )
     out_rest = swap(out_part)
     half_states = call(
         half_states_kernel,

time: 212 us -> 209 us (0.986)
  blocking collectives: 127 us -> 78 us
  waiting for transfers between devices: 26.6 us -> 56.8 us
  starting transfers between devices: 13.9 us -> 29.1 us
    all_to_all x6 -> x4, blocking collectives: 127 us -> 78 us  [exchange(): return lax.all_to_all(blocks, axis, 0, 0, axis_index_groups=groups)]
    all_to_all x1 -> x3, waiting for transfers between devices: 16.8 us -> 54 us  [exchange(): return lax.all_to_all(blocks, axis, 0, 0, axis_index_groups=groups)]
    all_to_all x1 -> x3, starting transfers between devices: 3.54 us -> 11.7 us  [exchange(): return lax.all_to_all(blocks, axis, 0, 0, axis_index_groups=groups)]
    ppermute x1 -> x0, waiting for transfers between devices: 7.7 us -> none  [shards(): out_sent = lax.ppermute(own[3, HS:], 'segment', [(0, 1)])]
    ppermute x2, starting transfers between devices: 5.33 us -> 12.1 us  [swap(): return lax.ppermute(block, 'segment', [(0, 1), (1, 0)])]
  transfers between devices with their start and end apart: 7 -> 8, of which waited for: 3 -> 5; matrix products, arithmetic and copies ran while one was open for 0% -> 1% of each run, Pallas kernels for 7% -> 8%
where the time goes in v5:
time: 209 us; the launch traced here: 207 us
  blocking collectives  78 us (37%)
  waiting for transfers between devices  56.8 us (27%)
  starting transfers between devices  29.1 us (14%)
  Pallas kernels  26.4 us (13%)
  between operations  13.5 us (6%)
    all_to_all x4, blocking collectives, exchange(): return lax.all_to_all(blocks, axis, 0, 0, axis_index_groups=groups)  78 us
    all_to_all x3, waiting for transfers between devices, exchange(): return lax.all_to_all(blocks, axis, 0, 0, axis_index_groups=groups)  54 us
    pallas_call x12, Pallas kernels, call(): pl.pallas_call(kernel, grid=(1,), out_shape=[out(index, *what) for index,...  26.4 us
    ppermute x2, starting transfers between devices, swap(): return lax.ppermute(block, 'segment', [(0, 1), (1, 0)])  12.1 us
    all_to_all x3, starting transfers between devices, exchange(): return lax.all_to_all(blocks, axis, 0, 0, axis_index_groups=groups)  11.7 us
  transfers between devices with their start and end apart: 8, of which 5 were waited for; matrix products, arithmetic and copies ran while one was open for 1% of the time, Pallas kernels for 8%

profile of v5, /device:TPU:1, one launch (start us, length us, event | category | flops | bytes accessed | tf_op | source)
XLA Modules:
  0.0 206.6 jit_solution(1720952342053139994)
XLA Ops:
  6.5 8.8 %collective-permute-start = (bf16[4,128,1280]{2,1,0:T(8,128)(2,1)}, bf16[4,128,1280]{2,1,0:T(8,128)(2,1)S(1)}, u32[]{:S(2)}, u32[]{:S(2)}) collective-permute-start(bf16[4,128,1280]{2,1,0:T(8,128)(2,1)} %bitcast.16), channel_id=1, source_target_pairs={{0,8},{8,0},{1,9},{9,1},{2,10},{10,2},{3,11},{11,3},{4,12},{12,4},... | collective-permute-start | bytes 3932168 | tf_op jit(solution)/shard_map/ppermute | solution.py:281
  15.3 0.0 copy-start.2
  15.3 0.9 copy-done.2
  16.2 0.0 copy-start.1
  16.2 0.0 copy-start.3
  16.2 0.0 copy-start.4
  16.2 0.9 shard_map.82
  17.1 4.7 %all-to-all-start = ((bf16[8,32,1280]{2,1,0:T(8,128)(2,1)}), bf16[8,32,1280]{2,1,0:T(8,128)(2,1)S(1)}, u32[]{:S(2)}, u32[]{:S(2)}) async-start(bf16[8,32,1280]{2,1,0:T(8,128)(2,1)} %shard_map.82), calls=%async_computation | async-start | bytes 1310720 | tf_op jit(solution)/shard_map/all_to_all | solution.py:303
  21.8 0.0 all-gather.3.cloned.1.call-start
  21.8 0.0 collective-permute-done.other
  21.9 0.0 copy-start
  21.9 1.8 slice_select_fusion
  23.7 0.0 all-gather.3.cloned.1.call-update
  23.7 18.9 %all-to-all-done = bf16[8,32,1280]{2,1,0:T(8,128)(2,1)S(1)} async-done(((bf16[8,32,1280]{2,1,0:T(8,128)(2,1)}), bf16[8,32,1280]{2,1,0:T(8,128)(2,1)S(1)}, u32[]{:S(2)}, u32[]{:S(2)}) %all-to-all-start) | async-done | bytes 655392 | tf_op jit(solution)/shard_map/all_to_all | solution.py:303
  42.6 0.0 copy-done.1
  42.6 0.0 copy-done.3
  42.6 0.0 copy-done.4
  42.6 4.0 %shard_map.83 = (bf16[256,1280]{1,0:T(8,128)(2,1)}, bf16[256,128]{1,0:T(8,128)(2,1)}, bf16[256,128]{1,0:T(8,128)(2,1)}, bf16[256,128]{1,0:T(8,128)(2,1)}, bf16[8...) custom-call(s32[1]{0:T(128)} %bitcast.core, s32[2,1,4]{2,1,0:T(1,128)S(1)} %copy-done.4, bf16[256,1280]{1,0:T(8,128)(2,1)S(1)} %bitcast.12, ...), custom_call_target="tpu_custom_call" | custom-call | flops 3000000000 | tf_op jit(solution)/shard_map/pallas_call | solution.py:263
  46.6 0.0 copy-done
  46.6 3.5 %all-to-all-start.1 = ((bf16[8,256,128]{2,1,0:T(8,128)(2,1)}), bf16[8,256,128]{2,1,0:T(8,128)(2,1)S(1)}, u32[]{:S(2)}, u32[]{:S(2)}) async-start(bf16[8,256,128]{2,1,0:T(8,128)(2,1)} %get-tuple-element.23), calls=%async_computation.1 | async-start | bytes 1048576 | tf_op jit(solution)/shard_map/all_to_all | solution.py:303
  50.1 3.0 %shard_map.84 = (bf16[64,128]{1,0:T(8,128)(2,1)}, bf16[64,128]{1,0:T(8,128)(2,1)}) custom-call(s32[1]{0:T(128)} %bitcast.core, bf16[2,64,1280]{2,1,0:T(8,128)(2,1)} %tokens.1, bf16[2,64,1280]{2,1,0:T(8,128)(2,1)} %upstream.3, bf16[4,128,1280]{2,1,0:T(8,128)(2,1)} %bitcast.19, bf16[4,128,1280]{2,1,0:T(8,128)(2,1)} %copy-done, f32[3,1280]{1,0:T(4,128)S(1)} %copy-done.1, ...), custom_call_target="tpu_custom_call" | custom-call | tf_op jit(solution)/shard_map/pallas_call | solution.py:263
  53.1 19.9 %all-to-all-done.1.context = bf16[8,256,128]{2,1,0:T(8,128)(2,1)S(1)} async-done(((bf16[8,256,128]{2,1,0:T(8,128)(2,1)}), bf16[8,256,128]{2,1,0:T(8,128)(2,1)S(1)}, u32[]{:S(2)}, u32[]{:S(2)}) %all-to-all-start.1) | async-done | bytes 524320 | tf_op jit(solution)/shard_map/all_to_all | solution.py:303
  73.0 0.0 all-gather.3.cloned.1.call-done
  73.0 3.3 %collective-permute-start.1 = (bf16[512,1280]{1,0:T(8,128)(2,1)}, bf16[512,1280]{1,0:T(8,128)(2,1)S(1)}, u32[]{:S(2)}, u32[]{:S(2)}) collective-permute-start(bf16[512,1280]{1,0:T(8,128)(2,1)} %bitcast.22), channel_id=1, source_target_pairs={{0,8},{8,0},{1,9},{9,1},{2,10},{10,2},{3,11},{11,3},{4,12},{12,4},... | collective-permute-start | bytes 3932168 | tf_op jit(solution)/shard_map/ppermute | solution.py:281
  76.3 0.0 copy-start.5
  76.3 2.1 %shard_map.85.half_states = f32[256,1280]{1,0:T(8,128)S(1)} custom-call(s32[1]{0:T(128)} %bitcast.core, bf16[256,1280]{1,0:T(8,128)(2,1)S(1)} %bitcast.13, bf16[8,256,128]{2,1,0:T(8,128)(2,1)S(1)} %all-to-all-done.1.context, bf16[512,1280]{1,0:T(8,128)(2,1)} %bitcast.23), custom_call_target="tpu_custom_call" | custom-call | tf_op jit(solution)/shard_map/pallas_call | solution.py:263
  78.5 0.7 collective-permute-done.1.out_rest
  79.2 0.0 copy-done.5
  79.2 5.0 %shard_map.86 = (bf16[256,1280]{1,0:T(8,128)(2,1)S(1)}, bf16[32,1280]{1,0:T(8,128)(2,1)}, bf16[256,1280]{1,0:T(8,128)(2,1)}, bf16[256,128]{1,0:T(8,128)(2,1)}, b...) custom-call(s32[1]{0:T(128)} %bitcast.core, s32[1]{0:T(128)} %bitcast.1.place, s32[2,1,4]{2,1,0:T(1,128)S(1)} %copy-done.4, ...), custom_call_target="tpu_custom_call" | custom-call | tf_op jit(solution)/shard_map/pallas_call | solution.py:263
  84.2 23.6 %all_to_all.35.pieces = bf16[8,32,1280]{2,1,0:T(8,128)(2,1)S(1)} all-to-all(bf16[8,32,1280]{2,1,0:T(8,128)(2,1)S(1)} %bitcast.15), channel_id=1, replica_groups=mesh['dp'=32,'segment'=2,'mp'=8] {'mp'}, dimensions={0} | all-to-all | bytes 1310720 | tf_op jit(solution)/shard_map/all_to_all | solution.py:303
  107.7 2.1 shard_map.87
  109.8 3.5 %all-to-all-start.3 = ((bf16[8,32,1280]{2,1,0:T(8,128)(2,1)}), bf16[8,32,1280]{2,1,0:T(8,128)(2,1)S(1)}, u32[]{:S(2)}, u32[]{:S(2)}) async-start(bf16[8,32,1280]{2,1,0:T(8,128)(2,1)} %shard_map.87), calls=%async_computation.3 | async-start | bytes 1310720 | tf_op jit(solution)/shard_map/all_to_all | solution.py:303
  113.3 2.7 %shard_map.89.dec_term = bf16[384,1280]{1,0:T(8,128)(2,1)} custom-call(s32[1]{0:T(128)} %bitcast.core, bf16[256,128]{1,0:T(8,128)(2,1)} %get-tuple-element.37.key_grad, bf16[256,128]{1,0:T(8,128)(2,1)} %get-tuple-element.38.value_grad, bf16[64,128]{1,0:T(8,128)(2,1)} %get-tuple-element.39.context, bf16[256,1280]{1,0:T(8,128)(2,1)} %get-tuple-element.40.normed, ...), custom_call_target="tpu_custom_call" | custom-call | tf_op jit(solution)/shard_map/pallas_call | solution.py:263
  116.0 1.3 collective-permute-start.3
  117.3 15.2 %all-to-all-done.3 = bf16[8,32,1280]{2,1,0:T(8,128)(2,1)S(1)} async-done(((bf16[8,32,1280]{2,1,0:T(8,128)(2,1)}), bf16[8,32,1280]{2,1,0:T(8,128)(2,1)S(1)}, u32[]{:S(2)}, u32[]{:S(2)}) %all-to-all-start.3) | async-done | bytes 655392 | tf_op jit(solution)/shard_map/all_to_all | solution.py:303
  132.5 3.4 %shard_map.88.enc_term = bf16[384,1280]{1,0:T(8,128)(2,1)S(1)} custom-call(s32[1]{0:T(128)} %bitcast.core, bf16[256,1280]{1,0:T(8,128)(2,1)S(1)} %bitcast.14, bf16[4,128,1280]{2,1,0:T(8,128)(2,1)} %bitcast.21, bf16[4,128,1280]{2,1,0:T(8,128)(2,1)} %copy-done, bf16[256,128]{1,0:T(8,128)(2,1)} %get-tuple-element.32.queries, ...), custom_call_target="tpu_custom_call" | custom-call | tf_op jit(solution)/shard_map/pallas_call | solution.py:263
  135.9 4.0 %collective-permute-start.2 = (bf16[384,1280]{1,0:T(8,128)(2,1)S(1)}, bf16[384,1280]{1,0:T(8,128)(2,1)S(1)}, u32[]{:S(2)}, u32[]{:S(2)}) collective-permute-start(bf16[384,1280]{1,0:T(8,128)(2,1)S(1)} %shard_map.88.enc_term), channel_id=1, source_target_pairs={{8,0},{9,1},{10,2},{11,3},{12,4},{13,5},{14,6},{15,7},{24,16},{25,... | collective-permute-start | bytes 2949128 | tf_op jit(solution)/shard_map/ppermute | solution.py:400
  139.9 0.0 collective-permute-done.3.dec_sent
  139.9 2.1 %collective-permute-done.2.enc_sent = bf16[384,1280]{1,0:T(8,128)(2,1)S(1)} collective-permute-done((bf16[384,1280]{1,0:T(8,128)(2,1)S(1)}, bf16[384,1280]{1,0:T(8,128)(2,1)S(1)}, u32[]{:S(2)}, u32[]{:S(2)}) %collective-permute-start.2) | collective-permute-done | bytes 983072 | tf_op jit(solution)/shard_map/ppermute | solution.py:400
  142.0 1.6 shard_map.90
  143.6 19.2 %all_to_all.36.pieces = bf16[8,60,8,128]{3,2,1,0:T(8,128)(2,1)S(1)} all-to-all(bf16[8,60,8,128]{3,2,1,0:T(8,128)(2,1)S(1)} %bitcast.10), channel_id=1, replica_groups={{0,16,128,144,256,272,384,400},{32,48,160,176,288,304,416,432},{64,80,1..., dimensions={0} | all-to-all | bytes 1966080 | tf_op jit(solution)/shard_map/all_to_all | solution.py:303
  162.8 0.1 shard_map.91
  163.0 18.2 %all_to_all.37.pieces = bf16[4,60,8,128]{3,2,1,0:T(8,128)(2,1)S(1)} all-to-all(bf16[4,60,8,128]{3,2,1,0:T(8,128)(2,1)S(1)} %shard_map.91), channel_id=1, replica_groups={{0,32,64,96},{16,48,80,112},{128,160,192,224},{144,176,208,240},{256,28..., dimensions={0} | all-to-all | bytes 983040 | tf_op jit(solution)/shard_map/all_to_all | solution.py:303
  181.2 0.1 shard_map.92
  181.2 17.1 %all_to_all.38 = bf16[8,60,8,128]{3,2,1,0:T(8,128)(2,1)S(1)} all-to-all(bf16[8,60,8,128]{3,2,1,0:T(8,128)(2,1)S(1)} %shard_map.92), channel_id=1, replica_groups={{0,16,128,144,256,272,384,400},{32,48,160,176,288,304,416,432},{64,80,1..., dimensions={0} | all-to-all | bytes 1966080 | tf_op jit(solution)/shard_map/all_to_all | solution.py:303
  198.3 1.4 shard_map.93
Async XLA Ops:
  6.5 15.3 %collective-permute-start = (bf16[4,128,1280]{2,1,0:T(8,128)(2,1)}, bf16[4,128,1280]{2,1,0:T(8,128)(2,1)S(1)}, u32[]{:S(2)}, u32[]{:S(2)}) collective-permute-start(bf16[4,128,1280]{2,1,0:T(8,128)(2,1)} %bitcast.16), channel_id=1, source_target_pairs={{0,8},{8,0},{1,9},{9,1},{2,10},{10,2},{3,11},{11,3},{4,12},{12,4},... | collective-permute-start | bytes 3932168 | tf_op jit(solution)/shard_map/ppermute | solution.py:281
  15.3 0.9 copy-start.2
  16.2 26.4 %copy-start.1 = (f32[3,1280]{1,0:T(4,128)S(1)}, f32[3,1280]{1,0:T(4,128)}, u32[]{:S(2)}) copy-start(f32[3,1280]{1,0:T(4,128)} %gains.7) | copy-start | bytes 46084
  16.2 26.4 %copy-start.3 = (f32[3,1280]{1,0:T(4,128)S(1)}, f32[3,1280]{1,0:T(4,128)}, u32[]{:S(2)}) copy-start(f32[3,1280]{1,0:T(4,128)} %biases.5) | copy-start | bytes 46084
  16.2 26.4 %copy-start.4 = (s32[2,1,4]{2,1,0:T(1,128)S(1)}, s32[2,1,4]{2,1,0:T(1,128)}, u32[]{:S(2)}) copy-start(s32[2,1,4]{2,1,0:T(1,128)} %frame_lens.1) | copy-start | bytes 100
  17.1 25.5 %all-to-all-start = ((bf16[8,32,1280]{2,1,0:T(8,128)(2,1)}), bf16[8,32,1280]{2,1,0:T(8,128)(2,1)S(1)}, u32[]{:S(2)}, u32[]{:S(2)}) async-start(bf16[8,32,1280]{2,1,0:T(8,128)(2,1)} %shard_map.82), calls=%async_computation | async-start | bytes 1310720 | tf_op jit(solution)/shard_map/all_to_all | solution.py:303
  21.8 51.2 %all-gather.3.cloned.1.call-start = ((), (), s32[]{:S(2)}) async-start(), calls=%async_computation.7 | async-start | bytes 1474560 | tf_op jit(solution)/shard_map/all_gather | solution.py:313
  21.9 24.7 %copy-start = (bf16[4,128,1280]{2,1,0:T(8,128)(2,1)}, bf16[4,128,1280]{2,1,0:T(8,128)(2,1)S(1)}, u32[]{:S(2)}) copy-start(bf16[4,128,1280]{2,1,0:T(8,128)(2,1)S(1)} %collective-permute-done.other) | copy-start | bytes 3932164
  46.6 26.4 %all-to-all-start.1 = ((bf16[8,256,128]{2,1,0:T(8,128)(2,1)}), bf16[8,256,128]{2,1,0:T(8,128)(2,1)S(1)}, u32[]{:S(2)}, u32[]{:S(2)}) async-start(bf16[8,256,128]{2,1,0:T(8,128)(2,1)} %get-tuple-element.23), calls=%async_computation.1 | async-start | bytes 1048576 | tf_op jit(solution)/shard_map/all_to_all | solution.py:303
  73.0 6.2 %collective-permute-start.1 = (bf16[512,1280]{1,0:T(8,128)(2,1)}, bf16[512,1280]{1,0:T(8,128)(2,1)S(1)}, u32[]{:S(2)}, u32[]{:S(2)}) collective-permute-start(bf16[512,1280]{1,0:T(8,128)(2,1)} %bitcast.22), channel_id=1, source_target_pairs={{0,8},{8,0},{1,9},{9,1},{2,10},{10,2},{3,11},{11,3},{4,12},{12,4},... | collective-permute-start | bytes 3932168 | tf_op jit(solution)/shard_map/ppermute | solution.py:281
  76.3 2.9 %copy-start.5 = (s32[2,1,4]{2,1,0:T(1,128)S(1)}, s32[2,1,4]{2,1,0:T(1,128)}, u32[]{:S(2)}) copy-start(s32[2,1,4]{2,1,0:T(1,128)} %token_lens.1) | copy-start | bytes 100
  109.8 22.7 %all-to-all-start.3 = ((bf16[8,32,1280]{2,1,0:T(8,128)(2,1)}), bf16[8,32,1280]{2,1,0:T(8,128)(2,1)S(1)}, u32[]{:S(2)}, u32[]{:S(2)}) async-start(bf16[8,32,1280]{2,1,0:T(8,128)(2,1)} %shard_map.87), calls=%async_computation.3 | async-start | bytes 1310720 | tf_op jit(solution)/shard_map/all_to_all | solution.py:303
  116.0 23.9 %collective-permute-start.3 = (bf16[384,1280]{1,0:T(8,128)(2,1)}, bf16[384,1280]{1,0:T(8,128)(2,1)S(1)}, u32[]{:S(2)}, u32[]{:S(2)}) collective-permute-start(bf16[384,1280]{1,0:T(8,128)(2,1)} %shard_map.89.dec_term), channel_id=1, source_target_pairs={{0,8},{1,9},{2,10},{3,11},{4,12},{5,13},{6,14},{7,15},{16,24},{17,... | collective-permute-start | bytes 2949128 | tf_op jit(solution)/shard_map/ppermute | solution.py:399
  135.9 6.1 %collective-permute-start.2 = (bf16[384,1280]{1,0:T(8,128)(2,1)S(1)}, bf16[384,1280]{1,0:T(8,128)(2,1)S(1)}, u32[]{:S(2)}, u32[]{:S(2)}) collective-permute-start(bf16[384,1280]{1,0:T(8,128)(2,1)S(1)} %shard_map.88.enc_term), channel_id=1, source_target_pairs={{8,0},{9,1},{10,2},{11,3},{12,4},{13,5},{14,6},{15,7},{24,16},{25,... | collective-permute-start | bytes 2949128 | tf_op jit(solution)/shard_map/ppermute | solution.py:400
Sparse Core Ops, SparseCore 0:
  24.7 45.7 all-gather.2

commit v6 on v5

--- a/solution.py
+++ b/solution.py
@@ -103,8 +103,9 @@
 
 def half_context(context, second):
     heads = []
-    for device in range(context.shape[0]):
-        block = context[device]
+    devices = context.shape[0]
+    for device in range(devices):
+        block = jnp.where(second, context[devices - 1 - device], context[device])
         heads.append(jnp.where(second, block[:, HS:], block[:, :HS]))
     return jnp.concatenate(heads, axis=1)
 
@@ -305,12 +306,20 @@
     core_id = core.astype(jnp.int32).reshape(1)
     place = lax.axis_index("mp").astype(jnp.int32).reshape(1)
 
+    copies = call(
+        pick_copies_kernel,
+        [((mp, shard_rows, features), bf16)],
+        (core_id,),
+        (frames,),
+        read=(0,),
+    )
+    copies, own = lax.optimization_barrier((copies, own))
     other = swap(own)
-    copies = call(
-        pick_copies_kernel, [((mp, shard_rows, features), bf16)], (core_id,), (frames,)
-    )
     out_part = jnp.where(first, own[3, :HS], other[3, HS:])
-    out_part = lax.all_gather(out_part, "mp", axis=0, tiled=True)
+    both_orders = [list(range(mp)), list(range(2 * mp - 1, mp - 1, -1))]
+    out_part = lax.all_gather(
+        out_part, ("segment", "mp"), axis=0, tiled=True, axis_index_groups=both_orders
+    )
     enc_full = exchange(copies).reshape(rows, features)
 
     token_queries, token_grads = call(
@@ -335,8 +344,7 @@
         (core_id, frame_lengths),
         (enc_full, own, other, norm_gains, norm_biases),
         {1: weight_block, 2: weight_block},
-        kept=(0, 1, 2, 3, 5),
-        read=(1,),
+        kept=(0, 1, 2, 3, 4, 5),
         cost=pl.CostEstimate(flops=3_000_000_000, transcendentals=0, bytes_accessed=0),
     )
     context_full, out_part, token_queries, token_grads = lax.optimization_barrier(

time: 209 us -> 209 us (level)
  transfers between devices with their start and end apart: 8 -> 8, of which waited for: 5 -> 5; matrix products, arithmetic and copies ran while one was open for 1% -> 0% of each run, Pallas kernels for 8% -> 7%
where the time goes in v6:
time: 209 us; the launch traced here: 206 us
  blocking collectives  76.9 us (37%)
  waiting for transfers between devices  57.5 us (28%)
  starting transfers between devices  30.9 us (15%)
  Pallas kernels  26.8 us (13%)
  between operations  13.5 us (6%)
    all_to_all x4, blocking collectives, exchange(): return lax.all_to_all(blocks, axis, 0, 0, axis_index_groups=groups)  76.9 us
    all_to_all x3, waiting for transfers between devices, exchange(): return lax.all_to_all(blocks, axis, 0, 0, axis_index_groups=groups)  54.7 us
    pallas_call x12, Pallas kernels, call(): pl.pallas_call(kernel, grid=(1,), out_shape=[out(index, *what) for index,...  26.8 us
    ppermute x2, starting transfers between devices, swap(): return lax.ppermute(block, 'segment', [(0, 1), (1, 0)])  13.9 us
    all_to_all x3, starting transfers between devices, exchange(): return lax.all_to_all(blocks, axis, 0, 0, axis_index_groups=groups)  11.7 us
  transfers between devices with their start and end apart: 8, of which 5 were waited for; matrix products, arithmetic and copies ran while one was open for 0% of the time, Pallas kernels for 7%

profile of v6, /device:TPU:1, one launch (start us, length us, event | category | flops | bytes accessed | tf_op | source)
XLA Modules:
  0.0 206.4 jit_solution(13789788766318924974)
XLA Ops:
  6.5 0.0 copy-start
  6.5 0.0 copy-start.2
  6.5 0.0 copy-start.3
  6.5 0.0 copy-start.4
  6.5 1.9 shard_map.82
  8.4 8.8 %collective-permute-start = (bf16[4,128,1280]{2,1,0:T(8,128)(2,1)}, bf16[4,128,1280]{2,1,0:T(8,128)(2,1)S(1)}, u32[]{:S(2)}, u32[]{:S(2)}) collective-permute-start(bf16[4,128,1280]{2,1,0:T(8,128)(2,1)} %bitcast.10), channel_id=1, source_target_pairs={{0,8},{8,0},{1,9},{9,1},{2,10},{10,2},{3,11},{11,3},{4,12},{12,4},... | collective-permute-start | bytes 3932168 | tf_op jit(solution)/shard_map/ppermute | solution.py:282
  17.2 4.7 %all-to-all-start = ((bf16[8,32,1280]{2,1,0:T(8,128)(2,1)}), bf16[8,32,1280]{2,1,0:T(8,128)(2,1)S(1)}, u32[]{:S(2)}, u32[]{:S(2)}) async-start(bf16[8,32,1280]{2,1,0:T(8,128)(2,1)} %shard_map.82), calls=%async_computation | async-start | bytes 1310720 | tf_op jit(solution)/shard_map/all_to_all | solution.py:304
  21.9 0.0 all-gather.3.cloned.1.call-start
  22.0 0.0 collective-permute-done.other
  22.0 0.0 copy-done
  22.0 0.0 copy-start.1
  22.0 0.7 slice_select_fusion
  22.7 0.0 all-gather.3.cloned.1.call-update
  22.8 19.9 %all-to-all-done = bf16[8,32,1280]{2,1,0:T(8,128)(2,1)S(1)} async-done(((bf16[8,32,1280]{2,1,0:T(8,128)(2,1)}), bf16[8,32,1280]{2,1,0:T(8,128)(2,1)S(1)}, u32[]{:S(2)}, u32[]{:S(2)}) %all-to-all-start) | async-done | bytes 655392 | tf_op jit(solution)/shard_map/all_to_all | solution.py:304
  42.7 0.0 copy-done.2
  42.7 0.0 copy-done.3
  42.7 0.0 copy-done.4
  42.7 3.4 %shard_map.83 = (bf16[256,1280]{1,0:T(8,128)(2,1)}, bf16[256,128]{1,0:T(8,128)(2,1)}, bf16[256,128]{1,0:T(8,128)(2,1)}, bf16[256,128]{1,0:T(8,128)(2,1)}, bf16[8...) custom-call(s32[1]{0:T(128)} %bitcast.core, s32[2,1,4]{2,1,0:T(1,128)S(1)} %copy-done.4, bf16[256,1280]{1,0:T(8,128)(2,1)S(1)} %bitcast.18, ...), custom_call_target="tpu_custom_call" | custom-call | flops 3000000000 | tf_op jit(solution)/shard_map/pallas_call | solution.py:264
  46.1 0.0 copy-done.1
  46.1 3.5 %all-to-all-start.1 = ((bf16[8,256,128]{2,1,0:T(8,128)(2,1)}), bf16[8,256,128]{2,1,0:T(8,128)(2,1)S(1)}, u32[]{:S(2)}, u32[]{:S(2)}) async-start(bf16[8,256,128]{2,1,0:T(8,128)(2,1)} %get-tuple-element.27), calls=%async_computation.1 | async-start | bytes 1048576 | tf_op jit(solution)/shard_map/all_to_all | solution.py:304
  49.6 3.0 %shard_map.84 = (bf16[64,128]{1,0:T(8,128)(2,1)}, bf16[64,128]{1,0:T(8,128)(2,1)}) custom-call(s32[1]{0:T(128)} %bitcast.core, bf16[2,64,1280]{2,1,0:T(8,128)(2,1)} %tokens.1, bf16[2,64,1280]{2,1,0:T(8,128)(2,1)} %upstream.3, bf16[4,128,1280]{2,1,0:T(8,128)(2,1)} %bitcast.11, bf16[4,128,1280]{2,1,0:T(8,128)(2,1)} %copy-done.1, f32[3,1280]{1,0:T(4,128)S(1)} %copy-done.2, ...), custom_call_target="tpu_custom_call" | custom-call | tf_op jit(solution)/shard_map/pallas_call | solution.py:264
  52.6 19.6 %all-to-all-done.1.context = bf16[8,256,128]{2,1,0:T(8,128)(2,1)S(1)} async-done(((bf16[8,256,128]{2,1,0:T(8,128)(2,1)}), bf16[8,256,128]{2,1,0:T(8,128)(2,1)S(1)}, u32[]{:S(2)}, u32[]{:S(2)}) %all-to-all-start.1) | async-done | bytes 524320 | tf_op jit(solution)/shard_map/all_to_all | solution.py:304
  72.2 0.0 all-gather.3.cloned.1.call-done
  72.2 5.1 %collective-permute-start.1 = (bf16[512,1280]{1,0:T(8,128)(2,1)}, bf16[512,1280]{1,0:T(8,128)(2,1)S(1)}, u32[]{:S(2)}, u32[]{:S(2)}) collective-permute-start(bf16[512,1280]{1,0:T(8,128)(2,1)} %bitcast.22), channel_id=1, source_target_pairs={{0,8},{8,0},{1,9},{9,1},{2,10},{10,2},{3,11},{11,3},{4,12},{12,4},... | collective-permute-start | bytes 3932168 | tf_op jit(solution)/shard_map/ppermute | solution.py:282
  77.3 0.0 copy-start.5
  77.3 2.1 %shard_map.85.half_states = f32[256,1280]{1,0:T(8,128)S(1)} custom-call(s32[1]{0:T(128)} %bitcast.core, bf16[256,1280]{1,0:T(8,128)(2,1)S(1)} %bitcast.19, bf16[8,256,128]{2,1,0:T(8,128)(2,1)S(1)} %all-to-all-done.1.context, bf16[512,1280]{1,0:T(8,128)(2,1)} %bitcast.23), custom_call_target="tpu_custom_call" | custom-call | tf_op jit(solution)/shard_map/pallas_call | solution.py:264
  79.5 0.7 collective-permute-done.1.out_rest
  80.2 0.0 copy-done.5
  80.2 5.0 %shard_map.86 = (bf16[256,1280]{1,0:T(8,128)(2,1)S(1)}, bf16[32,1280]{1,0:T(8,128)(2,1)}, bf16[256,1280]{1,0:T(8,128)(2,1)}, bf16[256,128]{1,0:T(8,128)(2,1)}, b...) custom-call(s32[1]{0:T(128)} %bitcast.core, s32[1]{0:T(128)} %bitcast.1.place, s32[2,1,4]{2,1,0:T(1,128)S(1)} %copy-done.4, ...), custom_call_target="tpu_custom_call" | custom-call | tf_op jit(solution)/shard_map/pallas_call | solution.py:264
  85.2 22.9 %all_to_all.35.pieces = bf16[8,32,1280]{2,1,0:T(8,128)(2,1)S(1)} all-to-all(bf16[8,32,1280]{2,1,0:T(8,128)(2,1)S(1)} %bitcast.21), channel_id=1, replica_groups=mesh['dp'=32,'segment'=2,'mp'=8] {'mp'}, dimensions={0} | all-to-all | bytes 1310720 | tf_op jit(solution)/shard_map/all_to_all | solution.py:304
  108.1 2.1 shard_map.87
  110.2 3.5 %all-to-all-start.3 = ((bf16[8,32,1280]{2,1,0:T(8,128)(2,1)}), bf16[8,32,1280]{2,1,0:T(8,128)(2,1)S(1)}, u32[]{:S(2)}, u32[]{:S(2)}) async-start(bf16[8,32,1280]{2,1,0:T(8,128)(2,1)} %shard_map.87), calls=%async_computation.3 | async-start | bytes 1310720 | tf_op jit(solution)/shard_map/all_to_all | solution.py:304
  113.7 2.7 %shard_map.89.dec_term = bf16[384,1280]{1,0:T(8,128)(2,1)} custom-call(s32[1]{0:T(128)} %bitcast.core, bf16[256,128]{1,0:T(8,128)(2,1)} %get-tuple-element.41.key_grad, bf16[256,128]{1,0:T(8,128)(2,1)} %get-tuple-element.42.value_grad, bf16[64,128]{1,0:T(8,128)(2,1)} %get-tuple-element.43.context, bf16[256,1280]{1,0:T(8,128)(2,1)} %get-tuple-element.44.normed, ...), custom_call_target="tpu_custom_call" | custom-call | tf_op jit(solution)/shard_map/pallas_call | solution.py:264
  116.4 1.3 collective-permute-start.3
  117.7 15.1 %all-to-all-done.3 = bf16[8,32,1280]{2,1,0:T(8,128)(2,1)S(1)} async-done(((bf16[8,32,1280]{2,1,0:T(8,128)(2,1)}), bf16[8,32,1280]{2,1,0:T(8,128)(2,1)S(1)}, u32[]{:S(2)}, u32[]{:S(2)}) %all-to-all-start.3) | async-done | bytes 655392 | tf_op jit(solution)/shard_map/all_to_all | solution.py:304
  132.8 3.4 %shard_map.88.enc_term = bf16[384,1280]{1,0:T(8,128)(2,1)S(1)} custom-call(s32[1]{0:T(128)} %bitcast.core, bf16[256,1280]{1,0:T(8,128)(2,1)S(1)} %bitcast.20, bf16[4,128,1280]{2,1,0:T(8,128)(2,1)} %bitcast.13, bf16[4,128,1280]{2,1,0:T(8,128)(2,1)} %copy-done.1, bf16[256,128]{1,0:T(8,128)(2,1)} %get-tuple-element.36.queries, ...), custom_call_target="tpu_custom_call" | custom-call | tf_op jit(solution)/shard_map/pallas_call | solution.py:264
  136.2 4.1 %collective-permute-start.2 = (bf16[384,1280]{1,0:T(8,128)(2,1)S(1)}, bf16[384,1280]{1,0:T(8,128)(2,1)S(1)}, u32[]{:S(2)}, u32[]{:S(2)}) collective-permute-start(bf16[384,1280]{1,0:T(8,128)(2,1)S(1)} %shard_map.88.enc_term), channel_id=1, source_target_pairs={{8,0},{9,1},{10,2},{11,3},{12,4},{13,5},{14,6},{15,7},{24,16},{25,... | collective-permute-start | bytes 2949128 | tf_op jit(solution)/shard_map/ppermute | solution.py:408
  140.3 0.0 collective-permute-done.3.dec_sent
  140.3 2.1 %collective-permute-done.2.enc_sent = bf16[384,1280]{1,0:T(8,128)(2,1)S(1)} collective-permute-done((bf16[384,1280]{1,0:T(8,128)(2,1)S(1)}, bf16[384,1280]{1,0:T(8,128)(2,1)S(1)}, u32[]{:S(2)}, u32[]{:S(2)}) %collective-permute-start.2) | collective-permute-done | bytes 983072 | tf_op jit(solution)/shard_map/ppermute | solution.py:408
  142.4 1.6 shard_map.90
  144.0 19.3 %all_to_all.36.pieces = bf16[8,60,8,128]{3,2,1,0:T(8,128)(2,1)S(1)} all-to-all(bf16[8,60,8,128]{3,2,1,0:T(8,128)(2,1)S(1)} %bitcast.16), channel_id=1, replica_groups={{0,16,128,144,256,272,384,400},{32,48,160,176,288,304,416,432},{64,80,1..., dimensions={0} | all-to-all | bytes 1966080 | tf_op jit(solution)/shard_map/all_to_all | solution.py:304
  163.3 0.1 shard_map.91
  163.4 17.6 %all_to_all.37.pieces = bf16[4,60,8,128]{3,2,1,0:T(8,128)(2,1)S(1)} all-to-all(bf16[4,60,8,128]{3,2,1,0:T(8,128)(2,1)S(1)} %shard_map.91), channel_id=1, replica_groups={{0,32,64,96},{16,48,80,112},{128,160,192,224},{144,176,208,240},{256,28..., dimensions={0} | all-to-all | bytes 983040 | tf_op jit(solution)/shard_map/all_to_all | solution.py:304
  181.0 0.1 shard_map.92
  181.1 17.1 %all_to_all.38 = bf16[8,60,8,128]{3,2,1,0:T(8,128)(2,1)S(1)} all-to-all(bf16[8,60,8,128]{3,2,1,0:T(8,128)(2,1)S(1)} %shard_map.92), channel_id=1, replica_groups={{0,16,128,144,256,272,384,400},{32,48,160,176,288,304,416,432},{64,80,1..., dimensions={0} | all-to-all | bytes 1966080 | tf_op jit(solution)/shard_map/all_to_all | solution.py:304
  198.2 1.4 shard_map.93
Async XLA Ops:
  6.5 15.4 %copy-start = (bf16[1,4,128,1280]{3,2,1,0:T(8,128)(2,1)S(1)}, bf16[1,4,128,1280]{3,2,1,0:T(8,128)(2,1)}, u32[]{:S(2)}) copy-start(bf16[1,4,128,1280]{3,2,1,0:T(8,128)(2,1)} %param.13) | copy-start | bytes 3932164
  6.5 36.2 %copy-start.2 = (f32[3,1280]{1,0:T(4,128)S(1)}, f32[3,1280]{1,0:T(4,128)}, u32[]{:S(2)}) copy-start(f32[3,1280]{1,0:T(4,128)} %gains.7) | copy-start | bytes 46084
  6.5 36.2 %copy-start.3 = (f32[3,1280]{1,0:T(4,128)S(1)}, f32[3,1280]{1,0:T(4,128)}, u32[]{:S(2)}) copy-start(f32[3,1280]{1,0:T(4,128)} %biases.5) | copy-start | bytes 46084
  6.5 36.2 %copy-start.4 = (s32[2,1,4]{2,1,0:T(1,128)S(1)}, s32[2,1,4]{2,1,0:T(1,128)}, u32[]{:S(2)}) copy-start(s32[2,1,4]{2,1,0:T(1,128)} %frame_lens.1) | copy-start | bytes 100
  8.4 13.5 %collective-permute-start = (bf16[4,128,1280]{2,1,0:T(8,128)(2,1)}, bf16[4,128,1280]{2,1,0:T(8,128)(2,1)S(1)}, u32[]{:S(2)}, u32[]{:S(2)}) collective-permute-start(bf16[4,128,1280]{2,1,0:T(8,128)(2,1)} %bitcast.10), channel_id=1, source_target_pairs={{0,8},{8,0},{1,9},{9,1},{2,10},{10,2},{3,11},{11,3},{4,12},{12,4},... | collective-permute-start | bytes 3932168 | tf_op jit(solution)/shard_map/ppermute | solution.py:282
  17.2 25.5 %all-to-all-start = ((bf16[8,32,1280]{2,1,0:T(8,128)(2,1)}), bf16[8,32,1280]{2,1,0:T(8,128)(2,1)S(1)}, u32[]{:S(2)}, u32[]{:S(2)}) async-start(bf16[8,32,1280]{2,1,0:T(8,128)(2,1)} %shard_map.82), calls=%async_computation | async-start | bytes 1310720 | tf_op jit(solution)/shard_map/all_to_all | solution.py:304
  21.9 50.3 %all-gather.3.cloned.1.call-start = ((), (), s32[]{:S(2)}) async-start(), calls=%async_computation.7 | async-start | bytes 1474560 | tf_op jit(solution)/shard_map/all_gather | solution.py:320
  22.0 24.1 %copy-start.1 = (bf16[4,128,1280]{2,1,0:T(8,128)(2,1)}, bf16[4,128,1280]{2,1,0:T(8,128)(2,1)S(1)}, u32[]{:S(2)}) copy-start(bf16[4,128,1280]{2,1,0:T(8,128)(2,1)S(1)} %collective-permute-done.other) | copy-start | bytes 3932164
  46.1 26.1 %all-to-all-start.1 = ((bf16[8,256,128]{2,1,0:T(8,128)(2,1)}), bf16[8,256,128]{2,1,0:T(8,128)(2,1)S(1)}, u32[]{:S(2)}, u32[]{:S(2)}) async-start(bf16[8,256,128]{2,1,0:T(8,128)(2,1)} %get-tuple-element.27), calls=%async_computation.1 | async-start | bytes 1048576 | tf_op jit(solution)/shard_map/all_to_all | solution.py:304
  72.2 7.9 %collective-permute-start.1 = (bf16[512,1280]{1,0:T(8,128)(2,1)}, bf16[512,1280]{1,0:T(8,128)(2,1)S(1)}, u32[]{:S(2)}, u32[]{:S(2)}) collective-permute-start(bf16[512,1280]{1,0:T(8,128)(2,1)} %bitcast.22), channel_id=1, source_target_pairs={{0,8},{8,0},{1,9},{9,1},{2,10},{10,2},{3,11},{11,3},{4,12},{12,4},... | collective-permute-start | bytes 3932168 | tf_op jit(solution)/shard_map/ppermute | solution.py:282
  77.3 2.9 %copy-start.5 = (s32[2,1,4]{2,1,0:T(1,128)S(1)}, s32[2,1,4]{2,1,0:T(1,128)}, u32[]{:S(2)}) copy-start(s32[2,1,4]{2,1,0:T(1,128)} %token_lens.1) | copy-start | bytes 100
  110.2 22.6 %all-to-all-start.3 = ((bf16[8,32,1280]{2,1,0:T(8,128)(2,1)}), bf16[8,32,1280]{2,1,0:T(8,128)(2,1)S(1)}, u32[]{:S(2)}, u32[]{:S(2)}) async-start(bf16[8,32,1280]{2,1,0:T(8,128)(2,1)} %shard_map.87), calls=%async_computation.3 | async-start | bytes 1310720 | tf_op jit(solution)/shard_map/all_to_all | solution.py:304
  116.4 23.9 %collective-permute-start.3 = (bf16[384,1280]{1,0:T(8,128)(2,1)}, bf16[384,1280]{1,0:T(8,128)(2,1)S(1)}, u32[]{:S(2)}, u32[]{:S(2)}) collective-permute-start(bf16[384,1280]{1,0:T(8,128)(2,1)} %shard_map.89.dec_term), channel_id=1, source_target_pairs={{0,8},{1,9},{2,10},{3,11},{4,12},{5,13},{6,14},{7,15},{16,24},{17,... | collective-permute-start | bytes 2949128 | tf_op jit(solution)/shard_map/ppermute | solution.py:407
  136.2 6.2 %collective-permute-start.2 = (bf16[384,1280]{1,0:T(8,128)(2,1)S(1)}, bf16[384,1280]{1,0:T(8,128)(2,1)S(1)}, u32[]{:S(2)}, u32[]{:S(2)}) collective-permute-start(bf16[384,1280]{1,0:T(8,128)(2,1)S(1)} %shard_map.88.enc_term), channel_id=1, source_target_pairs={{8,0},{9,1},{10,2},{11,3},{12,4},{13,5},{14,6},{15,7},{24,16},{25,... | collective-permute-start | bytes 2949128 | tf_op jit(solution)/shard_map/ppermute | solution.py:408
Sparse Core Ops, SparseCore 0:
  24.8 46.5 all-gather.2

commit v7 on v6

--- a/solution.py
+++ b/solution.py
@@ -101,28 +101,22 @@
     grad_context[...] = dot_nt(own_upstream, matrix).astype(jnp.bfloat16)
 
 
-def half_context(context, second):
-    heads = []
+def dec_kernel(
+    core, place, frame_lens, token_lens, x, context, own, other, token_queries, token_grads,
+    gains, biases, *refs,
+):
     devices = context.shape[0]
-    for device in range(devices):
-        block = jnp.where(second, context[devices - 1 - device], context[device])
-        heads.append(jnp.where(second, block[:, HS:], block[:, :HS]))
-    return jnp.concatenate(heads, axis=1)
-
-
-def half_states_kernel(core, x, context, out_part, states):
-    left = half_context(context, core[0] == 1)
-    states[...] = x[...].astype(jnp.float32) + dot_nn(left, out_part[...])
-
-
-def dec_kernel(
-    core, place, frame_lens, token_lens, half_states, context, out_rest, own, other, token_queries,
-    token_grads, gains, biases, partial, states, normed, key_grad, value_grad, dec_context, scratch,
-):
+    out_shards, refs = refs[:devices], refs[devices:]
+    partial, states, normed, key_grad, value_grad, dec_context, scratch = refs
     first = core[0] == 0
-    rows = half_states.shape[0]
-    left = half_context(context, core[0] == 0)
-    scratch[...] = half_states[...] + dot_nn(left, out_rest[...])
+    rows = x.shape[0]
+    summed = x[...].astype(jnp.float32)
+    for index in range(0, devices, 2):
+        pair = range(index, index + 2)
+        left = [context[(place[0] + devices - back) % devices] for back in pair]
+        right = [out_shards[back][...] for back in pair]
+        summed = summed + dot_nn(jnp.concatenate(left, axis=1), jnp.concatenate(right, axis=0))
+    scratch[...] = summed
     all_states = scratch[...].astype(jnp.bfloat16)
     shard = states.shape[0]
     start = pl.multiple_of(place[0] * shard, shard)
@@ -311,15 +305,18 @@
         [((mp, shard_rows, features), bf16)],
         (core_id,),
         (frames,),
+        kept=(0,),
         read=(0,),
     )
     copies, own = lax.optimization_barrier((copies, own))
     other = swap(own)
-    out_part = jnp.where(first, own[3, :HS], other[3, HS:])
-    both_orders = [list(range(mp)), list(range(2 * mp - 1, mp - 1, -1))]
-    out_part = lax.all_gather(
-        out_part, ("segment", "mp"), axis=0, tiled=True, axis_index_groups=both_orders
-    )
+    shard = jnp.where(first, own[3], other[3])
+    forward, backward = [shard], [shard]
+    for _ in range(mp // 2):
+        forward.append(lax.ppermute(forward[-1], "mp", [(i, (i + 1) % mp) for i in range(mp)]))
+    for _ in range(mp - mp // 2 - 1):
+        backward.append(lax.ppermute(backward[-1], "mp", [(i, (i - 1) % mp) for i in range(mp)]))
+    out_shards = forward + backward[:0:-1]
     enc_full = exchange(copies).reshape(rows, features)
 
     token_queries, token_grads = call(
@@ -347,16 +344,8 @@
         kept=(0, 1, 2, 3, 4, 5),
         cost=pl.CostEstimate(flops=3_000_000_000, transcendentals=0, bytes_accessed=0),
     )
-    context_full, out_part, token_queries, token_grads = lax.optimization_barrier(
-        (exchange(context_copies), out_part, token_queries, token_grads)
-    )
-    out_rest = swap(out_part)
-    half_states = call(
-        half_states_kernel,
-        [((rows, features), f32)],
-        (core_id,),
-        (enc_full, context_full, out_part),
-        read=(2,),
+    context_full, token_queries, token_grads, out_shards = lax.optimization_barrier(
+        (exchange(context_copies), token_queries, token_grads, out_shards)
     )
     partial, states, state_normed, dec_key_grad, dec_value_grad, dec_context = call(
         dec_kernel,
@@ -370,12 +359,12 @@
         ],
         (core_id, place, frame_lengths, token_lengths),
         (
-            half_states, context_full, out_rest, own, other, token_queries, token_grads,
-            norm_gains, norm_biases,
+            enc_full, context_full, own, other, token_queries, token_grads,
+            norm_gains, norm_biases, *out_shards,
         ),
         scratch=[pltpu.VMEM((rows, features), f32)],
         kept=(1, 2, 3, 4, 5),
-        read=(3, 4, 5, 6),
+        read=(2, 3, 4, 5),
     )
     pieces = exchange(partial.reshape(mp, shard_rows, features))
     whole = [((3 * head_cols, features), bf16)]

time: 209 us -> 208 us (level)
  starting transfers between devices: 30.9 us -> 52 us
  between operations: 13.5 us -> 0.2 us
  waiting for transfers between devices: 57.5 us -> 50 us
    all_to_all x3, waiting for transfers between devices: 54.7 us -> 12.1 us  [exchange(): return lax.all_to_all(blocks, axis, 0, 0, axis_index_groups=groups)]
    ppermute x0 -> x7, waiting for transfers between devices: none -> 35.9 us  [the longest x4 22.2 us: shards(): lax.ppermute(forward[-1], 'mp', [(i, (i + 1) % mp) for i in range(mp)])]
    ppermute x0 -> x7, starting transfers between devices: none -> 20.4 us  [the longest x3 11.3 us: shards(): lax.ppermute(backward[-1], 'mp', [(i, (i - 1) % mp) for i in range(mp)])]
    ppermute x2 -> x1, starting transfers between devices: 13.9 us -> 8.91 us  [swap(): return lax.ppermute(block, 'segment', [(0, 1), (1, 0)])]
    ppermute x1, starting transfers between devices: 4.06 us -> 7.16 us  [shards(): enc_sent = lax.ppermute(enc_term, 'segment', [(1, 0)])]
    all_to_all x3, starting transfers between devices: 11.7 us -> 14.3 us  [exchange(): return lax.all_to_all(blocks, axis, 0, 0, axis_index_groups=groups)]
    pallas_call x12 -> x11, Pallas kernels: 26.8 us -> 25.7 us  [call(): pl.pallas_call(kernel, grid=(1,), out_shape=[out(index, *what) for index,...]
  transfers between devices with their start and end apart: 8 -> 13, of which waited for: 5 -> 6; matrix products, arithmetic and copies ran while one was open for 0% -> 0% of each run, Pallas kernels for 7% -> 6%
where the time goes in v7:
time: 208 us; the launch traced here: 206 us
  blocking collectives  77.1 us (37%)
  starting transfers between devices  52 us (25%)
  waiting for transfers between devices  50 us (24%)
  Pallas kernels  25.7 us (12%)
    all_to_all x4, blocking collectives, exchange(): return lax.all_to_all(blocks, axis, 0, 0, axis_index_groups=groups)  77.1 us
    pallas_call x11, Pallas kernels, call(): pl.pallas_call(kernel, grid=(1,), out_shape=[out(index, *what) for index,...  25.7 us
    ppermute x4, waiting for transfers between devices, shards(): lax.ppermute(forward[-1], 'mp', [(i, (i + 1) % mp) for i in range(mp)])  22.2 us
    all_to_all x3, starting transfers between devices, exchange(): return lax.all_to_all(blocks, axis, 0, 0, axis_index_groups=groups)  14.3 us
    ppermute x3, waiting for transfers between devices, shards(): lax.ppermute(backward[-1], 'mp', [(i, (i - 1) % mp) for i in range(mp)])  13.7 us
    all_to_all x3, waiting for transfers between devices, exchange(): return lax.all_to_all(blocks, axis, 0, 0, axis_index_groups=groups)  12.1 us
    ppermute x3, starting transfers between devices, shards(): lax.ppermute(backward[-1], 'mp', [(i, (i - 1) % mp) for i in range(mp)])  11.3 us
    ppermute x4, starting transfers between devices, shards(): lax.ppermute(forward[-1], 'mp', [(i, (i + 1) % mp) for i in range(mp)])  9.1 us
  transfers between devices with their start and end apart: 13, of which 6 were waited for; matrix products, arithmetic and copies ran while one was open for 0% of the time, Pallas kernels for 6%

profile of v7, /device:TPU:1, one launch (start us, length us, event | category | flops | bytes accessed | tf_op | source)
XLA Modules:
  0.0 205.8 jit_solution(7744684676607808832)
XLA Ops:
  0.0 0.0 copy-start
  0.0 1.9 shard_map.82
  1.9 0.0 copy-start.2
  1.9 0.0 copy-start.3
  1.9 0.0 copy-start.4
  1.9 8.9 %collective-permute-start = (bf16[4,128,1280]{2,1,0:T(8,128)(2,1)}, bf16[4,128,1280]{2,1,0:T(8,128)(2,1)S(1)}, u32[]{:S(2)}, u32[]{:S(2)}) collective-permute-start(bf16[4,128,1280]{2,1,0:T(8,128)(2,1)} %bitcast.11), channel_id=1, source_target_pairs={{0,8},{8,0},{1,9},{9,1},{2,10},{10,2},{3,11},{11,3},{4,12},{12,4},... | collective-permute-start | bytes 3932168 | tf_op jit(solution)/shard_map/ppermute | solution.py:276
  10.9 4.7 %all-to-all-start = ((bf16[8,32,1280]{2,1,0:T(8,128)(2,1)}), bf16[8,32,1280]{2,1,0:T(8,128)(2,1)S(1)}, u32[]{:S(2)}, u32[]{:S(2)}) async-start(bf16[8,32,1280]{2,1,0:T(8,128)(2,1)} %shard_map.82), calls=%async_computation | async-start | bytes 1310720 | tf_op jit(solution)/shard_map/all_to_all | solution.py:298
  15.5 0.0 collective-permute-done.other
  15.5 0.0 copy-done
  15.5 0.0 copy-start.1
  15.6 0.8 fusion.refs_0_
  16.4 3.4 %collective-permute-start.1 = (bf16[128,1280]{1,0:T(8,128)(2,1)}, bf16[128,1280]{1,0:T(8,128)(2,1)}, u32[]{:S(2)}, u32[]{:S(2)}) collective-permute-start(bf16[128,1280]{1,0:T(8,128)(2,1)} %fusion.refs_0_), channel_id=1, source_target_pairs={{0,1},{1,2},{2,3},{3,4},{4,5},{5,6},{6,7},{7,0},{8,9},{9,10},{10,1... | collective-permute-start | bytes 983048 | tf_op jit(solution)/shard_map/ppermute | solution.py:316
  19.8 3.1 %collective-permute-start.5 = (bf16[128,1280]{1,0:T(8,128)(2,1)}, bf16[128,1280]{1,0:T(8,128)(2,1)}, u32[]{:S(2)}, u32[]{:S(2)}) collective-permute-start(bf16[128,1280]{1,0:T(8,128)(2,1)} %fusion.refs_0_), channel_id=1, source_target_pairs={{0,7},{1,0},{2,1},{3,2},{4,3},{5,4},{6,5},{7,6},{8,15},{9,8},{10,9... | collective-permute-start | bytes 983048 | tf_op jit(solution)/shard_map/ppermute | solution.py:318
  22.9 17.2 %collective-permute-done.1.refs_1_ = bf16[128,1280]{1,0:T(8,128)(2,1)} collective-permute-done((bf16[128,1280]{1,0:T(8,128)(2,1)}, bf16[128,1280]{1,0:T(8,128)(2,1)}, u32[]{:S(2)}, u32[]{:S(2)}) %collective-permute-start.1) | collective-permute-done | bytes 327712 | tf_op jit(solution)/shard_map/ppermute | solution.py:316
  40.1 1.9 collective-permute-start.2
  42.0 0.0 all-to-all-done
  42.0 0.0 copy-done.2
  42.0 0.0 copy-done.3
  42.1 0.0 copy-done.4
  42.1 3.4 %shard_map.83 = (bf16[256,1280]{1,0:T(8,128)(2,1)}, bf16[256,128]{1,0:T(8,128)(2,1)}, bf16[256,128]{1,0:T(8,128)(2,1)}, bf16[256,128]{1,0:T(8,128)(2,1)}, bf16[8...) custom-call(s32[1]{0:T(128)} %bitcast.core, s32[2,1,4]{2,1,0:T(1,128)S(1)} %copy-done.4, bf16[256,1280]{1,0:T(8,128)(2,1)S(1)} %bitcast.19, ...), custom_call_target="tpu_custom_call" | custom-call | flops 3000000000 | tf_op jit(solution)/shard_map/pallas_call | solution.py:258
  45.4 0.0 copy-done.1
  45.4 6.1 %all-to-all-start.1 = ((bf16[8,256,128]{2,1,0:T(8,128)(2,1)}), bf16[8,256,128]{2,1,0:T(8,128)(2,1)S(1)}, u32[]{:S(2)}, u32[]{:S(2)}) async-start(bf16[8,256,128]{2,1,0:T(8,128)(2,1)} %get-tuple-element.34), calls=%async_computation.1 | async-start | bytes 1048576 | tf_op jit(solution)/shard_map/all_to_all | solution.py:298
  51.5 0.0 collective-permute-done.5.refs_7_
  51.5 4.6 %collective-permute-start.6 = (bf16[128,1280]{1,0:T(8,128)(2,1)}, bf16[128,1280]{1,0:T(8,128)(2,1)S(1)}, u32[]{:S(2)}, u32[]{:S(2)}) collective-permute-start(bf16[128,1280]{1,0:T(8,128)(2,1)} %collective-permute-done.5.refs_7_), channel_id=1, source_target_pairs={{0,7},{1,0},{2,1},{3,2},{4,3},{5,4},{6,5},{7,6},{8,15},{9,8},{10,9... | collective-permute-start | bytes 983048 | tf_op jit(solution)/shard_map/ppermute | solution.py:318
  56.1 0.0 collective-permute-done.2.refs_2_
  56.1 1.9 collective-permute-start.3
  58.0 13.1 %collective-permute-done.6.refs_6_ = bf16[128,1280]{1,0:T(8,128)(2,1)S(1)} collective-permute-done((bf16[128,1280]{1,0:T(8,128)(2,1)}, bf16[128,1280]{1,0:T(8,128)(2,1)S(1)}, u32[]{:S(2)}, u32[]{:S(2)}) %collective-permute-start.6) | collective-permute-done | bytes 327712 | tf_op jit(solution)/shard_map/ppermute | solution.py:318
  71.1 3.6 %collective-permute-start.7 = (bf16[128,1280]{1,0:T(8,128)(2,1)S(1)}, bf16[128,1280]{1,0:T(8,128)(2,1)S(1)}, u32[]{:S(2)}, u32[]{:S(2)}) collective-permute-start(bf16[128,1280]{1,0:T(8,128)(2,1)S(1)} %collective-permute-done.6.refs_6_), channel_id=1, source_target_pairs={{0,7},{1,0},{2,1},{3,2},{4,3},{5,4},{6,5},{7,6},{8,15},{9,8},{10,9... | collective-permute-start | bytes 983048 | tf_op jit(solution)/shard_map/ppermute | solution.py:318
  74.7 0.0 collective-permute-done.3.refs_3_
  74.7 1.9 collective-permute-start.4
  76.6 0.0 copy-start.5
  76.6 3.0 %shard_map.84 = (bf16[64,128]{1,0:T(8,128)(2,1)}, bf16[64,128]{1,0:T(8,128)(2,1)}) custom-call(s32[1]{0:T(128)} %bitcast.core, bf16[2,64,1280]{2,1,0:T(8,128)(2,1)} %tokens.1, bf16[2,64,1280]{2,1,0:T(8,128)(2,1)} %upstream.3, bf16[4,128,1280]{2,1,0:T(8,128)(2,1)} %bitcast.12, bf16[4,128,1280]{2,1,0:T(8,128)(2,1)} %copy-done.1, f32[3,1280]{1,0:T(4,128)S(1)} %copy-done.2, ...), custom_call_target="tpu_custom_call" | custom-call | tf_op jit(solution)/shard_map/pallas_call | solution.py:258
  79.6 0.0 all-to-all-done.1.context
  79.6 0.6 collective-permute-done.7.refs_5_
  80.2 5.0 %collective-permute-done.4.refs_4_ = bf16[128,1280]{1,0:T(8,128)(2,1)S(1)} collective-permute-done((bf16[128,1280]{1,0:T(8,128)(2,1)S(1)}, bf16[128,1280]{1,0:T(8,128)(2,1)S(1)}, u32[]{:S(2)}, u32[]{:S(2)}) %collective-permute-start.4) | collective-permute-done | bytes 327712 | tf_op jit(solution)/shard_map/ppermute | solution.py:316
  85.2 0.0 copy-done.5
  85.2 6.0 %shard_map.85 = (bf16[256,1280]{1,0:T(8,128)(2,1)S(1)}, bf16[32,1280]{1,0:T(8,128)(2,1)}, bf16[256,1280]{1,0:T(8,128)(2,1)}, bf16[256,128]{1,0:T(8,128)(2,1)}, b...) custom-call(s32[1]{0:T(128)} %bitcast.core, s32[1]{0:T(128)} %bitcast.1.place, s32[2,1,4]{2,1,0:T(1,128)S(1)} %copy-done.4, ...), custom_call_target="tpu_custom_call" | custom-call | tf_op jit(solution)/shard_map/pallas_call | solution.py:258
  91.2 22.4 %all_to_all.35.pieces = bf16[8,32,1280]{2,1,0:T(8,128)(2,1)S(1)} all-to-all(bf16[8,32,1280]{2,1,0:T(8,128)(2,1)S(1)} %bitcast.22), channel_id=1, replica_groups=mesh['dp'=32,'segment'=2,'mp'=8] {'mp'}, dimensions={0} | all-to-all | bytes 1310720 | tf_op jit(solution)/shard_map/all_to_all | solution.py:298
  113.6 2.1 %shard_map.86 = bf16[8,32,1280]{2,1,0:T(8,128)(2,1)} custom-call(bf16[8,32,1280]{2,1,0:T(8,128)(2,1)S(1)} %all_to_all.35.pieces, bf16[32,1280]{1,0:T(8,128)(2,1)} %get-tuple-element.49.states, f32[3,1280]{1,0:T(4,128)S(1)} %copy-done.2), custom_call_target="tpu_custom_call" | custom-call | tf_op jit(solution)/shard_map/pallas_call | solution.py:258
  115.7 3.5 %all-to-all-start.3 = ((bf16[8,32,1280]{2,1,0:T(8,128)(2,1)}), bf16[8,32,1280]{2,1,0:T(8,128)(2,1)S(1)}, u32[]{:S(2)}, u32[]{:S(2)}) async-start(bf16[8,32,1280]{2,1,0:T(8,128)(2,1)} %shard_map.86), calls=%async_computation.3 | async-start | bytes 1310720 | tf_op jit(solution)/shard_map/all_to_all | solution.py:298
  119.2 2.7 %shard_map.88.dec_term = bf16[384,1280]{1,0:T(8,128)(2,1)} custom-call(s32[1]{0:T(128)} %bitcast.core, bf16[256,128]{1,0:T(8,128)(2,1)} %get-tuple-element.55.key_grad, bf16[256,128]{1,0:T(8,128)(2,1)} %get-tuple-element.56.value_grad, bf16[64,128]{1,0:T(8,128)(2,1)} %get-tuple-element.57.context, bf16[256,1280]{1,0:T(8,128)(2,1)} %get-tuple-element.58.normed, ...), custom_call_target="tpu_custom_call" | custom-call | tf_op jit(solution)/shard_map/pallas_call | solution.py:258
  121.9 1.3 collective-permute-start.9
  123.2 12.1 %all-to-all-done.3 = bf16[8,32,1280]{2,1,0:T(8,128)(2,1)S(1)} async-done(((bf16[8,32,1280]{2,1,0:T(8,128)(2,1)}), bf16[8,32,1280]{2,1,0:T(8,128)(2,1)S(1)}, u32[]{:S(2)}, u32[]{:S(2)}) %all-to-all-start.3) | async-done | bytes 655392 | tf_op jit(solution)/shard_map/all_to_all | solution.py:298
  135.2 3.4 %shard_map.87.enc_term = bf16[384,1280]{1,0:T(8,128)(2,1)S(1)} custom-call(s32[1]{0:T(128)} %bitcast.core, bf16[256,1280]{1,0:T(8,128)(2,1)S(1)} %bitcast.21, bf16[4,128,1280]{2,1,0:T(8,128)(2,1)} %bitcast.14, bf16[4,128,1280]{2,1,0:T(8,128)(2,1)} %copy-done.1, bf16[256,128]{1,0:T(8,128)(2,1)} %get-tuple-element.50.queries, ...), custom_call_target="tpu_custom_call" | custom-call | tf_op jit(solution)/shard_map/pallas_call | solution.py:258
  138.7 7.2 %collective-permute-start.8 = (bf16[384,1280]{1,0:T(8,128)(2,1)S(1)}, bf16[384,1280]{1,0:T(8,128)(2,1)S(1)}, u32[]{:S(2)}, u32[]{:S(2)}) collective-permute-start(bf16[384,1280]{1,0:T(8,128)(2,1)S(1)} %shard_map.87.enc_term), channel_id=1, source_target_pairs={{8,0},{9,1},{10,2},{11,3},{12,4},{13,5},{14,6},{15,7},{24,16},{25,... | collective-permute-start | bytes 2949128 | tf_op jit(solution)/shard_map/ppermute | solution.py:397
  145.8 0.0 collective-permute-done.9.dec_sent
  145.9 2.1 %collective-permute-done.8.enc_sent = bf16[384,1280]{1,0:T(8,128)(2,1)S(1)} collective-permute-done((bf16[384,1280]{1,0:T(8,128)(2,1)S(1)}, bf16[384,1280]{1,0:T(8,128)(2,1)S(1)}, u32[]{:S(2)}, u32[]{:S(2)}) %collective-permute-start.8) | collective-permute-done | bytes 983072 | tf_op jit(solution)/shard_map/ppermute | solution.py:397
  148.0 1.6 shard_map.89
  149.5 19.4 %all_to_all.36.pieces = bf16[8,60,8,128]{3,2,1,0:T(8,128)(2,1)S(1)} all-to-all(bf16[8,60,8,128]{3,2,1,0:T(8,128)(2,1)S(1)} %bitcast.17), channel_id=1, replica_groups={{0,16,128,144,256,272,384,400},{32,48,160,176,288,304,416,432},{64,80,1..., dimensions={0} | all-to-all | bytes 1966080 | tf_op jit(solution)/shard_map/all_to_all | solution.py:298
  168.9 0.1 shard_map.90
  169.0 18.2 %all_to_all.37.pieces = bf16[4,60,8,128]{3,2,1,0:T(8,128)(2,1)S(1)} all-to-all(bf16[4,60,8,128]{3,2,1,0:T(8,128)(2,1)S(1)} %shard_map.90), channel_id=1, replica_groups={{0,32,64,96},{16,48,80,112},{128,160,192,224},{144,176,208,240},{256,28..., dimensions={0} | all-to-all | bytes 983040 | tf_op jit(solution)/shard_map/all_to_all | solution.py:298
  187.3 0.1 shard_map.91
  187.3 17.1 %all_to_all.38 = bf16[8,60,8,128]{3,2,1,0:T(8,128)(2,1)S(1)} all-to-all(bf16[8,60,8,128]{3,2,1,0:T(8,128)(2,1)S(1)} %shard_map.91), channel_id=1, replica_groups={{0,16,128,144,256,272,384,400},{32,48,160,176,288,304,416,432},{64,80,1..., dimensions={0} | all-to-all | bytes 1966080 | tf_op jit(solution)/shard_map/all_to_all | solution.py:298
  204.4 1.4 shard_map.92
Async XLA Ops:
  0.0 15.5 %copy-start = (bf16[1,4,128,1280]{3,2,1,0:T(8,128)(2,1)S(1)}, bf16[1,4,128,1280]{3,2,1,0:T(8,128)(2,1)}, u32[]{:S(2)}) copy-start(bf16[1,4,128,1280]{3,2,1,0:T(8,128)(2,1)} %param.13) | copy-start | bytes 3932164
  1.9 40.1 %copy-start.2 = (f32[3,1280]{1,0:T(4,128)S(1)}, f32[3,1280]{1,0:T(4,128)}, u32[]{:S(2)}) copy-start(f32[3,1280]{1,0:T(4,128)} %gains.7) | copy-start | bytes 46084
  1.9 40.1 %copy-start.3 = (f32[3,1280]{1,0:T(4,128)S(1)}, f32[3,1280]{1,0:T(4,128)}, u32[]{:S(2)}) copy-start(f32[3,1280]{1,0:T(4,128)} %biases.5) | copy-start | bytes 46084
  1.9 40.1 %copy-start.4 = (s32[2,1,4]{2,1,0:T(1,128)S(1)}, s32[2,1,4]{2,1,0:T(1,128)}, u32[]{:S(2)}) copy-start(s32[2,1,4]{2,1,0:T(1,128)} %frame_lens.1) | copy-start | bytes 100
  1.9 13.6 %collective-permute-start = (bf16[4,128,1280]{2,1,0:T(8,128)(2,1)}, bf16[4,128,1280]{2,1,0:T(8,128)(2,1)S(1)}, u32[]{:S(2)}, u32[]{:S(2)}) collective-permute-start(bf16[4,128,1280]{2,1,0:T(8,128)(2,1)} %bitcast.11), channel_id=1, source_target_pairs={{0,8},{8,0},{1,9},{9,1},{2,10},{10,2},{3,11},{11,3},{4,12},{12,4},... | collective-permute-start | bytes 3932168 | tf_op jit(solution)/shard_map/ppermute | solution.py:276
  10.9 31.2 %all-to-all-start = ((bf16[8,32,1280]{2,1,0:T(8,128)(2,1)}), bf16[8,32,1280]{2,1,0:T(8,128)(2,1)S(1)}, u32[]{:S(2)}, u32[]{:S(2)}) async-start(bf16[8,32,1280]{2,1,0:T(8,128)(2,1)} %shard_map.82), calls=%async_computation | async-start | bytes 1310720 | tf_op jit(solution)/shard_map/all_to_all | solution.py:298
  15.5 29.9 %copy-start.1 = (bf16[4,128,1280]{2,1,0:T(8,128)(2,1)}, bf16[4,128,1280]{2,1,0:T(8,128)(2,1)S(1)}, u32[]{:S(2)}) copy-start(bf16[4,128,1280]{2,1,0:T(8,128)(2,1)S(1)} %collective-permute-done.other) | copy-start | bytes 3932164
  16.4 23.7 %collective-permute-start.1 = (bf16[128,1280]{1,0:T(8,128)(2,1)}, bf16[128,1280]{1,0:T(8,128)(2,1)}, u32[]{:S(2)}, u32[]{:S(2)}) collective-permute-start(bf16[128,1280]{1,0:T(8,128)(2,1)} %fusion.refs_0_), channel_id=1, source_target_pairs={{0,1},{1,2},{2,3},{3,4},{4,5},{5,6},{6,7},{7,0},{8,9},{9,10},{10,1... | collective-permute-start | bytes 983048 | tf_op jit(solution)/shard_map/ppermute | solution.py:316
  19.8 31.7 %collective-permute-start.5 = (bf16[128,1280]{1,0:T(8,128)(2,1)}, bf16[128,1280]{1,0:T(8,128)(2,1)}, u32[]{:S(2)}, u32[]{:S(2)}) collective-permute-start(bf16[128,1280]{1,0:T(8,128)(2,1)} %fusion.refs_0_), channel_id=1, source_target_pairs={{0,7},{1,0},{2,1},{3,2},{4,3},{5,4},{6,5},{7,6},{8,15},{9,8},{10,9... | collective-permute-start | bytes 983048 | tf_op jit(solution)/shard_map/ppermute | solution.py:318
  40.1 16.0 %collective-permute-start.2 = (bf16[128,1280]{1,0:T(8,128)(2,1)}, bf16[128,1280]{1,0:T(8,128)(2,1)}, u32[]{:S(2)}, u32[]{:S(2)}) collective-permute-start(bf16[128,1280]{1,0:T(8,128)(2,1)} %collective-permute-done.1.refs_1_), channel_id=1, source_target_pairs={{0,1},{1,2},{2,3},{3,4},{4,5},{5,6},{6,7},{7,0},{8,9},{9,10},{10,1... | collective-permute-start | bytes 983048 | tf_op jit(solution)/shard_map/ppermute | solution.py:316
  45.4 34.2 %all-to-all-start.1 = ((bf16[8,256,128]{2,1,0:T(8,128)(2,1)}), bf16[8,256,128]{2,1,0:T(8,128)(2,1)S(1)}, u32[]{:S(2)}, u32[]{:S(2)}) async-start(bf16[8,256,128]{2,1,0:T(8,128)(2,1)} %get-tuple-element.34), calls=%async_computation.1 | async-start | bytes 1048576 | tf_op jit(solution)/shard_map/all_to_all | solution.py:298
  51.5 19.6 %collective-permute-start.6 = (bf16[128,1280]{1,0:T(8,128)(2,1)}, bf16[128,1280]{1,0:T(8,128)(2,1)S(1)}, u32[]{:S(2)}, u32[]{:S(2)}) collective-permute-start(bf16[128,1280]{1,0:T(8,128)(2,1)} %collective-permute-done.5.refs_7_), channel_id=1, source_target_pairs={{0,7},{1,0},{2,1},{3,2},{4,3},{5,4},{6,5},{7,6},{8,15},{9,8},{10,9... | collective-permute-start | bytes 983048 | tf_op jit(solution)/shard_map/ppermute | solution.py:318
  56.1 18.6 %collective-permute-start.3 = (bf16[128,1280]{1,0:T(8,128)(2,1)}, bf16[128,1280]{1,0:T(8,128)(2,1)S(1)}, u32[]{:S(2)}, u32[]{:S(2)}) collective-permute-start(bf16[128,1280]{1,0:T(8,128)(2,1)} %collective-permute-done.2.refs_2_), channel_id=1, source_target_pairs={{0,1},{1,2},{2,3},{3,4},{4,5},{5,6},{6,7},{7,0},{8,9},{9,10},{10,1... | collective-permute-start | bytes 983048 | tf_op jit(solution)/shard_map/ppermute | solution.py:316
  71.1 9.1 %collective-permute-start.7 = (bf16[128,1280]{1,0:T(8,128)(2,1)S(1)}, bf16[128,1280]{1,0:T(8,128)(2,1)S(1)}, u32[]{:S(2)}, u32[]{:S(2)}) collective-permute-start(bf16[128,1280]{1,0:T(8,128)(2,1)S(1)} %collective-permute-done.6.refs_6_), channel_id=1, source_target_pairs={{0,7},{1,0},{2,1},{3,2},{4,3},{5,4},{6,5},{7,6},{8,15},{9,8},{10,9... | collective-permute-start | bytes 983048 | tf_op jit(solution)/shard_map/ppermute | solution.py:318
  74.7 10.5 %collective-permute-start.4 = (bf16[128,1280]{1,0:T(8,128)(2,1)S(1)}, bf16[128,1280]{1,0:T(8,128)(2,1)S(1)}, u32[]{:S(2)}, u32[]{:S(2)}) collective-permute-start(bf16[128,1280]{1,0:T(8,128)(2,1)S(1)} %collective-permute-done.3.refs_3_), channel_id=1, source_target_pairs={{0,1},{1,2},{2,3},{3,4},{4,5},{5,6},{6,7},{7,0},{8,9},{9,10},{10,1... | collective-permute-start | bytes 983048 | tf_op jit(solution)/shard_map/ppermute | solution.py:316
  76.6 8.6 %copy-start.5 = (s32[2,1,4]{2,1,0:T(1,128)S(1)}, s32[2,1,4]{2,1,0:T(1,128)}, u32[]{:S(2)}) copy-start(s32[2,1,4]{2,1,0:T(1,128)} %token_lens.1) | copy-start | bytes 100
  115.7 19.6 %all-to-all-start.3 = ((bf16[8,32,1280]{2,1,0:T(8,128)(2,1)}), bf16[8,32,1280]{2,1,0:T(8,128)(2,1)S(1)}, u32[]{:S(2)}, u32[]{:S(2)}) async-start(bf16[8,32,1280]{2,1,0:T(8,128)(2,1)} %shard_map.86), calls=%async_computation.3 | async-start | bytes 1310720 | tf_op jit(solution)/shard_map/all_to_all | solution.py:298
  121.9 24.0 %collective-permute-start.9 = (bf16[384,1280]{1,0:T(8,128)(2,1)}, bf16[384,1280]{1,0:T(8,128)(2,1)S(1)}, u32[]{:S(2)}, u32[]{:S(2)}) collective-permute-start(bf16[384,1280]{1,0:T(8,128)(2,1)} %shard_map.88.dec_term), channel_id=1, source_target_pairs={{0,8},{1,9},{2,10},{3,11},{4,12},{5,13},{6,14},{7,15},{16,24},{17,... | collective-permute-start | bytes 2949128 | tf_op jit(solution)/shard_map/ppermute | solution.py:396
  138.7 9.3 %collective-permute-start.8 = (bf16[384,1280]{1,0:T(8,128)(2,1)S(1)}, bf16[384,1280]{1,0:T(8,128)(2,1)S(1)}, u32[]{:S(2)}, u32[]{:S(2)}) collective-permute-start(bf16[384,1280]{1,0:T(8,128)(2,1)S(1)} %shard_map.87.enc_term), channel_id=1, source_target_pairs={{8,0},{9,1},{10,2},{11,3},{12,4},{13,5},{14,6},{15,7},{24,16},{25,... | collective-permute-start | bytes 2949128 | tf_op jit(solution)/shard_map/ppermute | solution.py:397

commit v8 on v7

--- a/solution.py
+++ b/solution.py
@@ -110,12 +110,20 @@
     partial, states, normed, key_grad, value_grad, dec_context, scratch = refs
     first = core[0] == 0
     rows = x.shape[0]
+    steps = devices // 2
+    passed, swapped = out_shards[: steps + 1], out_shards[steps + 1 :]
+
+    def context_at(back):
+        return context[(place[0] + jnp.where(first, devices - back, back)) % devices]
+
+    pairs = [(0, passed[0], steps, passed[steps])]
+    for back in range(1, steps):
+        pairs.append((back, passed[back], devices - back, swapped[back - 1]))
     summed = x[...].astype(jnp.float32)
-    for index in range(0, devices, 2):
-        pair = range(index, index + 2)
-        left = [context[(place[0] + devices - back) % devices] for back in pair]
-        right = [out_shards[back][...] for back in pair]
-        summed = summed + dot_nn(jnp.concatenate(left, axis=1), jnp.concatenate(right, axis=0))
+    for back, shard, far_back, far_shard in pairs:
+        left = jnp.concatenate([context_at(back), context_at(far_back)], axis=1)
+        right = jnp.concatenate([shard[...], far_shard[...]], axis=0)
+        summed = summed + dot_nn(left, right)
     scratch[...] = summed
     all_states = scratch[...].astype(jnp.bfloat16)
     shard = states.shape[0]
@@ -311,12 +319,13 @@
     copies, own = lax.optimization_barrier((copies, own))
     other = swap(own)
     shard = jnp.where(first, own[3], other[3])
-    forward, backward = [shard], [shard]
-    for _ in range(mp // 2):
-        forward.append(lax.ppermute(forward[-1], "mp", [(i, (i + 1) % mp) for i in range(mp)]))
-    for _ in range(mp - mp // 2 - 1):
-        backward.append(lax.ppermute(backward[-1], "mp", [(i, (i - 1) % mp) for i in range(mp)]))
-    out_shards = forward + backward[:0:-1]
+    step = [(i, (i + 1) % mp) for i in range(mp)] + [(mp + i, mp + (i - 1) % mp) for i in range(mp)]
+    passed, swapped = [shard], []
+    for index in range(mp // 2):
+        passed.append(lax.ppermute(passed[-1], ("segment", "mp"), step))
+        if index < mp // 2 - 1:
+            swapped.append(swap(passed[-1]))
+    out_shards = passed + swapped
     enc_full = exchange(copies).reshape(rows, features)
 
     token_queries, token_grads = call(

time: 208 us -> 200 us (0.962)
  waiting for transfers between devices: 50 us -> 41.5 us
    ppermute x7 -> x4, waiting for transfers between devices: 35.9 us -> 25.8 us  [shards(): passed.append(lax.ppermute(passed[-1], ('segment', 'mp'), step))]
    ppermute x1 -> x4, starting transfers between devices: 8.91 us -> 16.7 us  [swap(): return lax.ppermute(block, 'segment', [(0, 1), (1, 0)])]
    ppermute x7 -> x4, starting transfers between devices: 20.4 us -> 15.1 us  [shards(): passed.append(lax.ppermute(passed[-1], ('segment', 'mp'), step))]
  transfers between devices with their start and end apart: 13 -> 13, of which waited for: 6 -> 5; matrix products, arithmetic and copies ran while one was open for 0% -> 0% of each run, Pallas kernels for 6% -> 6%
where the time goes in v8:
time: 200 us; the launch traced here: 198 us
  blocking collectives  76.2 us (38%)
  starting transfers between devices  53.5 us (27%)
  waiting for transfers between devices  41.5 us (21%)
  Pallas kernels  25.4 us (13%)
    all_to_all x4, blocking collectives, exchange(): return lax.all_to_all(blocks, axis, 0, 0, axis_index_groups=groups)  76.2 us
    ppermute x4, waiting for transfers between devices, shards(): passed.append(lax.ppermute(passed[-1], ('segment', 'mp'), step))  25.8 us
    pallas_call x11, Pallas kernels, call(): pl.pallas_call(kernel, grid=(1,), out_shape=[out(index, *what) for index,...  25.4 us
    ppermute x4, starting transfers between devices, swap(): return lax.ppermute(block, 'segment', [(0, 1), (1, 0)])  16.7 us
    ppermute x4, starting transfers between devices, shards(): passed.append(lax.ppermute(passed[-1], ('segment', 'mp'), step))  15.1 us
    all_to_all x3, starting transfers between devices, exchange(): return lax.all_to_all(blocks, axis, 0, 0, axis_index_groups=groups)  14.8 us
    all_to_all x3, waiting for transfers between devices, exchange(): return lax.all_to_all(blocks, axis, 0, 0, axis_index_groups=groups)  13.7 us
    ppermute x1, starting transfers between devices, shards(): enc_sent = lax.ppermute(enc_term, 'segment', [(1, 0)])  5.56 us
  transfers between devices with their start and end apart: 13, of which 5 were waited for; matrix products, arithmetic and copies ran while one was open for 0% of the time, Pallas kernels for 6%

profile of v8, /device:TPU:1, one launch (start us, length us, event | category | flops | bytes accessed | tf_op | source)
XLA Modules:
  0.0 197.8 jit_solution(551239124712584681)
XLA Ops:
  0.0 0.0 copy-start
  0.0 1.9 shard_map.82
  1.9 0.0 copy-start.4
  1.9 0.0 copy-start.5
  1.9 0.0 copy-start.6
  1.9 8.9 %collective-permute-start = (bf16[4,128,1280]{2,1,0:T(8,128)(2,1)}, bf16[4,128,1280]{2,1,0:T(8,128)(2,1)S(1)}, u32[]{:S(2)}, u32[]{:S(2)}) collective-permute-start(bf16[4,128,1280]{2,1,0:T(8,128)(2,1)} %bitcast.11), channel_id=1, source_target_pairs={{0,8},{8,0},{1,9},{9,1},{2,10},{10,2},{3,11},{11,3},{4,12},{12,4},... | collective-permute-start | bytes 3932168 | tf_op jit(solution)/shard_map/ppermute | solution.py:284
  10.8 4.7 %all-to-all-start = ((bf16[8,32,1280]{2,1,0:T(8,128)(2,1)}), bf16[8,32,1280]{2,1,0:T(8,128)(2,1)S(1)}, u32[]{:S(2)}, u32[]{:S(2)}) async-start(bf16[8,32,1280]{2,1,0:T(8,128)(2,1)} %shard_map.82), calls=%async_computation | async-start | bytes 1310720 | tf_op jit(solution)/shard_map/all_to_all | solution.py:306
  15.5 0.0 collective-permute-done.other
  15.5 0.0 copy-done
  15.5 0.0 copy-start.1
  15.6 4.6 %collective-permute-start.1 = (bf16[128,1280]{1,0:T(8,128)(2,1)S(1)}, bf16[128,1280]{1,0:T(8,128)(2,1)}, u32[]{:S(2)}, u32[]{:S(2)}) collective-permute-start(bf16[128,1280]{1,0:T(8,128)(2,1)S(1)} %fusion.refs_0_), channel_id=1, source_target_pairs={{0,1},{1,2},{2,3},{3,4},{4,5},{5,6},{6,7},{7,0},{8,15},{9,8},{10,9... | collective-permute-start | bytes 983048 | tf_op jit(solution)/shard_map/ppermute | solution.py:325
  20.2 0.0 copy-start.2
  20.2 0.7 copy-done.2
  20.9 15.2 %collective-permute-done.1.refs_1_ = bf16[128,1280]{1,0:T(8,128)(2,1)} collective-permute-done((bf16[128,1280]{1,0:T(8,128)(2,1)S(1)}, bf16[128,1280]{1,0:T(8,128)(2,1)}, u32[]{:S(2)}, u32[]{:S(2)}) %collective-permute-start.1) | collective-permute-done | bytes 327712 | tf_op jit(solution)/shard_map/ppermute | solution.py:325
  36.1 2.8 %collective-permute-start.2 = (bf16[128,1280]{1,0:T(8,128)(2,1)}, bf16[128,1280]{1,0:T(8,128)(2,1)}, u32[]{:S(2)}, u32[]{:S(2)}) collective-permute-start(bf16[128,1280]{1,0:T(8,128)(2,1)} %collective-permute-done.1.refs_1_), channel_id=1, source_target_pairs={{0,1},{1,2},{2,3},{3,4},{4,5},{5,6},{6,7},{7,0},{8,15},{9,8},{10,9... | collective-permute-start | bytes 983048 | tf_op jit(solution)/shard_map/ppermute | solution.py:325
  38.9 0.0 all-to-all-done
  38.9 0.0 copy-done.4
  38.9 0.0 copy-done.5
  38.9 0.0 copy-done.6
  39.0 3.3 %shard_map.83 = (bf16[256,1280]{1,0:T(8,128)(2,1)}, bf16[256,128]{1,0:T(8,128)(2,1)}, bf16[256,128]{1,0:T(8,128)(2,1)}, bf16[256,128]{1,0:T(8,128)(2,1)}, bf16[8...) custom-call(s32[1]{0:T(128)} %bitcast.core, s32[2,1,4]{2,1,0:T(1,128)S(1)} %copy-done.6, bf16[256,1280]{1,0:T(8,128)(2,1)S(1)} %bitcast.19, ...), custom_call_target="tpu_custom_call" | custom-call | flops 3000000000 | tf_op jit(solution)/shard_map/pallas_call | solution.py:266
  42.3 0.0 copy-done.1
  42.3 6.6 %all-to-all-start.1 = ((bf16[8,256,128]{2,1,0:T(8,128)(2,1)}), bf16[8,256,128]{2,1,0:T(8,128)(2,1)S(1)}, u32[]{:S(2)}, u32[]{:S(2)}) async-start(bf16[8,256,128]{2,1,0:T(8,128)(2,1)} %get-tuple-element.34), calls=%async_computation.1 | async-start | bytes 1048576 | tf_op jit(solution)/shard_map/all_to_all | solution.py:306
  48.9 0.0 collective-permute-done.2.refs_2_
  48.9 4.6 %collective-permute-start.3 = (bf16[128,1280]{1,0:T(8,128)(2,1)}, bf16[128,1280]{1,0:T(8,128)(2,1)S(1)}, u32[]{:S(2)}, u32[]{:S(2)}) collective-permute-start(bf16[128,1280]{1,0:T(8,128)(2,1)} %collective-permute-done.2.refs_2_), channel_id=1, source_target_pairs={{0,1},{1,2},{2,3},{3,4},{4,5},{5,6},{6,7},{7,0},{8,15},{9,8},{10,9... | collective-permute-start | bytes 983048 | tf_op jit(solution)/shard_map/ppermute | solution.py:325
  53.5 1.9 collective-permute-start.5
  55.4 2.4 %collective-permute-start.6 = (bf16[128,1280]{1,0:T(8,128)(2,1)}, bf16[128,1280]{1,0:T(8,128)(2,1)S(1)}, u32[]{:S(2)}, u32[]{:S(2)}) collective-permute-start(bf16[128,1280]{1,0:T(8,128)(2,1)} %collective-permute-done.2.refs_2_), channel_id=1, source_target_pairs={{0,8},{8,0},{1,9},{9,1},{2,10},{10,2},{3,11},{11,3},{4,12},{12,4},... | collective-permute-start | bytes 983048 | tf_op jit(solution)/shard_map/ppermute | solution.py:284
  57.8 8.7 %collective-permute-done.3.refs_3_ = bf16[128,1280]{1,0:T(8,128)(2,1)S(1)} collective-permute-done((bf16[128,1280]{1,0:T(8,128)(2,1)}, bf16[128,1280]{1,0:T(8,128)(2,1)S(1)}, u32[]{:S(2)}, u32[]{:S(2)}) %collective-permute-start.3) | collective-permute-done | bytes 327712 | tf_op jit(solution)/shard_map/ppermute | solution.py:325
  66.6 3.5 %collective-permute-start.7 = (bf16[128,1280]{1,0:T(8,128)(2,1)S(1)}, bf16[128,1280]{1,0:T(8,128)(2,1)S(1)}, u32[]{:S(2)}, u32[]{:S(2)}) collective-permute-start(bf16[128,1280]{1,0:T(8,128)(2,1)S(1)} %collective-permute-done.3.refs_3_), channel_id=1, source_target_pairs={{0,8},{8,0},{1,9},{9,1},{2,10},{10,2},{3,11},{11,3},{4,12},{12,4},... | collective-permute-start | bytes 983048 | tf_op jit(solution)/shard_map/ppermute | solution.py:284
  70.1 3.1 %collective-permute-start.4 = (bf16[128,1280]{1,0:T(8,128)(2,1)S(1)}, bf16[128,1280]{1,0:T(8,128)(2,1)S(1)}, u32[]{:S(2)}, u32[]{:S(2)}) collective-permute-start(bf16[128,1280]{1,0:T(8,128)(2,1)S(1)} %collective-permute-done.3.refs_3_), channel_id=1, source_target_pairs={{0,1},{1,2},{2,3},{3,4},{4,5},{5,6},{6,7},{7,0},{8,15},{9,8},{10,9... | collective-permute-start | bytes 983048 | tf_op jit(solution)/shard_map/ppermute | solution.py:325
  73.2 0.0 copy-start.3
  73.2 0.0 copy-start.7
  73.3 3.1 %shard_map.84 = (bf16[64,128]{1,0:T(8,128)(2,1)}, bf16[64,128]{1,0:T(8,128)(2,1)}) custom-call(s32[1]{0:T(128)} %bitcast.core, bf16[2,64,1280]{2,1,0:T(8,128)(2,1)} %tokens.1, bf16[2,64,1280]{2,1,0:T(8,128)(2,1)} %upstream.3, bf16[4,128,1280]{2,1,0:T(8,128)(2,1)} %bitcast.12, bf16[4,128,1280]{2,1,0:T(8,128)(2,1)} %copy-done.1, f32[3,1280]{1,0:T(4,128)S(1)} %copy-done.4, ...), custom_call_target="tpu_custom_call" | custom-call | tf_op jit(solution)/shard_map/pallas_call | solution.py:266
  76.3 0.0 collective-permute-done.5.refs_5_
  76.3 0.0 all-to-all-done.1.context
  76.3 0.0 collective-permute-done.6.refs_6_
  76.3 0.0 collective-permute-done.7.refs_7_
  76.3 1.9 collective-permute-done.4.refs_4_
  78.2 0.0 copy-done.3
  78.2 0.0 copy-done.7
  78.2 5.8 %shard_map.85 = (bf16[256,1280]{1,0:T(8,128)(2,1)S(1)}, bf16[32,1280]{1,0:T(8,128)(2,1)}, bf16[256,1280]{1,0:T(8,128)(2,1)}, bf16[256,128]{1,0:T(8,128)(2,1)}, b...) custom-call(s32[1]{0:T(128)} %bitcast.core, s32[1]{0:T(128)} %bitcast.1.place, s32[2,1,4]{2,1,0:T(1,128)S(1)} %copy-done.6, ...), custom_call_target="tpu_custom_call" | custom-call | tf_op jit(solution)/shard_map/pallas_call | solution.py:266
  84.0 21.5 %all_to_all.35.pieces = bf16[8,32,1280]{2,1,0:T(8,128)(2,1)S(1)} all-to-all(bf16[8,32,1280]{2,1,0:T(8,128)(2,1)S(1)} %bitcast.22), channel_id=1, replica_groups=mesh['dp'=32,'segment'=2,'mp'=8] {'mp'}, dimensions={0} | all-to-all | bytes 1310720 | tf_op jit(solution)/shard_map/all_to_all | solution.py:306
  105.5 2.1 %shard_map.86 = bf16[8,32,1280]{2,1,0:T(8,128)(2,1)} custom-call(bf16[8,32,1280]{2,1,0:T(8,128)(2,1)S(1)} %all_to_all.35.pieces, bf16[32,1280]{1,0:T(8,128)(2,1)} %get-tuple-element.49.states, f32[3,1280]{1,0:T(4,128)S(1)} %copy-done.4), custom_call_target="tpu_custom_call" | custom-call | tf_op jit(solution)/shard_map/pallas_call | solution.py:266
  107.6 3.5 %all-to-all-start.3 = ((bf16[8,32,1280]{2,1,0:T(8,128)(2,1)}), bf16[8,32,1280]{2,1,0:T(8,128)(2,1)S(1)}, u32[]{:S(2)}, u32[]{:S(2)}) async-start(bf16[8,32,1280]{2,1,0:T(8,128)(2,1)} %shard_map.86), calls=%async_computation.3 | async-start | bytes 1310720 | tf_op jit(solution)/shard_map/all_to_all | solution.py:306
  111.2 2.7 %shard_map.88.dec_term = bf16[384,1280]{1,0:T(8,128)(2,1)} custom-call(s32[1]{0:T(128)} %bitcast.core, bf16[256,128]{1,0:T(8,128)(2,1)} %get-tuple-element.55.key_grad, bf16[256,128]{1,0:T(8,128)(2,1)} %get-tuple-element.56.value_grad, bf16[64,128]{1,0:T(8,128)(2,1)} %get-tuple-element.57.context, bf16[256,1280]{1,0:T(8,128)(2,1)} %get-tuple-element.58.normed, ...), custom_call_target="tpu_custom_call" | custom-call | tf_op jit(solution)/shard_map/pallas_call | solution.py:266
  113.8 1.3 collective-permute-start.9
  115.1 13.6 %all-to-all-done.3 = bf16[8,32,1280]{2,1,0:T(8,128)(2,1)S(1)} async-done(((bf16[8,32,1280]{2,1,0:T(8,128)(2,1)}), bf16[8,32,1280]{2,1,0:T(8,128)(2,1)S(1)}, u32[]{:S(2)}, u32[]{:S(2)}) %all-to-all-start.3) | async-done | bytes 655392 | tf_op jit(solution)/shard_map/all_to_all | solution.py:306
  128.8 3.4 %shard_map.87.enc_term = bf16[384,1280]{1,0:T(8,128)(2,1)S(1)} custom-call(s32[1]{0:T(128)} %bitcast.core, bf16[256,1280]{1,0:T(8,128)(2,1)S(1)} %bitcast.21, bf16[4,128,1280]{2,1,0:T(8,128)(2,1)} %bitcast.14, bf16[4,128,1280]{2,1,0:T(8,128)(2,1)} %copy-done.1, bf16[256,128]{1,0:T(8,128)(2,1)} %get-tuple-element.50.queries, ...), custom_call_target="tpu_custom_call" | custom-call | tf_op jit(solution)/shard_map/pallas_call | solution.py:266
  132.2 5.6 %collective-permute-start.8 = (bf16[384,1280]{1,0:T(8,128)(2,1)S(1)}, bf16[384,1280]{1,0:T(8,128)(2,1)S(1)}, u32[]{:S(2)}, u32[]{:S(2)}) collective-permute-start(bf16[384,1280]{1,0:T(8,128)(2,1)S(1)} %shard_map.87.enc_term), channel_id=1, source_target_pairs={{8,0},{9,1},{10,2},{11,3},{12,4},{13,5},{14,6},{15,7},{24,16},{25,... | collective-permute-start | bytes 2949128 | tf_op jit(solution)/shard_map/ppermute | solution.py:406
  137.8 0.0 collective-permute-done.9.dec_sent
  137.8 2.1 %collective-permute-done.8.enc_sent = bf16[384,1280]{1,0:T(8,128)(2,1)S(1)} collective-permute-done((bf16[384,1280]{1,0:T(8,128)(2,1)S(1)}, bf16[384,1280]{1,0:T(8,128)(2,1)S(1)}, u32[]{:S(2)}, u32[]{:S(2)}) %collective-permute-start.8) | collective-permute-done | bytes 983072 | tf_op jit(solution)/shard_map/ppermute | solution.py:406
  139.9 1.6 shard_map.89
  141.5 19.3 %all_to_all.36.pieces = bf16[8,60,8,128]{3,2,1,0:T(8,128)(2,1)S(1)} all-to-all(bf16[8,60,8,128]{3,2,1,0:T(8,128)(2,1)S(1)} %bitcast.17), channel_id=1, replica_groups={{0,16,128,144,256,272,384,400},{32,48,160,176,288,304,416,432},{64,80,1..., dimensions={0} | all-to-all | bytes 1966080 | tf_op jit(solution)/shard_map/all_to_all | solution.py:306
  160.8 0.1 shard_map.90
  160.9 18.3 %all_to_all.37.pieces = bf16[4,60,8,128]{3,2,1,0:T(8,128)(2,1)S(1)} all-to-all(bf16[4,60,8,128]{3,2,1,0:T(8,128)(2,1)S(1)} %shard_map.90), channel_id=1, replica_groups={{0,32,64,96},{16,48,80,112},{128,160,192,224},{144,176,208,240},{256,28..., dimensions={0} | all-to-all | bytes 983040 | tf_op jit(solution)/shard_map/all_to_all | solution.py:306
  179.2 0.1 shard_map.91
  179.3 17.1 %all_to_all.38 = bf16[8,60,8,128]{3,2,1,0:T(8,128)(2,1)S(1)} all-to-all(bf16[8,60,8,128]{3,2,1,0:T(8,128)(2,1)S(1)} %shard_map.91), channel_id=1, replica_groups={{0,16,128,144,256,272,384,400},{32,48,160,176,288,304,416,432},{64,80,1..., dimensions={0} | all-to-all | bytes 1966080 | tf_op jit(solution)/shard_map/all_to_all | solution.py:306
  196.3 1.4 shard_map.92
  (1 shorter events, 0.0 us)
Async XLA Ops:
  0.0 15.5 %copy-start = (bf16[1,4,128,1280]{3,2,1,0:T(8,128)(2,1)S(1)}, bf16[1,4,128,1280]{3,2,1,0:T(8,128)(2,1)}, u32[]{:S(2)}) copy-start(bf16[1,4,128,1280]{3,2,1,0:T(8,128)(2,1)} %param.13) | copy-start | bytes 3932164
  1.9 37.0 %copy-start.4 = (f32[3,1280]{1,0:T(4,128)S(1)}, f32[3,1280]{1,0:T(4,128)}, u32[]{:S(2)}) copy-start(f32[3,1280]{1,0:T(4,128)} %gains.7) | copy-start | bytes 46084
  1.9 37.0 %copy-start.5 = (f32[3,1280]{1,0:T(4,128)S(1)}, f32[3,1280]{1,0:T(4,128)}, u32[]{:S(2)}) copy-start(f32[3,1280]{1,0:T(4,128)} %biases.5) | copy-start | bytes 46084
  1.9 37.0 %copy-start.6 = (s32[2,1,4]{2,1,0:T(1,128)S(1)}, s32[2,1,4]{2,1,0:T(1,128)}, u32[]{:S(2)}) copy-start(s32[2,1,4]{2,1,0:T(1,128)} %frame_lens.1) | copy-start | bytes 100
  1.9 13.6 %collective-permute-start = (bf16[4,128,1280]{2,1,0:T(8,128)(2,1)}, bf16[4,128,1280]{2,1,0:T(8,128)(2,1)S(1)}, u32[]{:S(2)}, u32[]{:S(2)}) collective-permute-start(bf16[4,128,1280]{2,1,0:T(8,128)(2,1)} %bitcast.11), channel_id=1, source_target_pairs={{0,8},{8,0},{1,9},{9,1},{2,10},{10,2},{3,11},{11,3},{4,12},{12,4},... | collective-permute-start | bytes 3932168 | tf_op jit(solution)/shard_map/ppermute | solution.py:284
  10.8 28.1 %all-to-all-start = ((bf16[8,32,1280]{2,1,0:T(8,128)(2,1)}), bf16[8,32,1280]{2,1,0:T(8,128)(2,1)S(1)}, u32[]{:S(2)}, u32[]{:S(2)}) async-start(bf16[8,32,1280]{2,1,0:T(8,128)(2,1)} %shard_map.82), calls=%async_computation | async-start | bytes 1310720 | tf_op jit(solution)/shard_map/all_to_all | solution.py:306
  15.5 26.8 %copy-start.1 = (bf16[4,128,1280]{2,1,0:T(8,128)(2,1)}, bf16[4,128,1280]{2,1,0:T(8,128)(2,1)S(1)}, u32[]{:S(2)}) copy-start(bf16[4,128,1280]{2,1,0:T(8,128)(2,1)S(1)} %collective-permute-done.other) | copy-start | bytes 3932164
  15.6 20.5 %collective-permute-start.1 = (bf16[128,1280]{1,0:T(8,128)(2,1)S(1)}, bf16[128,1280]{1,0:T(8,128)(2,1)}, u32[]{:S(2)}, u32[]{:S(2)}) collective-permute-start(bf16[128,1280]{1,0:T(8,128)(2,1)S(1)} %fusion.refs_0_), channel_id=1, source_target_pairs={{0,1},{1,2},{2,3},{3,4},{4,5},{5,6},{6,7},{7,0},{8,15},{9,8},{10,9... | collective-permute-start | bytes 983048 | tf_op jit(solution)/shard_map/ppermute | solution.py:325
  20.2 0.7 copy-start.2
  36.1 12.8 %collective-permute-start.2 = (bf16[128,1280]{1,0:T(8,128)(2,1)}, bf16[128,1280]{1,0:T(8,128)(2,1)}, u32[]{:S(2)}, u32[]{:S(2)}) collective-permute-start(bf16[128,1280]{1,0:T(8,128)(2,1)} %collective-permute-done.1.refs_1_), channel_id=1, source_target_pairs={{0,1},{1,2},{2,3},{3,4},{4,5},{5,6},{6,7},{7,0},{8,15},{9,8},{10,9... | collective-permute-start | bytes 983048 | tf_op jit(solution)/shard_map/ppermute | solution.py:325
  42.3 34.0 %all-to-all-start.1 = ((bf16[8,256,128]{2,1,0:T(8,128)(2,1)}), bf16[8,256,128]{2,1,0:T(8,128)(2,1)S(1)}, u32[]{:S(2)}, u32[]{:S(2)}) async-start(bf16[8,256,128]{2,1,0:T(8,128)(2,1)} %get-tuple-element.34), calls=%async_computation.1 | async-start | bytes 1048576 | tf_op jit(solution)/shard_map/all_to_all | solution.py:306
  48.9 17.7 %collective-permute-start.3 = (bf16[128,1280]{1,0:T(8,128)(2,1)}, bf16[128,1280]{1,0:T(8,128)(2,1)S(1)}, u32[]{:S(2)}, u32[]{:S(2)}) collective-permute-start(bf16[128,1280]{1,0:T(8,128)(2,1)} %collective-permute-done.2.refs_2_), channel_id=1, source_target_pairs={{0,1},{1,2},{2,3},{3,4},{4,5},{5,6},{6,7},{7,0},{8,15},{9,8},{10,9... | collective-permute-start | bytes 983048 | tf_op jit(solution)/shard_map/ppermute | solution.py:325
  53.5 22.8 %collective-permute-start.5 = (bf16[128,1280]{1,0:T(8,128)(2,1)}, bf16[128,1280]{1,0:T(8,128)(2,1)S(1)}, u32[]{:S(2)}, u32[]{:S(2)}) collective-permute-start(bf16[128,1280]{1,0:T(8,128)(2,1)} %collective-permute-done.1.refs_1_), channel_id=1, source_target_pairs={{0,8},{8,0},{1,9},{9,1},{2,10},{10,2},{3,11},{11,3},{4,12},{12,4},... | collective-permute-start | bytes 983048 | tf_op jit(solution)/shard_map/ppermute | solution.py:284
  55.4 20.9 %collective-permute-start.6 = (bf16[128,1280]{1,0:T(8,128)(2,1)}, bf16[128,1280]{1,0:T(8,128)(2,1)S(1)}, u32[]{:S(2)}, u32[]{:S(2)}) collective-permute-start(bf16[128,1280]{1,0:T(8,128)(2,1)} %collective-permute-done.2.refs_2_), channel_id=1, source_target_pairs={{0,8},{8,0},{1,9},{9,1},{2,10},{10,2},{3,11},{11,3},{4,12},{12,4},... | collective-permute-start | bytes 983048 | tf_op jit(solution)/shard_map/ppermute | solution.py:284
  66.6 9.8 %collective-permute-start.7 = (bf16[128,1280]{1,0:T(8,128)(2,1)S(1)}, bf16[128,1280]{1,0:T(8,128)(2,1)S(1)}, u32[]{:S(2)}, u32[]{:S(2)}) collective-permute-start(bf16[128,1280]{1,0:T(8,128)(2,1)S(1)} %collective-permute-done.3.refs_3_), channel_id=1, source_target_pairs={{0,8},{8,0},{1,9},{9,1},{2,10},{10,2},{3,11},{11,3},{4,12},{12,4},... | collective-permute-start | bytes 983048 | tf_op jit(solution)/shard_map/ppermute | solution.py:284
  70.1 8.1 %collective-permute-start.4 = (bf16[128,1280]{1,0:T(8,128)(2,1)S(1)}, bf16[128,1280]{1,0:T(8,128)(2,1)S(1)}, u32[]{:S(2)}, u32[]{:S(2)}) collective-permute-start(bf16[128,1280]{1,0:T(8,128)(2,1)S(1)} %collective-permute-done.3.refs_3_), channel_id=1, source_target_pairs={{0,1},{1,2},{2,3},{3,4},{4,5},{5,6},{6,7},{7,0},{8,15},{9,8},{10,9... | collective-permute-start | bytes 983048 | tf_op jit(solution)/shard_map/ppermute | solution.py:325
  73.2 5.0 %copy-start.3 = (bf16[128,1280]{1,0:T(8,128)(2,1)S(1)}, bf16[128,1280]{1,0:T(8,128)(2,1)}, u32[]{:S(2)}) copy-start(bf16[128,1280]{1,0:T(8,128)(2,1)} %copy-done.2) | copy-start | bytes 983044
  73.2 5.0 %copy-start.7 = (s32[2,1,4]{2,1,0:T(1,128)S(1)}, s32[2,1,4]{2,1,0:T(1,128)}, u32[]{:S(2)}) copy-start(s32[2,1,4]{2,1,0:T(1,128)} %token_lens.1) | copy-start | bytes 100
  107.6 21.2 %all-to-all-start.3 = ((bf16[8,32,1280]{2,1,0:T(8,128)(2,1)}), bf16[8,32,1280]{2,1,0:T(8,128)(2,1)S(1)}, u32[]{:S(2)}, u32[]{:S(2)}) async-start(bf16[8,32,1280]{2,1,0:T(8,128)(2,1)} %shard_map.86), calls=%async_computation.3 | async-start | bytes 1310720 | tf_op jit(solution)/shard_map/all_to_all | solution.py:306
  113.8 23.9 %collective-permute-start.9 = (bf16[384,1280]{1,0:T(8,128)(2,1)}, bf16[384,1280]{1,0:T(8,128)(2,1)S(1)}, u32[]{:S(2)}, u32[]{:S(2)}) collective-permute-start(bf16[384,1280]{1,0:T(8,128)(2,1)} %shard_map.88.dec_term), channel_id=1, source_target_pairs={{0,8},{1,9},{2,10},{3,11},{4,12},{5,13},{6,14},{7,15},{16,24},{17,... | collective-permute-start | bytes 2949128 | tf_op jit(solution)/shard_map/ppermute | solution.py:405
  132.2 7.7 %collective-permute-start.8 = (bf16[384,1280]{1,0:T(8,128)(2,1)S(1)}, bf16[384,1280]{1,0:T(8,128)(2,1)S(1)}, u32[]{:S(2)}, u32[]{:S(2)}) collective-permute-start(bf16[384,1280]{1,0:T(8,128)(2,1)S(1)} %shard_map.87.enc_term), channel_id=1, source_target_pairs={{8,0},{9,1},{10,2},{11,3},{12,4},{13,5},{14,6},{15,7},{24,16},{25,... | collective-permute-start | bytes 2949128 | tf_op jit(solution)/shard_map/ppermute | solution.py:406

commit v9 on v8

--- a/solution.py
+++ b/solution.py
@@ -102,8 +102,8 @@
 
 
 def dec_kernel(
-    core, place, frame_lens, token_lens, x, context, own, other, token_queries, token_grads,
-    gains, biases, *refs,
+    core, place, frame_lens, token_lens, x, context, own_key, own_value, other_key, other_value,
+    token_queries, token_grads, gains, biases, *refs,
 ):
     devices = context.shape[0]
     out_shards, refs = refs[:devices], refs[devices:]
@@ -131,7 +131,10 @@
     states[...] = scratch[pl.ds(start, shard), :].astype(jnp.bfloat16)
     normed_rows = layer_norm(all_states, gains[2:3, :], biases[2:3, :])
     normed[...] = normed_rows
-    matrix = [jnp.where(first, other[kind], own[kind]) for kind in (1, 2)]
+    matrix = [
+        jnp.where(first, other_key[0], own_key[0]),
+        jnp.where(first, other_value[0], own_value[0]),
+    ]
     queries = token_queries[...]
     grad_context = token_grads[...]
     keys = dot_nt(normed_rows, matrix[0]).astype(jnp.bfloat16)
@@ -319,12 +322,16 @@
     copies, own = lax.optimization_barrier((copies, own))
     other = swap(own)
     shard = jnp.where(first, own[3], other[3])
-    step = [(i, (i + 1) % mp) for i in range(mp)] + [(mp + i, mp + (i - 1) % mp) for i in range(mp)]
+    def passing(block, hop):
+        up = [(i, (i + hop) % mp) for i in range(mp)]
+        down = [(mp + i, mp + (i - hop) % mp) for i in range(mp)]
+        return lax.ppermute(block, ("segment", "mp"), up + down)
+
     passed, swapped = [shard], []
-    for index in range(mp // 2):
-        passed.append(lax.ppermute(passed[-1], ("segment", "mp"), step))
-        if index < mp // 2 - 1:
-            swapped.append(swap(passed[-1]))
+    for index in range(mp // 2 - 1):
+        passed.append(passing(passed[-1], 1))
+        swapped.append(swap(passed[-1]))
+    passed.append(passing(passed[-2], 2))
     out_shards = passed + swapped
     enc_full = exchange(copies).reshape(rows, features)
 
@@ -335,6 +342,9 @@
         (dec_states, out_grad, own, other, norm_gains, norm_biases),
         kept=(0, 1),
         read=(0, 1, 2, 3),
+    )
+    enc_full, token_queries, token_grads = lax.optimization_barrier(
+        (enc_full, token_queries, token_grads)
     )
     weight_block = ((3, head_cols, features), (0, 0, 0))
     normed, queries, values, context, context_copies, probs = call(
@@ -353,9 +363,9 @@
         kept=(0, 1, 2, 3, 4, 5),
         cost=pl.CostEstimate(flops=3_000_000_000, transcendentals=0, bytes_accessed=0),
     )
-    context_full, token_queries, token_grads, out_shards = lax.optimization_barrier(
-        (exchange(context_copies), token_queries, token_grads, out_shards)
-    )
+    context_full, out_shards = lax.optimization_barrier((exchange(context_copies), out_shards))
+    key_block = ((1, head_cols, features), (1, 0, 0))
+    value_block = ((1, head_cols, features), (2, 0, 0))
     partial, states, state_normed, dec_key_grad, dec_value_grad, dec_context = call(
         dec_kernel,
         [
@@ -368,12 +378,13 @@
         ],
         (core_id, place, frame_lengths, token_lengths),
         (
-            enc_full, context_full, own, other, token_queries, token_grads,
+            enc_full, context_full, own, own, other, other, token_queries, token_grads,
             norm_gains, norm_biases, *out_shards,
         ),
+        {2: key_block, 3: value_block, 4: key_block, 5: value_block},
         scratch=[pltpu.VMEM((rows, features), f32)],
         kept=(1, 2, 3, 4, 5),
-        read=(2, 3, 4, 5),
+        read=(2, 3, 4, 5, 6, 7),
     )
     pieces = exchange(partial.reshape(mp, shard_rows, features))
     whole = [((3 * head_cols, features), bf16)]

time: 200 us -> 202 us (1.010)
  waiting for transfers between devices: 41.5 us -> 36.6 us
  local copies, waits for them, and re-layouts: 0.77 us -> 4.75 us
    ppermute x4, waiting for transfers between devices: 25.8 us -> 8.88 us  [passing(): return lax.ppermute(block, ('segment', 'mp'), up + down)]
    all_to_all x3, waiting for transfers between devices: 13.7 us -> 25.6 us  [exchange(): return lax.all_to_all(blocks, axis, 0, 0, axis_index_groups=groups)]
    unnamed x16 -> x22, local copies, waits for them, and re-layouts: 0.77 us -> 4.75 us
  transfers between devices with their start and end apart: 13 -> 13, of which waited for: 5 -> 5; matrix products, arithmetic and copies ran while one was open for 0% -> 1% of each run, Pallas kernels for 6% -> 6%
where the time goes in v9:
time: 202 us; the launch traced here: 200 us
  blocking collectives  78 us (39%)
  starting transfers between devices  53.4 us (26%)
  waiting for transfers between devices  36.6 us (18%)
  Pallas kernels  25 us (12%)
  local copies, waits for them, and re-layouts  4.75 us (2%)
    all_to_all x4, blocking collectives, exchange(): return lax.all_to_all(blocks, axis, 0, 0, axis_index_groups=groups)  78 us
    all_to_all x3, waiting for transfers between devices, exchange(): return lax.all_to_all(blocks, axis, 0, 0, axis_index_groups=groups)  25.6 us
    pallas_call x11, Pallas kernels, call(): pl.pallas_call(kernel, grid=(1,), out_shape=[out(index, *what) for index,...  25 us
    ppermute x4, starting transfers between devices, swap(): return lax.ppermute(block, 'segment', [(0, 1), (1, 0)])  16.7 us
    ppermute x4, starting transfers between devices, passing(): return lax.ppermute(block, ('segment', 'mp'), up + down)  15.8 us
    all_to_all x3, starting transfers between devices, exchange(): return lax.all_to_all(blocks, axis, 0, 0, axis_index_groups=groups)  14.9 us
    ppermute x4, waiting for transfers between devices, passing(): return lax.ppermute(block, ('segment', 'mp'), up + down)  8.88 us
    unnamed x22, local copies, waits for them, and re-layouts  4.75 us
  transfers between devices with their start and end apart: 13, of which 5 were waited for; matrix products, arithmetic and copies ran while one was open for 1% of the time, Pallas kernels for 6%

profile of v9, /device:TPU:1, one launch (start us, length us, event | category | flops | bytes accessed | tf_op | source)
XLA Modules:
  0.0 199.9 jit_solution(16567778580196139790)
XLA Ops:
  0.0 1.8 shard_map.82
  1.8 0.0 copy-start.7
  1.8 0.0 copy-start.8
  1.8 8.9 %collective-permute-start = (bf16[4,128,1280]{2,1,0:T(8,128)(2,1)}, bf16[4,128,1280]{2,1,0:T(8,128)(2,1)S(1)}, u32[]{:S(2)}, u32[]{:S(2)}) collective-permute-start(bf16[4,128,1280]{2,1,0:T(8,128)(2,1)} %bitcast.11), channel_id=1, source_target_pairs={{0,8},{8,0},{1,9},{9,1},{2,10},{10,2},{3,11},{11,3},{4,12},{12,4},... | collective-permute-start | bytes 3932168 | tf_op jit(solution)/shard_map/ppermute | solution.py:287
  10.7 4.7 %all-to-all-start = ((bf16[8,32,1280]{2,1,0:T(8,128)(2,1)}), bf16[8,32,1280]{2,1,0:T(8,128)(2,1)S(1)}, u32[]{:S(2)}, u32[]{:S(2)}) async-start(bf16[8,32,1280]{2,1,0:T(8,128)(2,1)} %shard_map.82), calls=%async_computation | async-start | bytes 1310720 | tf_op jit(solution)/shard_map/all_to_all | solution.py:309
  15.4 0.0 collective-permute-done.other.other_key.other_value
  15.4 0.0 copy-start.1
  15.4 2.0 fusion.refs_0_
  17.4 0.0 copy-start
  17.4 0.0 copy-start.9
  17.4 4.7 %collective-permute-start.1 = (bf16[128,1280]{1,0:T(8,128)(2,1)}, bf16[128,1280]{1,0:T(8,128)(2,1)}, u32[]{:S(2)}, u32[]{:S(2)}) collective-permute-start(bf16[128,1280]{1,0:T(8,128)(2,1)} %fusion.refs_0_), channel_id=1, source_target_pairs={{0,1},{1,2},{2,3},{3,4},{4,5},{5,6},{6,7},{7,0},{8,15},{9,8},{10,9... | collective-permute-start | bytes 983048 | tf_op jit(solution)/shard_map/ppermute | solution.py:328
  22.1 0.0 copy-done.1
  22.1 0.0 copy-done.7
  22.1 0.0 copy-done.8
  22.1 3.0 %shard_map.83 = (bf16[64,128]{1,0:T(8,128)(2,1)}, bf16[64,128]{1,0:T(8,128)(2,1)}) custom-call(s32[1]{0:T(128)} %bitcast.core, bf16[2,64,1280]{2,1,0:T(8,128)(2,1)} %tokens.1, bf16[2,64,1280]{2,1,0:T(8,128)(2,1)} %upstream.3, bf16[4,128,1280]{2,1,0:T(8,128)(2,1)} %bitcast.13, bf16[4,128,1280]{2,1,0:T(8,128)(2,1)} %copy-done.1, f32[3,1280]{1,0:T(4,128)S(1)} %copy-done.7, ...), custom_call_target="tpu_custom_call" | custom-call | tf_op jit(solution)/shard_map/pallas_call | solution.py:269
  25.1 11.0 %all-to-all-done = bf16[8,32,1280]{2,1,0:T(8,128)(2,1)S(1)} async-done(((bf16[8,32,1280]{2,1,0:T(8,128)(2,1)}), bf16[8,32,1280]{2,1,0:T(8,128)(2,1)S(1)}, u32[]{:S(2)}, u32[]{:S(2)}) %all-to-all-start) | async-done | bytes 655392 | tf_op jit(solution)/shard_map/all_to_all | solution.py:309
  36.2 0.0 copy-start.10
  36.2 0.0 collective-permute-done.1.refs_1_
  36.2 2.6 %collective-permute-start.2 = (bf16[128,1280]{1,0:T(8,128)(2,1)}, bf16[128,1280]{1,0:T(8,128)(2,1)S(1)}, u32[]{:S(2)}, u32[]{:S(2)}) collective-permute-start(bf16[128,1280]{1,0:T(8,128)(2,1)} %collective-permute-done.1.refs_1_), channel_id=1, source_target_pairs={{0,1},{1,2},{2,3},{3,4},{4,5},{5,6},{6,7},{7,0},{8,15},{9,8},{10,9... | collective-permute-start | bytes 983048 | tf_op jit(solution)/shard_map/ppermute | solution.py:328
  38.8 0.0 copy-done
  38.8 0.0 copy-done.9
  38.8 0.0 copy-start.2
  38.8 1.3 copy-done.2
  40.1 3.3 %shard_map.84 = (bf16[256,1280]{1,0:T(8,128)(2,1)}, bf16[256,128]{1,0:T(8,128)(2,1)}, bf16[256,128]{1,0:T(8,128)(2,1)}, bf16[256,128]{1,0:T(8,128)(2,1)}, bf16[8...) custom-call(s32[1]{0:T(128)} %bitcast.core, s32[2,1,4]{2,1,0:T(1,128)S(1)} %copy-done.9, bf16[256,1280]{1,0:T(8,128)(2,1)S(1)} %bitcast.20, ...), custom_call_target="tpu_custom_call" | custom-call | flops 3000000000 | tf_op jit(solution)/shard_map/pallas_call | solution.py:269
  43.5 6.7 %all-to-all-start.1 = ((bf16[8,256,128]{2,1,0:T(8,128)(2,1)}), bf16[8,256,128]{2,1,0:T(8,128)(2,1)S(1)}, u32[]{:S(2)}, u32[]{:S(2)}) async-start(bf16[8,256,128]{2,1,0:T(8,128)(2,1)} %get-tuple-element.38), calls=%async_computation.1 | async-start | bytes 1048576 | tf_op jit(solution)/shard_map/all_to_all | solution.py:309
  50.1 0.0 collective-permute-done.2.refs_2_
  50.1 4.6 %collective-permute-start.3 = (bf16[128,1280]{1,0:T(8,128)(2,1)S(1)}, bf16[128,1280]{1,0:T(8,128)(2,1)S(1)}, u32[]{:S(2)}, u32[]{:S(2)}) collective-permute-start(bf16[128,1280]{1,0:T(8,128)(2,1)S(1)} %collective-permute-done.2.refs_2_), channel_id=1, source_target_pairs={{0,1},{1,2},{2,3},{3,4},{4,5},{5,6},{6,7},{7,0},{8,15},{9,8},{10,9... | collective-permute-start | bytes 983048 | tf_op jit(solution)/shard_map/ppermute | solution.py:328
  54.7 1.9 collective-permute-start.5
  56.6 2.4 %collective-permute-start.6 = (bf16[128,1280]{1,0:T(8,128)(2,1)S(1)}, bf16[128,1280]{1,0:T(8,128)(2,1)S(1)}, u32[]{:S(2)}, u32[]{:S(2)}) collective-permute-start(bf16[128,1280]{1,0:T(8,128)(2,1)S(1)} %collective-permute-done.2.refs_2_), channel_id=1, source_target_pairs={{0,8},{8,0},{1,9},{9,1},{2,10},{10,2},{3,11},{11,3},{4,12},{12,4},... | collective-permute-start | bytes 983048 | tf_op jit(solution)/shard_map/ppermute | solution.py:287
  59.0 4.0 %collective-permute-start.4 = (bf16[128,1280]{1,0:T(8,128)(2,1)S(1)}, bf16[128,1280]{1,0:T(8,128)(2,1)S(1)}, u32[]{:S(2)}, u32[]{:S(2)}) collective-permute-start(bf16[128,1280]{1,0:T(8,128)(2,1)S(1)} %collective-permute-done.2.refs_2_), channel_id=1, source_target_pairs={{0,2},{1,3},{2,4},{3,5},{4,6},{5,7},{6,0},{7,1},{8,14},{9,15},{10,... | collective-permute-start | bytes 983048 | tf_op jit(solution)/shard_map/ppermute | solution.py:328
  63.0 4.7 %collective-permute-done.3.refs_3_ = bf16[128,1280]{1,0:T(8,128)(2,1)S(1)} collective-permute-done((bf16[128,1280]{1,0:T(8,128)(2,1)S(1)}, bf16[128,1280]{1,0:T(8,128)(2,1)S(1)}, u32[]{:S(2)}, u32[]{:S(2)}) %collective-permute-start.3) | collective-permute-done | bytes 327712 | tf_op jit(solution)/shard_map/ppermute | solution.py:328
  67.8 3.5 %collective-permute-start.7 = (bf16[128,1280]{1,0:T(8,128)(2,1)S(1)}, bf16[128,1280]{1,0:T(8,128)(2,1)S(1)}, u32[]{:S(2)}, u32[]{:S(2)}) collective-permute-start(bf16[128,1280]{1,0:T(8,128)(2,1)S(1)} %collective-permute-done.3.refs_3_), channel_id=1, source_target_pairs={{0,8},{8,0},{1,9},{9,1},{2,10},{10,2},{3,11},{11,3},{4,12},{12,4},... | collective-permute-start | bytes 983048 | tf_op jit(solution)/shard_map/ppermute | solution.py:287
  71.3 0.0 collective-permute-done.5.refs_5_
  71.3 0.0 all-to-all-done.1.context
  71.3 0.0 collective-permute-done.6.refs_6_
  71.3 4.1 %collective-permute-done.4.refs_4_ = bf16[128,1280]{1,0:T(8,128)(2,1)S(1)} collective-permute-done((bf16[128,1280]{1,0:T(8,128)(2,1)S(1)}, bf16[128,1280]{1,0:T(8,128)(2,1)S(1)}, u32[]{:S(2)}, u32[]{:S(2)}) %collective-permute-start.4) | collective-permute-done | bytes 327712 | tf_op jit(solution)/shard_map/ppermute | solution.py:328
  75.4 0.0 copy-start.3
  75.5 0.7 copy-done.3
  76.2 0.0 collective-permute-done.7.refs_7_
  76.2 0.0 copy-start.5
  76.2 0.7 copy-done.5
  76.9 0.0 copy-done.10
  76.9 0.0 copy-start.4
  76.9 1.0 copy-done.4
  77.9 0.0 copy-start.6
  77.9 1.0 copy-done.6
  78.9 5.4 %shard_map.85 = (bf16[256,1280]{1,0:T(8,128)(2,1)S(1)}, bf16[32,1280]{1,0:T(8,128)(2,1)}, bf16[256,1280]{1,0:T(8,128)(2,1)}, bf16[256,128]{1,0:T(8,128)(2,1)}, b...) custom-call(s32[1]{0:T(128)} %bitcast.core, s32[1]{0:T(128)} %bitcast.1.place, s32[2,1,4]{2,1,0:T(1,128)S(1)} %copy-done.9, ...), custom_call_target="tpu_custom_call" | custom-call | tf_op jit(solution)/shard_map/pallas_call | solution.py:269
  84.3 23.4 %all_to_all.35.pieces = bf16[8,32,1280]{2,1,0:T(8,128)(2,1)S(1)} all-to-all(bf16[8,32,1280]{2,1,0:T(8,128)(2,1)S(1)} %bitcast.23), channel_id=1, replica_groups=mesh['dp'=32,'segment'=2,'mp'=8] {'mp'}, dimensions={0} | all-to-all | bytes 1310720 | tf_op jit(solution)/shard_map/all_to_all | solution.py:309
  107.6 2.1 %shard_map.86 = bf16[8,32,1280]{2,1,0:T(8,128)(2,1)} custom-call(bf16[8,32,1280]{2,1,0:T(8,128)(2,1)S(1)} %all_to_all.35.pieces, bf16[32,1280]{1,0:T(8,128)(2,1)} %get-tuple-element.51.states, f32[3,1280]{1,0:T(4,128)S(1)} %copy-done.7), custom_call_target="tpu_custom_call" | custom-call | tf_op jit(solution)/shard_map/pallas_call | solution.py:269
  109.7 3.5 %all-to-all-start.3 = ((bf16[8,32,1280]{2,1,0:T(8,128)(2,1)}), bf16[8,32,1280]{2,1,0:T(8,128)(2,1)S(1)}, u32[]{:S(2)}, u32[]{:S(2)}) async-start(bf16[8,32,1280]{2,1,0:T(8,128)(2,1)} %shard_map.86), calls=%async_computation.3 | async-start | bytes 1310720 | tf_op jit(solution)/shard_map/all_to_all | solution.py:309
  113.2 2.7 %shard_map.88.dec_term = bf16[384,1280]{1,0:T(8,128)(2,1)} custom-call(s32[1]{0:T(128)} %bitcast.core, bf16[256,128]{1,0:T(8,128)(2,1)} %get-tuple-element.57.key_grad, bf16[256,128]{1,0:T(8,128)(2,1)} %get-tuple-element.58.value_grad, bf16[64,128]{1,0:T(8,128)(2,1)} %get-tuple-element.59.context, bf16[256,1280]{1,0:T(8,128)(2,1)} %get-tuple-element.60.normed, ...), custom_call_target="tpu_custom_call" | custom-call | tf_op jit(solution)/shard_map/pallas_call | solution.py:269
  115.9 1.3 collective-permute-start.9
  117.2 14.5 %all-to-all-done.3 = bf16[8,32,1280]{2,1,0:T(8,128)(2,1)S(1)} async-done(((bf16[8,32,1280]{2,1,0:T(8,128)(2,1)}), bf16[8,32,1280]{2,1,0:T(8,128)(2,1)S(1)}, u32[]{:S(2)}, u32[]{:S(2)}) %all-to-all-start.3) | async-done | bytes 655392 | tf_op jit(solution)/shard_map/all_to_all | solution.py:309
  131.7 3.4 %shard_map.87.enc_term = bf16[384,1280]{1,0:T(8,128)(2,1)S(1)} custom-call(s32[1]{0:T(128)} %bitcast.core, bf16[256,1280]{1,0:T(8,128)(2,1)S(1)} %bitcast.22, bf16[4,128,1280]{2,1,0:T(8,128)(2,1)} %bitcast.16, bf16[4,128,1280]{2,1,0:T(8,128)(2,1)} %copy-done.1, bf16[256,128]{1,0:T(8,128)(2,1)} %get-tuple-element.52.queries, ...), custom_call_target="tpu_custom_call" | custom-call | tf_op jit(solution)/shard_map/pallas_call | solution.py:269
  135.1 4.7 %collective-permute-start.8 = (bf16[384,1280]{1,0:T(8,128)(2,1)S(1)}, bf16[384,1280]{1,0:T(8,128)(2,1)S(1)}, u32[]{:S(2)}, u32[]{:S(2)}) collective-permute-start(bf16[384,1280]{1,0:T(8,128)(2,1)S(1)} %shard_map.87.enc_term), channel_id=1, source_target_pairs={{8,0},{9,1},{10,2},{11,3},{12,4},{13,5},{14,6},{15,7},{24,16},{25,... | collective-permute-start | bytes 2949128 | tf_op jit(solution)/shard_map/ppermute | solution.py:417
  139.8 0.0 collective-permute-done.9.dec_sent
  139.8 2.1 %collective-permute-done.8.enc_sent = bf16[384,1280]{1,0:T(8,128)(2,1)S(1)} collective-permute-done((bf16[384,1280]{1,0:T(8,128)(2,1)S(1)}, bf16[384,1280]{1,0:T(8,128)(2,1)S(1)}, u32[]{:S(2)}, u32[]{:S(2)}) %collective-permute-start.8) | collective-permute-done | bytes 983072 | tf_op jit(solution)/shard_map/ppermute | solution.py:417
  141.9 1.7 shard_map.89
  143.7 19.3 %all_to_all.36.pieces = bf16[8,60,8,128]{3,2,1,0:T(8,128)(2,1)S(1)} all-to-all(bf16[8,60,8,128]{3,2,1,0:T(8,128)(2,1)S(1)} %bitcast.18), channel_id=1, replica_groups={{0,16,128,144,256,272,384,400},{32,48,160,176,288,304,416,432},{64,80,1..., dimensions={0} | all-to-all | bytes 1966080 | tf_op jit(solution)/shard_map/all_to_all | solution.py:309
  163.0 0.1 shard_map.90
  163.1 18.3 %all_to_all.37.pieces = bf16[4,60,8,128]{3,2,1,0:T(8,128)(2,1)S(1)} all-to-all(bf16[4,60,8,128]{3,2,1,0:T(8,128)(2,1)S(1)} %shard_map.90), channel_id=1, replica_groups={{0,32,64,96},{16,48,80,112},{128,160,192,224},{144,176,208,240},{256,28..., dimensions={0} | all-to-all | bytes 983040 | tf_op jit(solution)/shard_map/all_to_all | solution.py:309
  181.4 0.1 shard_map.91
  181.4 17.1 %all_to_all.38 = bf16[8,60,8,128]{3,2,1,0:T(8,128)(2,1)S(1)} all-to-all(bf16[8,60,8,128]{3,2,1,0:T(8,128)(2,1)S(1)} %shard_map.91), channel_id=1, replica_groups={{0,16,128,144,256,272,384,400},{32,48,160,176,288,304,416,432},{64,80,1..., dimensions={0} | all-to-all | bytes 1966080 | tf_op jit(solution)/shard_map/all_to_all | solution.py:309
  198.5 1.4 shard_map.92
Async XLA Ops:
  1.8 20.3 %copy-start.7 = (f32[3,1280]{1,0:T(4,128)S(1)}, f32[3,1280]{1,0:T(4,128)}, u32[]{:S(2)}) copy-start(f32[3,1280]{1,0:T(4,128)} %gains.7) | copy-start | bytes 46084
  1.8 20.3 %copy-start.8 = (f32[3,1280]{1,0:T(4,128)S(1)}, f32[3,1280]{1,0:T(4,128)}, u32[]{:S(2)}) copy-start(f32[3,1280]{1,0:T(4,128)} %biases.5) | copy-start | bytes 46084
  1.8 13.6 %collective-permute-start = (bf16[4,128,1280]{2,1,0:T(8,128)(2,1)}, bf16[4,128,1280]{2,1,0:T(8,128)(2,1)S(1)}, u32[]{:S(2)}, u32[]{:S(2)}) collective-permute-start(bf16[4,128,1280]{2,1,0:T(8,128)(2,1)} %bitcast.11), channel_id=1, source_target_pairs={{0,8},{8,0},{1,9},{9,1},{2,10},{10,2},{3,11},{11,3},{4,12},{12,4},... | collective-permute-start | bytes 3932168 | tf_op jit(solution)/shard_map/ppermute | solution.py:287
  10.7 25.5 %all-to-all-start = ((bf16[8,32,1280]{2,1,0:T(8,128)(2,1)}), bf16[8,32,1280]{2,1,0:T(8,128)(2,1)S(1)}, u32[]{:S(2)}, u32[]{:S(2)}) async-start(bf16[8,32,1280]{2,1,0:T(8,128)(2,1)} %shard_map.82), calls=%async_computation | async-start | bytes 1310720 | tf_op jit(solution)/shard_map/all_to_all | solution.py:309
  15.4 6.7 %copy-start.1 = (bf16[4,128,1280]{2,1,0:T(8,128)(2,1)}, bf16[4,128,1280]{2,1,0:T(8,128)(2,1)S(1)}, u32[]{:S(2)}) copy-start(bf16[4,128,1280]{2,1,0:T(8,128)(2,1)S(1)} %collective-permute-done.other.other_key.other_value) | copy-start | bytes 3932164
  17.4 21.4 %copy-start = (bf16[1,4,128,1280]{3,2,1,0:T(8,128)(2,1)S(1)}, bf16[1,4,128,1280]{3,2,1,0:T(8,128)(2,1)}, u32[]{:S(2)}) copy-start(bf16[1,4,128,1280]{3,2,1,0:T(8,128)(2,1)} %param.13) | copy-start | bytes 3932164
  17.4 21.4 %copy-start.9 = (s32[2,1,4]{2,1,0:T(1,128)S(1)}, s32[2,1,4]{2,1,0:T(1,128)}, u32[]{:S(2)}) copy-start(s32[2,1,4]{2,1,0:T(1,128)} %frame_lens.1) | copy-start | bytes 100
  17.4 18.8 %collective-permute-start.1 = (bf16[128,1280]{1,0:T(8,128)(2,1)}, bf16[128,1280]{1,0:T(8,128)(2,1)}, u32[]{:S(2)}, u32[]{:S(2)}) collective-permute-start(bf16[128,1280]{1,0:T(8,128)(2,1)} %fusion.refs_0_), channel_id=1, source_target_pairs={{0,1},{1,2},{2,3},{3,4},{4,5},{5,6},{6,7},{7,0},{8,15},{9,8},{10,9... | collective-permute-start | bytes 983048 | tf_op jit(solution)/shard_map/ppermute | solution.py:328
  36.2 40.7 %copy-start.10 = (s32[2,1,4]{2,1,0:T(1,128)S(1)}, s32[2,1,4]{2,1,0:T(1,128)}, u32[]{:S(2)}) copy-start(s32[2,1,4]{2,1,0:T(1,128)} %token_lens.1) | copy-start | bytes 100
  36.2 13.9 %collective-permute-start.2 = (bf16[128,1280]{1,0:T(8,128)(2,1)}, bf16[128,1280]{1,0:T(8,128)(2,1)S(1)}, u32[]{:S(2)}, u32[]{:S(2)}) collective-permute-start(bf16[128,1280]{1,0:T(8,128)(2,1)} %collective-permute-done.1.refs_1_), channel_id=1, source_target_pairs={{0,1},{1,2},{2,3},{3,4},{4,5},{5,6},{6,7},{7,0},{8,15},{9,8},{10,9... | collective-permute-start | bytes 983048 | tf_op jit(solution)/shard_map/ppermute | solution.py:328
  38.8 1.3 copy-start.2
  43.5 27.8 %all-to-all-start.1 = ((bf16[8,256,128]{2,1,0:T(8,128)(2,1)}), bf16[8,256,128]{2,1,0:T(8,128)(2,1)S(1)}, u32[]{:S(2)}, u32[]{:S(2)}) async-start(bf16[8,256,128]{2,1,0:T(8,128)(2,1)} %get-tuple-element.38), calls=%async_computation.1 | async-start | bytes 1048576 | tf_op jit(solution)/shard_map/all_to_all | solution.py:309
  50.1 17.7 %collective-permute-start.3 = (bf16[128,1280]{1,0:T(8,128)(2,1)S(1)}, bf16[128,1280]{1,0:T(8,128)(2,1)S(1)}, u32[]{:S(2)}, u32[]{:S(2)}) collective-permute-start(bf16[128,1280]{1,0:T(8,128)(2,1)S(1)} %collective-permute-done.2.refs_2_), channel_id=1, source_target_pairs={{0,1},{1,2},{2,3},{3,4},{4,5},{5,6},{6,7},{7,0},{8,15},{9,8},{10,9... | collective-permute-start | bytes 983048 | tf_op jit(solution)/shard_map/ppermute | solution.py:328
  54.7 16.6 %collective-permute-start.5 = (bf16[128,1280]{1,0:T(8,128)(2,1)}, bf16[128,1280]{1,0:T(8,128)(2,1)S(1)}, u32[]{:S(2)}, u32[]{:S(2)}) collective-permute-start(bf16[128,1280]{1,0:T(8,128)(2,1)} %collective-permute-done.1.refs_1_), channel_id=1, source_target_pairs={{0,8},{8,0},{1,9},{9,1},{2,10},{10,2},{3,11},{11,3},{4,12},{12,4},... | collective-permute-start | bytes 983048 | tf_op jit(solution)/shard_map/ppermute | solution.py:287
  56.6 14.7 %collective-permute-start.6 = (bf16[128,1280]{1,0:T(8,128)(2,1)S(1)}, bf16[128,1280]{1,0:T(8,128)(2,1)S(1)}, u32[]{:S(2)}, u32[]{:S(2)}) collective-permute-start(bf16[128,1280]{1,0:T(8,128)(2,1)S(1)} %collective-permute-done.2.refs_2_), channel_id=1, source_target_pairs={{0,8},{8,0},{1,9},{9,1},{2,10},{10,2},{3,11},{11,3},{4,12},{12,4},... | collective-permute-start | bytes 983048 | tf_op jit(solution)/shard_map/ppermute | solution.py:287
  59.0 16.4 %collective-permute-start.4 = (bf16[128,1280]{1,0:T(8,128)(2,1)S(1)}, bf16[128,1280]{1,0:T(8,128)(2,1)S(1)}, u32[]{:S(2)}, u32[]{:S(2)}) collective-permute-start(bf16[128,1280]{1,0:T(8,128)(2,1)S(1)} %collective-permute-done.2.refs_2_), channel_id=1, source_target_pairs={{0,2},{1,3},{2,4},{3,5},{4,6},{5,7},{6,0},{7,1},{8,14},{9,15},{10,... | collective-permute-start | bytes 983048 | tf_op jit(solution)/shard_map/ppermute | solution.py:328
  67.8 8.4 %collective-permute-start.7 = (bf16[128,1280]{1,0:T(8,128)(2,1)S(1)}, bf16[128,1280]{1,0:T(8,128)(2,1)S(1)}, u32[]{:S(2)}, u32[]{:S(2)}) collective-permute-start(bf16[128,1280]{1,0:T(8,128)(2,1)S(1)} %collective-permute-done.3.refs_3_), channel_id=1, source_target_pairs={{0,8},{8,0},{1,9},{9,1},{2,10},{10,2},{3,11},{11,3},{4,12},{12,4},... | collective-permute-start | bytes 983048 | tf_op jit(solution)/shard_map/ppermute | solution.py:287
  75.4 0.7 copy-start.3
  76.2 0.7 copy-start.5
  76.9 1.0 copy-start.4
  77.9 1.0 copy-start.6
  109.7 22.0 %all-to-all-start.3 = ((bf16[8,32,1280]{2,1,0:T(8,128)(2,1)}), bf16[8,32,1280]{2,1,0:T(8,128)(2,1)S(1)}, u32[]{:S(2)}, u32[]{:S(2)}) async-start(bf16[8,32,1280]{2,1,0:T(8,128)(2,1)} %shard_map.86), calls=%async_computation.3 | async-start | bytes 1310720 | tf_op jit(solution)/shard_map/all_to_all | solution.py:309
  115.9 24.0 %collective-permute-start.9 = (bf16[384,1280]{1,0:T(8,128)(2,1)}, bf16[384,1280]{1,0:T(8,128)(2,1)S(1)}, u32[]{:S(2)}, u32[]{:S(2)}) collective-permute-start(bf16[384,1280]{1,0:T(8,128)(2,1)} %shard_map.88.dec_term), channel_id=1, source_target_pairs={{0,8},{1,9},{2,10},{3,11},{4,12},{5,13},{6,14},{7,15},{16,24},{17,... | collective-permute-start | bytes 2949128 | tf_op jit(solution)/shard_map/ppermute | solution.py:416
  135.1 6.8 %collective-permute-start.8 = (bf16[384,1280]{1,0:T(8,128)(2,1)S(1)}, bf16[384,1280]{1,0:T(8,128)(2,1)S(1)}, u32[]{:S(2)}, u32[]{:S(2)}) collective-permute-start(bf16[384,1280]{1,0:T(8,128)(2,1)S(1)} %shard_map.87.enc_term), channel_id=1, source_target_pairs={{8,0},{9,1},{10,2},{11,3},{12,4},{13,5},{14,6},{15,7},{24,16},{25,... | collective-permute-start | bytes 2949128 | tf_op jit(solution)/shard_map/ppermute | solution.py:417

commit v10 on v9

--- a/solution.py
+++ b/solution.py
@@ -327,11 +327,11 @@
         down = [(mp + i, mp + (i - hop) % mp) for i in range(mp)]
         return lax.ppermute(block, ("segment", "mp"), up + down)
 
-    passed, swapped = [shard], []
-    for index in range(mp // 2 - 1):
+    passed = [shard]
+    for _ in range(mp // 2 - 1):
         passed.append(passing(passed[-1], 1))
-        swapped.append(swap(passed[-1]))
     passed.append(passing(passed[-2], 2))
+    swapped = [swap(block) for block in passed[1:-1]]
     out_shards = passed + swapped
     enc_full = exchange(copies).reshape(rows, features)
 
@@ -341,7 +341,7 @@
         (core_id,),
         (dec_states, out_grad, own, other, norm_gains, norm_biases),
         kept=(0, 1),
-        read=(0, 1, 2, 3),
+        read=(0, 1),
     )
     enc_full, token_queries, token_grads = lax.optimization_barrier(
         (enc_full, token_queries, token_grads)
@@ -363,7 +363,7 @@
         kept=(0, 1, 2, 3, 4, 5),
         cost=pl.CostEstimate(flops=3_000_000_000, transcendentals=0, bytes_accessed=0),
     )
-    context_full, out_shards = lax.optimization_barrier((exchange(context_copies), out_shards))
+    context_full = exchange(context_copies)
     key_block = ((1, head_cols, features), (1, 0, 0))
     value_block = ((1, head_cols, features), (2, 0, 0))
     partial, states, state_normed, dec_key_grad, dec_value_grad, dec_context = call(
@@ -384,7 +384,7 @@
         {2: key_block, 3: value_block, 4: key_block, 5: value_block},
         scratch=[pltpu.VMEM((rows, features), f32)],
         kept=(1, 2, 3, 4, 5),
-        read=(2, 3, 4, 5, 6, 7),
+        read=(2, 3, 4, 5, 6, 7, 17),
     )
     pieces = exchange(partial.reshape(mp, shard_rows, features))
     whole = [((3 * head_cols, features), bf16)]

time: 202 us -> 198 us (0.980)
  local copies, waits for them, and re-layouts: 4.75 us -> 0.75 us
    unnamed x22 -> x14, local copies, waits for them, and re-layouts: 4.75 us -> 0.75 us
  transfers between devices with their start and end apart: 13 -> 13, of which waited for: 5 -> 5; matrix products, arithmetic and copies ran while one was open for 1% -> 0% of each run, Pallas kernels for 6% -> 6%
where the time goes in v10:
time: 198 us; the launch traced here: 196 us
  blocking collectives  78 us (39%)
  starting transfers between devices  53.4 us (27%)
  waiting for transfers between devices  38.5 us (19%)
  Pallas kernels  24.4 us (12%)
    all_to_all x4, blocking collectives, exchange(): return lax.all_to_all(blocks, axis, 0, 0, axis_index_groups=groups)  78 us
    all_to_all x3, waiting for transfers between devices, exchange(): return lax.all_to_all(blocks, axis, 0, 0, axis_index_groups=groups)  27.5 us
    pallas_call x11, Pallas kernels, call(): pl.pallas_call(kernel, grid=(1,), out_shape=[out(index, *what) for index,...  24.4 us
    ppermute x4, starting transfers between devices, swap(): return lax.ppermute(block, 'segment', [(0, 1), (1, 0)])  16.7 us
    ppermute x4, starting transfers between devices, passing(): return lax.ppermute(block, ('segment', 'mp'), up + down)  15.8 us
    all_to_all x3, starting transfers between devices, exchange(): return lax.all_to_all(blocks, axis, 0, 0, axis_index_groups=groups)  14.9 us
    ppermute x4, waiting for transfers between devices, passing(): return lax.ppermute(block, ('segment', 'mp'), up + down)  8.88 us
    ppermute x1, starting transfers between devices, shards(): enc_sent = lax.ppermute(enc_term, 'segment', [(1, 0)])  4.69 us
  transfers between devices with their start and end apart: 13, of which 5 were waited for; matrix products, arithmetic and copies ran while one was open for 0% of the time, Pallas kernels for 6%

profile of v10, /device:TPU:1, one launch (start us, length us, event | category | flops | bytes accessed | tf_op | source)
XLA Modules:
  0.0 196.1 jit_solution(10328042574929888202)
XLA Ops:
  0.0 0.0 copy-start
  0.0 1.9 shard_map.82
  1.9 0.0 copy-start.2
  1.9 0.0 copy-start.3
  1.9 8.9 %collective-permute-start = (bf16[4,128,1280]{2,1,0:T(8,128)(2,1)}, bf16[4,128,1280]{2,1,0:T(8,128)(2,1)S(1)}, u32[]{:S(2)}, u32[]{:S(2)}) collective-permute-start(bf16[4,128,1280]{2,1,0:T(8,128)(2,1)} %bitcast.11), channel_id=1, source_target_pairs={{0,8},{8,0},{1,9},{9,1},{2,10},{10,2},{3,11},{11,3},{4,12},{12,4},... | collective-permute-start | bytes 3932168 | tf_op jit(solution)/shard_map/ppermute | solution.py:287
  10.8 4.7 %all-to-all-start = ((bf16[8,32,1280]{2,1,0:T(8,128)(2,1)}), bf16[8,32,1280]{2,1,0:T(8,128)(2,1)S(1)}, u32[]{:S(2)}, u32[]{:S(2)}) async-start(bf16[8,32,1280]{2,1,0:T(8,128)(2,1)} %shard_map.82), calls=%async_computation | async-start | bytes 1310720 | tf_op jit(solution)/shard_map/all_to_all | solution.py:309
  15.5 0.0 collective-permute-done.other.other_key.other_value
  15.5 0.0 copy-done
  15.5 0.0 copy-start.1
  15.5 0.9 fusion.refs_0_
  16.4 0.0 copy-start.4
  16.4 4.7 %collective-permute-start.1 = (bf16[128,1280]{1,0:T(8,128)(2,1)}, bf16[128,1280]{1,0:T(8,128)(2,1)}, u32[]{:S(2)}, u32[]{:S(2)}) collective-permute-start(bf16[128,1280]{1,0:T(8,128)(2,1)} %fusion.refs_0_), channel_id=1, source_target_pairs={{0,1},{1,2},{2,3},{3,4},{4,5},{5,6},{6,7},{7,0},{8,15},{9,8},{10,9... | collective-permute-start | bytes 983048 | tf_op jit(solution)/shard_map/ppermute | solution.py:328
  21.1 0.0 copy-done.2
  21.1 0.0 copy-done.3
  21.1 2.2 %shard_map.83 = (bf16[64,128]{1,0:T(8,128)(2,1)}, bf16[64,128]{1,0:T(8,128)(2,1)}) custom-call(s32[1]{0:T(128)} %bitcast.core, bf16[2,64,1280]{2,1,0:T(8,128)(2,1)} %tokens.1, bf16[2,64,1280]{2,1,0:T(8,128)(2,1)} %upstream.3, bf16[4,128,1280]{2,1,0:T(8,128)(2,1)S(1)} %bitcast.16, bf16[4,128,1280]{2,1,0:T(8,128)(2,1)S(1)} %collective-permute-done.other.other_key.other_value, ...), custom_call_target="tpu_custom_call" | custom-call | tf_op jit(solution)/shard_map/pallas_call | solution.py:269
  23.3 13.0 %all-to-all-done = bf16[8,32,1280]{2,1,0:T(8,128)(2,1)S(1)} async-done(((bf16[8,32,1280]{2,1,0:T(8,128)(2,1)}), bf16[8,32,1280]{2,1,0:T(8,128)(2,1)S(1)}, u32[]{:S(2)}, u32[]{:S(2)}) %all-to-all-start) | async-done | bytes 655392 | tf_op jit(solution)/shard_map/all_to_all | solution.py:309
  36.3 0.0 copy-start.5
  36.3 0.0 collective-permute-done.1.refs_1_
  36.3 2.6 %collective-permute-start.2 = (bf16[128,1280]{1,0:T(8,128)(2,1)}, bf16[128,1280]{1,0:T(8,128)(2,1)}, u32[]{:S(2)}, u32[]{:S(2)}) collective-permute-start(bf16[128,1280]{1,0:T(8,128)(2,1)} %collective-permute-done.1.refs_1_), channel_id=1, source_target_pairs={{0,1},{1,2},{2,3},{3,4},{4,5},{5,6},{6,7},{7,0},{8,15},{9,8},{10,9... | collective-permute-start | bytes 983048 | tf_op jit(solution)/shard_map/ppermute | solution.py:328
  38.9 0.0 copy-done.1
  38.9 0.0 copy-done.4
  38.9 3.3 %shard_map.84 = (bf16[256,1280]{1,0:T(8,128)(2,1)}, bf16[256,128]{1,0:T(8,128)(2,1)}, bf16[256,128]{1,0:T(8,128)(2,1)}, bf16[256,128]{1,0:T(8,128)(2,1)}, bf16[8...) custom-call(s32[1]{0:T(128)} %bitcast.core, s32[2,1,4]{2,1,0:T(1,128)S(1)} %copy-done.4, bf16[256,1280]{1,0:T(8,128)(2,1)S(1)} %bitcast.20, ...), custom_call_target="tpu_custom_call" | custom-call | flops 3000000000 | tf_op jit(solution)/shard_map/pallas_call | solution.py:269
  42.3 6.6 %all-to-all-start.1 = ((bf16[8,256,128]{2,1,0:T(8,128)(2,1)}), bf16[8,256,128]{2,1,0:T(8,128)(2,1)S(1)}, u32[]{:S(2)}, u32[]{:S(2)}) async-start(bf16[8,256,128]{2,1,0:T(8,128)(2,1)} %get-tuple-element.29), calls=%async_computation.1 | async-start | bytes 1048576 | tf_op jit(solution)/shard_map/all_to_all | solution.py:309
  48.9 0.0 collective-permute-done.2.refs_2_
  48.9 4.6 %collective-permute-start.3 = (bf16[128,1280]{1,0:T(8,128)(2,1)}, bf16[128,1280]{1,0:T(8,128)(2,1)S(1)}, u32[]{:S(2)}, u32[]{:S(2)}) collective-permute-start(bf16[128,1280]{1,0:T(8,128)(2,1)} %collective-permute-done.2.refs_2_), channel_id=1, source_target_pairs={{0,1},{1,2},{2,3},{3,4},{4,5},{5,6},{6,7},{7,0},{8,15},{9,8},{10,9... | collective-permute-start | bytes 983048 | tf_op jit(solution)/shard_map/ppermute | solution.py:328
  53.5 1.9 collective-permute-start.5
  55.4 2.4 %collective-permute-start.6 = (bf16[128,1280]{1,0:T(8,128)(2,1)}, bf16[128,1280]{1,0:T(8,128)(2,1)S(1)}, u32[]{:S(2)}, u32[]{:S(2)}) collective-permute-start(bf16[128,1280]{1,0:T(8,128)(2,1)} %collective-permute-done.2.refs_2_), channel_id=1, source_target_pairs={{0,8},{8,0},{1,9},{9,1},{2,10},{10,2},{3,11},{11,3},{4,12},{12,4},... | collective-permute-start | bytes 983048 | tf_op jit(solution)/shard_map/ppermute | solution.py:287
  57.8 4.0 %collective-permute-start.4 = (bf16[128,1280]{1,0:T(8,128)(2,1)}, bf16[128,1280]{1,0:T(8,128)(2,1)S(1)}, u32[]{:S(2)}, u32[]{:S(2)}) collective-permute-start(bf16[128,1280]{1,0:T(8,128)(2,1)} %collective-permute-done.2.refs_2_), channel_id=1, source_target_pairs={{0,2},{1,3},{2,4},{3,5},{4,6},{5,7},{6,0},{7,1},{8,14},{9,15},{10,... | collective-permute-start | bytes 983048 | tf_op jit(solution)/shard_map/ppermute | solution.py:328
  61.8 4.7 %collective-permute-done.3.refs_3_ = bf16[128,1280]{1,0:T(8,128)(2,1)S(1)} collective-permute-done((bf16[128,1280]{1,0:T(8,128)(2,1)}, bf16[128,1280]{1,0:T(8,128)(2,1)S(1)}, u32[]{:S(2)}, u32[]{:S(2)}) %collective-permute-start.3) | collective-permute-done | bytes 327712 | tf_op jit(solution)/shard_map/ppermute | solution.py:328
  66.6 3.5 %collective-permute-start.7 = (bf16[128,1280]{1,0:T(8,128)(2,1)S(1)}, bf16[128,1280]{1,0:T(8,128)(2,1)S(1)}, u32[]{:S(2)}, u32[]{:S(2)}) collective-permute-start(bf16[128,1280]{1,0:T(8,128)(2,1)S(1)} %collective-permute-done.3.refs_3_), channel_id=1, source_target_pairs={{0,8},{8,0},{1,9},{9,1},{2,10},{10,2},{3,11},{11,3},{4,12},{12,4},... | collective-permute-start | bytes 983048 | tf_op jit(solution)/shard_map/ppermute | solution.py:287
  70.1 0.0 collective-permute-done.5.refs_5_
  70.1 0.0 all-to-all-done.1.context
  70.1 0.0 collective-permute-done.6.refs_6_
  70.1 4.1 %collective-permute-done.4.refs_4_ = bf16[128,1280]{1,0:T(8,128)(2,1)S(1)} collective-permute-done((bf16[128,1280]{1,0:T(8,128)(2,1)}, bf16[128,1280]{1,0:T(8,128)(2,1)S(1)}, u32[]{:S(2)}, u32[]{:S(2)}) %collective-permute-start.4) | collective-permute-done | bytes 327712 | tf_op jit(solution)/shard_map/ppermute | solution.py:328
  74.2 0.0 collective-permute-done.7.refs_7_
  74.2 0.0 copy-start.6
  74.2 0.7 copy-done.6
  75.0 0.0 copy-done.5
  75.0 5.6 %shard_map.85 = (bf16[256,1280]{1,0:T(8,128)(2,1)S(1)}, bf16[32,1280]{1,0:T(8,128)(2,1)}, bf16[256,1280]{1,0:T(8,128)(2,1)}, bf16[256,128]{1,0:T(8,128)(2,1)}, b...) custom-call(s32[1]{0:T(128)} %bitcast.core, s32[1]{0:T(128)} %bitcast.1.place, s32[2,1,4]{2,1,0:T(1,128)S(1)} %copy-done.4, ...), custom_call_target="tpu_custom_call" | custom-call | tf_op jit(solution)/shard_map/pallas_call | solution.py:269
  80.6 23.4 %all_to_all.35.pieces = bf16[8,32,1280]{2,1,0:T(8,128)(2,1)S(1)} all-to-all(bf16[8,32,1280]{2,1,0:T(8,128)(2,1)S(1)} %bitcast.23), channel_id=1, replica_groups=mesh['dp'=32,'segment'=2,'mp'=8] {'mp'}, dimensions={0} | all-to-all | bytes 1310720 | tf_op jit(solution)/shard_map/all_to_all | solution.py:309
  103.9 2.1 %shard_map.86 = bf16[8,32,1280]{2,1,0:T(8,128)(2,1)} custom-call(bf16[8,32,1280]{2,1,0:T(8,128)(2,1)S(1)} %all_to_all.35.pieces, bf16[32,1280]{1,0:T(8,128)(2,1)} %get-tuple-element.33.states, f32[3,1280]{1,0:T(4,128)S(1)} %copy-done.2), custom_call_target="tpu_custom_call" | custom-call | tf_op jit(solution)/shard_map/pallas_call | solution.py:269
  106.0 3.5 %all-to-all-start.3 = ((bf16[8,32,1280]{2,1,0:T(8,128)(2,1)}), bf16[8,32,1280]{2,1,0:T(8,128)(2,1)S(1)}, u32[]{:S(2)}, u32[]{:S(2)}) async-start(bf16[8,32,1280]{2,1,0:T(8,128)(2,1)} %shard_map.86), calls=%async_computation.3 | async-start | bytes 1310720 | tf_op jit(solution)/shard_map/all_to_all | solution.py:309
  109.6 2.7 %shard_map.88.dec_term = bf16[384,1280]{1,0:T(8,128)(2,1)} custom-call(s32[1]{0:T(128)} %bitcast.core, bf16[256,128]{1,0:T(8,128)(2,1)} %get-tuple-element.39.key_grad, bf16[256,128]{1,0:T(8,128)(2,1)} %get-tuple-element.40.value_grad, bf16[64,128]{1,0:T(8,128)(2,1)} %get-tuple-element.41.context, bf16[256,1280]{1,0:T(8,128)(2,1)} %get-tuple-element.42.normed, ...), custom_call_target="tpu_custom_call" | custom-call | tf_op jit(solution)/shard_map/pallas_call | solution.py:269
  112.2 1.3 collective-permute-start.9
  113.5 14.5 %all-to-all-done.3 = bf16[8,32,1280]{2,1,0:T(8,128)(2,1)S(1)} async-done(((bf16[8,32,1280]{2,1,0:T(8,128)(2,1)}), bf16[8,32,1280]{2,1,0:T(8,128)(2,1)S(1)}, u32[]{:S(2)}, u32[]{:S(2)}) %all-to-all-start.3) | async-done | bytes 655392 | tf_op jit(solution)/shard_map/all_to_all | solution.py:309
  128.0 3.4 %shard_map.87.enc_term = bf16[384,1280]{1,0:T(8,128)(2,1)S(1)} custom-call(s32[1]{0:T(128)} %bitcast.core, bf16[256,1280]{1,0:T(8,128)(2,1)S(1)} %bitcast.22, bf16[4,128,1280]{2,1,0:T(8,128)(2,1)} %bitcast.14, bf16[4,128,1280]{2,1,0:T(8,128)(2,1)} %copy-done.1, bf16[256,128]{1,0:T(8,128)(2,1)} %get-tuple-element.34.queries, ...), custom_call_target="tpu_custom_call" | custom-call | tf_op jit(solution)/shard_map/pallas_call | solution.py:269
  131.5 4.7 %collective-permute-start.8 = (bf16[384,1280]{1,0:T(8,128)(2,1)S(1)}, bf16[384,1280]{1,0:T(8,128)(2,1)S(1)}, u32[]{:S(2)}, u32[]{:S(2)}) collective-permute-start(bf16[384,1280]{1,0:T(8,128)(2,1)S(1)} %shard_map.87.enc_term), channel_id=1, source_target_pairs={{8,0},{9,1},{10,2},{11,3},{12,4},{13,5},{14,6},{15,7},{24,16},{25,... | collective-permute-start | bytes 2949128 | tf_op jit(solution)/shard_map/ppermute | solution.py:417
  136.2 0.0 collective-permute-done.9.dec_sent
  136.2 2.1 %collective-permute-done.8.enc_sent = bf16[384,1280]{1,0:T(8,128)(2,1)S(1)} collective-permute-done((bf16[384,1280]{1,0:T(8,128)(2,1)S(1)}, bf16[384,1280]{1,0:T(8,128)(2,1)S(1)}, u32[]{:S(2)}, u32[]{:S(2)}) %collective-permute-start.8) | collective-permute-done | bytes 983072 | tf_op jit(solution)/shard_map/ppermute | solution.py:417
  138.3 1.6 shard_map.89
  139.9 19.3 %all_to_all.36.pieces = bf16[8,60,8,128]{3,2,1,0:T(8,128)(2,1)S(1)} all-to-all(bf16[8,60,8,128]{3,2,1,0:T(8,128)(2,1)S(1)} %bitcast.18), channel_id=1, replica_groups={{0,16,128,144,256,272,384,400},{32,48,160,176,288,304,416,432},{64,80,1..., dimensions={0} | all-to-all | bytes 1966080 | tf_op jit(solution)/shard_map/all_to_all | solution.py:309
  159.1 0.1 shard_map.90
  159.3 18.3 %all_to_all.37.pieces = bf16[4,60,8,128]{3,2,1,0:T(8,128)(2,1)S(1)} all-to-all(bf16[4,60,8,128]{3,2,1,0:T(8,128)(2,1)S(1)} %shard_map.90), channel_id=1, replica_groups={{0,32,64,96},{16,48,80,112},{128,160,192,224},{144,176,208,240},{256,28..., dimensions={0} | all-to-all | bytes 983040 | tf_op jit(solution)/shard_map/all_to_all | solution.py:309
  177.6 0.1 shard_map.91
  177.6 17.1 %all_to_all.38 = bf16[8,60,8,128]{3,2,1,0:T(8,128)(2,1)S(1)} all-to-all(bf16[8,60,8,128]{3,2,1,0:T(8,128)(2,1)S(1)} %shard_map.91), channel_id=1, replica_groups={{0,16,128,144,256,272,384,400},{32,48,160,176,288,304,416,432},{64,80,1..., dimensions={0} | all-to-all | bytes 1966080 | tf_op jit(solution)/shard_map/all_to_all | solution.py:309
  194.7 1.4 shard_map.92
Async XLA Ops:
  0.0 15.5 %copy-start = (bf16[1,4,128,1280]{3,2,1,0:T(8,128)(2,1)S(1)}, bf16[1,4,128,1280]{3,2,1,0:T(8,128)(2,1)}, u32[]{:S(2)}) copy-start(bf16[1,4,128,1280]{3,2,1,0:T(8,128)(2,1)} %param.13) | copy-start | bytes 3932164
  1.9 19.2 %copy-start.2 = (f32[3,1280]{1,0:T(4,128)S(1)}, f32[3,1280]{1,0:T(4,128)}, u32[]{:S(2)}) copy-start(f32[3,1280]{1,0:T(4,128)} %gains.7) | copy-start | bytes 46084
  1.9 19.2 %copy-start.3 = (f32[3,1280]{1,0:T(4,128)S(1)}, f32[3,1280]{1,0:T(4,128)}, u32[]{:S(2)}) copy-start(f32[3,1280]{1,0:T(4,128)} %biases.5) | copy-start | bytes 46084
  1.9 13.6 %collective-permute-start = (bf16[4,128,1280]{2,1,0:T(8,128)(2,1)}, bf16[4,128,1280]{2,1,0:T(8,128)(2,1)S(1)}, u32[]{:S(2)}, u32[]{:S(2)}) collective-permute-start(bf16[4,128,1280]{2,1,0:T(8,128)(2,1)} %bitcast.11), channel_id=1, source_target_pairs={{0,8},{8,0},{1,9},{9,1},{2,10},{10,2},{3,11},{11,3},{4,12},{12,4},... | collective-permute-start | bytes 3932168 | tf_op jit(solution)/shard_map/ppermute | solution.py:287
  10.8 25.5 %all-to-all-start = ((bf16[8,32,1280]{2,1,0:T(8,128)(2,1)}), bf16[8,32,1280]{2,1,0:T(8,128)(2,1)S(1)}, u32[]{:S(2)}, u32[]{:S(2)}) async-start(bf16[8,32,1280]{2,1,0:T(8,128)(2,1)} %shard_map.82), calls=%async_computation | async-start | bytes 1310720 | tf_op jit(solution)/shard_map/all_to_all | solution.py:309
  15.5 23.4 %copy-start.1 = (bf16[4,128,1280]{2,1,0:T(8,128)(2,1)}, bf16[4,128,1280]{2,1,0:T(8,128)(2,1)S(1)}, u32[]{:S(2)}) copy-start(bf16[4,128,1280]{2,1,0:T(8,128)(2,1)S(1)} %collective-permute-done.other.other_key.other_value) | copy-start | bytes 3932164
  16.4 22.5 %copy-start.4 = (s32[2,1,4]{2,1,0:T(1,128)S(1)}, s32[2,1,4]{2,1,0:T(1,128)}, u32[]{:S(2)}) copy-start(s32[2,1,4]{2,1,0:T(1,128)} %frame_lens.1) | copy-start | bytes 100
  16.4 19.9 %collective-permute-start.1 = (bf16[128,1280]{1,0:T(8,128)(2,1)}, bf16[128,1280]{1,0:T(8,128)(2,1)}, u32[]{:S(2)}, u32[]{:S(2)}) collective-permute-start(bf16[128,1280]{1,0:T(8,128)(2,1)} %fusion.refs_0_), channel_id=1, source_target_pairs={{0,1},{1,2},{2,3},{3,4},{4,5},{5,6},{6,7},{7,0},{8,15},{9,8},{10,9... | collective-permute-start | bytes 983048 | tf_op jit(solution)/shard_map/ppermute | solution.py:328
  36.3 38.7 %copy-start.5 = (s32[2,1,4]{2,1,0:T(1,128)S(1)}, s32[2,1,4]{2,1,0:T(1,128)}, u32[]{:S(2)}) copy-start(s32[2,1,4]{2,1,0:T(1,128)} %token_lens.1) | copy-start | bytes 100
  36.3 12.6 %collective-permute-start.2 = (bf16[128,1280]{1,0:T(8,128)(2,1)}, bf16[128,1280]{1,0:T(8,128)(2,1)}, u32[]{:S(2)}, u32[]{:S(2)}) collective-permute-start(bf16[128,1280]{1,0:T(8,128)(2,1)} %collective-permute-done.1.refs_1_), channel_id=1, source_target_pairs={{0,1},{1,2},{2,3},{3,4},{4,5},{5,6},{6,7},{7,0},{8,15},{9,8},{10,9... | collective-permute-start | bytes 983048 | tf_op jit(solution)/shard_map/ppermute | solution.py:328
  42.3 27.8 %all-to-all-start.1 = ((bf16[8,256,128]{2,1,0:T(8,128)(2,1)}), bf16[8,256,128]{2,1,0:T(8,128)(2,1)S(1)}, u32[]{:S(2)}, u32[]{:S(2)}) async-start(bf16[8,256,128]{2,1,0:T(8,128)(2,1)} %get-tuple-element.29), calls=%async_computation.1 | async-start | bytes 1048576 | tf_op jit(solution)/shard_map/all_to_all | solution.py:309
  48.9 17.7 %collective-permute-start.3 = (bf16[128,1280]{1,0:T(8,128)(2,1)}, bf16[128,1280]{1,0:T(8,128)(2,1)S(1)}, u32[]{:S(2)}, u32[]{:S(2)}) collective-permute-start(bf16[128,1280]{1,0:T(8,128)(2,1)} %collective-permute-done.2.refs_2_), channel_id=1, source_target_pairs={{0,1},{1,2},{2,3},{3,4},{4,5},{5,6},{6,7},{7,0},{8,15},{9,8},{10,9... | collective-permute-start | bytes 983048 | tf_op jit(solution)/shard_map/ppermute | solution.py:328
  53.5 16.6 %collective-permute-start.5 = (bf16[128,1280]{1,0:T(8,128)(2,1)}, bf16[128,1280]{1,0:T(8,128)(2,1)S(1)}, u32[]{:S(2)}, u32[]{:S(2)}) collective-permute-start(bf16[128,1280]{1,0:T(8,128)(2,1)} %collective-permute-done.1.refs_1_), channel_id=1, source_target_pairs={{0,8},{8,0},{1,9},{9,1},{2,10},{10,2},{3,11},{11,3},{4,12},{12,4},... | collective-permute-start | bytes 983048 | tf_op jit(solution)/shard_map/ppermute | solution.py:287
  55.4 14.7 %collective-permute-start.6 = (bf16[128,1280]{1,0:T(8,128)(2,1)}, bf16[128,1280]{1,0:T(8,128)(2,1)S(1)}, u32[]{:S(2)}, u32[]{:S(2)}) collective-permute-start(bf16[128,1280]{1,0:T(8,128)(2,1)} %collective-permute-done.2.refs_2_), channel_id=1, source_target_pairs={{0,8},{8,0},{1,9},{9,1},{2,10},{10,2},{3,11},{11,3},{4,12},{12,4},... | collective-permute-start | bytes 983048 | tf_op jit(solution)/shard_map/ppermute | solution.py:287
  57.8 16.4 %collective-permute-start.4 = (bf16[128,1280]{1,0:T(8,128)(2,1)}, bf16[128,1280]{1,0:T(8,128)(2,1)S(1)}, u32[]{:S(2)}, u32[]{:S(2)}) collective-permute-start(bf16[128,1280]{1,0:T(8,128)(2,1)} %collective-permute-done.2.refs_2_), channel_id=1, source_target_pairs={{0,2},{1,3},{2,4},{3,5},{4,6},{5,7},{6,0},{7,1},{8,14},{9,15},{10,... | collective-permute-start | bytes 983048 | tf_op jit(solution)/shard_map/ppermute | solution.py:328
  66.6 7.7 %collective-permute-start.7 = (bf16[128,1280]{1,0:T(8,128)(2,1)S(1)}, bf16[128,1280]{1,0:T(8,128)(2,1)S(1)}, u32[]{:S(2)}, u32[]{:S(2)}) collective-permute-start(bf16[128,1280]{1,0:T(8,128)(2,1)S(1)} %collective-permute-done.3.refs_3_), channel_id=1, source_target_pairs={{0,8},{8,0},{1,9},{9,1},{2,10},{10,2},{3,11},{11,3},{4,12},{12,4},... | collective-permute-start | bytes 983048 | tf_op jit(solution)/shard_map/ppermute | solution.py:287
  74.2 0.7 copy-start.6
  106.0 22.0 %all-to-all-start.3 = ((bf16[8,32,1280]{2,1,0:T(8,128)(2,1)}), bf16[8,32,1280]{2,1,0:T(8,128)(2,1)S(1)}, u32[]{:S(2)}, u32[]{:S(2)}) async-start(bf16[8,32,1280]{2,1,0:T(8,128)(2,1)} %shard_map.86), calls=%async_computation.3 | async-start | bytes 1310720 | tf_op jit(solution)/shard_map/all_to_all | solution.py:309
  112.2 23.9 %collective-permute-start.9 = (bf16[384,1280]{1,0:T(8,128)(2,1)}, bf16[384,1280]{1,0:T(8,128)(2,1)S(1)}, u32[]{:S(2)}, u32[]{:S(2)}) collective-permute-start(bf16[384,1280]{1,0:T(8,128)(2,1)} %shard_map.88.dec_term), channel_id=1, source_target_pairs={{0,8},{1,9},{2,10},{3,11},{4,12},{5,13},{6,14},{7,15},{16,24},{17,... | collective-permute-start | bytes 2949128 | tf_op jit(solution)/shard_map/ppermute | solution.py:416
  131.5 6.8 %collective-permute-start.8 = (bf16[384,1280]{1,0:T(8,128)(2,1)S(1)}, bf16[384,1280]{1,0:T(8,128)(2,1)S(1)}, u32[]{:S(2)}, u32[]{:S(2)}) collective-permute-start(bf16[384,1280]{1,0:T(8,128)(2,1)S(1)} %shard_map.87.enc_term), channel_id=1, source_target_pairs={{8,0},{9,1},{10,2},{11,3},{12,4},{13,5},{14,6},{15,7},{24,16},{25,... | collective-permute-start | bytes 2949128 | tf_op jit(solution)/shard_map/ppermute | solution.py:417

commit v11 on v10

--- a/solution.py
+++ b/solution.py
@@ -383,10 +383,9 @@
         ),
         {2: key_block, 3: value_block, 4: key_block, 5: value_block},
         scratch=[pltpu.VMEM((rows, features), f32)],
-        kept=(1, 2, 3, 4, 5),
+        kept=(0, 1, 2, 3, 4, 5),
         read=(2, 3, 4, 5, 6, 7, 17),
     )
-    pieces = exchange(partial.reshape(mp, shard_rows, features))
     whole = [((3 * head_cols, features), bf16)]
     dec_term = call(
         dec_terms_kernel,
@@ -395,6 +394,9 @@
         (dec_key_grad, dec_value_grad, dec_context, state_normed, out_grad),
         kept=(0,),
         read=(0, 1, 2, 3, 4),
+    )
+    pieces, dec_term = lax.optimization_barrier(
+        (exchange(partial.reshape(mp, shard_rows, features)), dec_term)
     )
     grads = call(
         norm_backward_kernel,

time: 198 us -> 201 us (1.015)
  blocking collectives: 78 us -> 54.7 us
  waiting for transfers between devices: 38.5 us -> 61.5 us
  starting transfers between devices: 53.4 us -> 55.7 us
    all_to_all x4 -> x3, blocking collectives: 78 us -> 54.7 us  [exchange(): return lax.all_to_all(blocks, axis, 0, 0, axis_index_groups=groups)]
    all_to_all x3 -> x4, waiting for transfers between devices: 27.5 us -> 50.5 us  [exchange(): return lax.all_to_all(blocks, axis, 0, 0, axis_index_groups=groups)]
    all_to_all x3 -> x4, starting transfers between devices: 14.9 us -> 19.4 us  [exchange(): return lax.all_to_all(blocks, axis, 0, 0, axis_index_groups=groups)]
    ppermute x1, starting transfers between devices: 4.69 us -> 2.45 us  [shards(): enc_sent = lax.ppermute(enc_term, 'segment', [(1, 0)])]
  transfers between devices with their start and end apart: 13 -> 14, of which waited for: 5 -> 6; matrix products, arithmetic and copies ran while one was open for 0% -> 0% of each run, Pallas kernels for 6% -> 6%
where the time goes in v11:
time: 201 us; the launch traced here: 199 us
  waiting for transfers between devices  61.5 us (31%)
  starting transfers between devices  55.7 us (28%)
  blocking collectives  54.7 us (27%)
  Pallas kernels  25.3 us (13%)
    all_to_all x3, blocking collectives, exchange(): return lax.all_to_all(blocks, axis, 0, 0, axis_index_groups=groups)  54.7 us
    all_to_all x4, waiting for transfers between devices, exchange(): return lax.all_to_all(blocks, axis, 0, 0, axis_index_groups=groups)  50.5 us
    pallas_call x11, Pallas kernels, call(): pl.pallas_call(kernel, grid=(1,), out_shape=[out(index, *what) for index,...  25.3 us
    all_to_all x4, starting transfers between devices, exchange(): return lax.all_to_all(blocks, axis, 0, 0, axis_index_groups=groups)  19.4 us
    ppermute x4, starting transfers between devices, swap(): return lax.ppermute(block, 'segment', [(0, 1), (1, 0)])  16.7 us
    ppermute x4, starting transfers between devices, passing(): return lax.ppermute(block, ('segment', 'mp'), up + down)  15.8 us
    ppermute x4, waiting for transfers between devices, passing(): return lax.ppermute(block, ('segment', 'mp'), up + down)  8.88 us
  transfers between devices with their start and end apart: 14, of which 6 were waited for; matrix products, arithmetic and copies ran while one was open for 0% of the time, Pallas kernels for 6%

profile of v11, /device:TPU:1, one launch (start us, length us, event | category | flops | bytes accessed | tf_op | source)
XLA Modules:
  0.0 198.9 jit_solution(18322375774978243945)
XLA Ops:
  0.0 0.0 copy-start
  0.0 1.9 shard_map.82
  1.9 0.0 copy-start.2
  1.9 0.0 copy-start.3
  1.9 8.9 %collective-permute-start = (bf16[4,128,1280]{2,1,0:T(8,128)(2,1)}, bf16[4,128,1280]{2,1,0:T(8,128)(2,1)S(1)}, u32[]{:S(2)}, u32[]{:S(2)}) collective-permute-start(bf16[4,128,1280]{2,1,0:T(8,128)(2,1)} %bitcast.11), channel_id=1, source_target_pairs={{0,8},{8,0},{1,9},{9,1},{2,10},{10,2},{3,11},{11,3},{4,12},{12,4},... | collective-permute-start | bytes 3932168 | tf_op jit(solution)/shard_map/ppermute | solution.py:287
  10.8 4.7 %all-to-all-start = ((bf16[8,32,1280]{2,1,0:T(8,128)(2,1)}), bf16[8,32,1280]{2,1,0:T(8,128)(2,1)S(1)}, u32[]{:S(2)}, u32[]{:S(2)}) async-start(bf16[8,32,1280]{2,1,0:T(8,128)(2,1)} %shard_map.82), calls=%async_computation | async-start | bytes 1310720 | tf_op jit(solution)/shard_map/all_to_all | solution.py:309
  15.5 0.0 collective-permute-done.other.other_key.other_value
  15.5 0.0 copy-done
  15.5 0.0 copy-start.1
  15.5 0.8 fusion.refs_0_
  16.4 0.0 copy-start.4
  16.4 4.7 %collective-permute-start.1 = (bf16[128,1280]{1,0:T(8,128)(2,1)}, bf16[128,1280]{1,0:T(8,128)(2,1)}, u32[]{:S(2)}, u32[]{:S(2)}) collective-permute-start(bf16[128,1280]{1,0:T(8,128)(2,1)} %fusion.refs_0_), channel_id=1, source_target_pairs={{0,1},{1,2},{2,3},{3,4},{4,5},{5,6},{6,7},{7,0},{8,15},{9,8},{10,9... | collective-permute-start | bytes 983048 | tf_op jit(solution)/shard_map/ppermute | solution.py:328
  21.1 0.0 copy-done.2
  21.1 0.0 copy-done.3
  21.1 2.2 %shard_map.83 = (bf16[64,128]{1,0:T(8,128)(2,1)}, bf16[64,128]{1,0:T(8,128)(2,1)}) custom-call(s32[1]{0:T(128)} %bitcast.core, bf16[2,64,1280]{2,1,0:T(8,128)(2,1)} %tokens.1, bf16[2,64,1280]{2,1,0:T(8,128)(2,1)} %upstream.3, bf16[4,128,1280]{2,1,0:T(8,128)(2,1)S(1)} %bitcast.16, bf16[4,128,1280]{2,1,0:T(8,128)(2,1)S(1)} %collective-permute-done.other.other_key.other_value, ...), custom_call_target="tpu_custom_call" | custom-call | tf_op jit(solution)/shard_map/pallas_call | solution.py:269
  23.3 13.0 %all-to-all-done = bf16[8,32,1280]{2,1,0:T(8,128)(2,1)S(1)} async-done(((bf16[8,32,1280]{2,1,0:T(8,128)(2,1)}), bf16[8,32,1280]{2,1,0:T(8,128)(2,1)S(1)}, u32[]{:S(2)}, u32[]{:S(2)}) %all-to-all-start) | async-done | bytes 655392 | tf_op jit(solution)/shard_map/all_to_all | solution.py:309
  36.3 0.0 copy-start.5
  36.3 0.0 collective-permute-done.1.refs_1_
  36.3 2.6 %collective-permute-start.2 = (bf16[128,1280]{1,0:T(8,128)(2,1)}, bf16[128,1280]{1,0:T(8,128)(2,1)}, u32[]{:S(2)}, u32[]{:S(2)}) collective-permute-start(bf16[128,1280]{1,0:T(8,128)(2,1)} %collective-permute-done.1.refs_1_), channel_id=1, source_target_pairs={{0,1},{1,2},{2,3},{3,4},{4,5},{5,6},{6,7},{7,0},{8,15},{9,8},{10,9... | collective-permute-start | bytes 983048 | tf_op jit(solution)/shard_map/ppermute | solution.py:328
  38.9 0.0 copy-done.1
  38.9 0.0 copy-done.4
  38.9 3.3 %shard_map.84 = (bf16[256,1280]{1,0:T(8,128)(2,1)}, bf16[256,128]{1,0:T(8,128)(2,1)}, bf16[256,128]{1,0:T(8,128)(2,1)}, bf16[256,128]{1,0:T(8,128)(2,1)}, bf16[8...) custom-call(s32[1]{0:T(128)} %bitcast.core, s32[2,1,4]{2,1,0:T(1,128)S(1)} %copy-done.4, bf16[256,1280]{1,0:T(8,128)(2,1)S(1)} %bitcast.20, ...), custom_call_target="tpu_custom_call" | custom-call | flops 3000000000 | tf_op jit(solution)/shard_map/pallas_call | solution.py:269
  42.2 6.6 %all-to-all-start.1 = ((bf16[8,256,128]{2,1,0:T(8,128)(2,1)}), bf16[8,256,128]{2,1,0:T(8,128)(2,1)S(1)}, u32[]{:S(2)}, u32[]{:S(2)}) async-start(bf16[8,256,128]{2,1,0:T(8,128)(2,1)} %get-tuple-element.31), calls=%async_computation.1 | async-start | bytes 1048576 | tf_op jit(solution)/shard_map/all_to_all | solution.py:309
  48.9 0.0 collective-permute-done.2.refs_2_
  48.9 4.6 %collective-permute-start.3 = (bf16[128,1280]{1,0:T(8,128)(2,1)}, bf16[128,1280]{1,0:T(8,128)(2,1)S(1)}, u32[]{:S(2)}, u32[]{:S(2)}) collective-permute-start(bf16[128,1280]{1,0:T(8,128)(2,1)} %collective-permute-done.2.refs_2_), channel_id=1, source_target_pairs={{0,1},{1,2},{2,3},{3,4},{4,5},{5,6},{6,7},{7,0},{8,15},{9,8},{10,9... | collective-permute-start | bytes 983048 | tf_op jit(solution)/shard_map/ppermute | solution.py:328
  53.5 1.9 collective-permute-start.5
  55.4 2.4 %collective-permute-start.6 = (bf16[128,1280]{1,0:T(8,128)(2,1)}, bf16[128,1280]{1,0:T(8,128)(2,1)S(1)}, u32[]{:S(2)}, u32[]{:S(2)}) collective-permute-start(bf16[128,1280]{1,0:T(8,128)(2,1)} %collective-permute-done.2.refs_2_), channel_id=1, source_target_pairs={{0,8},{8,0},{1,9},{9,1},{2,10},{10,2},{3,11},{11,3},{4,12},{12,4},... | collective-permute-start | bytes 983048 | tf_op jit(solution)/shard_map/ppermute | solution.py:287
  57.8 4.0 %collective-permute-start.4 = (bf16[128,1280]{1,0:T(8,128)(2,1)}, bf16[128,1280]{1,0:T(8,128)(2,1)S(1)}, u32[]{:S(2)}, u32[]{:S(2)}) collective-permute-start(bf16[128,1280]{1,0:T(8,128)(2,1)} %collective-permute-done.2.refs_2_), channel_id=1, source_target_pairs={{0,2},{1,3},{2,4},{3,5},{4,6},{5,7},{6,0},{7,1},{8,14},{9,15},{10,... | collective-permute-start | bytes 983048 | tf_op jit(solution)/shard_map/ppermute | solution.py:328
  61.8 4.7 %collective-permute-done.3.refs_3_ = bf16[128,1280]{1,0:T(8,128)(2,1)S(1)} collective-permute-done((bf16[128,1280]{1,0:T(8,128)(2,1)}, bf16[128,1280]{1,0:T(8,128)(2,1)S(1)}, u32[]{:S(2)}, u32[]{:S(2)}) %collective-permute-start.3) | collective-permute-done | bytes 327712 | tf_op jit(solution)/shard_map/ppermute | solution.py:328
  66.5 3.5 %collective-permute-start.7 = (bf16[128,1280]{1,0:T(8,128)(2,1)S(1)}, bf16[128,1280]{1,0:T(8,128)(2,1)S(1)}, u32[]{:S(2)}, u32[]{:S(2)}) collective-permute-start(bf16[128,1280]{1,0:T(8,128)(2,1)S(1)} %collective-permute-done.3.refs_3_), channel_id=1, source_target_pairs={{0,8},{8,0},{1,9},{9,1},{2,10},{10,2},{3,11},{11,3},{4,12},{12,4},... | collective-permute-start | bytes 983048 | tf_op jit(solution)/shard_map/ppermute | solution.py:287
  70.1 0.0 collective-permute-done.5.refs_5_
  70.1 0.0 all-to-all-done.1.context
  70.1 0.0 collective-permute-done.6.refs_6_
  70.1 4.1 %collective-permute-done.4.refs_4_ = bf16[128,1280]{1,0:T(8,128)(2,1)S(1)} collective-permute-done((bf16[128,1280]{1,0:T(8,128)(2,1)}, bf16[128,1280]{1,0:T(8,128)(2,1)S(1)}, u32[]{:S(2)}, u32[]{:S(2)}) %collective-permute-start.4) | collective-permute-done | bytes 327712 | tf_op jit(solution)/shard_map/ppermute | solution.py:328
  74.2 0.0 collective-permute-done.7.refs_7_
  74.2 0.0 copy-start.7
  74.2 0.7 copy-done.7
  75.0 0.0 copy-done.5
  75.0 6.3 %shard_map.85 = (bf16[256,1280]{1,0:T(8,128)(2,1)}, bf16[32,1280]{1,0:T(8,128)(2,1)}, bf16[256,1280]{1,0:T(8,128)(2,1)}, bf16[256,128]{1,0:T(8,128)(2,1)}, bf16[...) custom-call(s32[1]{0:T(128)} %bitcast.core, s32[1]{0:T(128)} %bitcast.1.place, s32[2,1,4]{2,1,0:T(1,128)S(1)} %copy-done.4, ...), custom_call_target="tpu_custom_call" | custom-call | tf_op jit(solution)/shard_map/pallas_call | solution.py:269
  81.3 4.5 %all-to-all-start.2 = ((bf16[8,32,1280]{2,1,0:T(8,128)(2,1)}), bf16[8,32,1280]{2,1,0:T(8,128)(2,1)S(1)}, u32[]{:S(2)}, u32[]{:S(2)}) async-start(bf16[8,32,1280]{2,1,0:T(8,128)(2,1)} %bitcast.23), calls=%async_computation.2 | async-start | bytes 1310720 | tf_op jit(solution)/shard_map/all_to_all | solution.py:309
  85.8 2.7 %shard_map.86.dec_term = bf16[384,1280]{1,0:T(8,128)(2,1)} custom-call(s32[1]{0:T(128)} %bitcast.core, bf16[256,128]{1,0:T(8,128)(2,1)} %get-tuple-element.35.key_grad, bf16[256,128]{1,0:T(8,128)(2,1)} %get-tuple-element.36.value_grad, bf16[64,128]{1,0:T(8,128)(2,1)} %get-tuple-element.37.context, bf16[256,1280]{1,0:T(8,128)(2,1)} %get-tuple-element.38.normed, ...), custom_call_target="tpu_custom_call" | custom-call | tf_op jit(solution)/shard_map/pallas_call | solution.py:269
  88.5 18.1 %all-to-all-done.2.pieces = bf16[8,32,1280]{2,1,0:T(8,128)(2,1)S(1)} async-done(((bf16[8,32,1280]{2,1,0:T(8,128)(2,1)}), bf16[8,32,1280]{2,1,0:T(8,128)(2,1)S(1)}, u32[]{:S(2)}, u32[]{:S(2)}) %all-to-all-start.2) | async-done | bytes 655392 | tf_op jit(solution)/shard_map/all_to_all | solution.py:309
  106.6 0.0 copy-start.6
  106.6 2.1 %shard_map.87 = bf16[8,32,1280]{2,1,0:T(8,128)(2,1)} custom-call(bf16[8,32,1280]{2,1,0:T(8,128)(2,1)S(1)} %all-to-all-done.2.pieces, bf16[32,1280]{1,0:T(8,128)(2,1)} %get-tuple-element.40.states, f32[3,1280]{1,0:T(4,128)S(1)} %copy-done.2), custom_call_target="tpu_custom_call" | custom-call | tf_op jit(solution)/shard_map/pallas_call | solution.py:269
  108.7 3.5 %all-to-all-start.3 = ((bf16[8,32,1280]{2,1,0:T(8,128)(2,1)}), bf16[8,32,1280]{2,1,0:T(8,128)(2,1)S(1)}, u32[]{:S(2)}, u32[]{:S(2)}) async-start(bf16[8,32,1280]{2,1,0:T(8,128)(2,1)} %shard_map.87), calls=%async_computation.3 | async-start | bytes 1310720 | tf_op jit(solution)/shard_map/all_to_all | solution.py:309
  112.3 0.0 copy-done.6
  112.3 1.3 collective-permute-start.9
  113.6 19.4 %all-to-all-done.3 = bf16[8,32,1280]{2,1,0:T(8,128)(2,1)S(1)} async-done(((bf16[8,32,1280]{2,1,0:T(8,128)(2,1)}), bf16[8,32,1280]{2,1,0:T(8,128)(2,1)S(1)}, u32[]{:S(2)}, u32[]{:S(2)}) %all-to-all-start.3) | async-done | bytes 655392 | tf_op jit(solution)/shard_map/all_to_all | solution.py:309
  132.9 3.4 %shard_map.88.enc_term = bf16[384,1280]{1,0:T(8,128)(2,1)S(1)} custom-call(s32[1]{0:T(128)} %bitcast.core, bf16[256,1280]{1,0:T(8,128)(2,1)S(1)} %bitcast.22, bf16[4,128,1280]{2,1,0:T(8,128)(2,1)} %bitcast.14, bf16[4,128,1280]{2,1,0:T(8,128)(2,1)} %copy-done.1, bf16[256,128]{1,0:T(8,128)(2,1)} %get-tuple-element.41.queries, ...), custom_call_target="tpu_custom_call" | custom-call | tf_op jit(solution)/shard_map/pallas_call | solution.py:269
  136.4 2.5 %collective-permute-start.8 = (bf16[384,1280]{1,0:T(8,128)(2,1)S(1)}, bf16[384,1280]{1,0:T(8,128)(2,1)S(1)}, u32[]{:S(2)}, u32[]{:S(2)}) collective-permute-start(bf16[384,1280]{1,0:T(8,128)(2,1)S(1)} %shard_map.88.enc_term), channel_id=1, source_target_pairs={{8,0},{9,1},{10,2},{11,3},{12,4},{13,5},{14,6},{15,7},{24,16},{25,... | collective-permute-start | bytes 2949128 | tf_op jit(solution)/shard_map/ppermute | solution.py:419
  138.8 0.0 collective-permute-done.9.dec_sent
  138.9 2.1 %collective-permute-done.8.enc_sent = bf16[384,1280]{1,0:T(8,128)(2,1)S(1)} collective-permute-done((bf16[384,1280]{1,0:T(8,128)(2,1)S(1)}, bf16[384,1280]{1,0:T(8,128)(2,1)S(1)}, u32[]{:S(2)}, u32[]{:S(2)}) %collective-permute-start.8) | collective-permute-done | bytes 983072 | tf_op jit(solution)/shard_map/ppermute | solution.py:419
  141.0 1.7 shard_map.89
  142.7 19.3 %all_to_all.35.pieces = bf16[8,60,8,128]{3,2,1,0:T(8,128)(2,1)S(1)} all-to-all(bf16[8,60,8,128]{3,2,1,0:T(8,128)(2,1)S(1)} %bitcast.18), channel_id=1, replica_groups={{0,16,128,144,256,272,384,400},{32,48,160,176,288,304,416,432},{64,80,1..., dimensions={0} | all-to-all | bytes 1966080 | tf_op jit(solution)/shard_map/all_to_all | solution.py:309
  162.0 0.1 shard_map.90
  162.1 18.3 %all_to_all.36.pieces = bf16[4,60,8,128]{3,2,1,0:T(8,128)(2,1)S(1)} all-to-all(bf16[4,60,8,128]{3,2,1,0:T(8,128)(2,1)S(1)} %shard_map.90), channel_id=1, replica_groups={{0,32,64,96},{16,48,80,112},{128,160,192,224},{144,176,208,240},{256,28..., dimensions={0} | all-to-all | bytes 983040 | tf_op jit(solution)/shard_map/all_to_all | solution.py:309
  180.4 0.1 shard_map.91
  180.5 17.1 %all_to_all.37 = bf16[8,60,8,128]{3,2,1,0:T(8,128)(2,1)S(1)} all-to-all(bf16[8,60,8,128]{3,2,1,0:T(8,128)(2,1)S(1)} %shard_map.91), channel_id=1, replica_groups={{0,16,128,144,256,272,384,400},{32,48,160,176,288,304,416,432},{64,80,1..., dimensions={0} | all-to-all | bytes 1966080 | tf_op jit(solution)/shard_map/all_to_all | solution.py:309
  197.5 1.4 shard_map.92
Async XLA Ops:
  0.0 15.5 %copy-start = (bf16[1,4,128,1280]{3,2,1,0:T(8,128)(2,1)S(1)}, bf16[1,4,128,1280]{3,2,1,0:T(8,128)(2,1)}, u32[]{:S(2)}) copy-start(bf16[1,4,128,1280]{3,2,1,0:T(8,128)(2,1)} %param.13) | copy-start | bytes 3932164
  1.9 19.2 %copy-start.2 = (f32[3,1280]{1,0:T(4,128)S(1)}, f32[3,1280]{1,0:T(4,128)}, u32[]{:S(2)}) copy-start(f32[3,1280]{1,0:T(4,128)} %gains.7) | copy-start | bytes 46084
  1.9 19.2 %copy-start.3 = (f32[3,1280]{1,0:T(4,128)S(1)}, f32[3,1280]{1,0:T(4,128)}, u32[]{:S(2)}) copy-start(f32[3,1280]{1,0:T(4,128)} %biases.5) | copy-start | bytes 46084
  1.9 13.6 %collective-permute-start = (bf16[4,128,1280]{2,1,0:T(8,128)(2,1)}, bf16[4,128,1280]{2,1,0:T(8,128)(2,1)S(1)}, u32[]{:S(2)}, u32[]{:S(2)}) collective-permute-start(bf16[4,128,1280]{2,1,0:T(8,128)(2,1)} %bitcast.11), channel_id=1, source_target_pairs={{0,8},{8,0},{1,9},{9,1},{2,10},{10,2},{3,11},{11,3},{4,12},{12,4},... | collective-permute-start | bytes 3932168 | tf_op jit(solution)/shard_map/ppermute | solution.py:287
  10.8 25.5 %all-to-all-start = ((bf16[8,32,1280]{2,1,0:T(8,128)(2,1)}), bf16[8,32,1280]{2,1,0:T(8,128)(2,1)S(1)}, u32[]{:S(2)}, u32[]{:S(2)}) async-start(bf16[8,32,1280]{2,1,0:T(8,128)(2,1)} %shard_map.82), calls=%async_computation | async-start | bytes 1310720 | tf_op jit(solution)/shard_map/all_to_all | solution.py:309
  15.5 23.4 %copy-start.1 = (bf16[4,128,1280]{2,1,0:T(8,128)(2,1)}, bf16[4,128,1280]{2,1,0:T(8,128)(2,1)S(1)}, u32[]{:S(2)}) copy-start(bf16[4,128,1280]{2,1,0:T(8,128)(2,1)S(1)} %collective-permute-done.other.other_key.other_value) | copy-start | bytes 3932164
  16.4 22.5 %copy-start.4 = (s32[2,1,4]{2,1,0:T(1,128)S(1)}, s32[2,1,4]{2,1,0:T(1,128)}, u32[]{:S(2)}) copy-start(s32[2,1,4]{2,1,0:T(1,128)} %frame_lens.1) | copy-start | bytes 100
  16.4 19.9 %collective-permute-start.1 = (bf16[128,1280]{1,0:T(8,128)(2,1)}, bf16[128,1280]{1,0:T(8,128)(2,1)}, u32[]{:S(2)}, u32[]{:S(2)}) collective-permute-start(bf16[128,1280]{1,0:T(8,128)(2,1)} %fusion.refs_0_), channel_id=1, source_target_pairs={{0,1},{1,2},{2,3},{3,4},{4,5},{5,6},{6,7},{7,0},{8,15},{9,8},{10,9... | collective-permute-start | bytes 983048 | tf_op jit(solution)/shard_map/ppermute | solution.py:328
  36.3 38.7 %copy-start.5 = (s32[2,1,4]{2,1,0:T(1,128)S(1)}, s32[2,1,4]{2,1,0:T(1,128)}, u32[]{:S(2)}) copy-start(s32[2,1,4]{2,1,0:T(1,128)} %token_lens.1) | copy-start | bytes 100
  36.3 12.6 %collective-permute-start.2 = (bf16[128,1280]{1,0:T(8,128)(2,1)}, bf16[128,1280]{1,0:T(8,128)(2,1)}, u32[]{:S(2)}, u32[]{:S(2)}) collective-permute-start(bf16[128,1280]{1,0:T(8,128)(2,1)} %collective-permute-done.1.refs_1_), channel_id=1, source_target_pairs={{0,1},{1,2},{2,3},{3,4},{4,5},{5,6},{6,7},{7,0},{8,15},{9,8},{10,9... | collective-permute-start | bytes 983048 | tf_op jit(solution)/shard_map/ppermute | solution.py:328
  42.2 27.8 %all-to-all-start.1 = ((bf16[8,256,128]{2,1,0:T(8,128)(2,1)}), bf16[8,256,128]{2,1,0:T(8,128)(2,1)S(1)}, u32[]{:S(2)}, u32[]{:S(2)}) async-start(bf16[8,256,128]{2,1,0:T(8,128)(2,1)} %get-tuple-element.31), calls=%async_computation.1 | async-start | bytes 1048576 | tf_op jit(solution)/shard_map/all_to_all | solution.py:309
  48.9 17.7 %collective-permute-start.3 = (bf16[128,1280]{1,0:T(8,128)(2,1)}, bf16[128,1280]{1,0:T(8,128)(2,1)S(1)}, u32[]{:S(2)}, u32[]{:S(2)}) collective-permute-start(bf16[128,1280]{1,0:T(8,128)(2,1)} %collective-permute-done.2.refs_2_), channel_id=1, source_target_pairs={{0,1},{1,2},{2,3},{3,4},{4,5},{5,6},{6,7},{7,0},{8,15},{9,8},{10,9... | collective-permute-start | bytes 983048 | tf_op jit(solution)/shard_map/ppermute | solution.py:328
  53.5 16.6 %collective-permute-start.5 = (bf16[128,1280]{1,0:T(8,128)(2,1)}, bf16[128,1280]{1,0:T(8,128)(2,1)S(1)}, u32[]{:S(2)}, u32[]{:S(2)}) collective-permute-start(bf16[128,1280]{1,0:T(8,128)(2,1)} %collective-permute-done.1.refs_1_), channel_id=1, source_target_pairs={{0,8},{8,0},{1,9},{9,1},{2,10},{10,2},{3,11},{11,3},{4,12},{12,4},... | collective-permute-start | bytes 983048 | tf_op jit(solution)/shard_map/ppermute | solution.py:287
  55.4 14.7 %collective-permute-start.6 = (bf16[128,1280]{1,0:T(8,128)(2,1)}, bf16[128,1280]{1,0:T(8,128)(2,1)S(1)}, u32[]{:S(2)}, u32[]{:S(2)}) collective-permute-start(bf16[128,1280]{1,0:T(8,128)(2,1)} %collective-permute-done.2.refs_2_), channel_id=1, source_target_pairs={{0,8},{8,0},{1,9},{9,1},{2,10},{10,2},{3,11},{11,3},{4,12},{12,4},... | collective-permute-start | bytes 983048 | tf_op jit(solution)/shard_map/ppermute | solution.py:287
  57.8 16.4 %collective-permute-start.4 = (bf16[128,1280]{1,0:T(8,128)(2,1)}, bf16[128,1280]{1,0:T(8,128)(2,1)S(1)}, u32[]{:S(2)}, u32[]{:S(2)}) collective-permute-start(bf16[128,1280]{1,0:T(8,128)(2,1)} %collective-permute-done.2.refs_2_), channel_id=1, source_target_pairs={{0,2},{1,3},{2,4},{3,5},{4,6},{5,7},{6,0},{7,1},{8,14},{9,15},{10,... | collective-permute-start | bytes 983048 | tf_op jit(solution)/shard_map/ppermute | solution.py:328
  66.5 7.7 %collective-permute-start.7 = (bf16[128,1280]{1,0:T(8,128)(2,1)S(1)}, bf16[128,1280]{1,0:T(8,128)(2,1)S(1)}, u32[]{:S(2)}, u32[]{:S(2)}) collective-permute-start(bf16[128,1280]{1,0:T(8,128)(2,1)S(1)} %collective-permute-done.3.refs_3_), channel_id=1, source_target_pairs={{0,8},{8,0},{1,9},{9,1},{2,10},{10,2},{3,11},{11,3},{4,12},{12,4},... | collective-permute-start | bytes 983048 | tf_op jit(solution)/shard_map/ppermute | solution.py:287
  74.2 0.7 copy-start.7
  81.3 25.3 %all-to-all-start.2 = ((bf16[8,32,1280]{2,1,0:T(8,128)(2,1)}), bf16[8,32,1280]{2,1,0:T(8,128)(2,1)S(1)}, u32[]{:S(2)}, u32[]{:S(2)}) async-start(bf16[8,32,1280]{2,1,0:T(8,128)(2,1)} %bitcast.23), calls=%async_computation.2 | async-start | bytes 1310720 | tf_op jit(solution)/shard_map/all_to_all | solution.py:309
  106.6 5.7 %copy-start.6 = (bf16[384,1280]{1,0:T(8,128)(2,1)S(1)}, bf16[384,1280]{1,0:T(8,128)(2,1)}, u32[]{:S(2)}) copy-start(bf16[384,1280]{1,0:T(8,128)(2,1)} %shard_map.86.dec_term) | copy-start | bytes 2949124
  108.7 24.2 %all-to-all-start.3 = ((bf16[8,32,1280]{2,1,0:T(8,128)(2,1)}), bf16[8,32,1280]{2,1,0:T(8,128)(2,1)S(1)}, u32[]{:S(2)}, u32[]{:S(2)}) async-start(bf16[8,32,1280]{2,1,0:T(8,128)(2,1)} %shard_map.87), calls=%async_computation.3 | async-start | bytes 1310720 | tf_op jit(solution)/shard_map/all_to_all | solution.py:309
  112.3 26.6 %collective-permute-start.9 = (bf16[384,1280]{1,0:T(8,128)(2,1)S(1)}, bf16[384,1280]{1,0:T(8,128)(2,1)S(1)}, u32[]{:S(2)}, u32[]{:S(2)}) collective-permute-start(bf16[384,1280]{1,0:T(8,128)(2,1)S(1)} %copy-done.6), channel_id=1, source_target_pairs={{0,8},{1,9},{2,10},{3,11},{4,12},{5,13},{6,14},{7,15},{16,24},{17,... | collective-permute-start | bytes 2949128 | tf_op jit(solution)/shard_map/ppermute | solution.py:418
  136.4 4.6 %collective-permute-start.8 = (bf16[384,1280]{1,0:T(8,128)(2,1)S(1)}, bf16[384,1280]{1,0:T(8,128)(2,1)S(1)}, u32[]{:S(2)}, u32[]{:S(2)}) collective-permute-start(bf16[384,1280]{1,0:T(8,128)(2,1)S(1)} %shard_map.88.enc_term), channel_id=1, source_target_pairs={{8,0},{9,1},{10,2},{11,3},{12,4},{13,5},{14,6},{15,7},{24,16},{25,... | collective-permute-start | bytes 2949128 | tf_op jit(solution)/shard_map/ppermute | solution.py:419

commit v12 on v10

--- a/solution.py
+++ b/solution.py
@@ -90,7 +90,9 @@
         copies[copy] = block
 
 
-def token_kernel(core, tokens, upstream, own, other, gains, biases, queries, grad_context):
+def token_kernel(
+    core, tokens, upstream, own, other, gains, biases, queries, grad_context, picked
+):
     first = core[0] == 0
     own_tokens = jnp.where(first, tokens[0], tokens[1])
     normed_tokens = layer_norm(own_tokens, gains[1:2, :], biases[1:2, :])
@@ -99,11 +101,13 @@
     matrix = jnp.where(first, other[3], own[3])
     own_upstream = jnp.where(first, upstream[0], upstream[1])
     grad_context[...] = dot_nt(own_upstream, matrix).astype(jnp.bfloat16)
+    for kind in (1, 2):
+        picked[kind - 1] = jnp.where(first, other[kind], own[kind])
 
 
 def dec_kernel(
-    core, place, frame_lens, token_lens, x, context, own_key, own_value, other_key, other_value,
-    token_queries, token_grads, gains, biases, *refs,
+    core, place, frame_lens, token_lens, x, context, weights, token_queries, token_grads, gains, biases,
+    *refs,
 ):
     devices = context.shape[0]
     out_shards, refs = refs[:devices], refs[devices:]
@@ -131,10 +135,7 @@
     states[...] = scratch[pl.ds(start, shard), :].astype(jnp.bfloat16)
     normed_rows = layer_norm(all_states, gains[2:3, :], biases[2:3, :])
     normed[...] = normed_rows
-    matrix = [
-        jnp.where(first, other_key[0], own_key[0]),
-        jnp.where(first, other_value[0], own_value[0]),
-    ]
+    matrix = [weights[0], weights[1]]
     queries = token_queries[...]
     grad_context = token_grads[...]
     keys = dot_nt(normed_rows, matrix[0]).astype(jnp.bfloat16)
@@ -145,10 +146,10 @@
     key_parts, value_parts, context_parts = [], [], []
     for head in range(queries.shape[1] // HS):
         at = slice(head * HS, (head + 1) * HS)
-        weights = softmax(queries[:, at], keys[:, at], allowed)
-        rounded = weights.astype(jnp.bfloat16)
+        probs = softmax(queries[:, at], keys[:, at], allowed)
+        rounded = probs.astype(jnp.bfloat16)
         context_parts.append(dot_nn(rounded, values[:, at]))
-        grad_scores = scores_grad(weights, grad_context[:, at], values[:, at])
+        grad_scores = scores_grad(probs, grad_context[:, at], values[:, at])
         key_parts.append(dot_tn(grad_scores, queries[:, at]) * SCALING)
         value_parts.append(dot_tn(rounded, grad_context[:, at]))
     key_block, value_block = side_by_side(key_parts), side_by_side(value_parts)
@@ -193,11 +194,10 @@
 
 
 def enc_backward_kernel(
-    core, grads, own, other, queries, values, probs, context, normed, term
-):
-    first = core[0] == 0
+    grads, out_shard, queries, values, probs, context, normed, term
+):
     grad_rows = grads[...]
-    att_grad = dot_nt(grad_rows, jnp.where(first, own[0], other[0])).astype(jnp.bfloat16)
+    att_grad = dot_nt(grad_rows, out_shard[...]).astype(jnp.bfloat16)
     query_rows, value_rows = queries[...], values[...]
     key_parts, value_parts = [], []
     for head in range(query_rows.shape[1] // HS):
@@ -335,16 +335,16 @@
     out_shards = passed + swapped
     enc_full = exchange(copies).reshape(rows, features)
 
-    token_queries, token_grads = call(
+    token_queries, token_grads, dec_weights = call(
         token_kernel,
-        [((count, head_cols), bf16)] * 2,
+        [((count, head_cols), bf16)] * 2 + [((2, head_cols, features), bf16)],
         (core_id,),
         (dec_states, out_grad, own, other, norm_gains, norm_biases),
-        kept=(0, 1),
+        kept=(0, 1, 2),
         read=(0, 1),
     )
-    enc_full, token_queries, token_grads = lax.optimization_barrier(
-        (enc_full, token_queries, token_grads)
+    enc_full, token_queries, token_grads, dec_weights = lax.optimization_barrier(
+        (enc_full, token_queries, token_grads, dec_weights)
     )
     weight_block = ((3, head_cols, features), (0, 0, 0))
     normed, queries, values, context, context_copies, probs = call(
@@ -364,8 +364,6 @@
         cost=pl.CostEstimate(flops=3_000_000_000, transcendentals=0, bytes_accessed=0),
     )
     context_full = exchange(context_copies)
-    key_block = ((1, head_cols, features), (1, 0, 0))
-    value_block = ((1, head_cols, features), (2, 0, 0))
     partial, states, state_normed, dec_key_grad, dec_value_grad, dec_context = call(
         dec_kernel,
         [
@@ -378,13 +376,12 @@
         ],
         (core_id, place, frame_lengths, token_lengths),
         (
-            enc_full, context_full, own, own, other, other, token_queries, token_grads,
+            enc_full, context_full, dec_weights, token_queries, token_grads,
             norm_gains, norm_biases, *out_shards,
         ),
-        {2: key_block, 3: value_block, 4: key_block, 5: value_block},
         scratch=[pltpu.VMEM((rows, features), f32)],
-        kept=(1, 2, 3, 4, 5),
-        read=(2, 3, 4, 5, 6, 7, 17),
+        kept=(2, 3, 4, 5),
+        read=(2, 3, 4, 14),
     )
     pieces = exchange(partial.reshape(mp, shard_rows, features))
     whole = [((3 * head_cols, features), bf16)]
@@ -401,17 +398,14 @@
         [((mp, shard_rows, features), bf16)],
         (),
         (pieces, states, norm_gains),
-        read=(1,),
     )
     grads_full = exchange(grads).reshape(rows, features)
-    last_block = ((1, head_cols, features), (3, 0, 0))
     enc_term = call(
         enc_backward_kernel,
         whole,
-        (core_id,),
-        (grads_full, own, other, queries, values, probs, context, normed),
-        {1: last_block, 2: last_block},
-        read=(1, 2, 3, 4, 5, 6, 7),
+        (),
+        (grads_full, shard, queries, values, probs, context, normed),
+        read=(1, 2, 3, 4, 5, 6),
     )
     dec_sent = lax.ppermute(dec_term, "segment", [(0, 1)])
     enc_sent = lax.ppermute(enc_term, "segment", [(1, 0)])

time: 198 us -> 197 us (level)
  transfers between devices with their start and end apart: 13 -> 13, of which waited for: 5 -> 5; matrix products, arithmetic and copies ran while one was open for 0% -> 1% of each run, Pallas kernels for 6% -> 7%
where the time goes in v12:
time: 197 us; the launch traced here: 195 us
  blocking collectives  78 us (40%)
  starting transfers between devices  53.3 us (27%)
  waiting for transfers between devices  37.7 us (19%)
  Pallas kernels  24.3 us (12%)
    all_to_all x4, blocking collectives, exchange(): return lax.all_to_all(blocks, axis, 0, 0, axis_index_groups=groups)  78 us
    all_to_all x3, waiting for transfers between devices, exchange(): return lax.all_to_all(blocks, axis, 0, 0, axis_index_groups=groups)  26.6 us
    pallas_call x11, Pallas kernels, call(): pl.pallas_call(kernel, grid=(1,), out_shape=[out(index, *what) for index,...  24.3 us
    ppermute x4, starting transfers between devices, swap(): return lax.ppermute(block, 'segment', [(0, 1), (1, 0)])  16.7 us
    ppermute x4, starting transfers between devices, passing(): return lax.ppermute(block, ('segment', 'mp'), up + down)  15.8 us
    all_to_all x3, starting transfers between devices, exchange(): return lax.all_to_all(blocks, axis, 0, 0, axis_index_groups=groups)  14.9 us
    ppermute x4, waiting for transfers between devices, passing(): return lax.ppermute(block, ('segment', 'mp'), up + down)  8.98 us
    ppermute x1, starting transfers between devices, shards(): enc_sent = lax.ppermute(enc_term, 'segment', [(1, 0)])  4.69 us
  transfers between devices with their start and end apart: 13, of which 5 were waited for; matrix products, arithmetic and copies ran while one was open for 1% of the time, Pallas kernels for 7%

profile of v12, /device:TPU:1, one launch (start us, length us, event | category | flops | bytes accessed | tf_op | source)
XLA Modules:
  0.0 194.7 jit_solution(12048892482864737225)
XLA Ops:
  0.0 0.0 copy-start.1
  0.0 1.9 shard_map.82
  1.9 0.0 copy-start.2
  1.9 0.0 copy-start.3
  1.9 8.9 %collective-permute-start = (bf16[4,128,1280]{2,1,0:T(8,128)(2,1)}, bf16[4,128,1280]{2,1,0:T(8,128)(2,1)}, u32[]{:S(2)}, u32[]{:S(2)}) collective-permute-start(bf16[4,128,1280]{2,1,0:T(8,128)(2,1)} %bitcast.16), channel_id=1, source_target_pairs={{0,8},{8,0},{1,9},{9,1},{2,10},{10,2},{3,11},{11,3},{4,12},{12,4},... | collective-permute-start | bytes 3932168 | tf_op jit(solution)/shard_map/ppermute | solution.py:287
  10.8 4.7 %all-to-all-start = ((bf16[8,32,1280]{2,1,0:T(8,128)(2,1)}), bf16[8,32,1280]{2,1,0:T(8,128)(2,1)S(1)}, u32[]{:S(2)}, u32[]{:S(2)}) async-start(bf16[8,32,1280]{2,1,0:T(8,128)(2,1)} %shard_map.82), calls=%async_computation | async-start | bytes 1310720 | tf_op jit(solution)/shard_map/all_to_all | solution.py:309
  15.5 0.0 collective-permute-done.other
  15.5 0.0 copy-done.1
  15.5 1.0 fusion.refs_0_.out_shard
  16.5 0.0 copy-start
  16.5 0.0 copy-start.4
  16.6 4.7 %collective-permute-start.1 = (bf16[128,1280]{1,0:T(8,128)(2,1)S(1)}, bf16[128,1280]{1,0:T(8,128)(2,1)S(1)}, u32[]{:S(2)}, u32[]{:S(2)}) collective-permute-start(bf16[128,1280]{1,0:T(8,128)(2,1)S(1)} %fusion.refs_0_.out_shard), channel_id=1, source_target_pairs={{0,1},{1,2},{2,3},{3,4},{4,5},{5,6},{6,7},{7,0},{8,15},{9,8},{10,9... | collective-permute-start | bytes 983048 | tf_op jit(solution)/shard_map/ppermute | solution.py:328
  21.3 0.0 copy-done.2
  21.3 0.0 copy-done.3
  21.3 2.9 %shard_map.83 = (bf16[64,128]{1,0:T(8,128)(2,1)}, bf16[64,128]{1,0:T(8,128)(2,1)}, bf16[2,128,1280]{2,1,0:T(8,128)(2,1)}) custom-call(s32[1]{0:T(128)} %bitcast.core, bf16[2,64,1280]{2,1,0:T(8,128)(2,1)} %tokens.1, bf16[2,64,1280]{2,1,0:T(8,128)(2,1)} %upstream.3, bf16[4,128,1280]{2,1,0:T(8,128)(2,1)S(1)} %bitcast.18, ...), custom_call_target="tpu_custom_call" | custom-call | tf_op jit(solution)/shard_map/pallas_call | solution.py:269
  24.2 12.1 %all-to-all-done = bf16[8,32,1280]{2,1,0:T(8,128)(2,1)S(1)} async-done(((bf16[8,32,1280]{2,1,0:T(8,128)(2,1)}), bf16[8,32,1280]{2,1,0:T(8,128)(2,1)S(1)}, u32[]{:S(2)}, u32[]{:S(2)}) %all-to-all-start) | async-done | bytes 655392 | tf_op jit(solution)/shard_map/all_to_all | solution.py:309
  36.3 0.0 copy-start.5
  36.3 0.0 collective-permute-done.1.refs_1_
  36.3 2.5 %collective-permute-start.2 = (bf16[128,1280]{1,0:T(8,128)(2,1)S(1)}, bf16[128,1280]{1,0:T(8,128)(2,1)S(1)}, u32[]{:S(2)}, u32[]{:S(2)}) collective-permute-start(bf16[128,1280]{1,0:T(8,128)(2,1)S(1)} %collective-permute-done.1.refs_1_), channel_id=1, source_target_pairs={{0,1},{1,2},{2,3},{3,4},{4,5},{5,6},{6,7},{7,0},{8,15},{9,8},{10,9... | collective-permute-start | bytes 983048 | tf_op jit(solution)/shard_map/ppermute | solution.py:328
  38.8 0.0 copy-done.4
  38.8 4.0 %shard_map.84 = (bf16[256,1280]{1,0:T(8,128)(2,1)}, bf16[256,128]{1,0:T(8,128)(2,1)}, bf16[256,128]{1,0:T(8,128)(2,1)}, bf16[256,128]{1,0:T(8,128)(2,1)}, bf16[8...) custom-call(s32[1]{0:T(128)} %bitcast.core, s32[2,1,4]{2,1,0:T(1,128)S(1)} %copy-done.4, bf16[256,1280]{1,0:T(8,128)(2,1)S(1)} %bitcast.13, ...), custom_call_target="tpu_custom_call" | custom-call | flops 3000000000 | tf_op jit(solution)/shard_map/pallas_call | solution.py:269
  42.8 6.6 %all-to-all-start.1 = ((bf16[8,256,128]{2,1,0:T(8,128)(2,1)}), bf16[8,256,128]{2,1,0:T(8,128)(2,1)S(1)}, u32[]{:S(2)}, u32[]{:S(2)}) async-start(bf16[8,256,128]{2,1,0:T(8,128)(2,1)} %get-tuple-element.32), calls=%async_computation.1 | async-start | bytes 1048576 | tf_op jit(solution)/shard_map/all_to_all | solution.py:309
  49.4 0.0 collective-permute-done.2.refs_2_
  49.4 4.6 %collective-permute-start.3 = (bf16[128,1280]{1,0:T(8,128)(2,1)S(1)}, bf16[128,1280]{1,0:T(8,128)(2,1)S(1)}, u32[]{:S(2)}, u32[]{:S(2)}) collective-permute-start(bf16[128,1280]{1,0:T(8,128)(2,1)S(1)} %collective-permute-done.2.refs_2_), channel_id=1, source_target_pairs={{0,1},{1,2},{2,3},{3,4},{4,5},{5,6},{6,7},{7,0},{8,15},{9,8},{10,9... | collective-permute-start | bytes 983048 | tf_op jit(solution)/shard_map/ppermute | solution.py:328
  54.0 1.9 collective-permute-start.5
  55.9 2.4 %collective-permute-start.6 = (bf16[128,1280]{1,0:T(8,128)(2,1)S(1)}, bf16[128,1280]{1,0:T(8,128)(2,1)S(1)}, u32[]{:S(2)}, u32[]{:S(2)}) collective-permute-start(bf16[128,1280]{1,0:T(8,128)(2,1)S(1)} %collective-permute-done.2.refs_2_), channel_id=1, source_target_pairs={{0,8},{8,0},{1,9},{9,1},{2,10},{10,2},{3,11},{11,3},{4,12},{12,4},... | collective-permute-start | bytes 983048 | tf_op jit(solution)/shard_map/ppermute | solution.py:287
  58.3 4.0 %collective-permute-start.4 = (bf16[128,1280]{1,0:T(8,128)(2,1)S(1)}, bf16[128,1280]{1,0:T(8,128)(2,1)}, u32[]{:S(2)}, u32[]{:S(2)}) collective-permute-start(bf16[128,1280]{1,0:T(8,128)(2,1)S(1)} %collective-permute-done.2.refs_2_), channel_id=1, source_target_pairs={{0,2},{1,3},{2,4},{3,5},{4,6},{5,7},{6,0},{7,1},{8,14},{9,15},{10,... | collective-permute-start | bytes 983048 | tf_op jit(solution)/shard_map/ppermute | solution.py:328
  62.3 4.7 %collective-permute-done.3.refs_3_ = bf16[128,1280]{1,0:T(8,128)(2,1)S(1)} collective-permute-done((bf16[128,1280]{1,0:T(8,128)(2,1)S(1)}, bf16[128,1280]{1,0:T(8,128)(2,1)S(1)}, u32[]{:S(2)}, u32[]{:S(2)}) %collective-permute-start.3) | collective-permute-done | bytes 327712 | tf_op jit(solution)/shard_map/ppermute | solution.py:328
  67.1 3.5 %collective-permute-start.7 = (bf16[128,1280]{1,0:T(8,128)(2,1)S(1)}, bf16[128,1280]{1,0:T(8,128)(2,1)}, u32[]{:S(2)}, u32[]{:S(2)}) collective-permute-start(bf16[128,1280]{1,0:T(8,128)(2,1)S(1)} %collective-permute-done.3.refs_3_), channel_id=1, source_target_pairs={{0,8},{8,0},{1,9},{9,1},{2,10},{10,2},{3,11},{11,3},{4,12},{12,4},... | collective-permute-start | bytes 983048 | tf_op jit(solution)/shard_map/ppermute | solution.py:287
  70.6 0.0 collective-permute-done.5.refs_5_
  70.6 0.0 all-to-all-done.1.context
  70.6 0.0 collective-permute-done.6.refs_6_
  70.6 4.2 %collective-permute-done.4.refs_4_ = bf16[128,1280]{1,0:T(8,128)(2,1)} collective-permute-done((bf16[128,1280]{1,0:T(8,128)(2,1)S(1)}, bf16[128,1280]{1,0:T(8,128)(2,1)}, u32[]{:S(2)}, u32[]{:S(2)}) %collective-permute-start.4) | collective-permute-done | bytes 327712 | tf_op jit(solution)/shard_map/ppermute | solution.py:328
  74.9 0.0 collective-permute-done.7.refs_7_
  74.9 0.0 copy-done
  74.9 0.0 copy-done.5
  74.9 5.2 %shard_map.85 = (bf16[256,1280]{1,0:T(8,128)(2,1)S(1)}, bf16[32,1280]{1,0:T(8,128)(2,1)S(1)}, bf16[256,1280]{1,0:T(8,128)(2,1)}, bf16[256,128]{1,0:T(8,128)(2,1)...) custom-call(s32[1]{0:T(128)} %bitcast.core, s32[1]{0:T(128)} %bitcast.1.place, s32[2,1,4]{2,1,0:T(1,128)S(1)} %copy-done.4, ...), custom_call_target="tpu_custom_call" | custom-call | tf_op jit(solution)/shard_map/pallas_call | solution.py:269
  80.1 23.4 %all_to_all.35.pieces = bf16[8,32,1280]{2,1,0:T(8,128)(2,1)S(1)} all-to-all(bf16[8,32,1280]{2,1,0:T(8,128)(2,1)S(1)} %bitcast.20), channel_id=1, replica_groups=mesh['dp'=32,'segment'=2,'mp'=8] {'mp'}, dimensions={0} | all-to-all | bytes 1310720 | tf_op jit(solution)/shard_map/all_to_all | solution.py:309
  103.5 1.2 shard_map.86
  104.6 3.5 %all-to-all-start.3 = ((bf16[8,32,1280]{2,1,0:T(8,128)(2,1)}), bf16[8,32,1280]{2,1,0:T(8,128)(2,1)S(1)}, u32[]{:S(2)}, u32[]{:S(2)}) async-start(bf16[8,32,1280]{2,1,0:T(8,128)(2,1)} %shard_map.86), calls=%async_computation.3 | async-start | bytes 1310720 | tf_op jit(solution)/shard_map/all_to_all | solution.py:309
  108.2 2.6 %shard_map.88.dec_term = bf16[384,1280]{1,0:T(8,128)(2,1)} custom-call(s32[1]{0:T(128)} %bitcast.core, bf16[256,128]{1,0:T(8,128)(2,1)} %get-tuple-element.43.key_grad, bf16[256,128]{1,0:T(8,128)(2,1)} %get-tuple-element.44.value_grad, bf16[64,128]{1,0:T(8,128)(2,1)} %get-tuple-element.45.context, bf16[256,1280]{1,0:T(8,128)(2,1)} %get-tuple-element.46.normed, ...), custom_call_target="tpu_custom_call" | custom-call | tf_op jit(solution)/shard_map/pallas_call | solution.py:269
  110.8 1.3 collective-permute-start.9
  112.1 14.5 %all-to-all-done.3 = bf16[8,32,1280]{2,1,0:T(8,128)(2,1)S(1)} async-done(((bf16[8,32,1280]{2,1,0:T(8,128)(2,1)}), bf16[8,32,1280]{2,1,0:T(8,128)(2,1)S(1)}, u32[]{:S(2)}, u32[]{:S(2)}) %all-to-all-start.3) | async-done | bytes 655392 | tf_op jit(solution)/shard_map/all_to_all | solution.py:309
  126.7 3.3 %shard_map.87.enc_term = bf16[384,1280]{1,0:T(8,128)(2,1)S(1)} custom-call(bf16[256,1280]{1,0:T(8,128)(2,1)S(1)} %bitcast.15, bf16[128,1280]{1,0:T(8,128)(2,1)} %copy-done, bf16[256,128]{1,0:T(8,128)(2,1)} %get-tuple-element.38.queries, bf16[256,128]{1,0:T(8,128)(2,1)} %get-tuple-element.39.values, f32[2,256,256]{2,1,0:T(8,128)} %get-tuple-element.40.probs, ...), custom_call_target="tpu_custom_call" | custom-call | tf_op jit(solution)/shard_map/pallas_call | solution.py:269
  130.0 4.7 %collective-permute-start.8 = (bf16[384,1280]{1,0:T(8,128)(2,1)S(1)}, bf16[384,1280]{1,0:T(8,128)(2,1)S(1)}, u32[]{:S(2)}, u32[]{:S(2)}) collective-permute-start(bf16[384,1280]{1,0:T(8,128)(2,1)S(1)} %shard_map.87.enc_term), channel_id=1, source_target_pairs={{8,0},{9,1},{10,2},{11,3},{12,4},{13,5},{14,6},{15,7},{24,16},{25,... | collective-permute-start | bytes 2949128 | tf_op jit(solution)/shard_map/ppermute | solution.py:411
  134.7 0.0 collective-permute-done.9.dec_sent
  134.7 2.1 %collective-permute-done.8.enc_sent = bf16[384,1280]{1,0:T(8,128)(2,1)S(1)} collective-permute-done((bf16[384,1280]{1,0:T(8,128)(2,1)S(1)}, bf16[384,1280]{1,0:T(8,128)(2,1)S(1)}, u32[]{:S(2)}, u32[]{:S(2)}) %collective-permute-start.8) | collective-permute-done | bytes 983072 | tf_op jit(solution)/shard_map/ppermute | solution.py:411
  136.8 1.6 shard_map.89
  138.4 19.3 %all_to_all.36.pieces = bf16[8,60,8,128]{3,2,1,0:T(8,128)(2,1)S(1)} all-to-all(bf16[8,60,8,128]{3,2,1,0:T(8,128)(2,1)S(1)} %bitcast.11), channel_id=1, replica_groups={{0,16,128,144,256,272,384,400},{32,48,160,176,288,304,416,432},{64,80,1..., dimensions={0} | all-to-all | bytes 1966080 | tf_op jit(solution)/shard_map/all_to_all | solution.py:309
  157.7 0.1 shard_map.90
  157.8 18.3 %all_to_all.37.pieces = bf16[4,60,8,128]{3,2,1,0:T(8,128)(2,1)S(1)} all-to-all(bf16[4,60,8,128]{3,2,1,0:T(8,128)(2,1)S(1)} %shard_map.90), channel_id=1, replica_groups={{0,32,64,96},{16,48,80,112},{128,160,192,224},{144,176,208,240},{256,28..., dimensions={0} | all-to-all | bytes 983040 | tf_op jit(solution)/shard_map/all_to_all | solution.py:309
  176.1 0.1 shard_map.91
  176.2 17.1 %all_to_all.38 = bf16[8,60,8,128]{3,2,1,0:T(8,128)(2,1)S(1)} all-to-all(bf16[8,60,8,128]{3,2,1,0:T(8,128)(2,1)S(1)} %shard_map.91), channel_id=1, replica_groups={{0,16,128,144,256,272,384,400},{32,48,160,176,288,304,416,432},{64,80,1..., dimensions={0} | all-to-all | bytes 1966080 | tf_op jit(solution)/shard_map/all_to_all | solution.py:309
  193.3 1.4 shard_map.92
Async XLA Ops:
  0.0 15.5 %copy-start.1 = (bf16[1,4,128,1280]{3,2,1,0:T(8,128)(2,1)S(1)}, bf16[1,4,128,1280]{3,2,1,0:T(8,128)(2,1)}, u32[]{:S(2)}) copy-start(bf16[1,4,128,1280]{3,2,1,0:T(8,128)(2,1)} %param.13) | copy-start | bytes 3932164
  1.9 19.4 %copy-start.2 = (f32[3,1280]{1,0:T(4,128)S(1)}, f32[3,1280]{1,0:T(4,128)}, u32[]{:S(2)}) copy-start(f32[3,1280]{1,0:T(4,128)} %gains.7) | copy-start | bytes 46084
  1.9 19.4 %copy-start.3 = (f32[3,1280]{1,0:T(4,128)S(1)}, f32[3,1280]{1,0:T(4,128)}, u32[]{:S(2)}) copy-start(f32[3,1280]{1,0:T(4,128)} %biases.5) | copy-start | bytes 46084
  1.9 13.6 %collective-permute-start = (bf16[4,128,1280]{2,1,0:T(8,128)(2,1)}, bf16[4,128,1280]{2,1,0:T(8,128)(2,1)}, u32[]{:S(2)}, u32[]{:S(2)}) collective-permute-start(bf16[4,128,1280]{2,1,0:T(8,128)(2,1)} %bitcast.16), channel_id=1, source_target_pairs={{0,8},{8,0},{1,9},{9,1},{2,10},{10,2},{3,11},{11,3},{4,12},{12,4},... | collective-permute-start | bytes 3932168 | tf_op jit(solution)/shard_map/ppermute | solution.py:287
  10.8 25.5 %all-to-all-start = ((bf16[8,32,1280]{2,1,0:T(8,128)(2,1)}), bf16[8,32,1280]{2,1,0:T(8,128)(2,1)S(1)}, u32[]{:S(2)}, u32[]{:S(2)}) async-start(bf16[8,32,1280]{2,1,0:T(8,128)(2,1)} %shard_map.82), calls=%async_computation | async-start | bytes 1310720 | tf_op jit(solution)/shard_map/all_to_all | solution.py:309
  16.5 58.3 %copy-start = (bf16[128,1280]{1,0:T(8,128)(2,1)}, bf16[128,1280]{1,0:T(8,128)(2,1)S(1)}, u32[]{:S(2)}) copy-start(bf16[128,1280]{1,0:T(8,128)(2,1)S(1)} %fusion.refs_0_.out_shard) | copy-start | bytes 983044
  16.5 22.2 %copy-start.4 = (s32[2,1,4]{2,1,0:T(1,128)S(1)}, s32[2,1,4]{2,1,0:T(1,128)}, u32[]{:S(2)}) copy-start(s32[2,1,4]{2,1,0:T(1,128)} %frame_lens.1) | copy-start | bytes 100
  16.6 19.7 %collective-permute-start.1 = (bf16[128,1280]{1,0:T(8,128)(2,1)S(1)}, bf16[128,1280]{1,0:T(8,128)(2,1)S(1)}, u32[]{:S(2)}, u32[]{:S(2)}) collective-permute-start(bf16[128,1280]{1,0:T(8,128)(2,1)S(1)} %fusion.refs_0_.out_shard), channel_id=1, source_target_pairs={{0,1},{1,2},{2,3},{3,4},{4,5},{5,6},{6,7},{7,0},{8,15},{9,8},{10,9... | collective-permute-start | bytes 983048 | tf_op jit(solution)/shard_map/ppermute | solution.py:328
  36.3 38.6 %copy-start.5 = (s32[2,1,4]{2,1,0:T(1,128)S(1)}, s32[2,1,4]{2,1,0:T(1,128)}, u32[]{:S(2)}) copy-start(s32[2,1,4]{2,1,0:T(1,128)} %token_lens.1) | copy-start | bytes 100
  36.3 13.1 %collective-permute-start.2 = (bf16[128,1280]{1,0:T(8,128)(2,1)S(1)}, bf16[128,1280]{1,0:T(8,128)(2,1)S(1)}, u32[]{:S(2)}, u32[]{:S(2)}) collective-permute-start(bf16[128,1280]{1,0:T(8,128)(2,1)S(1)} %collective-permute-done.1.refs_1_), channel_id=1, source_target_pairs={{0,1},{1,2},{2,3},{3,4},{4,5},{5,6},{6,7},{7,0},{8,15},{9,8},{10,9... | collective-permute-start | bytes 983048 | tf_op jit(solution)/shard_map/ppermute | solution.py:328
  42.8 27.8 %all-to-all-start.1 = ((bf16[8,256,128]{2,1,0:T(8,128)(2,1)}), bf16[8,256,128]{2,1,0:T(8,128)(2,1)S(1)}, u32[]{:S(2)}, u32[]{:S(2)}) async-start(bf16[8,256,128]{2,1,0:T(8,128)(2,1)} %get-tuple-element.32), calls=%async_computation.1 | async-start | bytes 1048576 | tf_op jit(solution)/shard_map/all_to_all | solution.py:309
  49.4 17.7 %collective-permute-start.3 = (bf16[128,1280]{1,0:T(8,128)(2,1)S(1)}, bf16[128,1280]{1,0:T(8,128)(2,1)S(1)}, u32[]{:S(2)}, u32[]{:S(2)}) collective-permute-start(bf16[128,1280]{1,0:T(8,128)(2,1)S(1)} %collective-permute-done.2.refs_2_), channel_id=1, source_target_pairs={{0,1},{1,2},{2,3},{3,4},{4,5},{5,6},{6,7},{7,0},{8,15},{9,8},{10,9... | collective-permute-start | bytes 983048 | tf_op jit(solution)/shard_map/ppermute | solution.py:328
  54.0 16.6 %collective-permute-start.5 = (bf16[128,1280]{1,0:T(8,128)(2,1)S(1)}, bf16[128,1280]{1,0:T(8,128)(2,1)S(1)}, u32[]{:S(2)}, u32[]{:S(2)}) collective-permute-start(bf16[128,1280]{1,0:T(8,128)(2,1)S(1)} %collective-permute-done.1.refs_1_), channel_id=1, source_target_pairs={{0,8},{8,0},{1,9},{9,1},{2,10},{10,2},{3,11},{11,3},{4,12},{12,4},... | collective-permute-start | bytes 983048 | tf_op jit(solution)/shard_map/ppermute | solution.py:287
  55.9 14.7 %collective-permute-start.6 = (bf16[128,1280]{1,0:T(8,128)(2,1)S(1)}, bf16[128,1280]{1,0:T(8,128)(2,1)S(1)}, u32[]{:S(2)}, u32[]{:S(2)}) collective-permute-start(bf16[128,1280]{1,0:T(8,128)(2,1)S(1)} %collective-permute-done.2.refs_2_), channel_id=1, source_target_pairs={{0,8},{8,0},{1,9},{9,1},{2,10},{10,2},{3,11},{11,3},{4,12},{12,4},... | collective-permute-start | bytes 983048 | tf_op jit(solution)/shard_map/ppermute | solution.py:287
  58.3 16.5 %collective-permute-start.4 = (bf16[128,1280]{1,0:T(8,128)(2,1)S(1)}, bf16[128,1280]{1,0:T(8,128)(2,1)}, u32[]{:S(2)}, u32[]{:S(2)}) collective-permute-start(bf16[128,1280]{1,0:T(8,128)(2,1)S(1)} %collective-permute-done.2.refs_2_), channel_id=1, source_target_pairs={{0,2},{1,3},{2,4},{3,5},{4,6},{5,7},{6,0},{7,1},{8,14},{9,15},{10,... | collective-permute-start | bytes 983048 | tf_op jit(solution)/shard_map/ppermute | solution.py:328
  67.1 7.8 %collective-permute-start.7 = (bf16[128,1280]{1,0:T(8,128)(2,1)S(1)}, bf16[128,1280]{1,0:T(8,128)(2,1)}, u32[]{:S(2)}, u32[]{:S(2)}) collective-permute-start(bf16[128,1280]{1,0:T(8,128)(2,1)S(1)} %collective-permute-done.3.refs_3_), channel_id=1, source_target_pairs={{0,8},{8,0},{1,9},{9,1},{2,10},{10,2},{3,11},{11,3},{4,12},{12,4},... | collective-permute-start | bytes 983048 | tf_op jit(solution)/shard_map/ppermute | solution.py:287
  104.6 22.0 %all-to-all-start.3 = ((bf16[8,32,1280]{2,1,0:T(8,128)(2,1)}), bf16[8,32,1280]{2,1,0:T(8,128)(2,1)S(1)}, u32[]{:S(2)}, u32[]{:S(2)}) async-start(bf16[8,32,1280]{2,1,0:T(8,128)(2,1)} %shard_map.86), calls=%async_computation.3 | async-start | bytes 1310720 | tf_op jit(solution)/shard_map/all_to_all | solution.py:309
  110.8 23.9 %collective-permute-start.9 = (bf16[384,1280]{1,0:T(8,128)(2,1)}, bf16[384,1280]{1,0:T(8,128)(2,1)S(1)}, u32[]{:S(2)}, u32[]{:S(2)}) collective-permute-start(bf16[384,1280]{1,0:T(8,128)(2,1)} %shard_map.88.dec_term), channel_id=1, source_target_pairs={{0,8},{1,9},{2,10},{3,11},{4,12},{5,13},{6,14},{7,15},{16,24},{17,... | collective-permute-start | bytes 2949128 | tf_op jit(solution)/shard_map/ppermute | solution.py:410
  130.0 6.8 %collective-permute-start.8 = (bf16[384,1280]{1,0:T(8,128)(2,1)S(1)}, bf16[384,1280]{1,0:T(8,128)(2,1)S(1)}, u32[]{:S(2)}, u32[]{:S(2)}) collective-permute-start(bf16[384,1280]{1,0:T(8,128)(2,1)S(1)} %shard_map.87.enc_term), channel_id=1, source_target_pairs={{8,0},{9,1},{10,2},{11,3},{12,4},{13,5},{14,6},{15,7},{24,16},{25,... | collective-permute-start | bytes 2949128 | tf_op jit(solution)/shard_map/ppermute | solution.py:411

commit v13 on v12

--- a/solution.py
+++ b/solution.py
@@ -381,7 +381,7 @@
         ),
         scratch=[pltpu.VMEM((rows, features), f32)],
         kept=(2, 3, 4, 5),
-        read=(2, 3, 4, 14),
+        read=(14,),
     )
     pieces = exchange(partial.reshape(mp, shard_rows, features))
     whole = [((3 * head_cols, features), bf16)]
@@ -405,7 +405,6 @@
         whole,
         (),
         (grads_full, shard, queries, values, probs, context, normed),
-        read=(1, 2, 3, 4, 5, 6),
     )
     dec_sent = lax.ppermute(dec_term, "segment", [(0, 1)])
     enc_sent = lax.ppermute(enc_term, "segment", [(1, 0)])

time: 197 us -> 196 us (level)
  transfers between devices with their start and end apart: 13 -> 13, of which waited for: 5 -> 5; matrix products, arithmetic and copies ran while one was open for 1% -> 1% of each run, Pallas kernels for 7% -> 6%
where the time goes in v13:
time: 196 us; the launch traced here: 194 us
  blocking collectives  78 us (40%)
  starting transfers between devices  53.3 us (27%)
  waiting for transfers between devices  37.8 us (19%)
  Pallas kernels  23.2 us (12%)
    all_to_all x4, blocking collectives, exchange(): return lax.all_to_all(blocks, axis, 0, 0, axis_index_groups=groups)  78 us
    all_to_all x3, waiting for transfers between devices, exchange(): return lax.all_to_all(blocks, axis, 0, 0, axis_index_groups=groups)  26.7 us
    pallas_call x11, Pallas kernels, call(): pl.pallas_call(kernel, grid=(1,), out_shape=[out(index, *what) for index,...  23.2 us
    ppermute x4, starting transfers between devices, swap(): return lax.ppermute(block, 'segment', [(0, 1), (1, 0)])  16.7 us
    ppermute x4, starting transfers between devices, passing(): return lax.ppermute(block, ('segment', 'mp'), up + down)  15.6 us
    all_to_all x3, starting transfers between devices, exchange(): return lax.all_to_all(blocks, axis, 0, 0, axis_index_groups=groups)  15 us
    ppermute x4, waiting for transfers between devices, passing(): return lax.ppermute(block, ('segment', 'mp'), up + down)  8.98 us
    ppermute x1, starting transfers between devices, shards(): enc_sent = lax.ppermute(enc_term, 'segment', [(1, 0)])  4.69 us
  transfers between devices with their start and end apart: 13, of which 5 were waited for; matrix products, arithmetic and copies ran while one was open for 1% of the time, Pallas kernels for 6%

profile of v13, /device:TPU:1, one launch (start us, length us, event | category | flops | bytes accessed | tf_op | source)
XLA Modules:
  0.0 193.6 jit_solution(3966441578289710340)
XLA Ops:
  0.0 0.0 copy-start
  0.0 1.9 shard_map.82
  1.9 0.0 copy-start.4
  1.9 0.0 copy-start.5
  1.9 8.9 %collective-permute-start = (bf16[4,128,1280]{2,1,0:T(8,128)(2,1)}, bf16[4,128,1280]{2,1,0:T(8,128)(2,1)}, u32[]{:S(2)}, u32[]{:S(2)}) collective-permute-start(bf16[4,128,1280]{2,1,0:T(8,128)(2,1)} %bitcast.16), channel_id=1, source_target_pairs={{0,8},{8,0},{1,9},{9,1},{2,10},{10,2},{3,11},{11,3},{4,12},{12,4},... | collective-permute-start | bytes 3932168 | tf_op jit(solution)/shard_map/ppermute | solution.py:287
  10.8 4.7 %all-to-all-start = ((bf16[8,32,1280]{2,1,0:T(8,128)(2,1)}), bf16[8,32,1280]{2,1,0:T(8,128)(2,1)S(1)}, u32[]{:S(2)}, u32[]{:S(2)}) async-start(bf16[8,32,1280]{2,1,0:T(8,128)(2,1)} %shard_map.82), calls=%async_computation | async-start | bytes 1310720 | tf_op jit(solution)/shard_map/all_to_all | solution.py:309
  15.5 0.0 collective-permute-done.other
  15.5 0.0 copy-done
  15.5 1.0 fusion.refs_0_.out_shard
  16.5 0.0 copy-start.11
  16.6 4.6 %collective-permute-start.1 = (bf16[128,1280]{1,0:T(8,128)(2,1)S(1)}, bf16[128,1280]{1,0:T(8,128)(2,1)S(1)}, u32[]{:S(2)}, u32[]{:S(2)}) collective-permute-start(bf16[128,1280]{1,0:T(8,128)(2,1)S(1)} %fusion.refs_0_.out_shard), channel_id=1, source_target_pairs={{0,1},{1,2},{2,3},{3,4},{4,5},{5,6},{6,7},{7,0},{8,15},{9,8},{10,9... | collective-permute-start | bytes 983048 | tf_op jit(solution)/shard_map/ppermute | solution.py:328
  21.1 0.0 copy-done.4
  21.1 0.0 copy-done.5
  21.2 2.9 %shard_map.83 = (bf16[64,128]{1,0:T(8,128)(2,1)}, bf16[64,128]{1,0:T(8,128)(2,1)}, bf16[2,128,1280]{2,1,0:T(8,128)(2,1)}) custom-call(s32[1]{0:T(128)} %bitcast.core, bf16[2,64,1280]{2,1,0:T(8,128)(2,1)} %tokens.1, bf16[2,64,1280]{2,1,0:T(8,128)(2,1)} %upstream.3, bf16[4,128,1280]{2,1,0:T(8,128)(2,1)S(1)} %bitcast.18, ...), custom_call_target="tpu_custom_call" | custom-call | tf_op jit(solution)/shard_map/pallas_call | solution.py:269
  24.0 12.3 %all-to-all-done = bf16[8,32,1280]{2,1,0:T(8,128)(2,1)S(1)} async-done(((bf16[8,32,1280]{2,1,0:T(8,128)(2,1)}), bf16[8,32,1280]{2,1,0:T(8,128)(2,1)S(1)}, u32[]{:S(2)}, u32[]{:S(2)}) %all-to-all-start) | async-done | bytes 655392 | tf_op jit(solution)/shard_map/all_to_all | solution.py:309
  36.3 0.0 collective-permute-done.1.refs_1_
  36.3 2.5 %collective-permute-start.2 = (bf16[128,1280]{1,0:T(8,128)(2,1)S(1)}, bf16[128,1280]{1,0:T(8,128)(2,1)S(1)}, u32[]{:S(2)}, u32[]{:S(2)}) collective-permute-start(bf16[128,1280]{1,0:T(8,128)(2,1)S(1)} %collective-permute-done.1.refs_1_), channel_id=1, source_target_pairs={{0,1},{1,2},{2,3},{3,4},{4,5},{5,6},{6,7},{7,0},{8,15},{9,8},{10,9... | collective-permute-start | bytes 983048 | tf_op jit(solution)/shard_map/ppermute | solution.py:328
  38.8 0.0 copy-done.11
  38.8 4.0 %shard_map.84 = (bf16[256,1280]{1,0:T(8,128)(2,1)}, bf16[256,128]{1,0:T(8,128)(2,1)}, bf16[256,128]{1,0:T(8,128)(2,1)}, bf16[256,128]{1,0:T(8,128)(2,1)}, bf16[8...) custom-call(s32[1]{0:T(128)} %bitcast.core, s32[2,1,4]{2,1,0:T(1,128)S(1)} %copy-done.11, bf16[256,1280]{1,0:T(8,128)(2,1)S(1)} %bitcast.13, ...), custom_call_target="tpu_custom_call" | custom-call | flops 3000000000 | tf_op jit(solution)/shard_map/pallas_call | solution.py:269
  42.8 6.8 %all-to-all-start.1 = ((bf16[8,256,128]{2,1,0:T(8,128)(2,1)}), bf16[8,256,128]{2,1,0:T(8,128)(2,1)S(1)}, u32[]{:S(2)}, u32[]{:S(2)}) async-start(bf16[8,256,128]{2,1,0:T(8,128)(2,1)} %get-tuple-element.32), calls=%async_computation.1 | async-start | bytes 1048576 | tf_op jit(solution)/shard_map/all_to_all | solution.py:309
  49.6 0.0 collective-permute-done.2.refs_2_
  49.6 4.6 %collective-permute-start.3 = (bf16[128,1280]{1,0:T(8,128)(2,1)S(1)}, bf16[128,1280]{1,0:T(8,128)(2,1)S(1)}, u32[]{:S(2)}, u32[]{:S(2)}) collective-permute-start(bf16[128,1280]{1,0:T(8,128)(2,1)S(1)} %collective-permute-done.2.refs_2_), channel_id=1, source_target_pairs={{0,1},{1,2},{2,3},{3,4},{4,5},{5,6},{6,7},{7,0},{8,15},{9,8},{10,9... | collective-permute-start | bytes 983048 | tf_op jit(solution)/shard_map/ppermute | solution.py:328
  54.1 1.9 collective-permute-start.5
  56.1 2.4 %collective-permute-start.6 = (bf16[128,1280]{1,0:T(8,128)(2,1)S(1)}, bf16[128,1280]{1,0:T(8,128)(2,1)}, u32[]{:S(2)}, u32[]{:S(2)}) collective-permute-start(bf16[128,1280]{1,0:T(8,128)(2,1)S(1)} %collective-permute-done.2.refs_2_), channel_id=1, source_target_pairs={{0,8},{8,0},{1,9},{9,1},{2,10},{10,2},{3,11},{11,3},{4,12},{12,4},... | collective-permute-start | bytes 983048 | tf_op jit(solution)/shard_map/ppermute | solution.py:287
  58.5 4.0 %collective-permute-start.4 = (bf16[128,1280]{1,0:T(8,128)(2,1)S(1)}, bf16[128,1280]{1,0:T(8,128)(2,1)}, u32[]{:S(2)}, u32[]{:S(2)}) collective-permute-start(bf16[128,1280]{1,0:T(8,128)(2,1)S(1)} %collective-permute-done.2.refs_2_), channel_id=1, source_target_pairs={{0,2},{1,3},{2,4},{3,5},{4,6},{5,7},{6,0},{7,1},{8,14},{9,15},{10,... | collective-permute-start | bytes 983048 | tf_op jit(solution)/shard_map/ppermute | solution.py:328
  62.5 4.7 %collective-permute-done.3.refs_3_ = bf16[128,1280]{1,0:T(8,128)(2,1)S(1)} collective-permute-done((bf16[128,1280]{1,0:T(8,128)(2,1)S(1)}, bf16[128,1280]{1,0:T(8,128)(2,1)S(1)}, u32[]{:S(2)}, u32[]{:S(2)}) %collective-permute-start.3) | collective-permute-done | bytes 327712 | tf_op jit(solution)/shard_map/ppermute | solution.py:328
  67.2 3.5 %collective-permute-start.7 = (bf16[128,1280]{1,0:T(8,128)(2,1)S(1)}, bf16[128,1280]{1,0:T(8,128)(2,1)}, u32[]{:S(2)}, u32[]{:S(2)}) collective-permute-start(bf16[128,1280]{1,0:T(8,128)(2,1)S(1)} %collective-permute-done.3.refs_3_), channel_id=1, source_target_pairs={{0,8},{8,0},{1,9},{9,1},{2,10},{10,2},{3,11},{11,3},{4,12},{12,4},... | collective-permute-start | bytes 983048 | tf_op jit(solution)/shard_map/ppermute | solution.py:287
  70.7 0.0 collective-permute-done.5.refs_5_
  70.7 0.0 all-to-all-done.1.context
  70.7 0.0 collective-permute-done.6.refs_6_
  70.8 4.2 %collective-permute-done.4.refs_4_ = bf16[128,1280]{1,0:T(8,128)(2,1)} collective-permute-done((bf16[128,1280]{1,0:T(8,128)(2,1)S(1)}, bf16[128,1280]{1,0:T(8,128)(2,1)}, u32[]{:S(2)}, u32[]{:S(2)}) %collective-permute-start.4) | collective-permute-done | bytes 327712 | tf_op jit(solution)/shard_map/ppermute | solution.py:328
  75.0 0.0 collective-permute-done.7.refs_7_
  75.0 0.0 copy-done.9
  75.0 0.0 copy-done.10
  75.0 0.0 copy-done.12
  75.0 0.0 copy-done.2
  75.0 5.4 %shard_map.85 = (bf16[256,1280]{1,0:T(8,128)(2,1)S(1)}, bf16[32,1280]{1,0:T(8,128)(2,1)S(1)}, bf16[256,1280]{1,0:T(8,128)(2,1)}, bf16[256,128]{1,0:T(8,128)(2,1)...) custom-call(s32[1]{0:T(128)} %bitcast.core, s32[1]{0:T(128)} %bitcast.1.place, s32[2,1,4]{2,1,0:T(1,128)S(1)} %copy-done.11, ...), custom_call_target="tpu_custom_call" | custom-call | tf_op jit(solution)/shard_map/pallas_call | solution.py:269
  80.5 23.4 %all_to_all.35.pieces = bf16[8,32,1280]{2,1,0:T(8,128)(2,1)S(1)} all-to-all(bf16[8,32,1280]{2,1,0:T(8,128)(2,1)S(1)} %bitcast.20), channel_id=1, replica_groups=mesh['dp'=32,'segment'=2,'mp'=8] {'mp'}, dimensions={0} | all-to-all | bytes 1310720 | tf_op jit(solution)/shard_map/all_to_all | solution.py:309
  103.8 1.2 shard_map.86
  105.0 3.5 %all-to-all-start.3 = ((bf16[8,32,1280]{2,1,0:T(8,128)(2,1)}), bf16[8,32,1280]{2,1,0:T(8,128)(2,1)S(1)}, u32[]{:S(2)}, u32[]{:S(2)}) async-start(bf16[8,32,1280]{2,1,0:T(8,128)(2,1)} %shard_map.86), calls=%async_computation.3 | async-start | bytes 1310720 | tf_op jit(solution)/shard_map/all_to_all | solution.py:309
  108.5 0.0 copy-start.1
  108.6 0.0 copy-start.3
  108.6 0.0 copy-start.6
  108.6 0.0 copy-start.7
  108.6 0.0 copy-start.8
  108.6 2.7 %shard_map.88.dec_term = bf16[384,1280]{1,0:T(8,128)(2,1)} custom-call(s32[1]{0:T(128)} %bitcast.core, bf16[256,128]{1,0:T(8,128)(2,1)} %get-tuple-element.43.key_grad, bf16[256,128]{1,0:T(8,128)(2,1)} %get-tuple-element.44.value_grad, bf16[64,128]{1,0:T(8,128)(2,1)} %get-tuple-element.45.context, bf16[256,1280]{1,0:T(8,128)(2,1)} %get-tuple-element.46.normed, ...), custom_call_target="tpu_custom_call" | custom-call | tf_op jit(solution)/shard_map/pallas_call | solution.py:269
  111.3 1.3 collective-permute-start.9
  112.6 14.4 %all-to-all-done.3 = bf16[8,32,1280]{2,1,0:T(8,128)(2,1)S(1)} async-done(((bf16[8,32,1280]{2,1,0:T(8,128)(2,1)}), bf16[8,32,1280]{2,1,0:T(8,128)(2,1)S(1)}, u32[]{:S(2)}, u32[]{:S(2)}) %all-to-all-start.3) | async-done | bytes 655392 | tf_op jit(solution)/shard_map/all_to_all | solution.py:309
  127.0 0.0 copy-done.1
  127.0 0.0 copy-done.3
  127.0 0.0 copy-done.6
  127.0 0.0 copy-done.7
  127.0 0.0 copy-done.8
  127.0 1.9 shard_map.87.enc_term
  129.0 4.7 %collective-permute-start.8 = (bf16[384,1280]{1,0:T(8,128)(2,1)S(1)}, bf16[384,1280]{1,0:T(8,128)(2,1)S(1)}, u32[]{:S(2)}, u32[]{:S(2)}) collective-permute-start(bf16[384,1280]{1,0:T(8,128)(2,1)S(1)} %shard_map.87.enc_term), channel_id=1, source_target_pairs={{8,0},{9,1},{10,2},{11,3},{12,4},{13,5},{14,6},{15,7},{24,16},{25,... | collective-permute-start | bytes 2949128 | tf_op jit(solution)/shard_map/ppermute | solution.py:410
  133.7 0.0 collective-permute-done.9.dec_sent
  133.7 2.1 %collective-permute-done.8.enc_sent = bf16[384,1280]{1,0:T(8,128)(2,1)S(1)} collective-permute-done((bf16[384,1280]{1,0:T(8,128)(2,1)S(1)}, bf16[384,1280]{1,0:T(8,128)(2,1)S(1)}, u32[]{:S(2)}, u32[]{:S(2)}) %collective-permute-start.8) | collective-permute-done | bytes 983072 | tf_op jit(solution)/shard_map/ppermute | solution.py:410
  135.8 1.6 shard_map.89
  137.4 19.3 %all_to_all.36.pieces = bf16[8,60,8,128]{3,2,1,0:T(8,128)(2,1)S(1)} all-to-all(bf16[8,60,8,128]{3,2,1,0:T(8,128)(2,1)S(1)} %bitcast.11), channel_id=1, replica_groups={{0,16,128,144,256,272,384,400},{32,48,160,176,288,304,416,432},{64,80,1..., dimensions={0} | all-to-all | bytes 1966080 | tf_op jit(solution)/shard_map/all_to_all | solution.py:309
  156.7 0.1 shard_map.90
  156.8 18.3 %all_to_all.37.pieces = bf16[4,60,8,128]{3,2,1,0:T(8,128)(2,1)S(1)} all-to-all(bf16[4,60,8,128]{3,2,1,0:T(8,128)(2,1)S(1)} %shard_map.90), channel_id=1, replica_groups={{0,32,64,96},{16,48,80,112},{128,160,192,224},{144,176,208,240},{256,28..., dimensions={0} | all-to-all | bytes 983040 | tf_op jit(solution)/shard_map/all_to_all | solution.py:309
  175.1 0.1 shard_map.91
  175.1 17.1 %all_to_all.38 = bf16[8,60,8,128]{3,2,1,0:T(8,128)(2,1)S(1)} all-to-all(bf16[8,60,8,128]{3,2,1,0:T(8,128)(2,1)S(1)} %shard_map.91), channel_id=1, replica_groups={{0,16,128,144,256,272,384,400},{32,48,160,176,288,304,416,432},{64,80,1..., dimensions={0} | all-to-all | bytes 1966080 | tf_op jit(solution)/shard_map/all_to_all | solution.py:309
  192.2 1.4 shard_map.92
  (4 shorter events, 0.0 us)
Async XLA Ops:
  0.0 15.5 %copy-start = (bf16[1,4,128,1280]{3,2,1,0:T(8,128)(2,1)S(1)}, bf16[1,4,128,1280]{3,2,1,0:T(8,128)(2,1)}, u32[]{:S(2)}) copy-start(bf16[1,4,128,1280]{3,2,1,0:T(8,128)(2,1)} %param.13) | copy-start | bytes 3932164
  1.9 19.2 %copy-start.4 = (f32[3,1280]{1,0:T(4,128)S(1)}, f32[3,1280]{1,0:T(4,128)}, u32[]{:S(2)}) copy-start(f32[3,1280]{1,0:T(4,128)} %gains.7) | copy-start | bytes 46084
  1.9 19.2 %copy-start.5 = (f32[3,1280]{1,0:T(4,128)S(1)}, f32[3,1280]{1,0:T(4,128)}, u32[]{:S(2)}) copy-start(f32[3,1280]{1,0:T(4,128)} %biases.5) | copy-start | bytes 46084
  1.9 13.6 %collective-permute-start = (bf16[4,128,1280]{2,1,0:T(8,128)(2,1)}, bf16[4,128,1280]{2,1,0:T(8,128)(2,1)}, u32[]{:S(2)}, u32[]{:S(2)}) collective-permute-start(bf16[4,128,1280]{2,1,0:T(8,128)(2,1)} %bitcast.16), channel_id=1, source_target_pairs={{0,8},{8,0},{1,9},{9,1},{2,10},{10,2},{3,11},{11,3},{4,12},{12,4},... | collective-permute-start | bytes 3932168 | tf_op jit(solution)/shard_map/ppermute | solution.py:287
  10.8 25.5 %all-to-all-start = ((bf16[8,32,1280]{2,1,0:T(8,128)(2,1)}), bf16[8,32,1280]{2,1,0:T(8,128)(2,1)S(1)}, u32[]{:S(2)}, u32[]{:S(2)}) async-start(bf16[8,32,1280]{2,1,0:T(8,128)(2,1)} %shard_map.82), calls=%async_computation | async-start | bytes 1310720 | tf_op jit(solution)/shard_map/all_to_all | solution.py:309
  16.5 22.3 %copy-start.11 = (s32[2,1,4]{2,1,0:T(1,128)S(1)}, s32[2,1,4]{2,1,0:T(1,128)}, u32[]{:S(2)}) copy-start(s32[2,1,4]{2,1,0:T(1,128)} %frame_lens.1) | copy-start | bytes 100
  16.6 19.8 %collective-permute-start.1 = (bf16[128,1280]{1,0:T(8,128)(2,1)S(1)}, bf16[128,1280]{1,0:T(8,128)(2,1)S(1)}, u32[]{:S(2)}, u32[]{:S(2)}) collective-permute-start(bf16[128,1280]{1,0:T(8,128)(2,1)S(1)} %fusion.refs_0_.out_shard), channel_id=1, source_target_pairs={{0,1},{1,2},{2,3},{3,4},{4,5},{5,6},{6,7},{7,0},{8,15},{9,8},{10,9... | collective-permute-start | bytes 983048 | tf_op jit(solution)/shard_map/ppermute | solution.py:328
  36.3 38.7 %copy-start.9 = (bf16[64,128]{1,0:T(8,128)(2,1)S(1)}, bf16[64,128]{1,0:T(8,128)(2,1)}, u32[]{:S(2)}) copy-start(bf16[64,128]{1,0:T(8,128)(2,1)} %get-tuple-element.34.token_queries) | copy-start | bytes 49156
  36.3 38.7 %copy-start.10 = (bf16[64,128]{1,0:T(8,128)(2,1)S(1)}, bf16[64,128]{1,0:T(8,128)(2,1)}, u32[]{:S(2)}) copy-start(bf16[64,128]{1,0:T(8,128)(2,1)} %get-tuple-element.35.token_grads) | copy-start | bytes 49156
  36.3 38.7 %copy-start.12 = (s32[2,1,4]{2,1,0:T(1,128)S(1)}, s32[2,1,4]{2,1,0:T(1,128)}, u32[]{:S(2)}) copy-start(s32[2,1,4]{2,1,0:T(1,128)} %token_lens.1) | copy-start | bytes 100
  36.3 13.2 %collective-permute-start.2 = (bf16[128,1280]{1,0:T(8,128)(2,1)S(1)}, bf16[128,1280]{1,0:T(8,128)(2,1)S(1)}, u32[]{:S(2)}, u32[]{:S(2)}) collective-permute-start(bf16[128,1280]{1,0:T(8,128)(2,1)S(1)} %collective-permute-done.1.refs_1_), channel_id=1, source_target_pairs={{0,1},{1,2},{2,3},{3,4},{4,5},{5,6},{6,7},{7,0},{8,15},{9,8},{10,9... | collective-permute-start | bytes 983048 | tf_op jit(solution)/shard_map/ppermute | solution.py:328
  42.8 32.3 %copy-start.2 = (bf16[2,128,1280]{2,1,0:T(8,128)(2,1)S(1)}, bf16[2,128,1280]{2,1,0:T(8,128)(2,1)}, u32[]{:S(2)}) copy-start(bf16[2,128,1280]{2,1,0:T(8,128)(2,1)} %get-tuple-element.33.weights) | copy-start | bytes 1966084
  42.8 28.0 %all-to-all-start.1 = ((bf16[8,256,128]{2,1,0:T(8,128)(2,1)}), bf16[8,256,128]{2,1,0:T(8,128)(2,1)S(1)}, u32[]{:S(2)}, u32[]{:S(2)}) async-start(bf16[8,256,128]{2,1,0:T(8,128)(2,1)} %get-tuple-element.32), calls=%async_computation.1 | async-start | bytes 1048576 | tf_op jit(solution)/shard_map/all_to_all | solution.py:309
  49.6 17.7 %collective-permute-start.3 = (bf16[128,1280]{1,0:T(8,128)(2,1)S(1)}, bf16[128,1280]{1,0:T(8,128)(2,1)S(1)}, u32[]{:S(2)}, u32[]{:S(2)}) collective-permute-start(bf16[128,1280]{1,0:T(8,128)(2,1)S(1)} %collective-permute-done.2.refs_2_), channel_id=1, source_target_pairs={{0,1},{1,2},{2,3},{3,4},{4,5},{5,6},{6,7},{7,0},{8,15},{9,8},{10,9... | collective-permute-start | bytes 983048 | tf_op jit(solution)/shard_map/ppermute | solution.py:328
  54.1 16.6 %collective-permute-start.5 = (bf16[128,1280]{1,0:T(8,128)(2,1)S(1)}, bf16[128,1280]{1,0:T(8,128)(2,1)}, u32[]{:S(2)}, u32[]{:S(2)}) collective-permute-start(bf16[128,1280]{1,0:T(8,128)(2,1)S(1)} %collective-permute-done.1.refs_1_), channel_id=1, source_target_pairs={{0,8},{8,0},{1,9},{9,1},{2,10},{10,2},{3,11},{11,3},{4,12},{12,4},... | collective-permute-start | bytes 983048 | tf_op jit(solution)/shard_map/ppermute | solution.py:287
  56.1 14.7 %collective-permute-start.6 = (bf16[128,1280]{1,0:T(8,128)(2,1)S(1)}, bf16[128,1280]{1,0:T(8,128)(2,1)}, u32[]{:S(2)}, u32[]{:S(2)}) collective-permute-start(bf16[128,1280]{1,0:T(8,128)(2,1)S(1)} %collective-permute-done.2.refs_2_), channel_id=1, source_target_pairs={{0,8},{8,0},{1,9},{9,1},{2,10},{10,2},{3,11},{11,3},{4,12},{12,4},... | collective-permute-start | bytes 983048 | tf_op jit(solution)/shard_map/ppermute | solution.py:287
  58.5 16.5 %collective-permute-start.4 = (bf16[128,1280]{1,0:T(8,128)(2,1)S(1)}, bf16[128,1280]{1,0:T(8,128)(2,1)}, u32[]{:S(2)}, u32[]{:S(2)}) collective-permute-start(bf16[128,1280]{1,0:T(8,128)(2,1)S(1)} %collective-permute-done.2.refs_2_), channel_id=1, source_target_pairs={{0,2},{1,3},{2,4},{3,5},{4,6},{5,7},{6,0},{7,1},{8,14},{9,15},{10,... | collective-permute-start | bytes 983048 | tf_op jit(solution)/shard_map/ppermute | solution.py:328
  67.2 7.8 %collective-permute-start.7 = (bf16[128,1280]{1,0:T(8,128)(2,1)S(1)}, bf16[128,1280]{1,0:T(8,128)(2,1)}, u32[]{:S(2)}, u32[]{:S(2)}) collective-permute-start(bf16[128,1280]{1,0:T(8,128)(2,1)S(1)} %collective-permute-done.3.refs_3_), channel_id=1, source_target_pairs={{0,8},{8,0},{1,9},{9,1},{2,10},{10,2},{3,11},{11,3},{4,12},{12,4},... | collective-permute-start | bytes 983048 | tf_op jit(solution)/shard_map/ppermute | solution.py:287
  105.0 22.0 %all-to-all-start.3 = ((bf16[8,32,1280]{2,1,0:T(8,128)(2,1)}), bf16[8,32,1280]{2,1,0:T(8,128)(2,1)S(1)}, u32[]{:S(2)}, u32[]{:S(2)}) async-start(bf16[8,32,1280]{2,1,0:T(8,128)(2,1)} %shard_map.86), calls=%async_computation.3 | async-start | bytes 1310720 | tf_op jit(solution)/shard_map/all_to_all | solution.py:309
  108.5 18.5 %copy-start.1 = (bf16[256,1280]{1,0:T(8,128)(2,1)S(1)}, bf16[256,1280]{1,0:T(8,128)(2,1)}, u32[]{:S(2)}) copy-start(bf16[256,1280]{1,0:T(8,128)(2,1)} %get-tuple-element.42.normed) | copy-start | bytes 1966084
  108.6 18.5 %copy-start.3 = (f32[2,256,256]{2,1,0:T(8,128)S(1)}, f32[2,256,256]{2,1,0:T(8,128)}, u32[]{:S(2)}) copy-start(f32[2,256,256]{2,1,0:T(8,128)} %get-tuple-element.40.probs) | copy-start | bytes 1572868
  108.6 18.5 %copy-start.6 = (bf16[256,128]{1,0:T(8,128)(2,1)S(1)}, bf16[256,128]{1,0:T(8,128)(2,1)}, u32[]{:S(2)}) copy-start(bf16[256,128]{1,0:T(8,128)(2,1)} %get-tuple-element.38.queries) | copy-start | bytes 196612
  108.6 18.5 %copy-start.7 = (bf16[256,128]{1,0:T(8,128)(2,1)S(1)}, bf16[256,128]{1,0:T(8,128)(2,1)}, u32[]{:S(2)}) copy-start(bf16[256,128]{1,0:T(8,128)(2,1)} %get-tuple-element.39.values) | copy-start | bytes 196612
  108.6 18.5 %copy-start.8 = (bf16[256,128]{1,0:T(8,128)(2,1)S(1)}, bf16[256,128]{1,0:T(8,128)(2,1)}, u32[]{:S(2)}) copy-start(bf16[256,128]{1,0:T(8,128)(2,1)} %get-tuple-element.41.context) | copy-start | bytes 196612
  111.3 22.3 %collective-permute-start.9 = (bf16[384,1280]{1,0:T(8,128)(2,1)}, bf16[384,1280]{1,0:T(8,128)(2,1)S(1)}, u32[]{:S(2)}, u32[]{:S(2)}) collective-permute-start(bf16[384,1280]{1,0:T(8,128)(2,1)} %shard_map.88.dec_term), channel_id=1, source_target_pairs={{0,8},{1,9},{2,10},{3,11},{4,12},{5,13},{6,14},{7,15},{16,24},{17,... | collective-permute-start | bytes 2949128 | tf_op jit(solution)/shard_map/ppermute | solution.py:409
  129.0 6.8 %collective-permute-start.8 = (bf16[384,1280]{1,0:T(8,128)(2,1)S(1)}, bf16[384,1280]{1,0:T(8,128)(2,1)S(1)}, u32[]{:S(2)}, u32[]{:S(2)}) collective-permute-start(bf16[384,1280]{1,0:T(8,128)(2,1)S(1)} %shard_map.87.enc_term), channel_id=1, source_target_pairs={{8,0},{9,1},{10,2},{11,3},{12,4},{13,5},{14,6},{15,7},{24,16},{25,... | collective-permute-start | bytes 2949128 | tf_op jit(solution)/shard_map/ppermute | solution.py:410

commit v14 on v13

--- a/solution.py
+++ b/solution.py
@@ -105,29 +105,42 @@
         picked[kind - 1] = jnp.where(first, other[kind], own[kind])
 
 
-def dec_kernel(
-    core, place, frame_lens, token_lens, x, context, weights, token_queries, token_grads, gains, biases,
-    *refs,
-):
+def shard_products(core, place, context, pairs):
+    first = core[0] == 0
     devices = context.shape[0]
-    out_shards, refs = refs[:devices], refs[devices:]
-    partial, states, normed, key_grad, value_grad, dec_context, scratch = refs
-    first = core[0] == 0
-    rows = x.shape[0]
-    steps = devices // 2
-    passed, swapped = out_shards[: steps + 1], out_shards[steps + 1 :]
 
     def context_at(back):
         return context[(place[0] + jnp.where(first, devices - back, back)) % devices]
 
-    pairs = [(0, passed[0], steps, passed[steps])]
-    for back in range(1, steps):
-        pairs.append((back, passed[back], devices - back, swapped[back - 1]))
-    summed = x[...].astype(jnp.float32)
+    summed = 0.0
     for back, shard, far_back, far_shard in pairs:
         left = jnp.concatenate([context_at(back), context_at(far_back)], axis=1)
         right = jnp.concatenate([shard[...], far_shard[...]], axis=0)
         summed = summed + dot_nn(left, right)
+    return summed
+
+
+def half_states_kernel(core, place, x, context, *refs):
+    states, shards_in = refs[-1], refs[:-1]
+    devices = context.shape[0]
+    count = len(shards_in) // 2
+    pairs = [
+        (back + 1, shards_in[back], devices - 1 - back, shards_in[count + back])
+        for back in range(count)
+    ]
+    states[...] = x[...].astype(jnp.float32) + shard_products(core, place, context, pairs)
+
+
+def dec_kernel(
+    core, place, frame_lens, token_lens, half_states, context, weights, token_queries, token_grads,
+    gains, biases, *refs,
+):
+    near, near_swapped, own_shard, far, partial, states, normed = refs[:7]
+    key_grad, value_grad, dec_context, scratch = refs[7:]
+    rows = half_states.shape[0]
+    steps = context.shape[0] // 2
+    pairs = [(0, own_shard, steps, far), (steps - 1, near, steps + 1, near_swapped)]
+    summed = half_states[...] + shard_products(core, place, context, pairs)
     scratch[...] = summed
     all_states = scratch[...].astype(jnp.bfloat16)
     shard = states.shape[0]
@@ -332,7 +345,6 @@
         passed.append(passing(passed[-1], 1))
     passed.append(passing(passed[-2], 2))
     swapped = [swap(block) for block in passed[1:-1]]
-    out_shards = passed + swapped
     enc_full = exchange(copies).reshape(rows, features)
 
     token_queries, token_grads, dec_weights = call(
@@ -364,6 +376,12 @@
         cost=pl.CostEstimate(flops=3_000_000_000, transcendentals=0, bytes_accessed=0),
     )
     context_full = exchange(context_copies)
+    half_states = call(
+        half_states_kernel,
+        [((rows, features), f32)],
+        (core_id, place),
+        (enc_full, context_full, *passed[1:-2], *swapped[:-1]),
+    )
     partial, states, state_normed, dec_key_grad, dec_value_grad, dec_context = call(
         dec_kernel,
         [
@@ -376,12 +394,12 @@
         ],
         (core_id, place, frame_lengths, token_lengths),
         (
-            enc_full, context_full, dec_weights, token_queries, token_grads,
-            norm_gains, norm_biases, *out_shards,
+            half_states, context_full, dec_weights, token_queries, token_grads,
+            norm_gains, norm_biases, passed[-2], swapped[-1], shard, passed[-1],
         ),
         scratch=[pltpu.VMEM((rows, features), f32)],
         kept=(2, 3, 4, 5),
-        read=(14,),
+        read=(8,),
     )
     pieces = exchange(partial.reshape(mp, shard_rows, features))
     whole = [((3 * head_cols, features), bf16)]

time: 196 us -> 195 us (level)
    pallas_call x11 -> x12, Pallas kernels: 23.2 us -> 22.5 us  [call(): pl.pallas_call(kernel, grid=(1,), out_shape=[out(index, *what) for index,...]
where the time goes in v14:
time: 195 us; the launch traced here: 192 us
  blocking collectives  78 us (40%)
  starting transfers between devices  53.2 us (27%)
  waiting for transfers between devices  37.1 us (19%)
  Pallas kernels  22.5 us (12%)
    all_to_all x4, blocking collectives, exchange(): return lax.all_to_all(blocks, axis, 0, 0, axis_index_groups=groups)  78 us
    all_to_all x3, waiting for transfers between devices, exchange(): return lax.all_to_all(blocks, axis, 0, 0, axis_index_groups=groups)  26.7 us
    pallas_call x12, Pallas kernels, call(): pl.pallas_call(kernel, grid=(1,), out_shape=[out(index, *what) for index,...  22.5 us
    ppermute x4, starting transfers between devices, swap(): return lax.ppermute(block, 'segment', [(0, 1), (1, 0)])  16.7 us
    ppermute x4, starting transfers between devices, passing(): return lax.ppermute(block, ('segment', 'mp'), up + down)  15.6 us
    all_to_all x3, starting transfers between devices, exchange(): return lax.all_to_all(blocks, axis, 0, 0, axis_index_groups=groups)  14.9 us
    ppermute x4, waiting for transfers between devices, passing(): return lax.ppermute(block, ('segment', 'mp'), up + down)  8.32 us
    ppermute x1, starting transfers between devices, shards(): enc_sent = lax.ppermute(enc_term, 'segment', [(1, 0)])  4.69 us
  transfers between devices with their start and end apart: 13, of which 5 were waited for; matrix products, arithmetic and copies ran while one was open for 1% of the time, Pallas kernels for 6%

profile of v14, /device:TPU:1, one launch (start us, length us, event | category | flops | bytes accessed | tf_op | source)
XLA Modules:
  0.0 192.2 jit_solution(4701883208815425709)
XLA Ops:
  0.0 1.9 shard_map.82
  1.9 8.9 %collective-permute-start = (bf16[4,128,1280]{2,1,0:T(8,128)(2,1)}, bf16[4,128,1280]{2,1,0:T(8,128)(2,1)}, u32[]{:S(2)}, u32[]{:S(2)}) collective-permute-start(bf16[4,128,1280]{2,1,0:T(8,128)(2,1)} %bitcast.16), channel_id=1, source_target_pairs={{0,8},{8,0},{1,9},{9,1},{2,10},{10,2},{3,11},{11,3},{4,12},{12,4},... | collective-permute-start | bytes 3932168 | tf_op jit(solution)/shard_map/ppermute | solution.py:300
  10.8 4.7 %all-to-all-start = ((bf16[8,32,1280]{2,1,0:T(8,128)(2,1)}), bf16[8,32,1280]{2,1,0:T(8,128)(2,1)S(1)}, u32[]{:S(2)}, u32[]{:S(2)}) async-start(bf16[8,32,1280]{2,1,0:T(8,128)(2,1)} %shard_map.82), calls=%async_computation | async-start | bytes 1310720 | tf_op jit(solution)/shard_map/all_to_all | solution.py:322
  15.5 0.0 collective-permute-done.other
  15.5 0.0 copy-done
  15.5 1.0 fusion.refs_2_.out_shard
  16.5 0.0 copy-start.11
  16.5 4.6 %collective-permute-start.1 = (bf16[128,1280]{1,0:T(8,128)(2,1)S(1)}, bf16[128,1280]{1,0:T(8,128)(2,1)S(1)}, u32[]{:S(2)}, u32[]{:S(2)}) collective-permute-start(bf16[128,1280]{1,0:T(8,128)(2,1)S(1)} %fusion.refs_2_.out_shard), channel_id=1, source_target_pairs={{0,1},{1,2},{2,3},{3,4},{4,5},{5,6},{6,7},{7,0},{8,15},{9,8},{10,9... | collective-permute-start | bytes 983048 | tf_op jit(solution)/shard_map/ppermute | solution.py:341
  21.1 0.0 copy-done.4
  21.1 0.0 copy-done.5
  21.1 2.9 %shard_map.83 = (bf16[64,128]{1,0:T(8,128)(2,1)}, bf16[64,128]{1,0:T(8,128)(2,1)}, bf16[2,128,1280]{2,1,0:T(8,128)(2,1)}) custom-call(s32[1]{0:T(128)} %bitcast.core, bf16[2,64,1280]{2,1,0:T(8,128)(2,1)} %tokens.1, bf16[2,64,1280]{2,1,0:T(8,128)(2,1)} %upstream.3, bf16[4,128,1280]{2,1,0:T(8,128)(2,1)S(1)} %bitcast.18, ...), custom_call_target="tpu_custom_call" | custom-call | tf_op jit(solution)/shard_map/pallas_call | solution.py:282
  24.0 12.3 %all-to-all-done = bf16[8,32,1280]{2,1,0:T(8,128)(2,1)S(1)} async-done(((bf16[8,32,1280]{2,1,0:T(8,128)(2,1)}), bf16[8,32,1280]{2,1,0:T(8,128)(2,1)S(1)}, u32[]{:S(2)}, u32[]{:S(2)}) %all-to-all-start) | async-done | bytes 655392 | tf_op jit(solution)/shard_map/all_to_all | solution.py:322
  36.3 0.0 collective-permute-done.1.refs_0_
  36.3 2.5 %collective-permute-start.2 = (bf16[128,1280]{1,0:T(8,128)(2,1)S(1)}, bf16[128,1280]{1,0:T(8,128)(2,1)S(1)}, u32[]{:S(2)}, u32[]{:S(2)}) collective-permute-start(bf16[128,1280]{1,0:T(8,128)(2,1)S(1)} %collective-permute-done.1.refs_0_), channel_id=1, source_target_pairs={{0,1},{1,2},{2,3},{3,4},{4,5},{5,6},{6,7},{7,0},{8,15},{9,8},{10,9... | collective-permute-start | bytes 983048 | tf_op jit(solution)/shard_map/ppermute | solution.py:341
  38.8 0.0 copy-done.11
  38.8 3.9 %shard_map.84 = (bf16[256,1280]{1,0:T(8,128)(2,1)}, bf16[256,128]{1,0:T(8,128)(2,1)}, bf16[256,128]{1,0:T(8,128)(2,1)}, bf16[256,128]{1,0:T(8,128)(2,1)}, bf16[8...) custom-call(s32[1]{0:T(128)} %bitcast.core, s32[2,1,4]{2,1,0:T(1,128)S(1)} %copy-done.11, bf16[256,1280]{1,0:T(8,128)(2,1)S(1)} %bitcast.14, ...), custom_call_target="tpu_custom_call" | custom-call | flops 3000000000 | tf_op jit(solution)/shard_map/pallas_call | solution.py:282
  42.7 6.6 %all-to-all-start.1 = ((bf16[8,256,128]{2,1,0:T(8,128)(2,1)}), bf16[8,256,128]{2,1,0:T(8,128)(2,1)S(1)}, u32[]{:S(2)}, u32[]{:S(2)}) async-start(bf16[8,256,128]{2,1,0:T(8,128)(2,1)} %get-tuple-element.32), calls=%async_computation.1 | async-start | bytes 1048576 | tf_op jit(solution)/shard_map/all_to_all | solution.py:322
  49.4 0.0 collective-permute-done.2.refs_1_
  49.4 4.6 %collective-permute-start.5 = (bf16[128,1280]{1,0:T(8,128)(2,1)S(1)}, bf16[128,1280]{1,0:T(8,128)(2,1)S(1)}, u32[]{:S(2)}, u32[]{:S(2)}) collective-permute-start(bf16[128,1280]{1,0:T(8,128)(2,1)S(1)} %collective-permute-done.2.refs_1_), channel_id=1, source_target_pairs={{0,1},{1,2},{2,3},{3,4},{4,5},{5,6},{6,7},{7,0},{8,15},{9,8},{10,9... | collective-permute-start | bytes 983048 | tf_op jit(solution)/shard_map/ppermute | solution.py:341
  54.0 1.9 collective-permute-start.3
  55.9 2.4 %collective-permute-start.4 = (bf16[128,1280]{1,0:T(8,128)(2,1)S(1)}, bf16[128,1280]{1,0:T(8,128)(2,1)S(1)}, u32[]{:S(2)}, u32[]{:S(2)}) collective-permute-start(bf16[128,1280]{1,0:T(8,128)(2,1)S(1)} %collective-permute-done.2.refs_1_), channel_id=1, source_target_pairs={{0,8},{8,0},{1,9},{9,1},{2,10},{10,2},{3,11},{11,3},{4,12},{12,4},... | collective-permute-start | bytes 983048 | tf_op jit(solution)/shard_map/ppermute | solution.py:300
  58.3 4.0 %collective-permute-start.7 = (bf16[128,1280]{1,0:T(8,128)(2,1)S(1)}, bf16[128,1280]{1,0:T(8,128)(2,1)S(1)}, u32[]{:S(2)}, u32[]{:S(2)}) collective-permute-start(bf16[128,1280]{1,0:T(8,128)(2,1)S(1)} %collective-permute-done.2.refs_1_), channel_id=1, source_target_pairs={{0,2},{1,3},{2,4},{3,5},{4,6},{5,7},{6,0},{7,1},{8,14},{9,15},{10,... | collective-permute-start | bytes 983048 | tf_op jit(solution)/shard_map/ppermute | solution.py:341
  62.3 4.7 %collective-permute-done.5.refs_0_ = bf16[128,1280]{1,0:T(8,128)(2,1)S(1)} collective-permute-done((bf16[128,1280]{1,0:T(8,128)(2,1)S(1)}, bf16[128,1280]{1,0:T(8,128)(2,1)S(1)}, u32[]{:S(2)}, u32[]{:S(2)}) %collective-permute-start.5) | collective-permute-done | bytes 327712 | tf_op jit(solution)/shard_map/ppermute | solution.py:341
  67.1 3.5 %collective-permute-start.6 = (bf16[128,1280]{1,0:T(8,128)(2,1)S(1)}, bf16[128,1280]{1,0:T(8,128)(2,1)}, u32[]{:S(2)}, u32[]{:S(2)}) collective-permute-start(bf16[128,1280]{1,0:T(8,128)(2,1)S(1)} %collective-permute-done.5.refs_0_), channel_id=1, source_target_pairs={{0,8},{8,0},{1,9},{9,1},{2,10},{10,2},{3,11},{11,3},{4,12},{12,4},... | collective-permute-start | bytes 983048 | tf_op jit(solution)/shard_map/ppermute | solution.py:300
  70.6 0.0 collective-permute-done.3.refs_2_
  70.6 0.0 all-to-all-done.1.context
  70.6 0.0 collective-permute-done.4.refs_3_
  70.6 0.0 copy-start.2
  70.6 0.0 copy-start.9
  70.6 0.0 copy-start.10
  70.6 0.0 copy-start.12
  70.6 0.5 shard_map.85.half_states
  71.2 3.6 %collective-permute-done.7.refs_3_ = bf16[128,1280]{1,0:T(8,128)(2,1)S(1)} collective-permute-done((bf16[128,1280]{1,0:T(8,128)(2,1)S(1)}, bf16[128,1280]{1,0:T(8,128)(2,1)S(1)}, u32[]{:S(2)}, u32[]{:S(2)}) %collective-permute-start.7) | collective-permute-done | bytes 327712 | tf_op jit(solution)/shard_map/ppermute | solution.py:341
  74.7 0.0 collective-permute-done.6.refs_1_
  74.7 0.0 copy-done.2
  74.7 0.0 copy-done.9
  74.7 0.0 copy-done.10
  74.8 0.0 copy-done.12
  74.8 4.1 %shard_map.86 = (bf16[256,1280]{1,0:T(8,128)(2,1)S(1)}, bf16[32,1280]{1,0:T(8,128)(2,1)S(1)}, bf16[256,1280]{1,0:T(8,128)(2,1)}, bf16[256,128]{1,0:T(8,128)(2,1)...) custom-call(s32[1]{0:T(128)} %bitcast.core, s32[1]{0:T(128)} %bitcast.1.place, s32[2,1,4]{2,1,0:T(1,128)S(1)} %copy-done.11, ...), custom_call_target="tpu_custom_call" | custom-call | tf_op jit(solution)/shard_map/pallas_call | solution.py:282
  78.9 23.4 %all_to_all.35.pieces = bf16[8,32,1280]{2,1,0:T(8,128)(2,1)S(1)} all-to-all(bf16[8,32,1280]{2,1,0:T(8,128)(2,1)S(1)} %bitcast.20), channel_id=1, replica_groups=mesh['dp'=32,'segment'=2,'mp'=8] {'mp'}, dimensions={0} | all-to-all | bytes 1310720 | tf_op jit(solution)/shard_map/all_to_all | solution.py:322
  102.2 1.2 shard_map.87
  103.5 3.5 %all-to-all-start.3 = ((bf16[8,32,1280]{2,1,0:T(8,128)(2,1)}), bf16[8,32,1280]{2,1,0:T(8,128)(2,1)S(1)}, u32[]{:S(2)}, u32[]{:S(2)}) async-start(bf16[8,32,1280]{2,1,0:T(8,128)(2,1)} %shard_map.87), calls=%async_computation.3 | async-start | bytes 1310720 | tf_op jit(solution)/shard_map/all_to_all | solution.py:322
  107.0 0.0 copy-start.1
  107.0 0.0 copy-start.3
  107.0 0.0 copy-start.6
  107.0 0.0 copy-start.7
  107.0 0.0 copy-start.8
  107.1 2.7 %shard_map.89.dec_term = bf16[384,1280]{1,0:T(8,128)(2,1)} custom-call(s32[1]{0:T(128)} %bitcast.core, bf16[256,128]{1,0:T(8,128)(2,1)} %get-tuple-element.43.key_grad, bf16[256,128]{1,0:T(8,128)(2,1)} %get-tuple-element.44.value_grad, bf16[64,128]{1,0:T(8,128)(2,1)} %get-tuple-element.45.context, bf16[256,1280]{1,0:T(8,128)(2,1)} %get-tuple-element.46.normed, ...), custom_call_target="tpu_custom_call" | custom-call | tf_op jit(solution)/shard_map/pallas_call | solution.py:282
  109.8 1.3 collective-permute-start.9
  111.1 14.4 %all-to-all-done.3 = bf16[8,32,1280]{2,1,0:T(8,128)(2,1)S(1)} async-done(((bf16[8,32,1280]{2,1,0:T(8,128)(2,1)}), bf16[8,32,1280]{2,1,0:T(8,128)(2,1)S(1)}, u32[]{:S(2)}, u32[]{:S(2)}) %all-to-all-start.3) | async-done | bytes 655392 | tf_op jit(solution)/shard_map/all_to_all | solution.py:322
  125.5 0.0 copy-done.6
  125.5 0.0 copy-done.7
  125.5 0.0 copy-done.8
  125.5 1.9 shard_map.88.enc_term
  127.4 4.7 %collective-permute-start.8 = (bf16[384,1280]{1,0:T(8,128)(2,1)S(1)}, bf16[384,1280]{1,0:T(8,128)(2,1)S(1)}, u32[]{:S(2)}, u32[]{:S(2)}) collective-permute-start(bf16[384,1280]{1,0:T(8,128)(2,1)S(1)} %shard_map.88.enc_term), channel_id=1, source_target_pairs={{8,0},{9,1},{10,2},{11,3},{12,4},{13,5},{14,6},{15,7},{24,16},{25,... | collective-permute-start | bytes 2949128 | tf_op jit(solution)/shard_map/ppermute | solution.py:428
  132.1 0.0 collective-permute-done.9.dec_sent
  132.1 2.1 %collective-permute-done.8.enc_sent = bf16[384,1280]{1,0:T(8,128)(2,1)S(1)} collective-permute-done((bf16[384,1280]{1,0:T(8,128)(2,1)S(1)}, bf16[384,1280]{1,0:T(8,128)(2,1)S(1)}, u32[]{:S(2)}, u32[]{:S(2)}) %collective-permute-start.8) | collective-permute-done | bytes 983072 | tf_op jit(solution)/shard_map/ppermute | solution.py:428
  134.2 1.7 shard_map.90
  135.9 19.3 %all_to_all.36.pieces = bf16[8,60,8,128]{3,2,1,0:T(8,128)(2,1)S(1)} all-to-all(bf16[8,60,8,128]{3,2,1,0:T(8,128)(2,1)S(1)} %bitcast.11), channel_id=1, replica_groups={{0,16,128,144,256,272,384,400},{32,48,160,176,288,304,416,432},{64,80,1..., dimensions={0} | all-to-all | bytes 1966080 | tf_op jit(solution)/shard_map/all_to_all | solution.py:322
  155.2 0.1 shard_map.91
  155.4 18.3 %all_to_all.37.pieces = bf16[4,60,8,128]{3,2,1,0:T(8,128)(2,1)S(1)} all-to-all(bf16[4,60,8,128]{3,2,1,0:T(8,128)(2,1)S(1)} %shard_map.91), channel_id=1, replica_groups={{0,32,64,96},{16,48,80,112},{128,160,192,224},{144,176,208,240},{256,28..., dimensions={0} | all-to-all | bytes 983040 | tf_op jit(solution)/shard_map/all_to_all | solution.py:322
  173.7 0.1 shard_map.92
  173.7 17.1 %all_to_all.38 = bf16[8,60,8,128]{3,2,1,0:T(8,128)(2,1)S(1)} all-to-all(bf16[8,60,8,128]{3,2,1,0:T(8,128)(2,1)S(1)} %shard_map.92), channel_id=1, replica_groups={{0,16,128,144,256,272,384,400},{32,48,160,176,288,304,416,432},{64,80,1..., dimensions={0} | all-to-all | bytes 1966080 | tf_op jit(solution)/shard_map/all_to_all | solution.py:322
  190.8 1.4 shard_map.93
  (5 shorter events, 0.0 us)
Async XLA Ops:
  0.0 15.5 %copy-start = (bf16[1,4,128,1280]{3,2,1,0:T(8,128)(2,1)S(1)}, bf16[1,4,128,1280]{3,2,1,0:T(8,128)(2,1)}, u32[]{:S(2)}) copy-start(bf16[1,4,128,1280]{3,2,1,0:T(8,128)(2,1)} %param.13) | copy-start | bytes 3932164
  1.9 19.2 %copy-start.4 = (f32[3,1280]{1,0:T(4,128)S(1)}, f32[3,1280]{1,0:T(4,128)}, u32[]{:S(2)}) copy-start(f32[3,1280]{1,0:T(4,128)} %gains.7) | copy-start | bytes 46084
  1.9 19.2 %copy-start.5 = (f32[3,1280]{1,0:T(4,128)S(1)}, f32[3,1280]{1,0:T(4,128)}, u32[]{:S(2)}) copy-start(f32[3,1280]{1,0:T(4,128)} %biases.5) | copy-start | bytes 46084
  1.9 13.6 %collective-permute-start = (bf16[4,128,1280]{2,1,0:T(8,128)(2,1)}, bf16[4,128,1280]{2,1,0:T(8,128)(2,1)}, u32[]{:S(2)}, u32[]{:S(2)}) collective-permute-start(bf16[4,128,1280]{2,1,0:T(8,128)(2,1)} %bitcast.16), channel_id=1, source_target_pairs={{0,8},{8,0},{1,9},{9,1},{2,10},{10,2},{3,11},{11,3},{4,12},{12,4},... | collective-permute-start | bytes 3932168 | tf_op jit(solution)/shard_map/ppermute | solution.py:300
  10.8 25.5 %all-to-all-start = ((bf16[8,32,1280]{2,1,0:T(8,128)(2,1)}), bf16[8,32,1280]{2,1,0:T(8,128)(2,1)S(1)}, u32[]{:S(2)}, u32[]{:S(2)}) async-start(bf16[8,32,1280]{2,1,0:T(8,128)(2,1)} %shard_map.82), calls=%async_computation | async-start | bytes 1310720 | tf_op jit(solution)/shard_map/all_to_all | solution.py:322
  16.5 22.3 %copy-start.11 = (s32[2,1,4]{2,1,0:T(1,128)S(1)}, s32[2,1,4]{2,1,0:T(1,128)}, u32[]{:S(2)}) copy-start(s32[2,1,4]{2,1,0:T(1,128)} %frame_lens.1) | copy-start | bytes 100
  16.5 19.8 %collective-permute-start.1 = (bf16[128,1280]{1,0:T(8,128)(2,1)S(1)}, bf16[128,1280]{1,0:T(8,128)(2,1)S(1)}, u32[]{:S(2)}, u32[]{:S(2)}) collective-permute-start(bf16[128,1280]{1,0:T(8,128)(2,1)S(1)} %fusion.refs_2_.out_shard), channel_id=1, source_target_pairs={{0,1},{1,2},{2,3},{3,4},{4,5},{5,6},{6,7},{7,0},{8,15},{9,8},{10,9... | collective-permute-start | bytes 983048 | tf_op jit(solution)/shard_map/ppermute | solution.py:341
  36.3 13.1 %collective-permute-start.2 = (bf16[128,1280]{1,0:T(8,128)(2,1)S(1)}, bf16[128,1280]{1,0:T(8,128)(2,1)S(1)}, u32[]{:S(2)}, u32[]{:S(2)}) collective-permute-start(bf16[128,1280]{1,0:T(8,128)(2,1)S(1)} %collective-permute-done.1.refs_0_), channel_id=1, source_target_pairs={{0,1},{1,2},{2,3},{3,4},{4,5},{5,6},{6,7},{7,0},{8,15},{9,8},{10,9... | collective-permute-start | bytes 983048 | tf_op jit(solution)/shard_map/ppermute | solution.py:341
  42.7 27.8 %all-to-all-start.1 = ((bf16[8,256,128]{2,1,0:T(8,128)(2,1)}), bf16[8,256,128]{2,1,0:T(8,128)(2,1)S(1)}, u32[]{:S(2)}, u32[]{:S(2)}) async-start(bf16[8,256,128]{2,1,0:T(8,128)(2,1)} %get-tuple-element.32), calls=%async_computation.1 | async-start | bytes 1048576 | tf_op jit(solution)/shard_map/all_to_all | solution.py:322
  49.4 17.7 %collective-permute-start.5 = (bf16[128,1280]{1,0:T(8,128)(2,1)S(1)}, bf16[128,1280]{1,0:T(8,128)(2,1)S(1)}, u32[]{:S(2)}, u32[]{:S(2)}) collective-permute-start(bf16[128,1280]{1,0:T(8,128)(2,1)S(1)} %collective-permute-done.2.refs_1_), channel_id=1, source_target_pairs={{0,1},{1,2},{2,3},{3,4},{4,5},{5,6},{6,7},{7,0},{8,15},{9,8},{10,9... | collective-permute-start | bytes 983048 | tf_op jit(solution)/shard_map/ppermute | solution.py:341
  54.0 16.6 %collective-permute-start.3 = (bf16[128,1280]{1,0:T(8,128)(2,1)S(1)}, bf16[128,1280]{1,0:T(8,128)(2,1)S(1)}, u32[]{:S(2)}, u32[]{:S(2)}) collective-permute-start(bf16[128,1280]{1,0:T(8,128)(2,1)S(1)} %collective-permute-done.1.refs_0_), channel_id=1, source_target_pairs={{0,8},{8,0},{1,9},{9,1},{2,10},{10,2},{3,11},{11,3},{4,12},{12,4},... | collective-permute-start | bytes 983048 | tf_op jit(solution)/shard_map/ppermute | solution.py:300
  55.9 14.7 %collective-permute-start.4 = (bf16[128,1280]{1,0:T(8,128)(2,1)S(1)}, bf16[128,1280]{1,0:T(8,128)(2,1)S(1)}, u32[]{:S(2)}, u32[]{:S(2)}) collective-permute-start(bf16[128,1280]{1,0:T(8,128)(2,1)S(1)} %collective-permute-done.2.refs_1_), channel_id=1, source_target_pairs={{0,8},{8,0},{1,9},{9,1},{2,10},{10,2},{3,11},{11,3},{4,12},{12,4},... | collective-permute-start | bytes 983048 | tf_op jit(solution)/shard_map/ppermute | solution.py:300
  58.3 16.4 %collective-permute-start.7 = (bf16[128,1280]{1,0:T(8,128)(2,1)S(1)}, bf16[128,1280]{1,0:T(8,128)(2,1)S(1)}, u32[]{:S(2)}, u32[]{:S(2)}) collective-permute-start(bf16[128,1280]{1,0:T(8,128)(2,1)S(1)} %collective-permute-done.2.refs_1_), channel_id=1, source_target_pairs={{0,2},{1,3},{2,4},{3,5},{4,6},{5,7},{6,0},{7,1},{8,14},{9,15},{10,... | collective-permute-start | bytes 983048 | tf_op jit(solution)/shard_map/ppermute | solution.py:341
  67.1 7.7 %collective-permute-start.6 = (bf16[128,1280]{1,0:T(8,128)(2,1)S(1)}, bf16[128,1280]{1,0:T(8,128)(2,1)}, u32[]{:S(2)}, u32[]{:S(2)}) collective-permute-start(bf16[128,1280]{1,0:T(8,128)(2,1)S(1)} %collective-permute-done.5.refs_0_), channel_id=1, source_target_pairs={{0,8},{8,0},{1,9},{9,1},{2,10},{10,2},{3,11},{11,3},{4,12},{12,4},... | collective-permute-start | bytes 983048 | tf_op jit(solution)/shard_map/ppermute | solution.py:300
  70.6 4.1 %copy-start.2 = (bf16[2,128,1280]{2,1,0:T(8,128)(2,1)S(1)}, bf16[2,128,1280]{2,1,0:T(8,128)(2,1)}, u32[]{:S(2)}) copy-start(bf16[2,128,1280]{2,1,0:T(8,128)(2,1)} %get-tuple-element.33.weights) | copy-start | bytes 1966084
  70.6 4.1 %copy-start.9 = (bf16[64,128]{1,0:T(8,128)(2,1)S(1)}, bf16[64,128]{1,0:T(8,128)(2,1)}, u32[]{:S(2)}) copy-start(bf16[64,128]{1,0:T(8,128)(2,1)} %get-tuple-element.34.token_queries) | copy-start | bytes 49156
  70.6 4.1 %copy-start.10 = (bf16[64,128]{1,0:T(8,128)(2,1)S(1)}, bf16[64,128]{1,0:T(8,128)(2,1)}, u32[]{:S(2)}) copy-start(bf16[64,128]{1,0:T(8,128)(2,1)} %get-tuple-element.35.token_grads) | copy-start | bytes 49156
  70.6 4.1 %copy-start.12 = (s32[2,1,4]{2,1,0:T(1,128)S(1)}, s32[2,1,4]{2,1,0:T(1,128)}, u32[]{:S(2)}) copy-start(s32[2,1,4]{2,1,0:T(1,128)} %token_lens.1) | copy-start | bytes 100
  103.5 22.0 %all-to-all-start.3 = ((bf16[8,32,1280]{2,1,0:T(8,128)(2,1)}), bf16[8,32,1280]{2,1,0:T(8,128)(2,1)S(1)}, u32[]{:S(2)}, u32[]{:S(2)}) async-start(bf16[8,32,1280]{2,1,0:T(8,128)(2,1)} %shard_map.87), calls=%async_computation.3 | async-start | bytes 1310720 | tf_op jit(solution)/shard_map/all_to_all | solution.py:322
  107.0 18.5 %copy-start.1 = (bf16[256,1280]{1,0:T(8,128)(2,1)S(1)}, bf16[256,1280]{1,0:T(8,128)(2,1)}, u32[]{:S(2)}) copy-start(bf16[256,1280]{1,0:T(8,128)(2,1)} %get-tuple-element.42.normed) | copy-start | bytes 1966084
  107.0 18.5 %copy-start.3 = (f32[2,256,256]{2,1,0:T(8,128)S(1)}, f32[2,256,256]{2,1,0:T(8,128)}, u32[]{:S(2)}) copy-start(f32[2,256,256]{2,1,0:T(8,128)} %get-tuple-element.40.probs) | copy-start | bytes 1572868
  107.0 18.5 %copy-start.6 = (bf16[256,128]{1,0:T(8,128)(2,1)S(1)}, bf16[256,128]{1,0:T(8,128)(2,1)}, u32[]{:S(2)}) copy-start(bf16[256,128]{1,0:T(8,128)(2,1)} %get-tuple-element.38.queries) | copy-start | bytes 196612
  107.0 18.5 %copy-start.7 = (bf16[256,128]{1,0:T(8,128)(2,1)S(1)}, bf16[256,128]{1,0:T(8,128)(2,1)}, u32[]{:S(2)}) copy-start(bf16[256,128]{1,0:T(8,128)(2,1)} %get-tuple-element.39.values) | copy-start | bytes 196612
  107.0 18.5 %copy-start.8 = (bf16[256,128]{1,0:T(8,128)(2,1)S(1)}, bf16[256,128]{1,0:T(8,128)(2,1)}, u32[]{:S(2)}) copy-start(bf16[256,128]{1,0:T(8,128)(2,1)} %get-tuple-element.41.context) | copy-start | bytes 196612
  109.8 22.3 %collective-permute-start.9 = (bf16[384,1280]{1,0:T(8,128)(2,1)}, bf16[384,1280]{1,0:T(8,128)(2,1)S(1)}, u32[]{:S(2)}, u32[]{:S(2)}) collective-permute-start(bf16[384,1280]{1,0:T(8,128)(2,1)} %shard_map.89.dec_term), channel_id=1, source_target_pairs={{0,8},{1,9},{2,10},{3,11},{4,12},{5,13},{6,14},{7,15},{16,24},{17,... | collective-permute-start | bytes 2949128 | tf_op jit(solution)/shard_map/ppermute | solution.py:427
  127.4 6.8 %collective-permute-start.8 = (bf16[384,1280]{1,0:T(8,128)(2,1)S(1)}, bf16[384,1280]{1,0:T(8,128)(2,1)S(1)}, u32[]{:S(2)}, u32[]{:S(2)}) collective-permute-start(bf16[384,1280]{1,0:T(8,128)(2,1)S(1)} %shard_map.88.enc_term), channel_id=1, source_target_pairs={{8,0},{9,1},{10,2},{11,3},{12,4},{13,5},{14,6},{15,7},{24,16},{25,... | collective-permute-start | bytes 2949128 | tf_op jit(solution)/shard_map/ppermute | solution.py:428

commit v15 on v14

--- a/solution.py
+++ b/solution.py
@@ -64,30 +64,40 @@
     return jnp.concatenate(parts, axis=1).astype(jnp.bfloat16)
 
 
-def enc_forward_kernel(
-    core, lengths, x, own, other, gains, biases, normed, queries, values, context, copies, probs
-):
+def enc_attention(core, lengths, x, own, other, gains, biases):
     first = core[0] == 0
     rows = x.shape[0]
-    normed_rows = layer_norm(x[...], gains[0:1, :], biases[0:1, :])
-    normed[...] = normed_rows
-    projected = []
-    for kind in range(3):
-        matrix = jnp.where(first, own[kind], other[kind])
-        projected.append(dot_nt(normed_rows, matrix).astype(jnp.bfloat16))
-    queries[...] = projected[0]
-    values[...] = projected[2]
+    normed = layer_norm(x[...], gains[0:1, :], biases[0:1, :])
+    queries, keys, values = [
+        dot_nt(normed, jnp.where(first, own[kind], other[kind])).astype(jnp.bfloat16)
+        for kind in range(3)
+    ]
     allowed = ids_along(lengths, core[0], (rows, 1), 0) == ids_along(lengths, core[0], (1, rows), 1)
-    parts = []
-    for head in range(queries.shape[1] // HS):
-        at = slice(head * HS, (head + 1) * HS)
-        weights = softmax(projected[0][:, at], projected[1][:, at], allowed)
-        probs[head] = weights
-        parts.append(dot_nn(weights.astype(jnp.bfloat16), projected[2][:, at]))
-    block = side_by_side(parts)
-    context[...] = block
+    heads = [slice(at, at + HS) for at in range(0, queries.shape[1], HS)]
+    probs = [softmax(queries[:, at], keys[:, at], allowed) for at in heads]
+    return normed, queries, values, heads, probs
+
+
+def enc_forward_kernel(core, lengths, x, own, other, gains, biases, copies):
+    _, _, values, heads, probs = enc_attention(core, lengths, x, own, other, gains, biases)
+    block = side_by_side(
+        [
+            dot_nn(weights.astype(jnp.bfloat16), values[:, at])
+            for at, weights in zip(heads, probs, strict=True)
+        ]
+    )
     for copy in range(copies.shape[0]):
         copies[copy] = block
+
+
+def enc_keep_kernel(
+    core, lengths, x, own, other, gains, biases, copies, normed, queries, values, context, probs
+):
+    kept = enc_attention(core, lengths, x, own, other, gains, biases)
+    normed[...], queries[...], values[...] = kept[:3]
+    context[...] = copies[0]
+    for head, weights in enumerate(kept[4]):
+        probs[head] = weights
 
 
 def token_kernel(
@@ -359,21 +369,31 @@
         (enc_full, token_queries, token_grads, dec_weights)
     )
     weight_block = ((3, head_cols, features), (0, 0, 0))
-    normed, queries, values, context, context_copies, probs = call(
+    enc_scalars = (core_id, frame_lengths)
+    enc_arrays = (enc_full, own, other, norm_gains, norm_biases)
+    enc_blocks = {1: weight_block, 2: weight_block}
+    context_copies = call(
         enc_forward_kernel,
+        [((mp, rows, head_cols), bf16)],
+        enc_scalars,
+        enc_arrays,
+        enc_blocks,
+        kept=(0,),
+        cost=pl.CostEstimate(flops=3_000_000_000, transcendentals=0, bytes_accessed=0),
+    )
+    normed, queries, values, context, probs = call(
+        enc_keep_kernel,
         [
             ((rows, features), bf16),
             ((rows, head_cols), bf16),
             ((rows, head_cols), bf16),
             ((rows, head_cols), bf16),
-            ((mp, rows, head_cols), bf16),
             ((heads, rows, rows), f32),
         ],
-        (core_id, frame_lengths),
-        (enc_full, own, other, norm_gains, norm_biases),
-        {1: weight_block, 2: weight_block},
-        kept=(0, 1, 2, 3, 4, 5),
-        cost=pl.CostEstimate(flops=3_000_000_000, transcendentals=0, bytes_accessed=0),
+        enc_scalars,
+        (*enc_arrays, context_copies),
+        {**enc_blocks, 5: ((1, rows, head_cols), (0, 0, 0))},
+        kept=(0, 1, 2, 3, 4),
     )
     context_full = exchange(context_copies)
     half_states = call(
@@ -416,6 +436,7 @@
         [((mp, shard_rows, features), bf16)],
         (),
         (pieces, states, norm_gains),
+        kept=(0,),
     )
     grads_full = exchange(grads).reshape(rows, features)
     enc_term = call(
@@ -433,7 +454,6 @@
         [((size, 8, 128), bf16)],
         (core_id,),
         (enc_term, enc_sent, dec_term, dec_sent),
-        read=(2,),
     )
     parts = exchange(tiles.reshape(near, each, 8, 128), "dp", near_groups)
     parts = call(sum_copies_kernel, [((far, each, 8, 128), bf16)], (), (parts,))

time: 195 us -> 197 us (1.010)
  Pallas kernels: 22.5 us -> 26.9 us
  waiting for transfers between devices: 37.1 us -> 32.7 us
    pallas_call x12 -> x13, Pallas kernels: 22.5 us -> 26.9 us  [call(): pl.pallas_call(kernel, grid=(1,), out_shape=[out(index, *what) for index,...]
    all_to_all x3, waiting for transfers between devices: 26.7 us -> 23.7 us  [exchange(): return lax.all_to_all(blocks, axis, 0, 0, axis_index_groups=groups)]
  transfers between devices with their start and end apart: 13 -> 13, of which waited for: 5 -> 5; matrix products, arithmetic and copies ran while one was open for 1% -> 0% of each run, Pallas kernels for 6% -> 8%
where the time goes in v15:
time: 197 us; the launch traced here: 194 us
  blocking collectives  78.3 us (40%)
  starting transfers between devices  54 us (27%)
  waiting for transfers between devices  32.7 us (17%)
  Pallas kernels  26.9 us (14%)
    all_to_all x4, blocking collectives, exchange(): return lax.all_to_all(blocks, axis, 0, 0, axis_index_groups=groups)  78.3 us
    pallas_call x13, Pallas kernels, call(): pl.pallas_call(kernel, grid=(1,), out_shape=[out(index, *what) for index,...  26.9 us
    all_to_all x3, waiting for transfers between devices, exchange(): return lax.all_to_all(blocks, axis, 0, 0, axis_index_groups=groups)  23.7 us
    ppermute x4, starting transfers between devices, swap(): return lax.ppermute(block, 'segment', [(0, 1), (1, 0)])  16.7 us
    ppermute x4, starting transfers between devices, passing(): return lax.ppermute(block, ('segment', 'mp'), up + down)  15.9 us
    all_to_all x3, starting transfers between devices, exchange(): return lax.all_to_all(blocks, axis, 0, 0, axis_index_groups=groups)  15.5 us
    ppermute x4, waiting for transfers between devices, passing(): return lax.ppermute(block, ('segment', 'mp'), up + down)  6.93 us
    ppermute x1, starting transfers between devices, shards(): enc_sent = lax.ppermute(enc_term, 'segment', [(1, 0)])  4.65 us
  transfers between devices with their start and end apart: 13, of which 5 were waited for; matrix products, arithmetic and copies ran while one was open for 0% of the time, Pallas kernels for 8%

profile of v15, /device:TPU:1, one launch (start us, length us, event | category | flops | bytes accessed | tf_op | source)
XLA Modules:
  0.0 194.1 jit_solution(11864024531622645278)
XLA Ops:
  0.0 1.9 shard_map.82
  1.9 8.9 %collective-permute-start = (bf16[4,128,1280]{2,1,0:T(8,128)(2,1)}, bf16[4,128,1280]{2,1,0:T(8,128)(2,1)S(1)}, u32[]{:S(2)}, u32[]{:S(2)}) collective-permute-start(bf16[4,128,1280]{2,1,0:T(8,128)(2,1)} %bitcast.11), channel_id=1, source_target_pairs={{0,8},{8,0},{1,9},{9,1},{2,10},{10,2},{3,11},{11,3},{4,12},{12,4},... | collective-permute-start | bytes 3932168 | tf_op jit(solution)/shard_map/ppermute | solution.py:310
  10.8 4.7 %all-to-all-start = ((bf16[8,32,1280]{2,1,0:T(8,128)(2,1)}), bf16[8,32,1280]{2,1,0:T(8,128)(2,1)S(1)}, u32[]{:S(2)}, u32[]{:S(2)}) async-start(bf16[8,32,1280]{2,1,0:T(8,128)(2,1)} %shard_map.82), calls=%async_computation | async-start | bytes 1310720 | tf_op jit(solution)/shard_map/all_to_all | solution.py:332
  15.5 0.0 collective-permute-done.other
  15.5 0.0 copy-done
  15.5 0.8 fusion.refs_2_.out_shard
  16.3 4.7 %collective-permute-start.1 = (bf16[128,1280]{1,0:T(8,128)(2,1)}, bf16[128,1280]{1,0:T(8,128)(2,1)}, u32[]{:S(2)}, u32[]{:S(2)}) collective-permute-start(bf16[128,1280]{1,0:T(8,128)(2,1)} %fusion.refs_2_.out_shard), channel_id=1, source_target_pairs={{0,1},{1,2},{2,3},{3,4},{4,5},{5,6},{6,7},{7,0},{8,15},{9,8},{10,9... | collective-permute-start | bytes 983048 | tf_op jit(solution)/shard_map/ppermute | solution.py:351
  21.0 0.0 copy-done.6
  21.0 0.0 copy-done.7
  21.0 2.4 %shard_map.83 = (bf16[64,128]{1,0:T(8,128)(2,1)}, bf16[64,128]{1,0:T(8,128)(2,1)}, bf16[2,128,1280]{2,1,0:T(8,128)(2,1)}) custom-call(s32[1]{0:T(128)} %bitcast.core, bf16[2,64,1280]{2,1,0:T(8,128)(2,1)} %tokens.1, bf16[2,64,1280]{2,1,0:T(8,128)(2,1)} %upstream.3, bf16[4,128,1280]{2,1,0:T(8,128)(2,1)S(1)} %bitcast.13, ...), custom_call_target="tpu_custom_call" | custom-call | tf_op jit(solution)/shard_map/pallas_call | solution.py:292
  23.4 12.9 %all-to-all-done = bf16[8,32,1280]{2,1,0:T(8,128)(2,1)S(1)} async-done(((bf16[8,32,1280]{2,1,0:T(8,128)(2,1)}), bf16[8,32,1280]{2,1,0:T(8,128)(2,1)S(1)}, u32[]{:S(2)}, u32[]{:S(2)}) %all-to-all-start) | async-done | bytes 655392 | tf_op jit(solution)/shard_map/all_to_all | solution.py:332
  36.3 0.0 collective-permute-done.1.refs_0_
  36.3 2.6 %collective-permute-start.2 = (bf16[128,1280]{1,0:T(8,128)(2,1)}, bf16[128,1280]{1,0:T(8,128)(2,1)}, u32[]{:S(2)}, u32[]{:S(2)}) collective-permute-start(bf16[128,1280]{1,0:T(8,128)(2,1)} %collective-permute-done.1.refs_0_), channel_id=1, source_target_pairs={{0,1},{1,2},{2,3},{3,4},{4,5},{5,6},{6,7},{7,0},{8,15},{9,8},{10,9... | collective-permute-start | bytes 983048 | tf_op jit(solution)/shard_map/ppermute | solution.py:351
  38.9 0.0 copy-done.13
  38.9 3.1 %shard_map.84.copies = bf16[8,256,128]{2,1,0:T(8,128)(2,1)} custom-call(s32[1]{0:T(128)} %bitcast.core, s32[2,1,4]{2,1,0:T(1,128)S(1)} %copy-done.13, bf16[256,1280]{1,0:T(8,128)(2,1)S(1)} %bitcast.16, bf16[4,128,1280]{2,1,0:T(8,128)(2,1)S(1)} %bitcast.14, bf16[4,128,1280]{2,1,0:T(8,128)(2,1)S(1)} %collective-permute-done.other, f32[3,1280]{1,0:T(4,128)S(1)} %copy-done.6, ...), custom_call_target="tpu_custom_call" | custom-call | flops 3000000000 | tf_op jit(solution)/shard_map/pallas_call | solution.py:292
  42.0 6.6 %all-to-all-start.1 = ((bf16[8,256,128]{2,1,0:T(8,128)(2,1)}), bf16[8,256,128]{2,1,0:T(8,128)(2,1)}, u32[]{:S(2)}, u32[]{:S(2)}) async-start(bf16[8,256,128]{2,1,0:T(8,128)(2,1)} %shard_map.84.copies), calls=%async_computation.1 | async-start | bytes 1048576 | tf_op jit(solution)/shard_map/all_to_all | solution.py:332
  48.7 0.0 collective-permute-done.2.refs_1_
  48.7 4.6 %collective-permute-start.5 = (bf16[128,1280]{1,0:T(8,128)(2,1)}, bf16[128,1280]{1,0:T(8,128)(2,1)}, u32[]{:S(2)}, u32[]{:S(2)}) collective-permute-start(bf16[128,1280]{1,0:T(8,128)(2,1)} %collective-permute-done.2.refs_1_), channel_id=1, source_target_pairs={{0,1},{1,2},{2,3},{3,4},{4,5},{5,6},{6,7},{7,0},{8,15},{9,8},{10,9... | collective-permute-start | bytes 983048 | tf_op jit(solution)/shard_map/ppermute | solution.py:351
  53.3 1.9 collective-permute-start.3
  55.2 2.4 %collective-permute-start.4 = (bf16[128,1280]{1,0:T(8,128)(2,1)}, bf16[128,1280]{1,0:T(8,128)(2,1)}, u32[]{:S(2)}, u32[]{:S(2)}) collective-permute-start(bf16[128,1280]{1,0:T(8,128)(2,1)} %collective-permute-done.2.refs_1_), channel_id=1, source_target_pairs={{0,8},{8,0},{1,9},{9,1},{2,10},{10,2},{3,11},{11,3},{4,12},{12,4},... | collective-permute-start | bytes 983048 | tf_op jit(solution)/shard_map/ppermute | solution.py:310
  57.6 4.0 %collective-permute-start.7 = (bf16[128,1280]{1,0:T(8,128)(2,1)}, bf16[128,1280]{1,0:T(8,128)(2,1)}, u32[]{:S(2)}, u32[]{:S(2)}) collective-permute-start(bf16[128,1280]{1,0:T(8,128)(2,1)} %collective-permute-done.2.refs_1_), channel_id=1, source_target_pairs={{0,2},{1,3},{2,4},{3,5},{4,6},{5,7},{6,0},{7,1},{8,14},{9,15},{10,... | collective-permute-start | bytes 983048 | tf_op jit(solution)/shard_map/ppermute | solution.py:351
  61.6 4.8 %collective-permute-done.5.refs_0_ = bf16[128,1280]{1,0:T(8,128)(2,1)} collective-permute-done((bf16[128,1280]{1,0:T(8,128)(2,1)}, bf16[128,1280]{1,0:T(8,128)(2,1)}, u32[]{:S(2)}, u32[]{:S(2)}) %collective-permute-start.5) | collective-permute-done | bytes 327712 | tf_op jit(solution)/shard_map/ppermute | solution.py:351
  66.5 3.5 %collective-permute-start.6 = (bf16[128,1280]{1,0:T(8,128)(2,1)}, bf16[128,1280]{1,0:T(8,128)(2,1)}, u32[]{:S(2)}, u32[]{:S(2)}) collective-permute-start(bf16[128,1280]{1,0:T(8,128)(2,1)} %collective-permute-done.5.refs_0_), channel_id=1, source_target_pairs={{0,8},{8,0},{1,9},{9,1},{2,10},{10,2},{3,11},{11,3},{4,12},{12,4},... | collective-permute-start | bytes 983048 | tf_op jit(solution)/shard_map/ppermute | solution.py:310
  70.0 0.0 collective-permute-done.3.refs_2_
  70.0 0.0 all-to-all-done.1.context
  70.0 0.0 collective-permute-done.4.refs_3_
  70.0 0.0 copy-start.4
  70.0 0.0 copy-start.11
  70.0 0.0 copy-start.12
  70.0 0.0 copy-start.14
  70.0 2.0 %shard_map.85.half_states = f32[256,1280]{1,0:T(8,128)S(1)} custom-call(s32[1]{0:T(128)} %bitcast.core, s32[1]{0:T(128)} %bitcast.1.place, bf16[256,1280]{1,0:T(8,128)(2,1)S(1)} %bitcast.17, bf16[8,256,128]{2,1,0:T(8,128)(2,1)} %all-to-all-done.1.context, bf16[128,1280]{1,0:T(8,128)(2,1)} %collective-permute-done.1.refs_0_, ...), custom_call_target="tpu_custom_call" | custom-call | tf_op jit(solution)/shard_map/pallas_call | solution.py:292
  72.0 2.1 %collective-permute-done.7.refs_3_ = bf16[128,1280]{1,0:T(8,128)(2,1)} collective-permute-done((bf16[128,1280]{1,0:T(8,128)(2,1)}, bf16[128,1280]{1,0:T(8,128)(2,1)}, u32[]{:S(2)}, u32[]{:S(2)}) %collective-permute-start.7) | collective-permute-done | bytes 327712 | tf_op jit(solution)/shard_map/ppermute | solution.py:351
  74.1 0.0 collective-permute-done.6.refs_1_
  74.1 0.0 copy-done.4
  74.1 0.0 copy-done.11
  74.1 0.0 copy-done.12
  74.2 0.0 copy-done.14
  74.2 4.5 %shard_map.86 = (bf16[256,1280]{1,0:T(8,128)(2,1)S(1)}, bf16[32,1280]{1,0:T(8,128)(2,1)S(1)}, bf16[256,1280]{1,0:T(8,128)(2,1)}, bf16[256,128]{1,0:T(8,128)(2,1)...) custom-call(s32[1]{0:T(128)} %bitcast.core, s32[1]{0:T(128)} %bitcast.1.place, s32[2,1,4]{2,1,0:T(1,128)S(1)} %copy-done.13, ...), custom_call_target="tpu_custom_call" | custom-call | tf_op jit(solution)/shard_map/pallas_call | solution.py:292
  78.7 23.7 %all_to_all.35.pieces = bf16[8,32,1280]{2,1,0:T(8,128)(2,1)S(1)} all-to-all(bf16[8,32,1280]{2,1,0:T(8,128)(2,1)S(1)} %bitcast.21), channel_id=1, replica_groups=mesh['dp'=32,'segment'=2,'mp'=8] {'mp'}, dimensions={0} | all-to-all | bytes 1310720 | tf_op jit(solution)/shard_map/all_to_all | solution.py:332
  102.4 1.2 shard_map.87
  103.5 4.2 %all-to-all-start.3 = ((bf16[8,32,1280]{2,1,0:T(8,128)(2,1)}), bf16[8,32,1280]{2,1,0:T(8,128)(2,1)}, u32[]{:S(2)}, u32[]{:S(2)}) async-start(bf16[8,32,1280]{2,1,0:T(8,128)(2,1)} %shard_map.87), calls=%async_computation.3 | async-start | bytes 1310720 | tf_op jit(solution)/shard_map/all_to_all | solution.py:332
  107.7 0.0 copy-start.2
  107.7 1.0 copy-done.2
  108.8 2.7 %shard_map.88 = (bf16[256,1280]{1,0:T(8,128)(2,1)}, bf16[256,128]{1,0:T(8,128)(2,1)}, bf16[256,128]{1,0:T(8,128)(2,1)}, bf16[256,128]{1,0:T(8,128)(2,1)}, f32[2,256,256]{2,1,0:T(8,128)}) custom-call(s32[1]{0:T(128)} %bitcast.core, s32[2,1,4]{2,1,0:T(1,128)S(1)} %copy-done.13, bf16[256,1280]{1,0:T(8,128)(2,1)S(1)} %bitcast.18, ...), custom_call_target="tpu_custom_call" | custom-call | tf_op jit(solution)/shard_map/pallas_call | solution.py:292
  111.5 0.0 copy-start.10
  111.5 2.7 %shard_map.90.dec_term = bf16[384,1280]{1,0:T(8,128)(2,1)} custom-call(s32[1]{0:T(128)} %bitcast.core, bf16[256,128]{1,0:T(8,128)(2,1)} %get-tuple-element.41.key_grad, bf16[256,128]{1,0:T(8,128)(2,1)} %get-tuple-element.42.value_grad, bf16[64,128]{1,0:T(8,128)(2,1)} %get-tuple-element.43.context, bf16[256,1280]{1,0:T(8,128)(2,1)} %get-tuple-element.44.normed, ...), custom_call_target="tpu_custom_call" | custom-call | tf_op jit(solution)/shard_map/pallas_call | solution.py:292
  114.2 1.3 collective-permute-start.9
  115.5 10.8 %all-to-all-done.3 = bf16[8,32,1280]{2,1,0:T(8,128)(2,1)} async-done(((bf16[8,32,1280]{2,1,0:T(8,128)(2,1)}), bf16[8,32,1280]{2,1,0:T(8,128)(2,1)}, u32[]{:S(2)}, u32[]{:S(2)}) %all-to-all-start.3) | async-done | bytes 655392 | tf_op jit(solution)/shard_map/all_to_all | solution.py:332
  126.3 0.0 copy-done.3
  126.3 0.0 copy-done.5
  126.3 0.0 copy-done.8
  126.3 0.0 copy-done.9
  126.3 0.0 copy-start.1
  126.4 3.1 %shard_map.89.enc_term = bf16[384,1280]{1,0:T(8,128)(2,1)S(1)} custom-call(bf16[256,1280]{1,0:T(8,128)(2,1)} %bitcast.6.grads, bf16[128,1280]{1,0:T(8,128)(2,1)} %fusion.refs_2_.out_shard, bf16[256,128]{1,0:T(8,128)(2,1)S(1)} %copy-done.8, bf16[256,128]{1,0:T(8,128)(2,1)S(1)} %copy-done.9, f32[2,256,256]{2,1,0:T(8,128)S(1)} %copy-done.5, ...), custom_call_target="tpu_custom_call" | custom-call | tf_op jit(solution)/shard_map/pallas_call | solution.py:292
  129.5 4.6 %collective-permute-start.8 = (bf16[384,1280]{1,0:T(8,128)(2,1)S(1)}, bf16[384,1280]{1,0:T(8,128)(2,1)S(1)}, u32[]{:S(2)}, u32[]{:S(2)}) collective-permute-start(bf16[384,1280]{1,0:T(8,128)(2,1)S(1)} %shard_map.89.enc_term), channel_id=1, source_target_pairs={{8,0},{9,1},{10,2},{11,3},{12,4},{13,5},{14,6},{15,7},{24,16},{25,... | collective-permute-start | bytes 2949128 | tf_op jit(solution)/shard_map/ppermute | solution.py:449
  134.2 0.0 collective-permute-done.9.dec_sent
  134.2 2.1 %collective-permute-done.8.enc_sent = bf16[384,1280]{1,0:T(8,128)(2,1)S(1)} collective-permute-done((bf16[384,1280]{1,0:T(8,128)(2,1)S(1)}, bf16[384,1280]{1,0:T(8,128)(2,1)S(1)}, u32[]{:S(2)}, u32[]{:S(2)}) %collective-permute-start.8) | collective-permute-done | bytes 983072 | tf_op jit(solution)/shard_map/ppermute | solution.py:449
  136.3 1.6 shard_map.91
  137.9 19.3 %all_to_all.36.pieces = bf16[8,60,8,128]{3,2,1,0:T(8,128)(2,1)S(1)} all-to-all(bf16[8,60,8,128]{3,2,1,0:T(8,128)(2,1)S(1)} %bitcast.19), channel_id=1, replica_groups={{0,16,128,144,256,272,384,400},{32,48,160,176,288,304,416,432},{64,80,1..., dimensions={0} | all-to-all | bytes 1966080 | tf_op jit(solution)/shard_map/all_to_all | solution.py:332
  157.2 0.1 shard_map.92
  157.3 18.3 %all_to_all.37.pieces = bf16[4,60,8,128]{3,2,1,0:T(8,128)(2,1)S(1)} all-to-all(bf16[4,60,8,128]{3,2,1,0:T(8,128)(2,1)S(1)} %shard_map.92), channel_id=1, replica_groups={{0,32,64,96},{16,48,80,112},{128,160,192,224},{144,176,208,240},{256,28..., dimensions={0} | all-to-all | bytes 983040 | tf_op jit(solution)/shard_map/all_to_all | solution.py:332
  175.6 0.1 shard_map.93
  175.6 17.1 %all_to_all.38 = bf16[8,60,8,128]{3,2,1,0:T(8,128)(2,1)S(1)} all-to-all(bf16[8,60,8,128]{3,2,1,0:T(8,128)(2,1)S(1)} %shard_map.93), channel_id=1, replica_groups={{0,16,128,144,256,272,384,400},{32,48,160,176,288,304,416,432},{64,80,1..., dimensions={0} | all-to-all | bytes 1966080 | tf_op jit(solution)/shard_map/all_to_all | solution.py:332
  192.7 1.4 shard_map.94
  (10 shorter events, 0.0 us)
Async XLA Ops:
  0.0 15.5 %copy-start = (bf16[1,4,128,1280]{3,2,1,0:T(8,128)(2,1)S(1)}, bf16[1,4,128,1280]{3,2,1,0:T(8,128)(2,1)}, u32[]{:S(2)}) copy-start(bf16[1,4,128,1280]{3,2,1,0:T(8,128)(2,1)} %param.13) | copy-start | bytes 3932164
  1.9 19.1 %copy-start.6 = (f32[3,1280]{1,0:T(4,128)S(1)}, f32[3,1280]{1,0:T(4,128)}, u32[]{:S(2)}) copy-start(f32[3,1280]{1,0:T(4,128)} %gains.9) | copy-start | bytes 46084
  1.9 19.1 %copy-start.7 = (f32[3,1280]{1,0:T(4,128)S(1)}, f32[3,1280]{1,0:T(4,128)}, u32[]{:S(2)}) copy-start(f32[3,1280]{1,0:T(4,128)} %biases.7) | copy-start | bytes 46084
  1.9 13.6 %collective-permute-start = (bf16[4,128,1280]{2,1,0:T(8,128)(2,1)}, bf16[4,128,1280]{2,1,0:T(8,128)(2,1)S(1)}, u32[]{:S(2)}, u32[]{:S(2)}) collective-permute-start(bf16[4,128,1280]{2,1,0:T(8,128)(2,1)} %bitcast.11), channel_id=1, source_target_pairs={{0,8},{8,0},{1,9},{9,1},{2,10},{10,2},{3,11},{11,3},{4,12},{12,4},... | collective-permute-start | bytes 3932168 | tf_op jit(solution)/shard_map/ppermute | solution.py:310
  10.8 25.5 %all-to-all-start = ((bf16[8,32,1280]{2,1,0:T(8,128)(2,1)}), bf16[8,32,1280]{2,1,0:T(8,128)(2,1)S(1)}, u32[]{:S(2)}, u32[]{:S(2)}) async-start(bf16[8,32,1280]{2,1,0:T(8,128)(2,1)} %shard_map.82), calls=%async_computation | async-start | bytes 1310720 | tf_op jit(solution)/shard_map/all_to_all | solution.py:332
  16.3 22.6 %copy-start.13 = (s32[2,1,4]{2,1,0:T(1,128)S(1)}, s32[2,1,4]{2,1,0:T(1,128)}, u32[]{:S(2)}) copy-start(s32[2,1,4]{2,1,0:T(1,128)} %lengths.3) | copy-start | bytes 100
  16.3 20.0 %collective-permute-start.1 = (bf16[128,1280]{1,0:T(8,128)(2,1)}, bf16[128,1280]{1,0:T(8,128)(2,1)}, u32[]{:S(2)}, u32[]{:S(2)}) collective-permute-start(bf16[128,1280]{1,0:T(8,128)(2,1)} %fusion.refs_2_.out_shard), channel_id=1, source_target_pairs={{0,1},{1,2},{2,3},{3,4},{4,5},{5,6},{6,7},{7,0},{8,15},{9,8},{10,9... | collective-permute-start | bytes 983048 | tf_op jit(solution)/shard_map/ppermute | solution.py:351
  36.3 12.4 %collective-permute-start.2 = (bf16[128,1280]{1,0:T(8,128)(2,1)}, bf16[128,1280]{1,0:T(8,128)(2,1)}, u32[]{:S(2)}, u32[]{:S(2)}) collective-permute-start(bf16[128,1280]{1,0:T(8,128)(2,1)} %collective-permute-done.1.refs_0_), channel_id=1, source_target_pairs={{0,1},{1,2},{2,3},{3,4},{4,5},{5,6},{6,7},{7,0},{8,15},{9,8},{10,9... | collective-permute-start | bytes 983048 | tf_op jit(solution)/shard_map/ppermute | solution.py:351
  42.0 27.9 %all-to-all-start.1 = ((bf16[8,256,128]{2,1,0:T(8,128)(2,1)}), bf16[8,256,128]{2,1,0:T(8,128)(2,1)}, u32[]{:S(2)}, u32[]{:S(2)}) async-start(bf16[8,256,128]{2,1,0:T(8,128)(2,1)} %shard_map.84.copies), calls=%async_computation.1 | async-start | bytes 1048576 | tf_op jit(solution)/shard_map/all_to_all | solution.py:332
  48.7 17.8 %collective-permute-start.5 = (bf16[128,1280]{1,0:T(8,128)(2,1)}, bf16[128,1280]{1,0:T(8,128)(2,1)}, u32[]{:S(2)}, u32[]{:S(2)}) collective-permute-start(bf16[128,1280]{1,0:T(8,128)(2,1)} %collective-permute-done.2.refs_1_), channel_id=1, source_target_pairs={{0,1},{1,2},{2,3},{3,4},{4,5},{5,6},{6,7},{7,0},{8,15},{9,8},{10,9... | collective-permute-start | bytes 983048 | tf_op jit(solution)/shard_map/ppermute | solution.py:351
  53.3 16.7 %collective-permute-start.3 = (bf16[128,1280]{1,0:T(8,128)(2,1)}, bf16[128,1280]{1,0:T(8,128)(2,1)}, u32[]{:S(2)}, u32[]{:S(2)}) collective-permute-start(bf16[128,1280]{1,0:T(8,128)(2,1)} %collective-permute-done.1.refs_0_), channel_id=1, source_target_pairs={{0,8},{8,0},{1,9},{9,1},{2,10},{10,2},{3,11},{11,3},{4,12},{12,4},... | collective-permute-start | bytes 983048 | tf_op jit(solution)/shard_map/ppermute | solution.py:310
  55.2 14.8 %collective-permute-start.4 = (bf16[128,1280]{1,0:T(8,128)(2,1)}, bf16[128,1280]{1,0:T(8,128)(2,1)}, u32[]{:S(2)}, u32[]{:S(2)}) collective-permute-start(bf16[128,1280]{1,0:T(8,128)(2,1)} %collective-permute-done.2.refs_1_), channel_id=1, source_target_pairs={{0,8},{8,0},{1,9},{9,1},{2,10},{10,2},{3,11},{11,3},{4,12},{12,4},... | collective-permute-start | bytes 983048 | tf_op jit(solution)/shard_map/ppermute | solution.py:310
  57.6 16.5 %collective-permute-start.7 = (bf16[128,1280]{1,0:T(8,128)(2,1)}, bf16[128,1280]{1,0:T(8,128)(2,1)}, u32[]{:S(2)}, u32[]{:S(2)}) collective-permute-start(bf16[128,1280]{1,0:T(8,128)(2,1)} %collective-permute-done.2.refs_1_), channel_id=1, source_target_pairs={{0,2},{1,3},{2,4},{3,5},{4,6},{5,7},{6,0},{7,1},{8,14},{9,15},{10,... | collective-permute-start | bytes 983048 | tf_op jit(solution)/shard_map/ppermute | solution.py:351
  66.5 7.7 %collective-permute-start.6 = (bf16[128,1280]{1,0:T(8,128)(2,1)}, bf16[128,1280]{1,0:T(8,128)(2,1)}, u32[]{:S(2)}, u32[]{:S(2)}) collective-permute-start(bf16[128,1280]{1,0:T(8,128)(2,1)} %collective-permute-done.5.refs_0_), channel_id=1, source_target_pairs={{0,8},{8,0},{1,9},{9,1},{2,10},{10,2},{3,11},{11,3},{4,12},{12,4},... | collective-permute-start | bytes 983048 | tf_op jit(solution)/shard_map/ppermute | solution.py:310
  70.0 4.1 %copy-start.4 = (bf16[2,128,1280]{2,1,0:T(8,128)(2,1)S(1)}, bf16[2,128,1280]{2,1,0:T(8,128)(2,1)}, u32[]{:S(2)}) copy-start(bf16[2,128,1280]{2,1,0:T(8,128)(2,1)} %get-tuple-element.31.weights) | copy-start | bytes 1966084
  70.0 4.1 %copy-start.11 = (bf16[64,128]{1,0:T(8,128)(2,1)S(1)}, bf16[64,128]{1,0:T(8,128)(2,1)}, u32[]{:S(2)}) copy-start(bf16[64,128]{1,0:T(8,128)(2,1)} %get-tuple-element.32.token_queries) | copy-start | bytes 49156
  70.0 4.1 %copy-start.12 = (bf16[64,128]{1,0:T(8,128)(2,1)S(1)}, bf16[64,128]{1,0:T(8,128)(2,1)}, u32[]{:S(2)}) copy-start(bf16[64,128]{1,0:T(8,128)(2,1)} %get-tuple-element.33.token_grads) | copy-start | bytes 49156
  70.0 4.1 %copy-start.14 = (s32[2,1,4]{2,1,0:T(1,128)S(1)}, s32[2,1,4]{2,1,0:T(1,128)}, u32[]{:S(2)}) copy-start(s32[2,1,4]{2,1,0:T(1,128)} %token_lens.1) | copy-start | bytes 100
  103.5 22.8 %all-to-all-start.3 = ((bf16[8,32,1280]{2,1,0:T(8,128)(2,1)}), bf16[8,32,1280]{2,1,0:T(8,128)(2,1)}, u32[]{:S(2)}, u32[]{:S(2)}) async-start(bf16[8,32,1280]{2,1,0:T(8,128)(2,1)} %shard_map.87), calls=%async_computation.3 | async-start | bytes 1310720 | tf_op jit(solution)/shard_map/all_to_all | solution.py:332
  107.7 1.0 copy-start.2
  111.5 14.8 %copy-start.3 = (bf16[256,1280]{1,0:T(8,128)(2,1)S(1)}, bf16[256,1280]{1,0:T(8,128)(2,1)}, u32[]{:S(2)}) copy-start(bf16[256,1280]{1,0:T(8,128)(2,1)} %get-tuple-element.40.normed) | copy-start | bytes 1966084
  111.5 14.8 %copy-start.5 = (f32[2,256,256]{2,1,0:T(8,128)S(1)}, f32[2,256,256]{2,1,0:T(8,128)}, u32[]{:S(2)}) copy-start(f32[2,256,256]{2,1,0:T(8,128)} %get-tuple-element.38.probs) | copy-start | bytes 1572868
  111.5 14.8 %copy-start.8 = (bf16[256,128]{1,0:T(8,128)(2,1)S(1)}, bf16[256,128]{1,0:T(8,128)(2,1)}, u32[]{:S(2)}) copy-start(bf16[256,128]{1,0:T(8,128)(2,1)} %get-tuple-element.36.queries) | copy-start | bytes 196612
  111.5 14.8 %copy-start.9 = (bf16[256,128]{1,0:T(8,128)(2,1)S(1)}, bf16[256,128]{1,0:T(8,128)(2,1)}, u32[]{:S(2)}) copy-start(bf16[256,128]{1,0:T(8,128)(2,1)} %get-tuple-element.37.values) | copy-start | bytes 196612
  111.5 14.8 %copy-start.10 = (bf16[256,128]{1,0:T(8,128)(2,1)S(1)}, bf16[256,128]{1,0:T(8,128)(2,1)}, u32[]{:S(2)}) copy-start(bf16[256,128]{1,0:T(8,128)(2,1)} %get-tuple-element.39.context) | copy-start | bytes 196612
  114.2 19.9 %collective-permute-start.9 = (bf16[384,1280]{1,0:T(8,128)(2,1)}, bf16[384,1280]{1,0:T(8,128)(2,1)}, u32[]{:S(2)}, u32[]{:S(2)}) collective-permute-start(bf16[384,1280]{1,0:T(8,128)(2,1)} %shard_map.90.dec_term), channel_id=1, source_target_pairs={{0,8},{1,9},{2,10},{3,11},{4,12},{5,13},{6,14},{7,15},{16,24},{17,... | collective-permute-start | bytes 2949128 | tf_op jit(solution)/shard_map/ppermute | solution.py:448
  126.3 9.9 %copy-start.1 = (bf16[384,1280]{1,0:T(8,128)(2,1)S(1)}, bf16[384,1280]{1,0:T(8,128)(2,1)}, u32[]{:S(2)}) copy-start(bf16[384,1280]{1,0:T(8,128)(2,1)} %shard_map.90.dec_term) | copy-start | bytes 2949124
  129.5 6.8 %collective-permute-start.8 = (bf16[384,1280]{1,0:T(8,128)(2,1)S(1)}, bf16[384,1280]{1,0:T(8,128)(2,1)S(1)}, u32[]{:S(2)}, u32[]{:S(2)}) collective-permute-start(bf16[384,1280]{1,0:T(8,128)(2,1)S(1)} %shard_map.89.enc_term), channel_id=1, source_target_pairs={{8,0},{9,1},{10,2},{11,3},{12,4},{13,5},{14,6},{15,7},{24,16},{25,... | collective-permute-start | bytes 2949128 | tf_op jit(solution)/shard_map/ppermute | solution.py:449

commit v16 on v14

--- a/solution.py
+++ b/solution.py
@@ -433,7 +433,6 @@
         [((size, 8, 128), bf16)],
         (core_id,),
         (enc_term, enc_sent, dec_term, dec_sent),
-        read=(2,),
     )
     parts = exchange(tiles.reshape(near, each, 8, 128), "dp", near_groups)
     parts = call(sum_copies_kernel, [((far, each, 8, 128), bf16)], (), (parts,))

time: 195 us -> 193 us (0.990)
  no operation moved by 1% of the time
where the time goes in v16:
time: 193 us; the launch traced here: 191 us
  blocking collectives  78 us (40%)
  starting transfers between devices  53.2 us (28%)
  waiting for transfers between devices  37.1 us (19%)
  Pallas kernels  21.2 us (11%)
    all_to_all x4, blocking collectives, exchange(): return lax.all_to_all(blocks, axis, 0, 0, axis_index_groups=groups)  78 us
    all_to_all x3, waiting for transfers between devices, exchange(): return lax.all_to_all(blocks, axis, 0, 0, axis_index_groups=groups)  26.7 us
    pallas_call x12, Pallas kernels, call(): pl.pallas_call(kernel, grid=(1,), out_shape=[out(index, *what) for index,...  21.2 us
    ppermute x4, starting transfers between devices, swap(): return lax.ppermute(block, 'segment', [(0, 1), (1, 0)])  16.7 us
    ppermute x4, starting transfers between devices, passing(): return lax.ppermute(block, ('segment', 'mp'), up + down)  15.6 us
    all_to_all x3, starting transfers between devices, exchange(): return lax.all_to_all(blocks, axis, 0, 0, axis_index_groups=groups)  14.9 us
    ppermute x4, waiting for transfers between devices, passing(): return lax.ppermute(block, ('segment', 'mp'), up + down)  8.32 us
    ppermute x1, starting transfers between devices, shards(): enc_sent = lax.ppermute(enc_term, 'segment', [(1, 0)])  4.69 us
  transfers between devices with their start and end apart: 13, of which 5 were waited for; matrix products, arithmetic and copies ran while one was open for 1% of the time, Pallas kernels for 6%

profile of v16, /device:TPU:1, one launch (start us, length us, event | category | flops | bytes accessed | tf_op | source)
XLA Modules:
  0.0 191.0 jit_solution(5580772114846545852)
XLA Ops:
  0.0 1.9 shard_map.82
  1.9 8.9 %collective-permute-start = (bf16[4,128,1280]{2,1,0:T(8,128)(2,1)}, bf16[4,128,1280]{2,1,0:T(8,128)(2,1)}, u32[]{:S(2)}, u32[]{:S(2)}) collective-permute-start(bf16[4,128,1280]{2,1,0:T(8,128)(2,1)} %bitcast.16), channel_id=1, source_target_pairs={{0,8},{8,0},{1,9},{9,1},{2,10},{10,2},{3,11},{11,3},{4,12},{12,4},... | collective-permute-start | bytes 3932168 | tf_op jit(solution)/shard_map/ppermute | solution.py:300
  10.8 4.7 %all-to-all-start = ((bf16[8,32,1280]{2,1,0:T(8,128)(2,1)}), bf16[8,32,1280]{2,1,0:T(8,128)(2,1)S(1)}, u32[]{:S(2)}, u32[]{:S(2)}) async-start(bf16[8,32,1280]{2,1,0:T(8,128)(2,1)} %shard_map.82), calls=%async_computation | async-start | bytes 1310720 | tf_op jit(solution)/shard_map/all_to_all | solution.py:322
  15.5 0.0 collective-permute-done.other
  15.5 0.0 copy-done.1
  15.5 1.0 fusion.refs_2_.out_shard
  16.5 0.0 copy-start.12
  16.5 4.6 %collective-permute-start.1 = (bf16[128,1280]{1,0:T(8,128)(2,1)S(1)}, bf16[128,1280]{1,0:T(8,128)(2,1)S(1)}, u32[]{:S(2)}, u32[]{:S(2)}) collective-permute-start(bf16[128,1280]{1,0:T(8,128)(2,1)S(1)} %fusion.refs_2_.out_shard), channel_id=1, source_target_pairs={{0,1},{1,2},{2,3},{3,4},{4,5},{5,6},{6,7},{7,0},{8,15},{9,8},{10,9... | collective-permute-start | bytes 983048 | tf_op jit(solution)/shard_map/ppermute | solution.py:341
  21.1 0.0 copy-done.5
  21.1 0.0 copy-done.6
  21.1 2.9 %shard_map.83 = (bf16[64,128]{1,0:T(8,128)(2,1)}, bf16[64,128]{1,0:T(8,128)(2,1)}, bf16[2,128,1280]{2,1,0:T(8,128)(2,1)}) custom-call(s32[1]{0:T(128)} %bitcast.core, bf16[2,64,1280]{2,1,0:T(8,128)(2,1)} %tokens.1, bf16[2,64,1280]{2,1,0:T(8,128)(2,1)} %upstream.3, bf16[4,128,1280]{2,1,0:T(8,128)(2,1)S(1)} %bitcast.18, ...), custom_call_target="tpu_custom_call" | custom-call | tf_op jit(solution)/shard_map/pallas_call | solution.py:282
  24.0 12.3 %all-to-all-done = bf16[8,32,1280]{2,1,0:T(8,128)(2,1)S(1)} async-done(((bf16[8,32,1280]{2,1,0:T(8,128)(2,1)}), bf16[8,32,1280]{2,1,0:T(8,128)(2,1)S(1)}, u32[]{:S(2)}, u32[]{:S(2)}) %all-to-all-start) | async-done | bytes 655392 | tf_op jit(solution)/shard_map/all_to_all | solution.py:322
  36.3 0.0 collective-permute-done.1.refs_0_
  36.3 2.5 %collective-permute-start.2 = (bf16[128,1280]{1,0:T(8,128)(2,1)S(1)}, bf16[128,1280]{1,0:T(8,128)(2,1)S(1)}, u32[]{:S(2)}, u32[]{:S(2)}) collective-permute-start(bf16[128,1280]{1,0:T(8,128)(2,1)S(1)} %collective-permute-done.1.refs_0_), channel_id=1, source_target_pairs={{0,1},{1,2},{2,3},{3,4},{4,5},{5,6},{6,7},{7,0},{8,15},{9,8},{10,9... | collective-permute-start | bytes 983048 | tf_op jit(solution)/shard_map/ppermute | solution.py:341
  38.8 0.0 copy-done.12
  38.8 3.9 %shard_map.84 = (bf16[256,1280]{1,0:T(8,128)(2,1)}, bf16[256,128]{1,0:T(8,128)(2,1)}, bf16[256,128]{1,0:T(8,128)(2,1)}, bf16[256,128]{1,0:T(8,128)(2,1)}, bf16[8...) custom-call(s32[1]{0:T(128)} %bitcast.core, s32[2,1,4]{2,1,0:T(1,128)S(1)} %copy-done.12, bf16[256,1280]{1,0:T(8,128)(2,1)S(1)} %bitcast.14, ...), custom_call_target="tpu_custom_call" | custom-call | flops 3000000000 | tf_op jit(solution)/shard_map/pallas_call | solution.py:282
  42.7 6.6 %all-to-all-start.1 = ((bf16[8,256,128]{2,1,0:T(8,128)(2,1)}), bf16[8,256,128]{2,1,0:T(8,128)(2,1)S(1)}, u32[]{:S(2)}, u32[]{:S(2)}) async-start(bf16[8,256,128]{2,1,0:T(8,128)(2,1)} %get-tuple-element.32), calls=%async_computation.1 | async-start | bytes 1048576 | tf_op jit(solution)/shard_map/all_to_all | solution.py:322
  49.4 0.0 collective-permute-done.2.refs_1_
  49.4 4.6 %collective-permute-start.5 = (bf16[128,1280]{1,0:T(8,128)(2,1)S(1)}, bf16[128,1280]{1,0:T(8,128)(2,1)S(1)}, u32[]{:S(2)}, u32[]{:S(2)}) collective-permute-start(bf16[128,1280]{1,0:T(8,128)(2,1)S(1)} %collective-permute-done.2.refs_1_), channel_id=1, source_target_pairs={{0,1},{1,2},{2,3},{3,4},{4,5},{5,6},{6,7},{7,0},{8,15},{9,8},{10,9... | collective-permute-start | bytes 983048 | tf_op jit(solution)/shard_map/ppermute | solution.py:341
  54.0 1.9 %collective-permute-start.3 = (bf16[128,1280]{1,0:T(8,128)(2,1)S(1)}, bf16[128,1280]{1,0:T(8,128)(2,1)S(1)}, u32[]{:S(2)}, u32[]{:S(2)}) collective-permute-start(bf16[128,1280]{1,0:T(8,128)(2,1)S(1)} %collective-permute-done.1.refs_0_), channel_id=1, source_target_pairs={{0,8},{8,0},{1,9},{9,1},{2,10},{10,2},{3,11},{11,3},{4,12},{12,4},... | collective-permute-start | bytes 983048 | tf_op jit(solution)/shard_map/ppermute | solution.py:300
  55.9 2.4 %collective-permute-start.4 = (bf16[128,1280]{1,0:T(8,128)(2,1)S(1)}, bf16[128,1280]{1,0:T(8,128)(2,1)S(1)}, u32[]{:S(2)}, u32[]{:S(2)}) collective-permute-start(bf16[128,1280]{1,0:T(8,128)(2,1)S(1)} %collective-permute-done.2.refs_1_), channel_id=1, source_target_pairs={{0,8},{8,0},{1,9},{9,1},{2,10},{10,2},{3,11},{11,3},{4,12},{12,4},... | collective-permute-start | bytes 983048 | tf_op jit(solution)/shard_map/ppermute | solution.py:300
  58.3 4.0 %collective-permute-start.7 = (bf16[128,1280]{1,0:T(8,128)(2,1)S(1)}, bf16[128,1280]{1,0:T(8,128)(2,1)S(1)}, u32[]{:S(2)}, u32[]{:S(2)}) collective-permute-start(bf16[128,1280]{1,0:T(8,128)(2,1)S(1)} %collective-permute-done.2.refs_1_), channel_id=1, source_target_pairs={{0,2},{1,3},{2,4},{3,5},{4,6},{5,7},{6,0},{7,1},{8,14},{9,15},{10,... | collective-permute-start | bytes 983048 | tf_op jit(solution)/shard_map/ppermute | solution.py:341
  62.3 4.7 %collective-permute-done.5.refs_0_ = bf16[128,1280]{1,0:T(8,128)(2,1)S(1)} collective-permute-done((bf16[128,1280]{1,0:T(8,128)(2,1)S(1)}, bf16[128,1280]{1,0:T(8,128)(2,1)S(1)}, u32[]{:S(2)}, u32[]{:S(2)}) %collective-permute-start.5) | collective-permute-done | bytes 327712 | tf_op jit(solution)/shard_map/ppermute | solution.py:341
  67.1 3.5 %collective-permute-start.6 = (bf16[128,1280]{1,0:T(8,128)(2,1)S(1)}, bf16[128,1280]{1,0:T(8,128)(2,1)}, u32[]{:S(2)}, u32[]{:S(2)}) collective-permute-start(bf16[128,1280]{1,0:T(8,128)(2,1)S(1)} %collective-permute-done.5.refs_0_), channel_id=1, source_target_pairs={{0,8},{8,0},{1,9},{9,1},{2,10},{10,2},{3,11},{11,3},{4,12},{12,4},... | collective-permute-start | bytes 983048 | tf_op jit(solution)/shard_map/ppermute | solution.py:300
  70.6 0.0 collective-permute-done.3.refs_2_
  70.6 0.0 all-to-all-done.1.context
  70.6 0.0 collective-permute-done.4.refs_3_
  70.6 0.0 copy-start.3
  70.6 0.0 copy-start.10
  70.6 0.0 copy-start.11
  70.6 0.0 copy-start.13
  70.6 0.5 shard_map.85.half_states
  71.2 3.6 %collective-permute-done.7.refs_3_ = bf16[128,1280]{1,0:T(8,128)(2,1)S(1)} collective-permute-done((bf16[128,1280]{1,0:T(8,128)(2,1)S(1)}, bf16[128,1280]{1,0:T(8,128)(2,1)S(1)}, u32[]{:S(2)}, u32[]{:S(2)}) %collective-permute-start.7) | collective-permute-done | bytes 327712 | tf_op jit(solution)/shard_map/ppermute | solution.py:341
  74.7 0.0 collective-permute-done.6.refs_1_
  74.7 0.0 copy-done.3
  74.7 0.0 copy-done.10
  74.7 0.0 copy-done.11
  74.8 0.0 copy-done.13
  74.8 4.1 %shard_map.86 = (bf16[256,1280]{1,0:T(8,128)(2,1)S(1)}, bf16[32,1280]{1,0:T(8,128)(2,1)S(1)}, bf16[256,1280]{1,0:T(8,128)(2,1)}, bf16[256,128]{1,0:T(8,128)(2,1)...) custom-call(s32[1]{0:T(128)} %bitcast.core, s32[1]{0:T(128)} %bitcast.1.place, s32[2,1,4]{2,1,0:T(1,128)S(1)} %copy-done.12, ...), custom_call_target="tpu_custom_call" | custom-call | tf_op jit(solution)/shard_map/pallas_call | solution.py:282
  78.9 23.4 %all_to_all.35.pieces = bf16[8,32,1280]{2,1,0:T(8,128)(2,1)S(1)} all-to-all(bf16[8,32,1280]{2,1,0:T(8,128)(2,1)S(1)} %bitcast.20), channel_id=1, replica_groups=mesh['dp'=32,'segment'=2,'mp'=8] {'mp'}, dimensions={0} | all-to-all | bytes 1310720 | tf_op jit(solution)/shard_map/all_to_all | solution.py:322
  102.2 1.2 shard_map.87
  103.4 3.5 %all-to-all-start.3 = ((bf16[8,32,1280]{2,1,0:T(8,128)(2,1)}), bf16[8,32,1280]{2,1,0:T(8,128)(2,1)S(1)}, u32[]{:S(2)}, u32[]{:S(2)}) async-start(bf16[8,32,1280]{2,1,0:T(8,128)(2,1)} %shard_map.87), calls=%async_computation.3 | async-start | bytes 1310720 | tf_op jit(solution)/shard_map/all_to_all | solution.py:322
  107.0 0.0 copy-start.2
  107.0 0.0 copy-start.4
  107.0 0.0 copy-start.7
  107.0 0.0 copy-start.8
  107.0 0.0 copy-start.9
  107.0 2.7 %shard_map.89.dec_term = bf16[384,1280]{1,0:T(8,128)(2,1)} custom-call(s32[1]{0:T(128)} %bitcast.core, bf16[256,128]{1,0:T(8,128)(2,1)} %get-tuple-element.43.key_grad, bf16[256,128]{1,0:T(8,128)(2,1)} %get-tuple-element.44.value_grad, bf16[64,128]{1,0:T(8,128)(2,1)} %get-tuple-element.45.context, bf16[256,1280]{1,0:T(8,128)(2,1)} %get-tuple-element.46.normed, ...), custom_call_target="tpu_custom_call" | custom-call | tf_op jit(solution)/shard_map/pallas_call | solution.py:282
  109.7 1.3 collective-permute-start.9
  111.0 14.4 %all-to-all-done.3 = bf16[8,32,1280]{2,1,0:T(8,128)(2,1)S(1)} async-done(((bf16[8,32,1280]{2,1,0:T(8,128)(2,1)}), bf16[8,32,1280]{2,1,0:T(8,128)(2,1)S(1)}, u32[]{:S(2)}, u32[]{:S(2)}) %all-to-all-start.3) | async-done | bytes 655392 | tf_op jit(solution)/shard_map/all_to_all | solution.py:322
  125.4 0.0 copy-done.2
  125.4 0.0 copy-done.4
  125.5 0.0 copy-start
  125.5 1.9 shard_map.88.enc_term
  127.4 4.7 %collective-permute-start.8 = (bf16[384,1280]{1,0:T(8,128)(2,1)S(1)}, bf16[384,1280]{1,0:T(8,128)(2,1)S(1)}, u32[]{:S(2)}, u32[]{:S(2)}) collective-permute-start(bf16[384,1280]{1,0:T(8,128)(2,1)S(1)} %shard_map.88.enc_term), channel_id=1, source_target_pairs={{8,0},{9,1},{10,2},{11,3},{12,4},{13,5},{14,6},{15,7},{24,16},{25,... | collective-permute-start | bytes 2949128 | tf_op jit(solution)/shard_map/ppermute | solution.py:428
  132.1 0.0 collective-permute-done.9.dec_sent
  132.1 2.1 %collective-permute-done.8.enc_sent = bf16[384,1280]{1,0:T(8,128)(2,1)S(1)} collective-permute-done((bf16[384,1280]{1,0:T(8,128)(2,1)S(1)}, bf16[384,1280]{1,0:T(8,128)(2,1)S(1)}, u32[]{:S(2)}, u32[]{:S(2)}) %collective-permute-start.8) | collective-permute-done | bytes 983072 | tf_op jit(solution)/shard_map/ppermute | solution.py:428
  134.2 0.5 shard_map.90
  134.7 19.3 %all_to_all.36.pieces = bf16[8,60,8,128]{3,2,1,0:T(8,128)(2,1)S(1)} all-to-all(bf16[8,60,8,128]{3,2,1,0:T(8,128)(2,1)S(1)} %bitcast.11), channel_id=1, replica_groups={{0,16,128,144,256,272,384,400},{32,48,160,176,288,304,416,432},{64,80,1..., dimensions={0} | all-to-all | bytes 1966080 | tf_op jit(solution)/shard_map/all_to_all | solution.py:322
  154.0 0.1 shard_map.91
  154.2 18.3 %all_to_all.37.pieces = bf16[4,60,8,128]{3,2,1,0:T(8,128)(2,1)S(1)} all-to-all(bf16[4,60,8,128]{3,2,1,0:T(8,128)(2,1)S(1)} %shard_map.91), channel_id=1, replica_groups={{0,32,64,96},{16,48,80,112},{128,160,192,224},{144,176,208,240},{256,28..., dimensions={0} | all-to-all | bytes 983040 | tf_op jit(solution)/shard_map/all_to_all | solution.py:322
  172.4 0.1 shard_map.92
  172.5 17.1 %all_to_all.38 = bf16[8,60,8,128]{3,2,1,0:T(8,128)(2,1)S(1)} all-to-all(bf16[8,60,8,128]{3,2,1,0:T(8,128)(2,1)S(1)} %shard_map.92), channel_id=1, replica_groups={{0,16,128,144,256,272,384,400},{32,48,160,176,288,304,416,432},{64,80,1..., dimensions={0} | all-to-all | bytes 1966080 | tf_op jit(solution)/shard_map/all_to_all | solution.py:322
  189.6 1.4 shard_map.93
  (7 shorter events, 0.0 us)
Async XLA Ops:
  0.0 15.5 %copy-start.1 = (bf16[1,4,128,1280]{3,2,1,0:T(8,128)(2,1)S(1)}, bf16[1,4,128,1280]{3,2,1,0:T(8,128)(2,1)}, u32[]{:S(2)}) copy-start(bf16[1,4,128,1280]{3,2,1,0:T(8,128)(2,1)} %param.13) | copy-start | bytes 3932164
  1.9 19.2 %copy-start.5 = (f32[3,1280]{1,0:T(4,128)S(1)}, f32[3,1280]{1,0:T(4,128)}, u32[]{:S(2)}) copy-start(f32[3,1280]{1,0:T(4,128)} %gains.7) | copy-start | bytes 46084
  1.9 19.2 %copy-start.6 = (f32[3,1280]{1,0:T(4,128)S(1)}, f32[3,1280]{1,0:T(4,128)}, u32[]{:S(2)}) copy-start(f32[3,1280]{1,0:T(4,128)} %biases.5) | copy-start | bytes 46084
  1.9 13.6 %collective-permute-start = (bf16[4,128,1280]{2,1,0:T(8,128)(2,1)}, bf16[4,128,1280]{2,1,0:T(8,128)(2,1)}, u32[]{:S(2)}, u32[]{:S(2)}) collective-permute-start(bf16[4,128,1280]{2,1,0:T(8,128)(2,1)} %bitcast.16), channel_id=1, source_target_pairs={{0,8},{8,0},{1,9},{9,1},{2,10},{10,2},{3,11},{11,3},{4,12},{12,4},... | collective-permute-start | bytes 3932168 | tf_op jit(solution)/shard_map/ppermute | solution.py:300
  10.8 25.5 %all-to-all-start = ((bf16[8,32,1280]{2,1,0:T(8,128)(2,1)}), bf16[8,32,1280]{2,1,0:T(8,128)(2,1)S(1)}, u32[]{:S(2)}, u32[]{:S(2)}) async-start(bf16[8,32,1280]{2,1,0:T(8,128)(2,1)} %shard_map.82), calls=%async_computation | async-start | bytes 1310720 | tf_op jit(solution)/shard_map/all_to_all | solution.py:322
  16.5 22.3 %copy-start.12 = (s32[2,1,4]{2,1,0:T(1,128)S(1)}, s32[2,1,4]{2,1,0:T(1,128)}, u32[]{:S(2)}) copy-start(s32[2,1,4]{2,1,0:T(1,128)} %frame_lens.1) | copy-start | bytes 100
  16.5 19.8 %collective-permute-start.1 = (bf16[128,1280]{1,0:T(8,128)(2,1)S(1)}, bf16[128,1280]{1,0:T(8,128)(2,1)S(1)}, u32[]{:S(2)}, u32[]{:S(2)}) collective-permute-start(bf16[128,1280]{1,0:T(8,128)(2,1)S(1)} %fusion.refs_2_.out_shard), channel_id=1, source_target_pairs={{0,1},{1,2},{2,3},{3,4},{4,5},{5,6},{6,7},{7,0},{8,15},{9,8},{10,9... | collective-permute-start | bytes 983048 | tf_op jit(solution)/shard_map/ppermute | solution.py:341
  36.3 13.1 %collective-permute-start.2 = (bf16[128,1280]{1,0:T(8,128)(2,1)S(1)}, bf16[128,1280]{1,0:T(8,128)(2,1)S(1)}, u32[]{:S(2)}, u32[]{:S(2)}) collective-permute-start(bf16[128,1280]{1,0:T(8,128)(2,1)S(1)} %collective-permute-done.1.refs_0_), channel_id=1, source_target_pairs={{0,1},{1,2},{2,3},{3,4},{4,5},{5,6},{6,7},{7,0},{8,15},{9,8},{10,9... | collective-permute-start | bytes 983048 | tf_op jit(solution)/shard_map/ppermute | solution.py:341
  42.7 27.8 %all-to-all-start.1 = ((bf16[8,256,128]{2,1,0:T(8,128)(2,1)}), bf16[8,256,128]{2,1,0:T(8,128)(2,1)S(1)}, u32[]{:S(2)}, u32[]{:S(2)}) async-start(bf16[8,256,128]{2,1,0:T(8,128)(2,1)} %get-tuple-element.32), calls=%async_computation.1 | async-start | bytes 1048576 | tf_op jit(solution)/shard_map/all_to_all | solution.py:322
  49.4 17.7 %collective-permute-start.5 = (bf16[128,1280]{1,0:T(8,128)(2,1)S(1)}, bf16[128,1280]{1,0:T(8,128)(2,1)S(1)}, u32[]{:S(2)}, u32[]{:S(2)}) collective-permute-start(bf16[128,1280]{1,0:T(8,128)(2,1)S(1)} %collective-permute-done.2.refs_1_), channel_id=1, source_target_pairs={{0,1},{1,2},{2,3},{3,4},{4,5},{5,6},{6,7},{7,0},{8,15},{9,8},{10,9... | collective-permute-start | bytes 983048 | tf_op jit(solution)/shard_map/ppermute | solution.py:341
  54.0 16.6 %collective-permute-start.3 = (bf16[128,1280]{1,0:T(8,128)(2,1)S(1)}, bf16[128,1280]{1,0:T(8,128)(2,1)S(1)}, u32[]{:S(2)}, u32[]{:S(2)}) collective-permute-start(bf16[128,1280]{1,0:T(8,128)(2,1)S(1)} %collective-permute-done.1.refs_0_), channel_id=1, source_target_pairs={{0,8},{8,0},{1,9},{9,1},{2,10},{10,2},{3,11},{11,3},{4,12},{12,4},... | collective-permute-start | bytes 983048 | tf_op jit(solution)/shard_map/ppermute | solution.py:300
  55.9 14.7 %collective-permute-start.4 = (bf16[128,1280]{1,0:T(8,128)(2,1)S(1)}, bf16[128,1280]{1,0:T(8,128)(2,1)S(1)}, u32[]{:S(2)}, u32[]{:S(2)}) collective-permute-start(bf16[128,1280]{1,0:T(8,128)(2,1)S(1)} %collective-permute-done.2.refs_1_), channel_id=1, source_target_pairs={{0,8},{8,0},{1,9},{9,1},{2,10},{10,2},{3,11},{11,3},{4,12},{12,4},... | collective-permute-start | bytes 983048 | tf_op jit(solution)/shard_map/ppermute | solution.py:300
  58.3 16.4 %collective-permute-start.7 = (bf16[128,1280]{1,0:T(8,128)(2,1)S(1)}, bf16[128,1280]{1,0:T(8,128)(2,1)S(1)}, u32[]{:S(2)}, u32[]{:S(2)}) collective-permute-start(bf16[128,1280]{1,0:T(8,128)(2,1)S(1)} %collective-permute-done.2.refs_1_), channel_id=1, source_target_pairs={{0,2},{1,3},{2,4},{3,5},{4,6},{5,7},{6,0},{7,1},{8,14},{9,15},{10,... | collective-permute-start | bytes 983048 | tf_op jit(solution)/shard_map/ppermute | solution.py:341
  67.1 7.7 %collective-permute-start.6 = (bf16[128,1280]{1,0:T(8,128)(2,1)S(1)}, bf16[128,1280]{1,0:T(8,128)(2,1)}, u32[]{:S(2)}, u32[]{:S(2)}) collective-permute-start(bf16[128,1280]{1,0:T(8,128)(2,1)S(1)} %collective-permute-done.5.refs_0_), channel_id=1, source_target_pairs={{0,8},{8,0},{1,9},{9,1},{2,10},{10,2},{3,11},{11,3},{4,12},{12,4},... | collective-permute-start | bytes 983048 | tf_op jit(solution)/shard_map/ppermute | solution.py:300
  70.6 4.1 %copy-start.3 = (bf16[2,128,1280]{2,1,0:T(8,128)(2,1)S(1)}, bf16[2,128,1280]{2,1,0:T(8,128)(2,1)}, u32[]{:S(2)}) copy-start(bf16[2,128,1280]{2,1,0:T(8,128)(2,1)} %get-tuple-element.33.weights) | copy-start | bytes 1966084
  70.6 4.1 %copy-start.10 = (bf16[64,128]{1,0:T(8,128)(2,1)S(1)}, bf16[64,128]{1,0:T(8,128)(2,1)}, u32[]{:S(2)}) copy-start(bf16[64,128]{1,0:T(8,128)(2,1)} %get-tuple-element.34.token_queries) | copy-start | bytes 49156
  70.6 4.1 %copy-start.11 = (bf16[64,128]{1,0:T(8,128)(2,1)S(1)}, bf16[64,128]{1,0:T(8,128)(2,1)}, u32[]{:S(2)}) copy-start(bf16[64,128]{1,0:T(8,128)(2,1)} %get-tuple-element.35.token_grads) | copy-start | bytes 49156
  70.6 4.1 %copy-start.13 = (s32[2,1,4]{2,1,0:T(1,128)S(1)}, s32[2,1,4]{2,1,0:T(1,128)}, u32[]{:S(2)}) copy-start(s32[2,1,4]{2,1,0:T(1,128)} %token_lens.1) | copy-start | bytes 100
  103.4 22.0 %all-to-all-start.3 = ((bf16[8,32,1280]{2,1,0:T(8,128)(2,1)}), bf16[8,32,1280]{2,1,0:T(8,128)(2,1)S(1)}, u32[]{:S(2)}, u32[]{:S(2)}) async-start(bf16[8,32,1280]{2,1,0:T(8,128)(2,1)} %shard_map.87), calls=%async_computation.3 | async-start | bytes 1310720 | tf_op jit(solution)/shard_map/all_to_all | solution.py:322
  107.0 18.5 %copy-start.2 = (bf16[256,1280]{1,0:T(8,128)(2,1)S(1)}, bf16[256,1280]{1,0:T(8,128)(2,1)}, u32[]{:S(2)}) copy-start(bf16[256,1280]{1,0:T(8,128)(2,1)} %get-tuple-element.42.normed) | copy-start | bytes 1966084
  107.0 18.5 %copy-start.4 = (f32[2,256,256]{2,1,0:T(8,128)S(1)}, f32[2,256,256]{2,1,0:T(8,128)}, u32[]{:S(2)}) copy-start(f32[2,256,256]{2,1,0:T(8,128)} %get-tuple-element.40.probs) | copy-start | bytes 1572868
  107.0 18.5 %copy-start.7 = (bf16[256,128]{1,0:T(8,128)(2,1)S(1)}, bf16[256,128]{1,0:T(8,128)(2,1)}, u32[]{:S(2)}) copy-start(bf16[256,128]{1,0:T(8,128)(2,1)} %get-tuple-element.38.queries) | copy-start | bytes 196612
  107.0 18.5 %copy-start.8 = (bf16[256,128]{1,0:T(8,128)(2,1)S(1)}, bf16[256,128]{1,0:T(8,128)(2,1)}, u32[]{:S(2)}) copy-start(bf16[256,128]{1,0:T(8,128)(2,1)} %get-tuple-element.39.values) | copy-start | bytes 196612
  107.0 18.5 %copy-start.9 = (bf16[256,128]{1,0:T(8,128)(2,1)S(1)}, bf16[256,128]{1,0:T(8,128)(2,1)}, u32[]{:S(2)}) copy-start(bf16[256,128]{1,0:T(8,128)(2,1)} %get-tuple-element.41.context) | copy-start | bytes 196612
  109.7 22.3 %collective-permute-start.9 = (bf16[384,1280]{1,0:T(8,128)(2,1)}, bf16[384,1280]{1,0:T(8,128)(2,1)S(1)}, u32[]{:S(2)}, u32[]{:S(2)}) collective-permute-start(bf16[384,1280]{1,0:T(8,128)(2,1)} %shard_map.89.dec_term), channel_id=1, source_target_pairs={{0,8},{1,9},{2,10},{3,11},{4,12},{5,13},{6,14},{7,15},{16,24},{17,... | collective-permute-start | bytes 2949128 | tf_op jit(solution)/shard_map/ppermute | solution.py:427
  125.5 8.7 %copy-start = (bf16[384,1280]{1,0:T(8,128)(2,1)S(1)}, bf16[384,1280]{1,0:T(8,128)(2,1)}, u32[]{:S(2)}) copy-start(bf16[384,1280]{1,0:T(8,128)(2,1)} %shard_map.89.dec_term) | copy-start | bytes 2949124
  127.4 6.8 %collective-permute-start.8 = (bf16[384,1280]{1,0:T(8,128)(2,1)S(1)}, bf16[384,1280]{1,0:T(8,128)(2,1)S(1)}, u32[]{:S(2)}, u32[]{:S(2)}) collective-permute-start(bf16[384,1280]{1,0:T(8,128)(2,1)S(1)} %shard_map.88.enc_term), channel_id=1, source_target_pairs={{8,0},{9,1},{10,2},{11,3},{12,4},{13,5},{14,6},{15,7},{24,16},{25,... | collective-permute-start | bytes 2949128 | tf_op jit(solution)/shard_map/ppermute | solution.py:428

commit v17 on v16

--- a/solution.py
+++ b/solution.py
@@ -399,7 +399,7 @@
         ),
         scratch=[pltpu.VMEM((rows, features), f32)],
         kept=(2, 3, 4, 5),
-        read=(8,),
+
     )
     pieces = exchange(partial.reshape(mp, shard_rows, features))
     whole = [((3 * head_cols, features), bf16)]

time: 193 us -> 193 us (level)
  transfers between devices with their start and end apart: 13 -> 13, of which waited for: 5 -> 5; matrix products, arithmetic and copies ran while one was open for 1% -> 1% of each run, Pallas kernels for 6% -> 7%
where the time goes in v17:
time: 193 us; the launch traced here: 191 us
  blocking collectives  78 us (40%)
  starting transfers between devices  53.2 us (28%)
  waiting for transfers between devices  36.1 us (19%)
  Pallas kernels  22 us (11%)
    all_to_all x4, blocking collectives, exchange(): return lax.all_to_all(blocks, axis, 0, 0, axis_index_groups=groups)  78 us
    all_to_all x3, waiting for transfers between devices, exchange(): return lax.all_to_all(blocks, axis, 0, 0, axis_index_groups=groups)  26.7 us
    pallas_call x12, Pallas kernels, call(): pl.pallas_call(kernel, grid=(1,), out_shape=[out(index, *what) for index,...  22 us
    ppermute x4, starting transfers between devices, swap(): return lax.ppermute(block, 'segment', [(0, 1), (1, 0)])  16.7 us
    ppermute x4, starting transfers between devices, passing(): return lax.ppermute(block, ('segment', 'mp'), up + down)  15.6 us
    all_to_all x3, starting transfers between devices, exchange(): return lax.all_to_all(blocks, axis, 0, 0, axis_index_groups=groups)  14.9 us
    ppermute x4, waiting for transfers between devices, passing(): return lax.ppermute(block, ('segment', 'mp'), up + down)  7.29 us
    ppermute x1, starting transfers between devices, shards(): enc_sent = lax.ppermute(enc_term, 'segment', [(1, 0)])  4.7 us
  transfers between devices with their start and end apart: 13, of which 5 were waited for; matrix products, arithmetic and copies ran while one was open for 1% of the time, Pallas kernels for 7%

profile of v17, /device:TPU:1, one launch (start us, length us, event | category | flops | bytes accessed | tf_op | source)
XLA Modules:
  0.0 190.8 jit_solution(4304577520339568890)
XLA Ops:
  0.0 1.9 shard_map.82
  1.9 8.9 %collective-permute-start = (bf16[4,128,1280]{2,1,0:T(8,128)(2,1)}, bf16[4,128,1280]{2,1,0:T(8,128)(2,1)}, u32[]{:S(2)}, u32[]{:S(2)}) collective-permute-start(bf16[4,128,1280]{2,1,0:T(8,128)(2,1)} %bitcast.16), channel_id=1, source_target_pairs={{0,8},{8,0},{1,9},{9,1},{2,10},{10,2},{3,11},{11,3},{4,12},{12,4},... | collective-permute-start | bytes 3932168 | tf_op jit(solution)/shard_map/ppermute | solution.py:300
  10.8 4.7 %all-to-all-start = ((bf16[8,32,1280]{2,1,0:T(8,128)(2,1)}), bf16[8,32,1280]{2,1,0:T(8,128)(2,1)S(1)}, u32[]{:S(2)}, u32[]{:S(2)}) async-start(bf16[8,32,1280]{2,1,0:T(8,128)(2,1)} %shard_map.82), calls=%async_computation | async-start | bytes 1310720 | tf_op jit(solution)/shard_map/all_to_all | solution.py:322
  15.5 0.0 collective-permute-done.other
  15.5 0.0 copy-done.1
  15.5 1.0 fusion.refs_2_.out_shard
  16.5 0.0 copy-start.12
  16.5 4.6 %collective-permute-start.1 = (bf16[128,1280]{1,0:T(8,128)(2,1)S(1)}, bf16[128,1280]{1,0:T(8,128)(2,1)S(1)}, u32[]{:S(2)}, u32[]{:S(2)}) collective-permute-start(bf16[128,1280]{1,0:T(8,128)(2,1)S(1)} %fusion.refs_2_.out_shard), channel_id=1, source_target_pairs={{0,1},{1,2},{2,3},{3,4},{4,5},{5,6},{6,7},{7,0},{8,15},{9,8},{10,9... | collective-permute-start | bytes 983048 | tf_op jit(solution)/shard_map/ppermute | solution.py:341
  21.1 0.0 copy-done.5
  21.1 0.0 copy-done.6
  21.1 2.9 %shard_map.83 = (bf16[64,128]{1,0:T(8,128)(2,1)}, bf16[64,128]{1,0:T(8,128)(2,1)}, bf16[2,128,1280]{2,1,0:T(8,128)(2,1)}) custom-call(s32[1]{0:T(128)} %bitcast.core, bf16[2,64,1280]{2,1,0:T(8,128)(2,1)} %tokens.1, bf16[2,64,1280]{2,1,0:T(8,128)(2,1)} %upstream.3, bf16[4,128,1280]{2,1,0:T(8,128)(2,1)S(1)} %bitcast.18, ...), custom_call_target="tpu_custom_call" | custom-call | tf_op jit(solution)/shard_map/pallas_call | solution.py:282
  24.0 12.3 %all-to-all-done = bf16[8,32,1280]{2,1,0:T(8,128)(2,1)S(1)} async-done(((bf16[8,32,1280]{2,1,0:T(8,128)(2,1)}), bf16[8,32,1280]{2,1,0:T(8,128)(2,1)S(1)}, u32[]{:S(2)}, u32[]{:S(2)}) %all-to-all-start) | async-done | bytes 655392 | tf_op jit(solution)/shard_map/all_to_all | solution.py:322
  36.3 0.0 collective-permute-done.1.refs_0_
  36.3 2.5 %collective-permute-start.2 = (bf16[128,1280]{1,0:T(8,128)(2,1)S(1)}, bf16[128,1280]{1,0:T(8,128)(2,1)S(1)}, u32[]{:S(2)}, u32[]{:S(2)}) collective-permute-start(bf16[128,1280]{1,0:T(8,128)(2,1)S(1)} %collective-permute-done.1.refs_0_), channel_id=1, source_target_pairs={{0,1},{1,2},{2,3},{3,4},{4,5},{5,6},{6,7},{7,0},{8,15},{9,8},{10,9... | collective-permute-start | bytes 983048 | tf_op jit(solution)/shard_map/ppermute | solution.py:341
  38.8 0.0 copy-done.12
  38.8 3.9 %shard_map.84 = (bf16[256,1280]{1,0:T(8,128)(2,1)}, bf16[256,128]{1,0:T(8,128)(2,1)}, bf16[256,128]{1,0:T(8,128)(2,1)}, bf16[256,128]{1,0:T(8,128)(2,1)}, bf16[8...) custom-call(s32[1]{0:T(128)} %bitcast.core, s32[2,1,4]{2,1,0:T(1,128)S(1)} %copy-done.12, bf16[256,1280]{1,0:T(8,128)(2,1)S(1)} %bitcast.14, ...), custom_call_target="tpu_custom_call" | custom-call | flops 3000000000 | tf_op jit(solution)/shard_map/pallas_call | solution.py:282
  42.7 6.6 %all-to-all-start.1 = ((bf16[8,256,128]{2,1,0:T(8,128)(2,1)}), bf16[8,256,128]{2,1,0:T(8,128)(2,1)S(1)}, u32[]{:S(2)}, u32[]{:S(2)}) async-start(bf16[8,256,128]{2,1,0:T(8,128)(2,1)} %get-tuple-element.32), calls=%async_computation.1 | async-start | bytes 1048576 | tf_op jit(solution)/shard_map/all_to_all | solution.py:322
  49.4 0.0 collective-permute-done.2.refs_1_
  49.4 4.6 %collective-permute-start.5 = (bf16[128,1280]{1,0:T(8,128)(2,1)S(1)}, bf16[128,1280]{1,0:T(8,128)(2,1)S(1)}, u32[]{:S(2)}, u32[]{:S(2)}) collective-permute-start(bf16[128,1280]{1,0:T(8,128)(2,1)S(1)} %collective-permute-done.2.refs_1_), channel_id=1, source_target_pairs={{0,1},{1,2},{2,3},{3,4},{4,5},{5,6},{6,7},{7,0},{8,15},{9,8},{10,9... | collective-permute-start | bytes 983048 | tf_op jit(solution)/shard_map/ppermute | solution.py:341
  54.0 1.9 %collective-permute-start.3 = (bf16[128,1280]{1,0:T(8,128)(2,1)S(1)}, bf16[128,1280]{1,0:T(8,128)(2,1)S(1)}, u32[]{:S(2)}, u32[]{:S(2)}) collective-permute-start(bf16[128,1280]{1,0:T(8,128)(2,1)S(1)} %collective-permute-done.1.refs_0_), channel_id=1, source_target_pairs={{0,8},{8,0},{1,9},{9,1},{2,10},{10,2},{3,11},{11,3},{4,12},{12,4},... | collective-permute-start | bytes 983048 | tf_op jit(solution)/shard_map/ppermute | solution.py:300
  55.9 2.4 %collective-permute-start.4 = (bf16[128,1280]{1,0:T(8,128)(2,1)S(1)}, bf16[128,1280]{1,0:T(8,128)(2,1)}, u32[]{:S(2)}, u32[]{:S(2)}) collective-permute-start(bf16[128,1280]{1,0:T(8,128)(2,1)S(1)} %collective-permute-done.2.refs_1_), channel_id=1, source_target_pairs={{0,8},{8,0},{1,9},{9,1},{2,10},{10,2},{3,11},{11,3},{4,12},{12,4},... | collective-permute-start | bytes 983048 | tf_op jit(solution)/shard_map/ppermute | solution.py:300
  58.3 4.0 %collective-permute-start.7 = (bf16[128,1280]{1,0:T(8,128)(2,1)S(1)}, bf16[128,1280]{1,0:T(8,128)(2,1)S(1)}, u32[]{:S(2)}, u32[]{:S(2)}) collective-permute-start(bf16[128,1280]{1,0:T(8,128)(2,1)S(1)} %collective-permute-done.2.refs_1_), channel_id=1, source_target_pairs={{0,2},{1,3},{2,4},{3,5},{4,6},{5,7},{6,0},{7,1},{8,14},{9,15},{10,... | collective-permute-start | bytes 983048 | tf_op jit(solution)/shard_map/ppermute | solution.py:341
  62.3 4.7 %collective-permute-done.5.refs_0_ = bf16[128,1280]{1,0:T(8,128)(2,1)S(1)} collective-permute-done((bf16[128,1280]{1,0:T(8,128)(2,1)S(1)}, bf16[128,1280]{1,0:T(8,128)(2,1)S(1)}, u32[]{:S(2)}, u32[]{:S(2)}) %collective-permute-start.5) | collective-permute-done | bytes 327712 | tf_op jit(solution)/shard_map/ppermute | solution.py:341
  67.1 3.5 %collective-permute-start.6 = (bf16[128,1280]{1,0:T(8,128)(2,1)S(1)}, bf16[128,1280]{1,0:T(8,128)(2,1)S(1)}, u32[]{:S(2)}, u32[]{:S(2)}) collective-permute-start(bf16[128,1280]{1,0:T(8,128)(2,1)S(1)} %collective-permute-done.5.refs_0_), channel_id=1, source_target_pairs={{0,8},{8,0},{1,9},{9,1},{2,10},{10,2},{3,11},{11,3},{4,12},{12,4},... | collective-permute-start | bytes 983048 | tf_op jit(solution)/shard_map/ppermute | solution.py:300
  70.6 0.0 collective-permute-done.3.refs_2_
  70.6 0.0 all-to-all-done.1.context
  70.6 0.0 collective-permute-done.4.refs_3_
  70.6 0.0 copy-start.3
  70.6 0.0 copy-start.10
  70.6 0.0 copy-start.11
  70.6 0.0 copy-start.13
  70.6 1.5 shard_map.85.half_states
  72.2 2.6 %collective-permute-done.7.refs_3_ = bf16[128,1280]{1,0:T(8,128)(2,1)S(1)} collective-permute-done((bf16[128,1280]{1,0:T(8,128)(2,1)S(1)}, bf16[128,1280]{1,0:T(8,128)(2,1)S(1)}, u32[]{:S(2)}, u32[]{:S(2)}) %collective-permute-start.7) | collective-permute-done | bytes 327712 | tf_op jit(solution)/shard_map/ppermute | solution.py:341
  74.7 0.0 collective-permute-done.6.refs_1_
  74.7 0.0 copy-done.3
  74.7 0.0 copy-done.10
  74.7 0.0 copy-done.11
  74.8 0.0 copy-done.13
  74.8 3.8 %shard_map.86 = (bf16[256,1280]{1,0:T(8,128)(2,1)S(1)}, bf16[32,1280]{1,0:T(8,128)(2,1)S(1)}, bf16[256,1280]{1,0:T(8,128)(2,1)}, bf16[256,128]{1,0:T(8,128)(2,1)...) custom-call(s32[1]{0:T(128)} %bitcast.core, s32[1]{0:T(128)} %bitcast.1.place, s32[2,1,4]{2,1,0:T(1,128)S(1)} %copy-done.12, ...), custom_call_target="tpu_custom_call" | custom-call | tf_op jit(solution)/shard_map/pallas_call | solution.py:282
  78.6 23.4 %all_to_all.35.pieces = bf16[8,32,1280]{2,1,0:T(8,128)(2,1)S(1)} all-to-all(bf16[8,32,1280]{2,1,0:T(8,128)(2,1)S(1)} %bitcast.20), channel_id=1, replica_groups=mesh['dp'=32,'segment'=2,'mp'=8] {'mp'}, dimensions={0} | all-to-all | bytes 1310720 | tf_op jit(solution)/shard_map/all_to_all | solution.py:322
  102.0 1.2 shard_map.87
  103.2 3.5 %all-to-all-start.3 = ((bf16[8,32,1280]{2,1,0:T(8,128)(2,1)}), bf16[8,32,1280]{2,1,0:T(8,128)(2,1)S(1)}, u32[]{:S(2)}, u32[]{:S(2)}) async-start(bf16[8,32,1280]{2,1,0:T(8,128)(2,1)} %shard_map.87), calls=%async_computation.3 | async-start | bytes 1310720 | tf_op jit(solution)/shard_map/all_to_all | solution.py:322
  106.7 0.0 copy-start.2
  106.8 0.0 copy-start.4
  106.8 0.0 copy-start.7
  106.8 0.0 copy-start.8
  106.8 0.0 copy-start.9
  106.8 2.7 %shard_map.89.dec_term = bf16[384,1280]{1,0:T(8,128)(2,1)} custom-call(s32[1]{0:T(128)} %bitcast.core, bf16[256,128]{1,0:T(8,128)(2,1)} %get-tuple-element.43.key_grad, bf16[256,128]{1,0:T(8,128)(2,1)} %get-tuple-element.44.value_grad, bf16[64,128]{1,0:T(8,128)(2,1)} %get-tuple-element.45.context, bf16[256,1280]{1,0:T(8,128)(2,1)} %get-tuple-element.46.normed, ...), custom_call_target="tpu_custom_call" | custom-call | tf_op jit(solution)/shard_map/pallas_call | solution.py:282
  109.5 1.3 collective-permute-start.9
  110.8 14.4 %all-to-all-done.3 = bf16[8,32,1280]{2,1,0:T(8,128)(2,1)S(1)} async-done(((bf16[8,32,1280]{2,1,0:T(8,128)(2,1)}), bf16[8,32,1280]{2,1,0:T(8,128)(2,1)S(1)}, u32[]{:S(2)}, u32[]{:S(2)}) %all-to-all-start.3) | async-done | bytes 655392 | tf_op jit(solution)/shard_map/all_to_all | solution.py:322
  125.2 0.0 copy-done.2
  125.2 0.0 copy-done.4
  125.2 0.0 copy-start
  125.3 1.9 shard_map.88.enc_term
  127.2 4.7 %collective-permute-start.8 = (bf16[384,1280]{1,0:T(8,128)(2,1)S(1)}, bf16[384,1280]{1,0:T(8,128)(2,1)S(1)}, u32[]{:S(2)}, u32[]{:S(2)}) collective-permute-start(bf16[384,1280]{1,0:T(8,128)(2,1)S(1)} %shard_map.88.enc_term), channel_id=1, source_target_pairs={{8,0},{9,1},{10,2},{11,3},{12,4},{13,5},{14,6},{15,7},{24,16},{25,... | collective-permute-start | bytes 2949128 | tf_op jit(solution)/shard_map/ppermute | solution.py:428
  131.9 0.0 collective-permute-done.9.dec_sent
  131.9 2.1 %collective-permute-done.8.enc_sent = bf16[384,1280]{1,0:T(8,128)(2,1)S(1)} collective-permute-done((bf16[384,1280]{1,0:T(8,128)(2,1)S(1)}, bf16[384,1280]{1,0:T(8,128)(2,1)S(1)}, u32[]{:S(2)}, u32[]{:S(2)}) %collective-permute-start.8) | collective-permute-done | bytes 983072 | tf_op jit(solution)/shard_map/ppermute | solution.py:428
  134.0 0.5 shard_map.90
  134.5 19.3 %all_to_all.36.pieces = bf16[8,60,8,128]{3,2,1,0:T(8,128)(2,1)S(1)} all-to-all(bf16[8,60,8,128]{3,2,1,0:T(8,128)(2,1)S(1)} %bitcast.11), channel_id=1, replica_groups={{0,16,128,144,256,272,384,400},{32,48,160,176,288,304,416,432},{64,80,1..., dimensions={0} | all-to-all | bytes 1966080 | tf_op jit(solution)/shard_map/all_to_all | solution.py:322
  153.8 0.1 shard_map.91
  153.9 18.3 %all_to_all.37.pieces = bf16[4,60,8,128]{3,2,1,0:T(8,128)(2,1)S(1)} all-to-all(bf16[4,60,8,128]{3,2,1,0:T(8,128)(2,1)S(1)} %shard_map.91), channel_id=1, replica_groups={{0,32,64,96},{16,48,80,112},{128,160,192,224},{144,176,208,240},{256,28..., dimensions={0} | all-to-all | bytes 983040 | tf_op jit(solution)/shard_map/all_to_all | solution.py:322
  172.2 0.1 shard_map.92
  172.3 17.1 %all_to_all.38 = bf16[8,60,8,128]{3,2,1,0:T(8,128)(2,1)S(1)} all-to-all(bf16[8,60,8,128]{3,2,1,0:T(8,128)(2,1)S(1)} %shard_map.92), channel_id=1, replica_groups={{0,16,128,144,256,272,384,400},{32,48,160,176,288,304,416,432},{64,80,1..., dimensions={0} | all-to-all | bytes 1966080 | tf_op jit(solution)/shard_map/all_to_all | solution.py:322
  189.4 1.4 shard_map.93
  (7 shorter events, 0.0 us)
Async XLA Ops:
  0.0 15.5 %copy-start.1 = (bf16[1,4,128,1280]{3,2,1,0:T(8,128)(2,1)S(1)}, bf16[1,4,128,1280]{3,2,1,0:T(8,128)(2,1)}, u32[]{:S(2)}) copy-start(bf16[1,4,128,1280]{3,2,1,0:T(8,128)(2,1)} %param.13) | copy-start | bytes 3932164
  1.9 19.2 %copy-start.5 = (f32[3,1280]{1,0:T(4,128)S(1)}, f32[3,1280]{1,0:T(4,128)}, u32[]{:S(2)}) copy-start(f32[3,1280]{1,0:T(4,128)} %gains.7) | copy-start | bytes 46084
  1.9 19.2 %copy-start.6 = (f32[3,1280]{1,0:T(4,128)S(1)}, f32[3,1280]{1,0:T(4,128)}, u32[]{:S(2)}) copy-start(f32[3,1280]{1,0:T(4,128)} %biases.5) | copy-start | bytes 46084
  1.9 13.6 %collective-permute-start = (bf16[4,128,1280]{2,1,0:T(8,128)(2,1)}, bf16[4,128,1280]{2,1,0:T(8,128)(2,1)}, u32[]{:S(2)}, u32[]{:S(2)}) collective-permute-start(bf16[4,128,1280]{2,1,0:T(8,128)(2,1)} %bitcast.16), channel_id=1, source_target_pairs={{0,8},{8,0},{1,9},{9,1},{2,10},{10,2},{3,11},{11,3},{4,12},{12,4},... | collective-permute-start | bytes 3932168 | tf_op jit(solution)/shard_map/ppermute | solution.py:300
  10.8 25.5 %all-to-all-start = ((bf16[8,32,1280]{2,1,0:T(8,128)(2,1)}), bf16[8,32,1280]{2,1,0:T(8,128)(2,1)S(1)}, u32[]{:S(2)}, u32[]{:S(2)}) async-start(bf16[8,32,1280]{2,1,0:T(8,128)(2,1)} %shard_map.82), calls=%async_computation | async-start | bytes 1310720 | tf_op jit(solution)/shard_map/all_to_all | solution.py:322
  16.5 22.3 %copy-start.12 = (s32[2,1,4]{2,1,0:T(1,128)S(1)}, s32[2,1,4]{2,1,0:T(1,128)}, u32[]{:S(2)}) copy-start(s32[2,1,4]{2,1,0:T(1,128)} %frame_lens.1) | copy-start | bytes 100
  16.5 19.8 %collective-permute-start.1 = (bf16[128,1280]{1,0:T(8,128)(2,1)S(1)}, bf16[128,1280]{1,0:T(8,128)(2,1)S(1)}, u32[]{:S(2)}, u32[]{:S(2)}) collective-permute-start(bf16[128,1280]{1,0:T(8,128)(2,1)S(1)} %fusion.refs_2_.out_shard), channel_id=1, source_target_pairs={{0,1},{1,2},{2,3},{3,4},{4,5},{5,6},{6,7},{7,0},{8,15},{9,8},{10,9... | collective-permute-start | bytes 983048 | tf_op jit(solution)/shard_map/ppermute | solution.py:341
  36.3 13.1 %collective-permute-start.2 = (bf16[128,1280]{1,0:T(8,128)(2,1)S(1)}, bf16[128,1280]{1,0:T(8,128)(2,1)S(1)}, u32[]{:S(2)}, u32[]{:S(2)}) collective-permute-start(bf16[128,1280]{1,0:T(8,128)(2,1)S(1)} %collective-permute-done.1.refs_0_), channel_id=1, source_target_pairs={{0,1},{1,2},{2,3},{3,4},{4,5},{5,6},{6,7},{7,0},{8,15},{9,8},{10,9... | collective-permute-start | bytes 983048 | tf_op jit(solution)/shard_map/ppermute | solution.py:341
  42.7 27.8 %all-to-all-start.1 = ((bf16[8,256,128]{2,1,0:T(8,128)(2,1)}), bf16[8,256,128]{2,1,0:T(8,128)(2,1)S(1)}, u32[]{:S(2)}, u32[]{:S(2)}) async-start(bf16[8,256,128]{2,1,0:T(8,128)(2,1)} %get-tuple-element.32), calls=%async_computation.1 | async-start | bytes 1048576 | tf_op jit(solution)/shard_map/all_to_all | solution.py:322
  49.4 17.7 %collective-permute-start.5 = (bf16[128,1280]{1,0:T(8,128)(2,1)S(1)}, bf16[128,1280]{1,0:T(8,128)(2,1)S(1)}, u32[]{:S(2)}, u32[]{:S(2)}) collective-permute-start(bf16[128,1280]{1,0:T(8,128)(2,1)S(1)} %collective-permute-done.2.refs_1_), channel_id=1, source_target_pairs={{0,1},{1,2},{2,3},{3,4},{4,5},{5,6},{6,7},{7,0},{8,15},{9,8},{10,9... | collective-permute-start | bytes 983048 | tf_op jit(solution)/shard_map/ppermute | solution.py:341
  54.0 16.6 %collective-permute-start.3 = (bf16[128,1280]{1,0:T(8,128)(2,1)S(1)}, bf16[128,1280]{1,0:T(8,128)(2,1)S(1)}, u32[]{:S(2)}, u32[]{:S(2)}) collective-permute-start(bf16[128,1280]{1,0:T(8,128)(2,1)S(1)} %collective-permute-done.1.refs_0_), channel_id=1, source_target_pairs={{0,8},{8,0},{1,9},{9,1},{2,10},{10,2},{3,11},{11,3},{4,12},{12,4},... | collective-permute-start | bytes 983048 | tf_op jit(solution)/shard_map/ppermute | solution.py:300
  55.9 14.7 %collective-permute-start.4 = (bf16[128,1280]{1,0:T(8,128)(2,1)S(1)}, bf16[128,1280]{1,0:T(8,128)(2,1)}, u32[]{:S(2)}, u32[]{:S(2)}) collective-permute-start(bf16[128,1280]{1,0:T(8,128)(2,1)S(1)} %collective-permute-done.2.refs_1_), channel_id=1, source_target_pairs={{0,8},{8,0},{1,9},{9,1},{2,10},{10,2},{3,11},{11,3},{4,12},{12,4},... | collective-permute-start | bytes 983048 | tf_op jit(solution)/shard_map/ppermute | solution.py:300
  58.3 16.4 %collective-permute-start.7 = (bf16[128,1280]{1,0:T(8,128)(2,1)S(1)}, bf16[128,1280]{1,0:T(8,128)(2,1)S(1)}, u32[]{:S(2)}, u32[]{:S(2)}) collective-permute-start(bf16[128,1280]{1,0:T(8,128)(2,1)S(1)} %collective-permute-done.2.refs_1_), channel_id=1, source_target_pairs={{0,2},{1,3},{2,4},{3,5},{4,6},{5,7},{6,0},{7,1},{8,14},{9,15},{10,... | collective-permute-start | bytes 983048 | tf_op jit(solution)/shard_map/ppermute | solution.py:341
  67.1 7.7 %collective-permute-start.6 = (bf16[128,1280]{1,0:T(8,128)(2,1)S(1)}, bf16[128,1280]{1,0:T(8,128)(2,1)S(1)}, u32[]{:S(2)}, u32[]{:S(2)}) collective-permute-start(bf16[128,1280]{1,0:T(8,128)(2,1)S(1)} %collective-permute-done.5.refs_0_), channel_id=1, source_target_pairs={{0,8},{8,0},{1,9},{9,1},{2,10},{10,2},{3,11},{11,3},{4,12},{12,4},... | collective-permute-start | bytes 983048 | tf_op jit(solution)/shard_map/ppermute | solution.py:300
  70.6 4.1 %copy-start.3 = (bf16[2,128,1280]{2,1,0:T(8,128)(2,1)S(1)}, bf16[2,128,1280]{2,1,0:T(8,128)(2,1)}, u32[]{:S(2)}) copy-start(bf16[2,128,1280]{2,1,0:T(8,128)(2,1)} %get-tuple-element.33.weights) | copy-start | bytes 1966084
  70.6 4.1 %copy-start.10 = (bf16[64,128]{1,0:T(8,128)(2,1)S(1)}, bf16[64,128]{1,0:T(8,128)(2,1)}, u32[]{:S(2)}) copy-start(bf16[64,128]{1,0:T(8,128)(2,1)} %get-tuple-element.34.token_queries) | copy-start | bytes 49156
  70.6 4.1 %copy-start.11 = (bf16[64,128]{1,0:T(8,128)(2,1)S(1)}, bf16[64,128]{1,0:T(8,128)(2,1)}, u32[]{:S(2)}) copy-start(bf16[64,128]{1,0:T(8,128)(2,1)} %get-tuple-element.35.token_grads) | copy-start | bytes 49156
  70.6 4.1 %copy-start.13 = (s32[2,1,4]{2,1,0:T(1,128)S(1)}, s32[2,1,4]{2,1,0:T(1,128)}, u32[]{:S(2)}) copy-start(s32[2,1,4]{2,1,0:T(1,128)} %token_lens.1) | copy-start | bytes 100
  103.2 22.0 %all-to-all-start.3 = ((bf16[8,32,1280]{2,1,0:T(8,128)(2,1)}), bf16[8,32,1280]{2,1,0:T(8,128)(2,1)S(1)}, u32[]{:S(2)}, u32[]{:S(2)}) async-start(bf16[8,32,1280]{2,1,0:T(8,128)(2,1)} %shard_map.87), calls=%async_computation.3 | async-start | bytes 1310720 | tf_op jit(solution)/shard_map/all_to_all | solution.py:322
  106.7 18.5 %copy-start.2 = (bf16[256,1280]{1,0:T(8,128)(2,1)S(1)}, bf16[256,1280]{1,0:T(8,128)(2,1)}, u32[]{:S(2)}) copy-start(bf16[256,1280]{1,0:T(8,128)(2,1)} %get-tuple-element.42.normed) | copy-start | bytes 1966084
  106.8 18.5 %copy-start.4 = (f32[2,256,256]{2,1,0:T(8,128)S(1)}, f32[2,256,256]{2,1,0:T(8,128)}, u32[]{:S(2)}) copy-start(f32[2,256,256]{2,1,0:T(8,128)} %get-tuple-element.40.probs) | copy-start | bytes 1572868
  106.8 18.5 %copy-start.7 = (bf16[256,128]{1,0:T(8,128)(2,1)S(1)}, bf16[256,128]{1,0:T(8,128)(2,1)}, u32[]{:S(2)}) copy-start(bf16[256,128]{1,0:T(8,128)(2,1)} %get-tuple-element.38.queries) | copy-start | bytes 196612
  106.8 18.5 %copy-start.8 = (bf16[256,128]{1,0:T(8,128)(2,1)S(1)}, bf16[256,128]{1,0:T(8,128)(2,1)}, u32[]{:S(2)}) copy-start(bf16[256,128]{1,0:T(8,128)(2,1)} %get-tuple-element.39.values) | copy-start | bytes 196612
  106.8 18.5 %copy-start.9 = (bf16[256,128]{1,0:T(8,128)(2,1)S(1)}, bf16[256,128]{1,0:T(8,128)(2,1)}, u32[]{:S(2)}) copy-start(bf16[256,128]{1,0:T(8,128)(2,1)} %get-tuple-element.41.context) | copy-start | bytes 196612
  109.5 22.3 %collective-permute-start.9 = (bf16[384,1280]{1,0:T(8,128)(2,1)}, bf16[384,1280]{1,0:T(8,128)(2,1)S(1)}, u32[]{:S(2)}, u32[]{:S(2)}) collective-permute-start(bf16[384,1280]{1,0:T(8,128)(2,1)} %shard_map.89.dec_term), channel_id=1, source_target_pairs={{0,8},{1,9},{2,10},{3,11},{4,12},{5,13},{6,14},{7,15},{16,24},{17,... | collective-permute-start | bytes 2949128 | tf_op jit(solution)/shard_map/ppermute | solution.py:427
  125.2 8.7 %copy-start = (bf16[384,1280]{1,0:T(8,128)(2,1)S(1)}, bf16[384,1280]{1,0:T(8,128)(2,1)}, u32[]{:S(2)}) copy-start(bf16[384,1280]{1,0:T(8,128)(2,1)} %shard_map.89.dec_term) | copy-start | bytes 2949124
  127.2 6.8 %collective-permute-start.8 = (bf16[384,1280]{1,0:T(8,128)(2,1)S(1)}, bf16[384,1280]{1,0:T(8,128)(2,1)S(1)}, u32[]{:S(2)}, u32[]{:S(2)}) collective-permute-start(bf16[384,1280]{1,0:T(8,128)(2,1)S(1)} %shard_map.88.enc_term), channel_id=1, source_target_pairs={{8,0},{9,1},{10,2},{11,3},{12,4},{13,5},{14,6},{15,7},{24,16},{25,... | collective-permute-start | bytes 2949128 | tf_op jit(solution)/shard_map/ppermute | solution.py:428

commit v18 on v17

--- a/solution.py
+++ b/solution.py
@@ -330,7 +330,6 @@
         (core_id,),
         (frames,),
         kept=(0,),
-        read=(0,),
     )
     copies, own = lax.optimization_barrier((copies, own))
     other = swap(own)

time: 193 us -> 193 us (level)
  no operation moved by 1% of the time
where the time goes in v18:
time: 193 us; the launch traced here: 191 us
  blocking collectives  78 us (40%)
  starting transfers between devices  53.2 us (28%)
  waiting for transfers between devices  36.1 us (19%)
  Pallas kernels  21 us (11%)
    all_to_all x4, blocking collectives, exchange(): return lax.all_to_all(blocks, axis, 0, 0, axis_index_groups=groups)  78 us
    all_to_all x3, waiting for transfers between devices, exchange(): return lax.all_to_all(blocks, axis, 0, 0, axis_index_groups=groups)  26.7 us
    pallas_call x12, Pallas kernels, call(): pl.pallas_call(kernel, grid=(1,), out_shape=[out(index, *what) for index,...  21 us
    ppermute x4, starting transfers between devices, swap(): return lax.ppermute(block, 'segment', [(0, 1), (1, 0)])  16.7 us
    ppermute x4, starting transfers between devices, passing(): return lax.ppermute(block, ('segment', 'mp'), up + down)  15.6 us
    all_to_all x3, starting transfers between devices, exchange(): return lax.all_to_all(blocks, axis, 0, 0, axis_index_groups=groups)  14.9 us
    ppermute x4, waiting for transfers between devices, passing(): return lax.ppermute(block, ('segment', 'mp'), up + down)  7.29 us
    ppermute x1, starting transfers between devices, shards(): enc_sent = lax.ppermute(enc_term, 'segment', [(1, 0)])  4.69 us
  transfers between devices with their start and end apart: 13, of which 5 were waited for; matrix products, arithmetic and copies ran while one was open for 1% of the time, Pallas kernels for 7%

profile of v18, /device:TPU:1, one launch (start us, length us, event | category | flops | bytes accessed | tf_op | source)
XLA Modules:
  0.0 190.7 jit_solution(8653924066734771569)
XLA Ops:
  0.0 1.0 copy-done.6
  1.0 0.9 shard_map.82
  1.9 8.9 %collective-permute-start = (bf16[4,128,1280]{2,1,0:T(8,128)(2,1)}, bf16[4,128,1280]{2,1,0:T(8,128)(2,1)}, u32[]{:S(2)}, u32[]{:S(2)}) collective-permute-start(bf16[4,128,1280]{2,1,0:T(8,128)(2,1)} %bitcast.16), channel_id=1, source_target_pairs={{0,8},{8,0},{1,9},{9,1},{2,10},{10,2},{3,11},{11,3},{4,12},{12,4},... | collective-permute-start | bytes 3932168 | tf_op jit(solution)/shard_map/ppermute | solution.py:300
  10.8 4.7 %all-to-all-start = ((bf16[8,32,1280]{2,1,0:T(8,128)(2,1)}), bf16[8,32,1280]{2,1,0:T(8,128)(2,1)S(1)}, u32[]{:S(2)}, u32[]{:S(2)}) async-start(bf16[8,32,1280]{2,1,0:T(8,128)(2,1)} %shard_map.82), calls=%async_computation | async-start | bytes 1310720 | tf_op jit(solution)/shard_map/all_to_all | solution.py:322
  15.5 0.0 collective-permute-done.other
  15.5 0.0 copy-done.1
  15.5 1.0 fusion.refs_2_.out_shard
  16.5 0.0 copy-start.13
  16.5 4.6 %collective-permute-start.1 = (bf16[128,1280]{1,0:T(8,128)(2,1)S(1)}, bf16[128,1280]{1,0:T(8,128)(2,1)S(1)}, u32[]{:S(2)}, u32[]{:S(2)}) collective-permute-start(bf16[128,1280]{1,0:T(8,128)(2,1)S(1)} %fusion.refs_2_.out_shard), channel_id=1, source_target_pairs={{0,1},{1,2},{2,3},{3,4},{4,5},{5,6},{6,7},{7,0},{8,15},{9,8},{10,9... | collective-permute-start | bytes 983048 | tf_op jit(solution)/shard_map/ppermute | solution.py:340
  21.1 0.0 copy-done.5
  21.1 0.0 copy-done.7
  21.1 2.9 %shard_map.83 = (bf16[64,128]{1,0:T(8,128)(2,1)}, bf16[64,128]{1,0:T(8,128)(2,1)}, bf16[2,128,1280]{2,1,0:T(8,128)(2,1)}) custom-call(s32[1]{0:T(128)} %bitcast.core, bf16[2,64,1280]{2,1,0:T(8,128)(2,1)} %tokens.1, bf16[2,64,1280]{2,1,0:T(8,128)(2,1)} %upstream.3, bf16[4,128,1280]{2,1,0:T(8,128)(2,1)S(1)} %bitcast.18, ...), custom_call_target="tpu_custom_call" | custom-call | tf_op jit(solution)/shard_map/pallas_call | solution.py:282
  24.0 12.3 %all-to-all-done = bf16[8,32,1280]{2,1,0:T(8,128)(2,1)S(1)} async-done(((bf16[8,32,1280]{2,1,0:T(8,128)(2,1)}), bf16[8,32,1280]{2,1,0:T(8,128)(2,1)S(1)}, u32[]{:S(2)}, u32[]{:S(2)}) %all-to-all-start) | async-done | bytes 655392 | tf_op jit(solution)/shard_map/all_to_all | solution.py:322
  36.3 0.0 collective-permute-done.1.refs_0_
  36.3 2.5 %collective-permute-start.2 = (bf16[128,1280]{1,0:T(8,128)(2,1)S(1)}, bf16[128,1280]{1,0:T(8,128)(2,1)S(1)}, u32[]{:S(2)}, u32[]{:S(2)}) collective-permute-start(bf16[128,1280]{1,0:T(8,128)(2,1)S(1)} %collective-permute-done.1.refs_0_), channel_id=1, source_target_pairs={{0,1},{1,2},{2,3},{3,4},{4,5},{5,6},{6,7},{7,0},{8,15},{9,8},{10,9... | collective-permute-start | bytes 983048 | tf_op jit(solution)/shard_map/ppermute | solution.py:340
  38.8 0.0 copy-done.13
  38.8 3.9 %shard_map.84 = (bf16[256,1280]{1,0:T(8,128)(2,1)}, bf16[256,128]{1,0:T(8,128)(2,1)}, bf16[256,128]{1,0:T(8,128)(2,1)}, bf16[256,128]{1,0:T(8,128)(2,1)}, bf16[8...) custom-call(s32[1]{0:T(128)} %bitcast.core, s32[2,1,4]{2,1,0:T(1,128)S(1)} %copy-done.13, bf16[256,1280]{1,0:T(8,128)(2,1)S(1)} %bitcast.14, ...), custom_call_target="tpu_custom_call" | custom-call | flops 3000000000 | tf_op jit(solution)/shard_map/pallas_call | solution.py:282
  42.7 6.6 %all-to-all-start.1 = ((bf16[8,256,128]{2,1,0:T(8,128)(2,1)}), bf16[8,256,128]{2,1,0:T(8,128)(2,1)S(1)}, u32[]{:S(2)}, u32[]{:S(2)}) async-start(bf16[8,256,128]{2,1,0:T(8,128)(2,1)} %get-tuple-element.32), calls=%async_computation.1 | async-start | bytes 1048576 | tf_op jit(solution)/shard_map/all_to_all | solution.py:322
  49.4 0.0 collective-permute-done.2.refs_1_
  49.4 4.6 %collective-permute-start.5 = (bf16[128,1280]{1,0:T(8,128)(2,1)S(1)}, bf16[128,1280]{1,0:T(8,128)(2,1)S(1)}, u32[]{:S(2)}, u32[]{:S(2)}) collective-permute-start(bf16[128,1280]{1,0:T(8,128)(2,1)S(1)} %collective-permute-done.2.refs_1_), channel_id=1, source_target_pairs={{0,1},{1,2},{2,3},{3,4},{4,5},{5,6},{6,7},{7,0},{8,15},{9,8},{10,9... | collective-permute-start | bytes 983048 | tf_op jit(solution)/shard_map/ppermute | solution.py:340
  54.0 1.9 %collective-permute-start.3 = (bf16[128,1280]{1,0:T(8,128)(2,1)S(1)}, bf16[128,1280]{1,0:T(8,128)(2,1)S(1)}, u32[]{:S(2)}, u32[]{:S(2)}) collective-permute-start(bf16[128,1280]{1,0:T(8,128)(2,1)S(1)} %collective-permute-done.1.refs_0_), channel_id=1, source_target_pairs={{0,8},{8,0},{1,9},{9,1},{2,10},{10,2},{3,11},{11,3},{4,12},{12,4},... | collective-permute-start | bytes 983048 | tf_op jit(solution)/shard_map/ppermute | solution.py:300
  55.9 2.4 %collective-permute-start.4 = (bf16[128,1280]{1,0:T(8,128)(2,1)S(1)}, bf16[128,1280]{1,0:T(8,128)(2,1)}, u32[]{:S(2)}, u32[]{:S(2)}) collective-permute-start(bf16[128,1280]{1,0:T(8,128)(2,1)S(1)} %collective-permute-done.2.refs_1_), channel_id=1, source_target_pairs={{0,8},{8,0},{1,9},{9,1},{2,10},{10,2},{3,11},{11,3},{4,12},{12,4},... | collective-permute-start | bytes 983048 | tf_op jit(solution)/shard_map/ppermute | solution.py:300
  58.3 4.0 %collective-permute-start.7 = (bf16[128,1280]{1,0:T(8,128)(2,1)S(1)}, bf16[128,1280]{1,0:T(8,128)(2,1)S(1)}, u32[]{:S(2)}, u32[]{:S(2)}) collective-permute-start(bf16[128,1280]{1,0:T(8,128)(2,1)S(1)} %collective-permute-done.2.refs_1_), channel_id=1, source_target_pairs={{0,2},{1,3},{2,4},{3,5},{4,6},{5,7},{6,0},{7,1},{8,14},{9,15},{10,... | collective-permute-start | bytes 983048 | tf_op jit(solution)/shard_map/ppermute | solution.py:340
  62.3 4.7 %collective-permute-done.5.refs_0_ = bf16[128,1280]{1,0:T(8,128)(2,1)S(1)} collective-permute-done((bf16[128,1280]{1,0:T(8,128)(2,1)S(1)}, bf16[128,1280]{1,0:T(8,128)(2,1)S(1)}, u32[]{:S(2)}, u32[]{:S(2)}) %collective-permute-start.5) | collective-permute-done | bytes 327712 | tf_op jit(solution)/shard_map/ppermute | solution.py:340
  67.1 3.5 %collective-permute-start.6 = (bf16[128,1280]{1,0:T(8,128)(2,1)S(1)}, bf16[128,1280]{1,0:T(8,128)(2,1)S(1)}, u32[]{:S(2)}, u32[]{:S(2)}) collective-permute-start(bf16[128,1280]{1,0:T(8,128)(2,1)S(1)} %collective-permute-done.5.refs_0_), channel_id=1, source_target_pairs={{0,8},{8,0},{1,9},{9,1},{2,10},{10,2},{3,11},{11,3},{4,12},{12,4},... | collective-permute-start | bytes 983048 | tf_op jit(solution)/shard_map/ppermute | solution.py:300
  70.6 0.0 collective-permute-done.3.refs_2_
  70.6 0.0 all-to-all-done.1.context
  70.6 0.0 collective-permute-done.4.refs_3_
  70.6 0.0 copy-start.3
  70.6 0.0 copy-start.11
  70.6 0.0 copy-start.12
  70.6 0.0 copy-start.14
  70.6 1.5 shard_map.85.half_states
  72.2 2.6 %collective-permute-done.7.refs_3_ = bf16[128,1280]{1,0:T(8,128)(2,1)S(1)} collective-permute-done((bf16[128,1280]{1,0:T(8,128)(2,1)S(1)}, bf16[128,1280]{1,0:T(8,128)(2,1)S(1)}, u32[]{:S(2)}, u32[]{:S(2)}) %collective-permute-start.7) | collective-permute-done | bytes 327712 | tf_op jit(solution)/shard_map/ppermute | solution.py:340
  74.7 0.0 collective-permute-done.6.refs_1_
  74.7 0.0 copy-done.3
  74.7 0.0 copy-done.11
  74.8 0.0 copy-done.12
  74.8 0.0 copy-done.14
  74.8 3.8 %shard_map.86 = (bf16[256,1280]{1,0:T(8,128)(2,1)S(1)}, bf16[32,1280]{1,0:T(8,128)(2,1)S(1)}, bf16[256,1280]{1,0:T(8,128)(2,1)}, bf16[256,128]{1,0:T(8,128)(2,1)...) custom-call(s32[1]{0:T(128)} %bitcast.core, s32[1]{0:T(128)} %bitcast.1.place, s32[2,1,4]{2,1,0:T(1,128)S(1)} %copy-done.13, ...), custom_call_target="tpu_custom_call" | custom-call | tf_op jit(solution)/shard_map/pallas_call | solution.py:282
  78.6 23.4 %all_to_all.35.pieces = bf16[8,32,1280]{2,1,0:T(8,128)(2,1)S(1)} all-to-all(bf16[8,32,1280]{2,1,0:T(8,128)(2,1)S(1)} %bitcast.20), channel_id=1, replica_groups=mesh['dp'=32,'segment'=2,'mp'=8] {'mp'}, dimensions={0} | all-to-all | bytes 1310720 | tf_op jit(solution)/shard_map/all_to_all | solution.py:322
  102.0 1.2 shard_map.87
  103.2 3.5 %all-to-all-start.3 = ((bf16[8,32,1280]{2,1,0:T(8,128)(2,1)}), bf16[8,32,1280]{2,1,0:T(8,128)(2,1)S(1)}, u32[]{:S(2)}, u32[]{:S(2)}) async-start(bf16[8,32,1280]{2,1,0:T(8,128)(2,1)} %shard_map.87), calls=%async_computation.3 | async-start | bytes 1310720 | tf_op jit(solution)/shard_map/all_to_all | solution.py:322
  106.7 0.0 copy-start.2
  106.7 0.0 copy-start.4
  106.7 0.0 copy-start.8
  106.8 0.0 copy-start.9
  106.8 2.7 %shard_map.89.dec_term = bf16[384,1280]{1,0:T(8,128)(2,1)} custom-call(s32[1]{0:T(128)} %bitcast.core, bf16[256,128]{1,0:T(8,128)(2,1)} %get-tuple-element.43.key_grad, bf16[256,128]{1,0:T(8,128)(2,1)} %get-tuple-element.44.value_grad, bf16[64,128]{1,0:T(8,128)(2,1)} %get-tuple-element.45.context, bf16[256,1280]{1,0:T(8,128)(2,1)} %get-tuple-element.46.normed, ...), custom_call_target="tpu_custom_call" | custom-call | tf_op jit(solution)/shard_map/pallas_call | solution.py:282
  109.5 1.3 collective-permute-start.9
  110.8 14.4 %all-to-all-done.3 = bf16[8,32,1280]{2,1,0:T(8,128)(2,1)S(1)} async-done(((bf16[8,32,1280]{2,1,0:T(8,128)(2,1)}), bf16[8,32,1280]{2,1,0:T(8,128)(2,1)S(1)}, u32[]{:S(2)}, u32[]{:S(2)}) %all-to-all-start.3) | async-done | bytes 655392 | tf_op jit(solution)/shard_map/all_to_all | solution.py:322
  125.2 0.0 copy-done.9
  125.2 0.0 copy-done.10
  125.2 0.0 copy-start
  125.2 1.9 shard_map.88.enc_term
  127.1 4.7 %collective-permute-start.8 = (bf16[384,1280]{1,0:T(8,128)(2,1)S(1)}, bf16[384,1280]{1,0:T(8,128)(2,1)S(1)}, u32[]{:S(2)}, u32[]{:S(2)}) collective-permute-start(bf16[384,1280]{1,0:T(8,128)(2,1)S(1)} %shard_map.88.enc_term), channel_id=1, source_target_pairs={{8,0},{9,1},{10,2},{11,3},{12,4},{13,5},{14,6},{15,7},{24,16},{25,... | collective-permute-start | bytes 2949128 | tf_op jit(solution)/shard_map/ppermute | solution.py:427
  131.8 0.0 collective-permute-done.9.dec_sent
  131.9 2.1 %collective-permute-done.8.enc_sent = bf16[384,1280]{1,0:T(8,128)(2,1)S(1)} collective-permute-done((bf16[384,1280]{1,0:T(8,128)(2,1)S(1)}, bf16[384,1280]{1,0:T(8,128)(2,1)S(1)}, u32[]{:S(2)}, u32[]{:S(2)}) %collective-permute-start.8) | collective-permute-done | bytes 983072 | tf_op jit(solution)/shard_map/ppermute | solution.py:427
  134.0 0.5 shard_map.90
  134.5 19.3 %all_to_all.36.pieces = bf16[8,60,8,128]{3,2,1,0:T(8,128)(2,1)S(1)} all-to-all(bf16[8,60,8,128]{3,2,1,0:T(8,128)(2,1)S(1)} %bitcast.11), channel_id=1, replica_groups={{0,16,128,144,256,272,384,400},{32,48,160,176,288,304,416,432},{64,80,1..., dimensions={0} | all-to-all | bytes 1966080 | tf_op jit(solution)/shard_map/all_to_all | solution.py:322
  153.8 0.1 shard_map.91
  153.9 18.3 %all_to_all.37.pieces = bf16[4,60,8,128]{3,2,1,0:T(8,128)(2,1)S(1)} all-to-all(bf16[4,60,8,128]{3,2,1,0:T(8,128)(2,1)S(1)} %shard_map.91), channel_id=1, replica_groups={{0,32,64,96},{16,48,80,112},{128,160,192,224},{144,176,208,240},{256,28..., dimensions={0} | all-to-all | bytes 983040 | tf_op jit(solution)/shard_map/all_to_all | solution.py:322
  172.2 0.1 shard_map.92
  172.2 17.1 %all_to_all.38 = bf16[8,60,8,128]{3,2,1,0:T(8,128)(2,1)S(1)} all-to-all(bf16[8,60,8,128]{3,2,1,0:T(8,128)(2,1)S(1)} %shard_map.92), channel_id=1, replica_groups={{0,16,128,144,256,272,384,400},{32,48,160,176,288,304,416,432},{64,80,1..., dimensions={0} | all-to-all | bytes 1966080 | tf_op jit(solution)/shard_map/all_to_all | solution.py:322
  189.3 1.4 shard_map.93
  (9 shorter events, 0.0 us)
Async XLA Ops:
  0.0 15.5 %copy-start.1 = (bf16[1,4,128,1280]{3,2,1,0:T(8,128)(2,1)S(1)}, bf16[1,4,128,1280]{3,2,1,0:T(8,128)(2,1)}, u32[]{:S(2)}) copy-start(bf16[1,4,128,1280]{3,2,1,0:T(8,128)(2,1)} %param.13) | copy-start | bytes 3932164
  0.0 1.0 copy-start.6
  1.9 19.2 %copy-start.5 = (f32[3,1280]{1,0:T(4,128)S(1)}, f32[3,1280]{1,0:T(4,128)}, u32[]{:S(2)}) copy-start(f32[3,1280]{1,0:T(4,128)} %gains.7) | copy-start | bytes 46084
  1.9 19.2 %copy-start.7 = (f32[3,1280]{1,0:T(4,128)S(1)}, f32[3,1280]{1,0:T(4,128)}, u32[]{:S(2)}) copy-start(f32[3,1280]{1,0:T(4,128)} %biases.5) | copy-start | bytes 46084
  1.9 13.6 %collective-permute-start = (bf16[4,128,1280]{2,1,0:T(8,128)(2,1)}, bf16[4,128,1280]{2,1,0:T(8,128)(2,1)}, u32[]{:S(2)}, u32[]{:S(2)}) collective-permute-start(bf16[4,128,1280]{2,1,0:T(8,128)(2,1)} %bitcast.16), channel_id=1, source_target_pairs={{0,8},{8,0},{1,9},{9,1},{2,10},{10,2},{3,11},{11,3},{4,12},{12,4},... | collective-permute-start | bytes 3932168 | tf_op jit(solution)/shard_map/ppermute | solution.py:300
  10.8 25.5 %all-to-all-start = ((bf16[8,32,1280]{2,1,0:T(8,128)(2,1)}), bf16[8,32,1280]{2,1,0:T(8,128)(2,1)S(1)}, u32[]{:S(2)}, u32[]{:S(2)}) async-start(bf16[8,32,1280]{2,1,0:T(8,128)(2,1)} %shard_map.82), calls=%async_computation | async-start | bytes 1310720 | tf_op jit(solution)/shard_map/all_to_all | solution.py:322
  16.5 22.3 %copy-start.13 = (s32[2,1,4]{2,1,0:T(1,128)S(1)}, s32[2,1,4]{2,1,0:T(1,128)}, u32[]{:S(2)}) copy-start(s32[2,1,4]{2,1,0:T(1,128)} %frame_lens.1) | copy-start | bytes 100
  16.5 19.8 %collective-permute-start.1 = (bf16[128,1280]{1,0:T(8,128)(2,1)S(1)}, bf16[128,1280]{1,0:T(8,128)(2,1)S(1)}, u32[]{:S(2)}, u32[]{:S(2)}) collective-permute-start(bf16[128,1280]{1,0:T(8,128)(2,1)S(1)} %fusion.refs_2_.out_shard), channel_id=1, source_target_pairs={{0,1},{1,2},{2,3},{3,4},{4,5},{5,6},{6,7},{7,0},{8,15},{9,8},{10,9... | collective-permute-start | bytes 983048 | tf_op jit(solution)/shard_map/ppermute | solution.py:340
  36.3 13.1 %collective-permute-start.2 = (bf16[128,1280]{1,0:T(8,128)(2,1)S(1)}, bf16[128,1280]{1,0:T(8,128)(2,1)S(1)}, u32[]{:S(2)}, u32[]{:S(2)}) collective-permute-start(bf16[128,1280]{1,0:T(8,128)(2,1)S(1)} %collective-permute-done.1.refs_0_), channel_id=1, source_target_pairs={{0,1},{1,2},{2,3},{3,4},{4,5},{5,6},{6,7},{7,0},{8,15},{9,8},{10,9... | collective-permute-start | bytes 983048 | tf_op jit(solution)/shard_map/ppermute | solution.py:340
  42.7 27.8 %all-to-all-start.1 = ((bf16[8,256,128]{2,1,0:T(8,128)(2,1)}), bf16[8,256,128]{2,1,0:T(8,128)(2,1)S(1)}, u32[]{:S(2)}, u32[]{:S(2)}) async-start(bf16[8,256,128]{2,1,0:T(8,128)(2,1)} %get-tuple-element.32), calls=%async_computation.1 | async-start | bytes 1048576 | tf_op jit(solution)/shard_map/all_to_all | solution.py:322
  49.4 17.7 %collective-permute-start.5 = (bf16[128,1280]{1,0:T(8,128)(2,1)S(1)}, bf16[128,1280]{1,0:T(8,128)(2,1)S(1)}, u32[]{:S(2)}, u32[]{:S(2)}) collective-permute-start(bf16[128,1280]{1,0:T(8,128)(2,1)S(1)} %collective-permute-done.2.refs_1_), channel_id=1, source_target_pairs={{0,1},{1,2},{2,3},{3,4},{4,5},{5,6},{6,7},{7,0},{8,15},{9,8},{10,9... | collective-permute-start | bytes 983048 | tf_op jit(solution)/shard_map/ppermute | solution.py:340
  54.0 16.6 %collective-permute-start.3 = (bf16[128,1280]{1,0:T(8,128)(2,1)S(1)}, bf16[128,1280]{1,0:T(8,128)(2,1)S(1)}, u32[]{:S(2)}, u32[]{:S(2)}) collective-permute-start(bf16[128,1280]{1,0:T(8,128)(2,1)S(1)} %collective-permute-done.1.refs_0_), channel_id=1, source_target_pairs={{0,8},{8,0},{1,9},{9,1},{2,10},{10,2},{3,11},{11,3},{4,12},{12,4},... | collective-permute-start | bytes 983048 | tf_op jit(solution)/shard_map/ppermute | solution.py:300
  55.9 14.7 %collective-permute-start.4 = (bf16[128,1280]{1,0:T(8,128)(2,1)S(1)}, bf16[128,1280]{1,0:T(8,128)(2,1)}, u32[]{:S(2)}, u32[]{:S(2)}) collective-permute-start(bf16[128,1280]{1,0:T(8,128)(2,1)S(1)} %collective-permute-done.2.refs_1_), channel_id=1, source_target_pairs={{0,8},{8,0},{1,9},{9,1},{2,10},{10,2},{3,11},{11,3},{4,12},{12,4},... | collective-permute-start | bytes 983048 | tf_op jit(solution)/shard_map/ppermute | solution.py:300
  58.3 16.4 %collective-permute-start.7 = (bf16[128,1280]{1,0:T(8,128)(2,1)S(1)}, bf16[128,1280]{1,0:T(8,128)(2,1)S(1)}, u32[]{:S(2)}, u32[]{:S(2)}) collective-permute-start(bf16[128,1280]{1,0:T(8,128)(2,1)S(1)} %collective-permute-done.2.refs_1_), channel_id=1, source_target_pairs={{0,2},{1,3},{2,4},{3,5},{4,6},{5,7},{6,0},{7,1},{8,14},{9,15},{10,... | collective-permute-start | bytes 983048 | tf_op jit(solution)/shard_map/ppermute | solution.py:340
  67.1 7.7 %collective-permute-start.6 = (bf16[128,1280]{1,0:T(8,128)(2,1)S(1)}, bf16[128,1280]{1,0:T(8,128)(2,1)S(1)}, u32[]{:S(2)}, u32[]{:S(2)}) collective-permute-start(bf16[128,1280]{1,0:T(8,128)(2,1)S(1)} %collective-permute-done.5.refs_0_), channel_id=1, source_target_pairs={{0,8},{8,0},{1,9},{9,1},{2,10},{10,2},{3,11},{11,3},{4,12},{12,4},... | collective-permute-start | bytes 983048 | tf_op jit(solution)/shard_map/ppermute | solution.py:300
  70.6 4.1 %copy-start.3 = (bf16[2,128,1280]{2,1,0:T(8,128)(2,1)S(1)}, bf16[2,128,1280]{2,1,0:T(8,128)(2,1)}, u32[]{:S(2)}) copy-start(bf16[2,128,1280]{2,1,0:T(8,128)(2,1)} %get-tuple-element.33.weights) | copy-start | bytes 1966084
  70.6 4.1 %copy-start.11 = (bf16[64,128]{1,0:T(8,128)(2,1)S(1)}, bf16[64,128]{1,0:T(8,128)(2,1)}, u32[]{:S(2)}) copy-start(bf16[64,128]{1,0:T(8,128)(2,1)} %get-tuple-element.34.token_queries) | copy-start | bytes 49156
  70.6 4.1 %copy-start.12 = (bf16[64,128]{1,0:T(8,128)(2,1)S(1)}, bf16[64,128]{1,0:T(8,128)(2,1)}, u32[]{:S(2)}) copy-start(bf16[64,128]{1,0:T(8,128)(2,1)} %get-tuple-element.35.token_grads) | copy-start | bytes 49156
  70.6 4.1 %copy-start.14 = (s32[2,1,4]{2,1,0:T(1,128)S(1)}, s32[2,1,4]{2,1,0:T(1,128)}, u32[]{:S(2)}) copy-start(s32[2,1,4]{2,1,0:T(1,128)} %token_lens.1) | copy-start | bytes 100
  103.2 22.0 %all-to-all-start.3 = ((bf16[8,32,1280]{2,1,0:T(8,128)(2,1)}), bf16[8,32,1280]{2,1,0:T(8,128)(2,1)S(1)}, u32[]{:S(2)}, u32[]{:S(2)}) async-start(bf16[8,32,1280]{2,1,0:T(8,128)(2,1)} %shard_map.87), calls=%async_computation.3 | async-start | bytes 1310720 | tf_op jit(solution)/shard_map/all_to_all | solution.py:322
  106.7 18.5 %copy-start.2 = (bf16[256,1280]{1,0:T(8,128)(2,1)S(1)}, bf16[256,1280]{1,0:T(8,128)(2,1)}, u32[]{:S(2)}) copy-start(bf16[256,1280]{1,0:T(8,128)(2,1)} %get-tuple-element.42.normed) | copy-start | bytes 1966084
  106.7 18.5 %copy-start.4 = (f32[2,256,256]{2,1,0:T(8,128)S(1)}, f32[2,256,256]{2,1,0:T(8,128)}, u32[]{:S(2)}) copy-start(f32[2,256,256]{2,1,0:T(8,128)} %get-tuple-element.40.probs) | copy-start | bytes 1572868
  106.7 18.5 %copy-start.8 = (bf16[256,128]{1,0:T(8,128)(2,1)S(1)}, bf16[256,128]{1,0:T(8,128)(2,1)}, u32[]{:S(2)}) copy-start(bf16[256,128]{1,0:T(8,128)(2,1)} %get-tuple-element.38.queries) | copy-start | bytes 196612
  106.8 18.5 %copy-start.9 = (bf16[256,128]{1,0:T(8,128)(2,1)S(1)}, bf16[256,128]{1,0:T(8,128)(2,1)}, u32[]{:S(2)}) copy-start(bf16[256,128]{1,0:T(8,128)(2,1)} %get-tuple-element.39.values) | copy-start | bytes 196612
  106.8 18.5 %copy-start.10 = (bf16[256,128]{1,0:T(8,128)(2,1)S(1)}, bf16[256,128]{1,0:T(8,128)(2,1)}, u32[]{:S(2)}) copy-start(bf16[256,128]{1,0:T(8,128)(2,1)} %get-tuple-element.41.context) | copy-start | bytes 196612
  109.5 22.3 %collective-permute-start.9 = (bf16[384,1280]{1,0:T(8,128)(2,1)}, bf16[384,1280]{1,0:T(8,128)(2,1)S(1)}, u32[]{:S(2)}, u32[]{:S(2)}) collective-permute-start(bf16[384,1280]{1,0:T(8,128)(2,1)} %shard_map.89.dec_term), channel_id=1, source_target_pairs={{0,8},{1,9},{2,10},{3,11},{4,12},{5,13},{6,14},{7,15},{16,24},{17,... | collective-permute-start | bytes 2949128 | tf_op jit(solution)/shard_map/ppermute | solution.py:426
  125.2 8.7 %copy-start = (bf16[384,1280]{1,0:T(8,128)(2,1)S(1)}, bf16[384,1280]{1,0:T(8,128)(2,1)}, u32[]{:S(2)}) copy-start(bf16[384,1280]{1,0:T(8,128)(2,1)} %shard_map.89.dec_term) | copy-start | bytes 2949124
  127.1 6.8 %collective-permute-start.8 = (bf16[384,1280]{1,0:T(8,128)(2,1)S(1)}, bf16[384,1280]{1,0:T(8,128)(2,1)S(1)}, u32[]{:S(2)}, u32[]{:S(2)}) collective-permute-start(bf16[384,1280]{1,0:T(8,128)(2,1)S(1)} %shard_map.88.enc_term), channel_id=1, source_target_pairs={{8,0},{9,1},{10,2},{11,3},{12,4},{13,5},{14,6},{15,7},{24,16},{25,... | collective-permute-start | bytes 2949128 | tf_op jit(solution)/shard_map/ppermute | solution.py:427
